TPU v7x, 128 devices: a whole 4x4x4 slice. The times are simulated.
128 devices in a mesh: dp: 8 (over z, y_lo), neg: 16 (over x, y_hi, core).
Axes of the slice: x: 4, y: 4 (y_hi: 2, y_lo: 2; y = y_hi * 2 + y_lo), z: 4, core: 2. Of those that a mesh axis runs over, the one named last changes fastest.
Arguments:
- query_emb: bfloat16 [512, 32, 128], P(('dp', 'neg')), may hold values from -6 to 6
- positive: int32 [512], P(('dp', 'neg')), may hold values from 0 to 127
- passage_emb: bfloat16 [128, 512, 128], P(('dp', 'neg')), may hold values from -6 to 6
- lengths: int32 [128], P(('dp', 'neg')), may hold values from 256 to 512
- residual: bfloat16 [65536, 1024], P(('dp', 'neg')), may hold values from -6 to 6
- context: bfloat16 [65536, 1024], P(('dp', 'neg')), may hold values from -6 to 6
- out_proj: bfloat16 [1024, 1024], replicated, may hold values from -0.1875 to 0.1875
- norm_gain: float32 [1024], replicated, may hold values from 0.5 to 1.5
- colbert_proj: bfloat16 [1024, 128], replicated, may hold values from -0.1875 to 0.1875
Outputs:
- loss: float32 [], replicated
- query_grad: float32 [512, 32, 128], P(('dp', 'neg'))
- residual_grad: bfloat16 [65536, 1024], P(('dp', 'neg'))
- context_grad: bfloat16 [65536, 1024], P(('dp', 'neg'))
- out_proj_grad: float32 [1024, 1024], replicated
- colbert_grad: float32 [1024, 128], replicated
- gain_grad: float32 [1024], replicated
Inputs may be any that keep to these rules, and one draw needn't show every extreme that they name: A passage's first lengths[p] token slots are real, the rest padding.
All inputs are finite; a program needn't handle non-finite values.
Results may differ from a plain program's by a relative error of at most 0.0065.
Values may be sent and summed in bfloat16 or wider, within the bound.
No kernel may reach another device: no remote copies, remote signals or barrier semaphores. Data moves between devices by JAX's collectives and lax.ppermute only.
A program may use at most 64 MiB of HBM per device.

v0:
```python
import math

import jax
import jax.numpy as jnp
from jax import lax
from jax.sharding import Mesh
from jax.sharding import PartitionSpec as P

NEG = ("neg_0", "neg_1", "neg_2")
DP_NEG = ("dp", "neg_0", "neg_1", "neg_2")


def joined_along(pieces, dim):
    pieces = jnp.moveaxis(pieces, 0, dim)
    shape = pieces.shape
    return pieces.reshape(*shape[:dim], shape[dim] * shape[dim + 1], *shape[dim + 2 :])


def from_everyone(array, axis):
    copies = jnp.broadcast_to(array, (lax.axis_size(axis), *array.shape))
    return lax.all_to_all(copies, axis, split_axis=0, concat_axis=0, tiled=True)


def gathered_copies(array, axis, dim):
    return joined_along(from_everyone(array, axis), dim)


def collected_together(array, axis):
    leaves = jax.tree.leaves(array)
    order = sorted(range(len(leaves)), key=lambda k: -leaves[k].size)
    width = (1, *leaves[order[0]].shape)[-1]
    lines = [
        jnp.pad(leaves[k].reshape(-1), (0, -leaves[k].size % width)).reshape(-1, width)
        for k in order
    ]
    both, at, found = (from_everyone(jnp.concatenate(lines), axis), 0, {})
    for k, line in zip(order, lines):
        slab = both[:, at : at + len(line)].reshape(len(both), -1)
        found[k] = slab[:, : leaves[k].size].reshape(-1, *leaves[k].shape)
        at += len(line)
    numbers = iter(range(len(leaves)))
    return jax.tree.map(lambda _: found[next(numbers)], array)


def joined_by_halves(pieces, combine):
    while len(jax.tree.leaves(pieces)[0]) > 1:
        pieces = jax.vmap(combine)(
            *(jax.tree.map(lambda part: part[side::2], pieces) for side in (0, 1))
        )
    return jax.tree.map(lambda part: part[0], pieces)


def combined_all(array, axis, combine):
    pieces = collected_together(array, axis)
    return joined_by_halves(pieces, combine)


def split_up(array, dim, size):
    before, after = (array.shape[:dim], array.shape[dim + 1 :])
    return jnp.moveaxis(array.reshape(*before, size, -1, *after), dim, 0)


def summed_rows(array, chips, core, dim):
    sizes = (lax.axis_size(chips), lax.axis_size(core))
    pieces = split_up(array, dim, sizes[0] * sizes[1])
    inside = pieces.shape[1:]
    pieces = pieces.reshape(*sizes, *inside).swapaxes(0, 1).reshape(-1, *inside)
    pieces = lax.psum_scatter(pieces, core, scatter_dimension=0, tiled=True)
    return lax.psum_scatter(pieces, chips, scatter_dimension=0, tiled=True)[0]


def sum_at_owner(array, axis, dim):
    size = lax.axis_size(axis)
    pieces = lax.all_to_all(split_up(array, dim, size), axis, 0, 0, tiled=True)
    return jnp.sum(pieces, axis=0)


def block_plan(query_count, query_len):
    return math.gcd(query_count, max(1, 2048 // query_len))


def masked_scores(query_block, passage_one, usable):
    scores = jnp.einsum("rd,jd->rj", query_block, passage_one, preferred_element_type=jnp.float32)
    return jnp.where(usable, scores, -1e30)


def tile_forward(query_tokens, query_pos, passage_tokens, passage_len, passage_ids):
    query_count, query_len, emb_width = query_tokens.shape
    per_block = block_plan(query_count, query_len)
    query_blocks = query_tokens.reshape(query_count // per_block, per_block * query_len, emb_width)

    def per_passage(inputs):
        passage_one, length = inputs
        usable = (jnp.arange(passage_one.shape[0]) < length)[None, :]

        def per_query(query_block):
            masked = masked_scores(query_block, passage_one, usable)
            highest = jnp.max(masked, axis=1, keepdims=True)
            return highest[:, 0] + jnp.log(jnp.sum(jnp.exp(masked - highest), axis=1))

        inner_lse = lax.map(per_query, query_blocks).reshape(query_count, query_len)
        shifted = inner_lse - jnp.log(length.astype(jnp.float32))
        return (inner_lse, jnp.sum(shifted, axis=1))

    inner_all, similar = lax.map(per_passage, (passage_tokens, passage_len))
    similar = similar.T
    is_positive = passage_ids[None, :] == query_pos[:, None]
    highest = jnp.max(similar, axis=1)
    exp_total = jnp.sum(jnp.exp(similar - highest[:, None]), axis=1)
    positive_score = jnp.sum(jnp.where(is_positive, similar, 0.0), axis=1)
    return (inner_all, similar, is_positive, (highest, exp_total, positive_score))


def combine_totals(earlier, later):
    highest = jnp.maximum(earlier[0], later[0])
    exp_total = earlier[1] * jnp.exp(earlier[0] - highest) + later[1] * jnp.exp(later[0] - highest)
    return (highest, exp_total, earlier[2] + later[2])


def finish_rows(similar, is_positive, totals, own_block, query_dev):
    log_total = totals[0] + jnp.log(totals[1])
    coefficient = jnp.exp(similar - log_total[:, None]) - is_positive.astype(jnp.float32)
    own_terms = lax.dynamic_slice_in_dim(log_total - totals[2], own_block * query_dev, query_dev)
    return (coefficient, jnp.sum(own_terms))


def tile_backward(query_tokens, passage_tokens, passage_len, inner_all, coefficient):
    query_count, query_len, emb_width = query_tokens.shape
    per_block = block_plan(query_count, query_len)
    block_count = query_count // per_block
    query_blocks = query_tokens.reshape(block_count, per_block * query_len, emb_width)

    def per_passage(running, inputs):
        passage_one, length, inner_lse, column = inputs
        usable = (jnp.arange(passage_one.shape[0]) < length)[None, :]

        def per_query(pieces):
            query_block, inner_block, column_block = pieces
            masked = masked_scores(query_block, passage_one, usable)
            spread = jnp.exp(masked - inner_block.reshape(-1)[:, None]).reshape(
                per_block, query_len, -1
            )
            weight = (
                (spread * column_block[:, None, None])
                .reshape(per_block * query_len, -1)
                .astype(jnp.bfloat16)
            )
            query_part = jnp.dot(weight, passage_one, preferred_element_type=jnp.float32)
            passage_part = jnp.einsum(
                "rj,rd->jd", weight, query_block, preferred_element_type=jnp.float32
            )
            return (query_part, passage_part)

        query_parts, passage_parts = lax.map(
            per_query,
            (
                query_blocks,
                inner_lse.reshape(block_count, per_block, query_len),
                column.reshape(block_count, per_block),
            ),
        )
        return (running + query_parts.reshape(running.shape), jnp.sum(passage_parts, axis=0))

    start = jnp.zeros((query_count * query_len, emb_width), jnp.float32)
    query_sum, passage_sum = lax.scan(
        per_passage, start, (passage_tokens, passage_len, inner_all, coefficient.T)
    )
    return (query_sum.reshape(query_count, query_len, emb_width), passage_sum)


def window_rows(resid_rows, context_rows, grad_rows, out_proj, norm_gain, colbert_proj):
    hidden = resid_rows.astype(jnp.float32) + jnp.dot(
        context_rows, out_proj, preferred_element_type=jnp.float32
    )
    row_mean = jnp.mean(hidden, axis=1, keepdims=True)
    centred = hidden - row_mean
    variance = jnp.mean(centred * centred, axis=1, keepdims=True)
    inv_std = 1.0 / jnp.sqrt(variance + 1e-05)
    normed = centred * inv_std
    scaled = (normed * norm_gain).astype(jnp.bfloat16)
    colbert_part = jnp.dot(scaled.T, grad_rows, preferred_element_type=jnp.float32)
    scaled_grad = jnp.dot(grad_rows, colbert_proj.T, preferred_element_type=jnp.float32)
    gain_part = jnp.sum(scaled_grad * normed, axis=0)
    gained = scaled_grad * norm_gain
    hidden_grad = (
        inv_std
        * (
            gained
            - jnp.mean(gained, axis=1, keepdims=True)
            - normed * jnp.mean(gained * normed, axis=1, keepdims=True)
        )
    ).astype(jnp.bfloat16)
    context_grad = jnp.dot(hidden_grad, out_proj.T, preferred_element_type=jnp.float32).astype(
        jnp.bfloat16
    )
    proj_part = jnp.dot(context_rows.T, hidden_grad, preferred_element_type=jnp.float32)
    return (hidden_grad, context_grad, proj_part, colbert_part, gain_part)


def body(
    query_emb, positive, passage_emb, lengths, residual, context, out_proj, norm_gain, colbert_proj
):
    query_dev = query_emb.shape[0]
    passage_dev = passage_emb.shape[0]
    neg_size = lax.axis_size(NEG)
    neg_place = lax.axis_index(NEG)
    query_tokens, query_pos = (
        gathered_copies(query_emb, NEG, 0),
        gathered_copies(positive, NEG, 0),
    )
    passage_tokens, passage_len = (
        gathered_copies(passage_emb, "dp", 0),
        gathered_copies(lengths, "dp", 0),
    )
    position = jnp.arange(passage_tokens.shape[0], dtype=jnp.int32)
    passage_ids = (
        position // passage_dev * neg_size + neg_place
    ) * passage_dev + position % passage_dev
    inner_all, similar, is_positive, stats = tile_forward(
        query_tokens, query_pos, passage_tokens, passage_len, passage_ids
    )
    totals = combined_all(stats, NEG, combine_totals)
    coefficient, loss_part = finish_rows(similar, is_positive, totals, neg_place, query_dev)
    query_sum, passage_sum = tile_backward(
        query_tokens, passage_tokens, passage_len, inner_all, coefficient
    )
    query_grad = summed_rows(query_sum, ("neg_0", "neg_1"), "neg_2", 0)
    emb_sum = sum_at_owner(passage_sum, "dp", 0)
    emb_grad = emb_sum.astype(jnp.bfloat16).reshape(
        passage_dev * emb_sum.shape[1], emb_sum.shape[2]
    )
    residual_grad, context_grad, proj_part, colbert_part, gain_part = window_rows(
        residual, context, emb_grad, out_proj, norm_gain, colbert_proj
    )
    out_proj_grad, colbert_grad, gain_grad, loss_total = lax.psum(
        (proj_part, colbert_part, gain_part, loss_part), DP_NEG
    )
    loss = loss_total / (query_dev * lax.axis_size("dp") * neg_size)
    return (loss, query_grad, residual_grad, context_grad, out_proj_grad, colbert_grad, gain_grad)


def solution(mesh):
    split = Mesh(mesh.devices.reshape(mesh.shape["dp"], 4, 2, 2), ("dp", "neg_0", "neg_1", "neg_2"))
    placed = (
        P(DP_NEG, None, None),
        P(DP_NEG),
        P(DP_NEG, None, None),
        P(DP_NEG),
        P(DP_NEG, None),
        P(DP_NEG, None),
        P(),
        P(),
        P(),
    )
    return jax.shard_map(
        body,
        mesh=split,
        in_specs=placed,
        out_specs=(P(), P(DP_NEG, None, None), P(DP_NEG, None), P(DP_NEG, None), P(), P(), P()),
        check_vma=False,
    )
```

profile of v0, /device:TPU:1, one launch (start us, length us, event | category | flops | bytes accessed | tf_op | source)
XLA Modules:
  0.0 411.8 jit_solution(12545838481604680773)
XLA Ops:
  8.8 11.7 %all_to_all.32 = s32[8,1,1]{2,1,0:T(1,128)S(1)} all-to-all(s32[8,1,1]{2,1,0:T(1,128)S(1)} %broadcast_in_dim.95), channel_id=1, replica_groups=mesh['dp'=8,'neg_0'=4,'neg_1'=2,'neg_2'=2] {'dp'}, dimensions={0} | all-to-all | bytes 64 | tf_op jit(solution)/shard_map/all_to_all | solution.py:21
  21.2 15.5 %all_to_all.33 = s32[16,1,4]{2,1,0:T(1,128)S(1)} all-to-all(s32[16,1,4]{2,1,0:T(1,128)S(1)} %broadcast_in_dim.98), channel_id=1, replica_groups=mesh['dp'=8,'neg_0'=4,'neg_1'=2,'neg_2'=2] {'neg_0','neg_1','neg_2'}, dimensions={0} | all-to-all | bytes 512 | tf_op jit(solution)/shard_map/all_to_all | solution.py:21
  37.5 14.3 %all_to_all.34 = bf16[16,4,32,128]{3,2,1,0:T(8,128)(2,1)S(1)} all-to-all(bf16[16,4,32,128]{3,2,1,0:T(8,128)(2,1)S(1)} %broadcast_in_dim.97), channel_id=1, replica_groups=mesh['dp'=8,'neg_0'=4,'neg_1'=2,'neg_2'=2] {'neg_0','neg_1','neg_2'}, dimensions={0} | all-to-all | bytes 1048576 | tf_op jit(solution)/shard_map/all_to_all | solution.py:21
  51.8 2.0 broadcast_in_dim.96
  53.9 4.2 %all-to-all-start.1 = ((bf16[8,1,512,128]{3,2,1,0:T(8,128)(2,1)}), bf16[8,1,512,128]{3,2,1,0:T(8,128)(2,1)}, u32[]{:S(2)}, u32[]{:S(2)}) async-start(bf16[8,1,512,128]{3,2,1,0:T(8,128)(2,1)} %broadcast_in_dim.96), calls=%async_computation.1 | async-start | bytes 2097152 | tf_op jit(solution)/shard_map/all_to_all | solution.py:21
  59.7 12.5 %all-to-all-done.1 = bf16[8,1,512,128]{3,2,1,0:T(8,128)(2,1)} async-done(((bf16[8,1,512,128]{3,2,1,0:T(8,128)(2,1)}), bf16[8,1,512,128]{3,2,1,0:T(8,128)(2,1)}, u32[]{:S(2)}, u32[]{:S(2)}) %all-to-all-start.1) | async-done | bytes 1048608 | tf_op jit(solution)/shard_map/all_to_all | solution.py:21
  72.2 37.5 %while.24 = (s32[]{:T(128)}, f32[8,64,32]{2,1,0:T(8,128)S(1)}, f32[8,64]{1,0:T(8,128)S(1)}, s32[8]{0:T(128)S(1)}, bf16[8,512,128]{2,1,0:T(8,128)(2,1)}, /*index=...) while((s32[]{:T(128)}, f32[8,64,32]{2,1,0:T(8,128)S(1)}, f32[8,64]{1,0:T(8,128)S(1)}, ...), condition=%wide.region_4.5_spmd, body=%wide.region_0.4_spmd.sunk | while | flops 273680832 | bytes 9210765 | solution.py:105
  73.4 1.6 select_reduce_fusion.2
  78.1 1.6 select_reduce_fusion.2
  82.8 1.6 select_reduce_fusion.2
  87.5 1.6 select_reduce_fusion.2
  92.2 1.6 select_reduce_fusion.2
  96.9 1.6 select_reduce_fusion.2
  101.5 1.6 select_reduce_fusion.2
  106.2 1.6 select_reduce_fusion.2
  110.5 6.1 %all-to-all-start.4 = ((f32[16,1,192]{2,1,0:T(1,128)}), f32[16,1,192]{2,1,0:T(1,128)S(1)}, u32[]{:S(2)}, u32[]{:S(2)}) async-start(f32[16,1,192]{2,1,0:T(1,128)} %reshape.178), calls=%async_computation.4 | async-start | bytes 32768 | tf_op jit(solution)/shard_map/all_to_all | solution.py:21
  116.6 7.3 %all-to-all-done.4 = f32[16,1,192]{2,1,0:T(1,128)S(1)} async-done(((f32[16,1,192]{2,1,0:T(1,128)}), f32[16,1,192]{2,1,0:T(1,128)S(1)}, u32[]{:S(2)}, u32[]{:S(2)}) %all-to-all-start.4) | async-done | bytes 12320 | tf_op jit(solution)/shard_map/all_to_all | solution.py:21
  125.7 77.7 %while.25 = (s32[]{:T(128)}, f32[2048,128]{1,0:T(8,128)}, f32[8,512,128]{2,1,0:T(8,128)}, s32[8]{0:T(128)S(1)}, bf16[8,512,128]{2,1,0:T(8,128)(2,1)}, /*index=5*...) while((s32[]{:T(128)}, f32[2048,128]{1,0:T(8,128)}, ...), condition=%wide.region_11.12_spmd.clone, body=%wide.region_10.11_spmd.clone.sunk | while | flops 810025472 | bytes 18427300 | solution.py:165
  127.2 1.9 multiply_convert_fusion.5
  129.1 1.3 copy-done.1
  130.4 1.4 fusion.55
  131.8 3.3 convolution_add_fusion.2
  136.6 1.9 multiply_convert_fusion.5
  138.6 1.3 copy-done.1
  139.9 1.4 fusion.55
  141.3 3.6 convolution_add_fusion.2
  146.4 1.9 multiply_convert_fusion.5
  148.3 1.3 copy-done.1
  149.6 1.4 fusion.55
  151.0 3.6 convolution_add_fusion.2
  156.1 1.9 multiply_convert_fusion.5
  158.1 1.3 copy-done.1
  159.4 1.4 fusion.55
  160.8 3.6 convolution_add_fusion.2
  165.9 1.9 multiply_convert_fusion.5
  167.8 1.3 copy-done.1
  169.1 1.4 fusion.55
  170.6 3.6 convolution_add_fusion.2
  175.6 1.9 multiply_convert_fusion.5
  177.6 1.3 copy-done.1
  178.9 1.4 fusion.55
  180.3 3.6 convolution_add_fusion.2
  185.4 1.9 multiply_convert_fusion.5
  187.3 1.3 copy-done.1
  188.6 1.4 fusion.55
  190.0 3.6 convolution_add_fusion.2
  195.1 1.9 multiply_convert_fusion.5
  197.1 1.3 copy-done.1
  198.4 1.4 fusion.55
  199.8 3.6 convolution_add_fusion.2
  203.4 4.3 %all-to-all-start.5 = ((f32[8,1,512,128]{3,2,1,0:T(8,128)}), f32[8,1,512,128]{3,2,1,0:T(8,128)}, u32[]{:S(2)}, u32[]{:S(2)}) async-start(f32[8,1,512,128]{3,2,1,0:T(8,128)} %bitcast.21), calls=%async_computation.7 | async-start | bytes 4194304 | tf_op jit(solution)/shard_map/all_to_all | solution.py:74
  207.8 4.2 %fusion.28 = (f32[512]{0:T(512)S(1)}, f32[512,1024]{1,0:T(8,128)}) fusion(bf16[512,1024]{1,0:T(8,128)(2,1)} %param.18, bf16[1024,1024]{1,0:T(8,128)(2,1)S(1)} %copy-done, bf16[512,1024]{1,0:T(8,128)(2,1)} %param.17), kind=kOutput, calls=%fused_computation.66 | convolution fusion | flops 1075314176 | bytes 6293504 | tf_op jit(solution)/shard_map/dot_general | solution.py:172
  212.0 1.1 copy.24
  213.2 2.0 multiply_reduce_fusion.2
  215.2 19.3 %all-to-all-done.5 = f32[8,1,512,128]{3,2,1,0:T(8,128)} async-done(((f32[8,1,512,128]{3,2,1,0:T(8,128)}), f32[8,1,512,128]{3,2,1,0:T(8,128)}, u32[]{:S(2)}, u32[]{:S(2)}) %all-to-all-start.5) | async-done | bytes 2097184 | tf_op jit(solution)/shard_map/all_to_all | solution.py:74
  234.5 1.7 reduce_sum.109
  236.2 2.6 multiply_reduce_fusion
  238.8 1.6 fusion.15
  241.0 1.0 copy-done.4
  242.0 3.3 convolution_bitcast_fusion.1
  246.8 64.3 %all-reduce = (f32[]{:T(128)}, f32[1024]{0:T(1024)}) all-reduce(f32[]{:T(128)} %dynamic-slice_reduce_fusion, f32[1024]{0:T(1024)S(1)} %get-tuple-element.181), channel_id=1, replica_groups=mesh['dp'=8,'neg_0'=4,'neg_1'=2,'neg_2'=2] {'dp','neg_0','neg_1','neg_2'}, use_global_device_ids=true, to_apply=%region_9.10 | all-reduce | flops 1025 | bytes 8200 | tf_op jit(solution)/shard_map/psum | solution.py:235
  311.7 3.5 convolution_convert_fusion
  315.2 81.8 %all-reduce.4.cloned.1.call-done = (f32[1024,1024]{0,1:T(8,128)}, f32[1024,128]{1,0:T(8,128)}) async-done(((f32[1024,1024]{0,1:T(8,128)}, f32[1024,128]{1,0:T(8,128)}), (f32[1024,1024]{0,1:T(8,128)}, f32[1024,128]{1,0:T(8,128)})) %all-reduce.4.cloned.1.call-update) | async-done | bytes 4718608 | tf_op jit(solution)/shard_map/psum | solution.py:235
  397.0 5.4 %copy.25 = f32[1024,1024]{1,0:T(8,128)} copy(f32[1024,1024]{0,1:T(8,128)} %get-tuple-element.216) | data formatting | bytes 8388608
  (212 shorter events, 39.0 us)
Async XLA Ops:
  8.0 199.8 %copy-start = (bf16[1024,1024]{1,0:T(8,128)(2,1)S(1)}, bf16[1024,1024]{1,0:T(8,128)(2,1)}, u32[]{:S(2)}) copy-start(bf16[1024,1024]{1,0:T(8,128)(2,1)} %param.19) | copy-start | bytes 6291460
  53.9 18.3 %all-to-all-start.1 = ((bf16[8,1,512,128]{3,2,1,0:T(8,128)(2,1)}), bf16[8,1,512,128]{3,2,1,0:T(8,128)(2,1)}, u32[]{:S(2)}, u32[]{:S(2)}) async-start(bf16[8,1,512,128]{3,2,1,0:T(8,128)(2,1)} %broadcast_in_dim.96), calls=%async_computation.1 | async-start | bytes 2097152 | tf_op jit(solution)/shard_map/all_to_all | solution.py:21
  110.5 13.4 %all-to-all-start.4 = ((f32[16,1,192]{2,1,0:T(1,128)}), f32[16,1,192]{2,1,0:T(1,128)S(1)}, u32[]{:S(2)}, u32[]{:S(2)}) async-start(f32[16,1,192]{2,1,0:T(1,128)} %reshape.178), calls=%async_computation.4 | async-start | bytes 32768 | tf_op jit(solution)/shard_map/all_to_all | solution.py:21
  129.1 1.3 copy-start.1
  138.6 1.3 copy-start.1
  148.3 1.3 copy-start.1
  158.0 1.3 copy-start.1
  167.8 1.3 copy-start.1
  177.6 1.3 copy-start.1
  187.3 1.3 copy-start.1
  197.1 1.3 copy-start.1
  203.4 31.1 %all-to-all-start.5 = ((f32[8,1,512,128]{3,2,1,0:T(8,128)}), f32[8,1,512,128]{3,2,1,0:T(8,128)}, u32[]{:S(2)}, u32[]{:S(2)}) async-start(f32[8,1,512,128]{3,2,1,0:T(8,128)} %bitcast.21), calls=%async_computation.7 | async-start | bytes 4194304 | tf_op jit(solution)/shard_map/all_to_all | solution.py:74
  207.7 37.7 %reduce-scatter.3.cloned.1.call-start = ((), (), s32[]{:S(2)}) async-start(), calls=%async_computation.8 | async-start | bytes 1572864 | tf_op jit(solution)/shard_map/reduce_scatter | solution.py:68
  207.8 4.2 %copy-start.2 = (f32[2048,128]{1,0:T(8,128)S(1)}, f32[2048,128]{1,0:T(8,128)}, u32[]{:S(2)}) copy-start(f32[2048,128]{1,0:T(8,128)} %get-tuple-element.124) | copy-start | bytes 3145732
  213.1 183.9 %all-reduce.4.cloned.1.call-start = ((), (), s32[]{:S(2)}) async-start(), calls=%async_computation.10 | async-start | bytes 9437184 | tf_op jit(solution)/shard_map/psum | solution.py:235
  213.2 23.0 %copy-start.7 = (bf16[1024,128]{1,0:T(8,128)(2,1)S(1)}, bf16[1024,128]{1,0:T(8,128)(2,1)}, u32[]{:S(2)}) copy-start(bf16[1024,128]{1,0:T(8,128)(2,1)} %param.21) | copy-start | bytes 786436
  213.2 23.0 %copy-start.8 = (f32[1024]{0:T(1024)S(1)}, f32[1024]{0:T(1024)}, u32[]{:S(2)}) copy-start(f32[1024]{0:T(1024)} %param.20) | copy-start | bytes 12292
  236.2 2.6 copy-start.3
  240.4 1.6 copy-start.5
  241.0 1.0 copy-start.4
  245.3 157.1 %reduce-scatter.5.cloned.1.call-start = ((), (), s32[]{:S(2)}) async-start(), calls=%async_computation.9 | async-start | bytes 589824 | tf_op jit(solution)/shard_map/reduce_scatter | solution.py:69
  397.0 5.4 %copy-start.6 = (f32[1024,128]{1,0:T(8,128)S(1)}, f32[1024,128]{1,0:T(8,128)}, u32[]{:S(2)}) copy-start(f32[1024,128]{1,0:T(8,128)} %get-tuple-element.394) | copy-start | bytes 1572868
Sparse Core Ops, SparseCore 0:
  213.2 9.5 reduce-scatter.2
  250.7 65.2 reduce-scatter.4
Sparse Core Ops, SparseCore 1:
  245.4 151.5 all-reduce.3
where the time goes:
time: 413 us; the launch traced here: 412 us
  waiting for transfers between devices  122 us (30%)
  blocking collectives  106 us (26%)
  matrix products  83.4 us (20%)
  local copies, waits for them, and re-layouts  37.3 us (9%)
  other arithmetic  24.4 us (6%)
  between operations  18.3 us (4%)
  starting transfers between devices  14.7 us (4%)
  loops' own time  6.1 us (1%)
    psum x1, waiting for transfers between devices, body(): lax.psum((proj_part, colbert_part, gain_part, loss_part), DP_NEG)  81.8 us
    psum x1, blocking collectives, body(): lax.psum((proj_part, colbert_part, gain_part, loss_part), DP_NEG)  64.3 us
    all_to_all x3, blocking collectives, from_everyone(): return lax.all_to_all(copies, axis, split_axis=0, concat_axis=0, tiled=True)  41.5 us
    dot_general x8, matrix products, per_query(): jnp.dot(weight, passage_one, preferred_element_type=jnp.float32)  28.6 us
    dot_general x16, matrix products, masked_scores(): jnp.einsum('rd,jd->rj', query_block, passage_one, preferred_element_type=...  28.3 us
    all_to_all x2, waiting for transfers between devices, from_everyone(): return lax.all_to_all(copies, axis, split_axis=0, concat_axis=0, tiled=True)  19.8 us
    all_to_all x1, waiting for transfers between devices, sum_at_owner(): pieces = lax.all_to_all(split_up(array, dim, size), axis, 0, 0, tiled=True)  19.3 us
    dot_general x8, matrix products, per_query(): jnp.einsum('rj,rd->jd', weight, query_block, preferred_element_type=jnp.f...  11.3 us
  transfers between devices with their start and end apart: 6, of which 4 were waited for; matrix products, arithmetic and copies ran while one was open for 7% of the time, Pallas kernels for 0%

commit v1 on v0

v1 whole, which is shorter than its diff:
```python
import functools

import jax
import jax.numpy as jnp
from jax import lax
from jax.experimental import pallas as pl
from jax.experimental.pallas import tpu as pltpu
from jax.sharding import Mesh
from jax.sharding import PartitionSpec as P

DP = ("dp_0", "dp_1")
NEG = ("neg_0", "neg_1", "neg_2")
CROSS = ("neg_0", "neg_1")
CORE = "neg_2"
DP_NEG = DP + NEG
BF16 = jnp.bfloat16
F32 = jnp.float32
EXTRA = 8
LEAST = 256
MIB = 1 << 20


def dot(a, b, dims, precision=None):
    return lax.dot_general(a, b, (dims, ((), ())), precision=precision, preferred_element_type=F32)


def token_query(rows, queries, query_len, transposed=False):
    shape = (queries, rows) if transposed else (rows, queries)
    row = lax.broadcasted_iota(jnp.int32, shape, 1 if transposed else 0)
    query = lax.broadcasted_iota(jnp.int32, shape, 0 if transposed else 1)
    first = query * query_len
    return ((row >= first) & (row < first + query_len)).astype(F32)


def whole(shape):
    return pl.BlockSpec(shape, lambda *_: (0,) * len(shape))


def forward_kernel(
    query_len, group, q_ref, p_ref, ids_ref, exp_ref, mix_ref, inv_ref, sim_ref, stats_ref, lse_ref
):
    passage = pl.program_id(0)
    parts, q_rows, width = q_ref.shape[0], q_ref.shape[1] - EXTRA, q_ref.shape[2]
    slots = p_ref.shape[1] - EXTRA
    rows = parts * q_rows
    queries = rows // query_len
    tokens = p_ref[0, :slots, :]
    tokens_t = tokens.T
    length = p_ref[0, slots : slots + 1, :].astype(F32) + float(LEAST)
    chunk = group * q_rows
    wide = jnp.concatenate([length] * (chunk // width), axis=1)
    position = lax.broadcasted_iota(jnp.int32, (slots - LEAST, chunk), 0).astype(F32) + float(LEAST)
    usable = position < wide
    log_length = jnp.log(wide)

    steps = parts // group

    def scores(step):
        block = jnp.concatenate([q_ref[step * group + k, :q_rows, :] for k in range(group)], axis=0)
        return dot(tokens, block, ((1,), (1,)))

    ahead = scores(0)
    late = None
    for step in range(steps):
        now = ahead
        if step + 1 < steps:
            ahead = scores(step + 1)
        if late is not None:
            mix_ref[passage, :, pl.ds((step - 1) * chunk, chunk)] = dot(tokens_t, late, ((1,), (0,)))
        sure, rest = now[:LEAST], jnp.where(usable, now[LEAST:], -1e30)
        highest = jnp.max(sure, axis=0, keepdims=True)
        highest = jnp.maximum(highest, jnp.max(rest, axis=0, keepdims=True))
        sure = jnp.exp(sure - highest)
        rest = jnp.exp(rest - highest)
        total = jnp.sum(sure, axis=0, keepdims=True) + jnp.sum(rest, axis=0, keepdims=True)
        late = jnp.concatenate([sure.astype(BF16), rest.astype(BF16)], axis=0)
        at = pl.ds(step * chunk, chunk)
        exp_ref[passage, :, at] = late
        inv_ref[pl.ds(passage, 1), at] = 1.0 / total
        lse_ref[pl.ds(passage, 1), at] = highest + jnp.log(total) - log_length
    mix_ref[passage, :, pl.ds((steps - 1) * chunk, chunk)] = dot(tokens_t, late, ((1,), (0,)))

    @pl.when(passage == pl.num_programs(0) - 1)
    def _():
        similar = dot(
            lse_ref[...], token_query(rows, queries, query_len), ((1,), (0,)), lax.Precision.HIGHEST
        )
        wanted = jnp.sum(q_ref[:, q_rows, :].astype(F32), axis=0, keepdims=True)[:, :queries]
        hit = (wanted == ids_ref[:, :queries]).astype(F32)
        highest = jnp.max(similar, axis=0, keepdims=True)
        total = jnp.sum(jnp.exp(similar - highest), axis=0, keepdims=True)
        positive = jnp.sum(jnp.where(hit > 0.0, similar, 0.0), axis=0, keepdims=True)
        sim_ref[0] = similar
        sim_ref[1] = hit
        stats = jnp.concatenate(
            [highest, total, positive, jnp.zeros((5, queries), F32)], axis=0
        )
        stats = jnp.concatenate([stats, jnp.zeros((8, width - queries), F32)], axis=1)
        stats_ref[...] = jnp.broadcast_to(stats[None], stats_ref.shape)


def forward_tile(query_pack, passage_pack, ids, query_len, group=2):
    parts, q_rows, width = query_pack.shape
    q_rows -= EXTRA
    count, slots = passage_pack.shape[0], passage_pack.shape[1] - EXTRA
    rows = parts * q_rows
    queries = rows // query_len
    work = rows * slots * count
    return pl.pallas_call(
        functools.partial(forward_kernel, query_len, group),
        name="forward_tile",
        grid=(count,),
        in_specs=[
            whole(query_pack.shape),
            pl.BlockSpec((1, slots + EXTRA, width), lambda p: (p, 0, 0)),
            whole(ids.shape),
        ],
        out_specs=[
            pl.BlockSpec(memory_space=pltpu.VMEM),
            pl.BlockSpec(memory_space=pltpu.VMEM),
            whole((count, rows)),
            whole((2, count, queries)),
            whole((parts, 8, width)),
        ],
        out_shape=[
            pltpu.VMEM((count, slots, rows), BF16),
            pltpu.VMEM((count, width, rows), F32),
            jax.ShapeDtypeStruct((count, rows), F32),
            jax.ShapeDtypeStruct((2, count, queries), F32),
            jax.ShapeDtypeStruct((parts, 8, width), F32),
        ],
        scratch_shapes=[pltpu.VMEM((count, rows), F32)],
        compiler_params=pltpu.CompilerParams(vmem_limit_bytes=20 * MIB),
        cost_estimate=pl.CostEstimate(
            flops=4 * work * width, transcendentals=work, bytes_accessed=4 * work
        ),
    )(query_pack, passage_pack, ids)


def backward_kernel(
    query_len, q_ref, exp_ref, mix_ref, inv_ref, sim_ref, stats_ref, pg_ref, qg_ref, qt, scale, sums
):
    passage = pl.program_id(0)
    parts, q_rows, width = q_ref.shape[0], q_ref.shape[1] - EXTRA, q_ref.shape[2]
    slots = exp_ref.shape[1]
    rows = parts * q_rows
    queries = rows // query_len

    @pl.when(passage == 0)
    def _():
        highest_of = stats_ref[:, 0, :queries]
        highest = jnp.max(highest_of, axis=0, keepdims=True)
        total = jnp.sum(
            stats_ref[:, 1, :queries] * jnp.exp(highest_of - highest), axis=0, keepdims=True
        )
        positive = jnp.sum(stats_ref[:, 2, :queries], axis=0, keepdims=True)
        log_total = highest + jnp.log(total)
        coefficient = jnp.exp(sim_ref[0] - log_total) - sim_ref[1]
        spread = dot(
            coefficient,
            token_query(rows, queries, query_len, True),
            ((1,), (0,)),
            lax.Precision.HIGHEST,
        )
        scale[...] = spread * inv_ref[...]
        loss = jnp.broadcast_to(
            jnp.sum(log_total - positive, axis=1, keepdims=True), (EXTRA, width)
        )
        high = loss.astype(BF16).astype(F32)
        low = (loss - high).astype(BF16).astype(F32)
        last = loss - high - low
        row = lax.broadcasted_iota(jnp.int32, (EXTRA, width), 0)
        lines = jnp.where(row == 0, high, jnp.where(row == 1, low, jnp.where(row == 2, last, 0.0)))
        for k in range(pg_ref.shape[0]):
            pg_ref[k, slots:, :] = lines.astype(BF16)
        for k in range(parts):
            qt[:, k * q_rows : (k + 1) * q_rows] = q_ref[k, :q_rows, :].T
        sums[...] = jnp.zeros_like(sums)

    factor = scale[pl.ds(passage, 1), :]
    weighted = (qt[...].astype(F32) * factor).astype(BF16)
    grad_t = dot(weighted, exp_ref[passage], ((1,), (1,)))
    pg_ref[passage, :slots, :] = grad_t.T.astype(BF16)
    sums[...] += mix_ref[passage] * factor

    @pl.when(passage == pl.num_programs(0) - 1)
    def _():
        for k in range(parts):
            qg_ref[k % 2, k // 2] = sums[:, k * q_rows : (k + 1) * q_rows].T.astype(BF16)


def backward_tile(query_pack, spread, mixed, inverse, similar, stats, query_len):
    parts, q_rows, width = query_pack.shape
    q_rows -= EXTRA
    count, slots, rows = spread.shape
    work = rows * slots * count
    return pl.pallas_call(
        functools.partial(backward_kernel, query_len),
        name="backward_tile",
        grid=(count,),
        in_specs=[
            whole(query_pack.shape),
            pl.BlockSpec(memory_space=pltpu.VMEM),
            pl.BlockSpec(memory_space=pltpu.VMEM),
            whole(inverse.shape),
            whole(similar.shape),
            whole(stats.shape),
        ],
        out_specs=[whole((count, slots + EXTRA, width)), whole((2, parts // 2, q_rows, width))],
        out_shape=[
            jax.ShapeDtypeStruct((count, slots + EXTRA, width), BF16),
            jax.ShapeDtypeStruct((2, parts // 2, q_rows, width), BF16),
        ],
        scratch_shapes=[
            pltpu.VMEM((width, rows), BF16),
            pltpu.VMEM((count, rows), F32),
            pltpu.VMEM((width, rows), F32),
        ],
        compiler_params=pltpu.CompilerParams(vmem_limit_bytes=20 * MIB),
        cost_estimate=pl.CostEstimate(
            flops=2 * work * width, transcendentals=0, bytes_accessed=3 * work
        ),
    )(query_pack, spread, mixed, inverse, similar, stats)


def early_kernel(resid_ref, context_ref, proj_ref, normed_ref, inv_ref, context_t_ref):
    context = context_ref[...]
    hidden = resid_ref[...].astype(F32) + dot(context, proj_ref[...], ((1,), (0,)))
    centred = hidden - jnp.mean(hidden, axis=1, keepdims=True)
    variance = jnp.mean(centred * centred, axis=1, keepdims=True)
    inv_std = 1.0 / jnp.sqrt(variance + 1e-05)
    normed_ref[...] = centred * inv_std
    inv_ref[...] = jnp.broadcast_to(inv_std, inv_ref.shape)
    context_t_ref[...] = context.T


def early_rows(residual, context, out_proj, block=128):
    rows, width = residual.shape
    return pl.pallas_call(
        early_kernel,
        name="early_rows",
        grid=(rows // block,),
        in_specs=[
            pl.BlockSpec((block, width), lambda r: (r, 0)),
            pl.BlockSpec((block, width), lambda r: (r, 0)),
            whole(out_proj.shape),
        ],
        out_specs=[
            pl.BlockSpec((block, width), lambda r: (r, 0)),
            pl.BlockSpec((block, 128), lambda r: (r, 0)),
            pl.BlockSpec((width, block), lambda r: (0, r)),
        ],
        out_shape=[
            jax.ShapeDtypeStruct((rows, width), F32),
            jax.ShapeDtypeStruct((rows, 128), F32),
            jax.ShapeDtypeStruct((width, rows), BF16),
        ],
        compiler_params=pltpu.CompilerParams(vmem_limit_bytes=24 * MIB),
        cost_estimate=pl.CostEstimate(
            flops=2 * rows * width * width, transcendentals=0, bytes_accessed=10 * rows * width
        ),
    )(residual, context, out_proj)


def late_kernel(
    parts_ref, normed_ref, inv_ref, gain_ref, colbert_ref, context_t_ref, resid_ref, sums_ref, loss_ref
):
    slots = parts_ref.shape[1] - EXTRA
    count = parts_ref.shape[0]
    width = normed_ref.shape[1]
    total = parts_ref[0].astype(F32)
    for k in range(1, count):
        total = total + parts_ref[k].astype(F32)
    loss_ref[...] = jnp.broadcast_to(
        jnp.sum(total[slots:], axis=0, keepdims=True), loss_ref.shape
    )
    grad = total[:slots].astype(BF16)
    normed = normed_ref[...]
    gain = gain_ref[...]
    inv_std = inv_ref[:, :1]
    gained = dot(grad, colbert_ref[...], ((1,), (1,))) * gain
    resid = inv_std * (
        gained
        - jnp.mean(gained, axis=1, keepdims=True)
        - normed * jnp.mean(gained * normed, axis=1, keepdims=True)
    )
    resid = resid.astype(BF16)
    resid_ref[...] = resid
    scaled = (normed * gain).astype(BF16)
    sums_ref[width:, :] = dot(grad.T, scaled, ((1,), (0,))).astype(BF16)
    step = 256
    for k in range(width // step):
        sums_ref[k * step : (k + 1) * step, :] = dot(
            context_t_ref[k * step : (k + 1) * step, :], resid, ((1,), (0,))
        ).astype(BF16)


def late_rows(pieces, normed, inv_std, gain, colbert_proj, context_t):
    rows, width = normed.shape
    emb = colbert_proj.shape[1]
    return pl.pallas_call(
        late_kernel,
        name="late_rows",
        out_shape=[
            jax.ShapeDtypeStruct((rows, width), BF16),
            jax.ShapeDtypeStruct((width + emb, width), BF16),
            jax.ShapeDtypeStruct((8, emb), F32),
        ],
        compiler_params=pltpu.CompilerParams(vmem_limit_bytes=40 * MIB),
        cost_estimate=pl.CostEstimate(
            flops=2 * rows * width * (width + 2 * emb),
            transcendentals=0,
            bytes_accessed=14 * rows * width,
        ),
    )(pieces, normed, inv_std, gain, colbert_proj, context_t)


def exchange(pieces, axis):
    return lax.all_to_all(pieces, axis, 0, 0, tiled=True)


def to_everyone(array, axis):
    size = lax.axis_size(axis)
    return exchange(jnp.broadcast_to(array[None], (size, *array.shape)), axis)


def summed(pieces):
    return jnp.sum(pieces.astype(F32), axis=0).astype(BF16)


def finish_kernel(core_ref, half_ref, other_ref, colbert_ref, gain_ref, proj_ref, grad_ref, gain_grad_ref):
    rows = half_ref.shape[0]
    top = proj_ref.shape[0] - rows
    even = core_ref[0] == 0
    half, other = half_ref[...], other_ref[...]
    proj_ref[:rows, :] = jnp.where(even, half, other).astype(F32)
    second = jnp.where(even, other, half).astype(F32)
    proj_ref[rows:, :] = second[:top]
    colbert_grad = second[top:]
    colbert_t = colbert_ref[...].astype(F32).T
    gain_grad_ref[...] = (
        jnp.sum(colbert_grad * colbert_t, axis=0, keepdims=True) / gain_ref[...]
    )
    grad_ref[...] = colbert_grad.T


def finish(core, half, other, colbert_proj, gain, block=256):
    rows, width = half.shape
    emb = colbert_proj.shape[1]
    return pl.pallas_call(
        finish_kernel,
        name="finish",
        grid=(width // block,),
        in_specs=[
            pl.BlockSpec(memory_space=pltpu.SMEM),
            pl.BlockSpec((rows, block), lambda k: (0, k)),
            pl.BlockSpec((rows, block), lambda k: (0, k)),
            pl.BlockSpec((block, emb), lambda k: (k, 0)),
            pl.BlockSpec((1, block), lambda k: (0, k)),
        ],
        out_specs=[
            pl.BlockSpec((2 * rows - emb, block), lambda k: (0, k)),
            pl.BlockSpec((block, emb), lambda k: (k, 0)),
            pl.BlockSpec((1, block), lambda k: (0, k)),
        ],
        out_shape=[
            jax.ShapeDtypeStruct((2 * rows - emb, width), F32),
            jax.ShapeDtypeStruct((width, emb), F32),
            jax.ShapeDtypeStruct((1, width), F32),
        ],
        compiler_params=pltpu.CompilerParams(vmem_limit_bytes=24 * MIB),
        cost_estimate=pl.CostEstimate(
            flops=4 * rows * width, transcendentals=0, bytes_accessed=16 * rows * width
        ),
    )(core[None], half, other, colbert_proj, gain)


def core_halves(halves, core):
    given = lax.dynamic_index_in_dim(halves, 1 - core, 0, False)
    kept = lax.dynamic_index_in_dim(halves, core, 0, False)
    taken = lax.ppermute(given, CORE, [(0, 1), (1, 0)])
    return (kept.astype(F32) + taken.astype(F32)).astype(BF16)


def body(
    query_emb, positive, passage_emb, lengths, residual, context, out_proj, norm_gain, colbert_proj
):
    query_dev, query_len, emb = query_emb.shape
    neg_size, dp_size, cross_size = lax.axis_size(NEG), lax.axis_size(DP), lax.axis_size(CROSS)
    place, core = lax.axis_index(NEG), lax.axis_index(CORE)
    width = out_proj.shape[0]
    spot = jnp.arange(emb)[None] - place * query_dev
    wanted = jnp.sum(
        jnp.where(spot == jnp.arange(query_dev)[:, None], positive[:, None], 0), axis=0
    )
    query_own = jnp.concatenate(
        [
            query_emb.reshape(query_dev * query_len, emb),
            jnp.broadcast_to(wanted.astype(BF16)[None], (EXTRA, emb)),
        ]
    )
    passage_own = jnp.concatenate(
        [
            passage_emb.reshape(-1, emb),
            jnp.broadcast_to((lengths - LEAST).astype(BF16)[:, None], (EXTRA, emb)),
        ]
    )
    query_pack = lax.all_gather(query_own, NEG)
    passage_pack = to_everyone(passage_own, DP)
    ids = jnp.broadcast_to(
        (jnp.arange(dp_size) * neg_size + place).astype(F32)[:, None], (dp_size, emb)
    )
    early = early_rows(residual, context, out_proj)
    (query_pack, passage_pack), early = lax.optimization_barrier(
        ((query_pack, passage_pack), early)
    )
    normed, inv_std, context_t = early
    spread, mixed, inverse, similar, stats = forward_tile(query_pack, passage_pack, ids, query_len)
    stats = exchange(stats, NEG)
    passage_parts, query_parts = backward_tile(
        query_pack, spread, mixed, inverse, similar, stats, query_len
    )
    query_half = core_halves(query_parts, core)
    passage_parts = exchange(passage_parts, DP)
    passage_parts, query_half = lax.optimization_barrier((passage_parts, query_half))
    residual_grad, partial, loss_sum = late_rows(
        passage_parts, normed, inv_std, norm_gain[None], colbert_proj, context_t
    )
    half = core_halves(partial.reshape(2, -1, width), core)
    context_grad = jnp.dot(residual_grad, out_proj.T, preferred_element_type=F32).astype(BF16)
    slabs = exchange(half.reshape(dp_size, -1, width), DP)
    slabs, context_grad = lax.optimization_barrier((slabs, context_grad))
    slab = summed(slabs)
    lines = slab.shape[0]
    tiles = slab.reshape(lines, cross_size, -1).swapaxes(0, 1)
    tiles = exchange(jnp.concatenate([tiles, query_half], axis=1), CROSS)
    tile = jnp.sum(tiles.astype(F32), axis=0)
    query_grad = tile[lines:].reshape(query_dev, query_len, emb)
    slab = to_everyone(tile[:lines].astype(BF16), CROSS).swapaxes(0, 1).reshape(lines, width)
    half = to_everyone(slab, DP).reshape(-1, width)
    other = lax.ppermute(half, CORE, [(0, 1), (1, 0)])
    out_proj_grad, colbert_grad, gain_grad = finish(
        core, half, other, colbert_proj, norm_gain[None]
    )
    loss = loss_sum[0, 0] / (query_dev * dp_size * neg_size)
    return (
        loss,
        query_grad,
        residual_grad,
        context_grad,
        out_proj_grad,
        colbert_grad,
        gain_grad[0],
    )


def solution(mesh):
    split = Mesh(mesh.devices.reshape(mesh.shape["dp"] // 2, 2, 4, 2, 2), DP_NEG)
    placed = (
        P(DP_NEG, None, None),
        P(DP_NEG),
        P(DP_NEG, None, None),
        P(DP_NEG),
        P(DP_NEG, None),
        P(DP_NEG, None),
        P(),
        P(),
        P(),
    )
    return jax.shard_map(
        body,
        mesh=split,
        in_specs=placed,
        out_specs=(P(), P(DP_NEG, None, None), P(DP_NEG, None), P(DP_NEG, None), P(), P(), P()),
        check_vma=False,
    )
```

time: 413 us -> 185 us (0.45)
  waiting for transfers between devices: 122 us -> 31 us
  matrix products: 83.4 us -> 3.49 us
  Pallas kernels: 0 us -> 34.4 us
  blocking collectives: 106 us -> 74.8 us
  local copies, waits for them, and re-layouts: 37.3 us -> 11.8 us
  other arithmetic: 24.4 us -> 3.22 us
  between operations: 18.3 us -> 3.41 us
  starting transfers between devices: 14.7 us -> 22.5 us
  loops' own time: 6.1 us -> 0 us
    psum x1 -> x0, waiting for transfers between devices: 81.8 us -> none  [body(): lax.psum((proj_part, colbert_part, gain_part, loss_part), DP_NEG)]
    dot_general x37 -> x1, matrix products: 83.4 us -> 3.49 us  [body(): jnp.dot(residual_grad, out_proj.T, preferred_element_type=F32).astype(BF16)]
    psum x1 -> x0, blocking collectives: 64.3 us -> none  [body(): lax.psum((proj_part, colbert_part, gain_part, loss_part), DP_NEG)]
    pallas_call x0 -> x5, Pallas kernels: none -> 34.4 us  [the longest x1 17.1 us: forward_tile(): pl.pallas_call(functools.partial(forward_kernel, query_len, group), name=...]
    all_gather x0 -> x1, blocking collectives: none -> 26.4 us  [body(): query_pack = lax.all_gather(query_own, NEG)]
    all_to_all x3, waiting for transfers between devices: 39.1 us -> 26.7 us  [exchange(): return lax.all_to_all(pieces, axis, 0, 0, tiled=True)]
    while x16 -> x0, local copies, waits for them, and re-layouts: 10.5 us -> none
    lt x16 -> x0, other arithmetic: 10.4 us -> none  [per_passage(): usable = (jnp.arange(passage_one.shape[0]) < length)[None, :]]
  transfers between devices with their start and end apart: 6 -> 6, of which waited for: 4 -> 5; matrix products, arithmetic and copies ran while one was open for 7% -> 3% of each run, Pallas kernels for 0% -> 2%
where the time goes in v1:
time: 185 us
  blocking collectives  74.8 us (40%)
  Pallas kernels  34.4 us (19%)
  waiting for transfers between devices  31 us (17%)
  starting transfers between devices  22.5 us (12%)
  local copies, waits for them, and re-layouts  11.8 us (6%)
  matrix products  3.49 us (2%)
  between operations  3.41 us (2%)
  other arithmetic  3.22 us (2%)
    all_to_all x4, blocking collectives, exchange(): return lax.all_to_all(pieces, axis, 0, 0, tiled=True)  48.5 us
    all_to_all x3, waiting for transfers between devices, exchange(): return lax.all_to_all(pieces, axis, 0, 0, tiled=True)  26.7 us
    all_gather x1, blocking collectives, body(): query_pack = lax.all_gather(query_own, NEG)  26.4 us
    pallas_call x1, Pallas kernels, forward_tile(): pl.pallas_call(functools.partial(forward_kernel, query_len, group), name=...  17.1 us
    all_to_all x3, starting transfers between devices, exchange(): return lax.all_to_all(pieces, axis, 0, 0, tiled=True)  16 us
    pallas_call x1, Pallas kernels, backward_tile(): pl.pallas_call(functools.partial(backward_kernel, query_len), name='backw...  9.21 us
    unnamed x28, local copies, waits for them, and re-layouts  8.27 us
    ppermute x1, starting transfers between devices, body(): other = lax.ppermute(half, CORE, [(0, 1), (1, 0)])  4.07 us
  transfers between devices with their start and end apart: 6, of which 5 were waited for; matrix products, arithmetic and copies ran while one was open for 3% of the time, Pallas kernels for 2%

profile of v1, /device:TPU:1, one launch (start us, length us, event | category | flops | bytes accessed | tf_op | source)
XLA Modules:
  0.0 184.7 jit_solution(2476939317328482090)
XLA Ops:
  0.6 0.0 copy-start.13
  0.6 0.0 copy-start
  1.5 0.9 concatenate.10
  2.4 1.1 broadcast_in_dim.34
  3.5 6.9 %all-to-all-start = ((bf16[8,520,128]{2,1,0:T(8,128)(2,1)}), bf16[8,520,128]{2,1,0:T(8,128)(2,1)S(1)}, u32[]{:S(2)}, u32[]{:S(2)}) async-start(bf16[8,520,128]{2,1,0:T(8,128)(2,1)} %broadcast_in_dim.34), calls=%async_computation | async-start | bytes 2129920 | tf_op jit(solution)/shard_map/all_to_all | solution.py:319
  10.4 0.0 copy-done.13
  10.4 0.1 select_reduce_fusion
  10.5 0.0 copy-done
  10.5 0.0 copy-start.2
  10.5 1.2 copy-done.2
  11.7 0.0 copy-start.3
  11.7 1.2 copy-done.3
  12.9 0.0 copy-start.12
  13.0 2.9 %early_rows.1 = (f32[512,1024]{1,0:T(8,128)S(1)}, f32[512,128]{1,0:T(8,128)S(1)}, bf16[1024,512]{1,0:T(8,128)(2,1)S(1)}) custom-call(bf16[512,1024]{1,0:T(8,128)(2,1)S(1)} %copy-done.2, bf16[512,1024]{1,0:T(8,128)(2,1)S(1)} %copy-done.3, bf16[1024,1024]{1,0:T(8,128)(2,1)S(1)} %copy-done), custom_call_target="tpu_custom_call" | custom-call | flops 1073741824 | bytes 5242880 | tf_op jit(solution)/shard_map/early_rows/pallas_call | solution.py:239
  15.8 0.0 copy-start.6
  15.8 1.3 copy-done.6
  17.2 0.0 copy-start.8
  17.2 1.0 copy-done.8
  18.1 0.0 copy-start.10
  18.1 0.7 copy-done.10
  18.8 0.0 copy-done.12
  18.9 26.4 %all-gather = bf16[2176,128]{1,0:T(8,128)(2,1)S(1)} all-gather(bf16[136,128]{1,0:T(8,128)(2,1)S(1)} %pad_maximum_fusion.1), channel_id=2, replica_groups=mesh['dp_0'=4,'dp_1'=2,'neg_0'=4,'neg_1'=2,'neg_2'=2] {'neg_0','neg_1','..., dimensions={0}, use_global_device_ids=true | all-gather | bytes 591872 | tf_op jit(solution)/shard_map/all_gather | solution.py:408
  45.2 0.0 all-to-all-done.p_ref
  45.2 0.1 broadcast_in_dim.35.ids_ref
  45.3 17.1 %forward_tile.1 = (bf16[8,512,2048]{2,1,0:T(8,128)(2,1)S(1)}, f32[8,128,2048]{2,1,0:T(8,128)S(1)}, f32[8,2048]{1,0:T(8,128)S(1)}, f32[2,8,64]{2,1,0:T(8,128)S(1)}, f32[16,8,128]{2,1,0:T(8,128)S(1)}) custom-call(bf16[16,136,128]{2,1,0:T(8,128)(2,1)S(1)} %bitcast.41, bf16[8,520,128]{2,1,0:T(8,128)(2,1)S(1)} %all-to-all-done.p_ref, ...), custom_call_target="tpu_custom_call" | custom-call | flops 4294967296 | bytes 33554432 | tf_op jit(solution)/shard_map/forward_tile/pallas_call | solution.py:109
  62.4 10.0 %all_to_all.35.stats_ref = f32[16,8,128]{2,1,0:T(8,128)S(1)} all-to-all(f32[16,8,128]{2,1,0:T(8,128)S(1)} %get-tuple-element.41), channel_id=1, replica_groups=mesh['dp_0'=4,'dp_1'=2,'neg_0'=4,'neg_1'=2,'neg_2'=2] {'neg_0','neg_1','..., dimensions={0} | all-to-all | bytes 131072 | tf_op jit(solution)/shard_map/all_to_all | solution.py:319
  72.4 9.2 %backward_tile.1 = (bf16[8,520,128]{2,1,0:T(8,128)(2,1)}, bf16[2,8,128,128]{3,2,1,0:T(8,128)(2,1)S(1)}) custom-call(bf16[16,136,128]{2,1,0:T(8,128)(2,1)S(1)} %bitcast.42, bf16[8,512,2048]{2,1,0:T(8,128)(2,1)S(1)} %get-tuple-element.37.exp_ref, f32[8,128,2048]{2,1,0:T(8,128)S(1)} %get-tuple-element.38.mix_ref, f32[8,2048]{1,0:T(8,128)S(1)} %get-tuple-element.39.inv_ref, ...), custom_call_target="tpu_custom_call" | custom-call | flops 2147483648 | bytes 25165824 | tf_op jit(solution)/shard_map/backward_tile/pallas_call | solution.py:197
  81.6 0.0 copy-start.4
  81.6 0.0 copy-start.5
  81.6 0.0 copy-start.11
  81.6 4.9 %all-to-all-start.2 = ((bf16[8,520,128]{2,1,0:T(8,128)(2,1)}), bf16[8,520,128]{2,1,0:T(8,128)(2,1)S(1)}, u32[]{:S(2)}, u32[]{:S(2)}) async-start(bf16[8,520,128]{2,1,0:T(8,128)(2,1)} %get-tuple-element.42), calls=%async_computation.2 | async-start | bytes 2129920 | tf_op jit(solution)/shard_map/all_to_all | solution.py:319
  86.6 0.8 collective-permute-start
  87.3 1.2 collective-permute-done
  88.5 0.1 fusion.1
  88.5 13.3 %all-to-all-done.2.parts_ref = bf16[8,520,128]{2,1,0:T(8,128)(2,1)S(1)} async-done(((bf16[8,520,128]{2,1,0:T(8,128)(2,1)}), bf16[8,520,128]{2,1,0:T(8,128)(2,1)S(1)}, u32[]{:S(2)}, u32[]{:S(2)}) %all-to-all-start.2) | async-done | bytes 1064992 | tf_op jit(solution)/shard_map/all_to_all | solution.py:319
  101.9 0.0 copy-done.4
  101.9 0.0 copy-done.5
  101.9 0.0 copy-done.11
  101.9 0.0 copy-start.7
  101.9 1.6 copy-done.7
  103.5 0.0 copy-start.9
  103.5 1.2 copy-done.9
  104.7 2.3 %late_rows.1 = (bf16[512,1024]{1,0:T(8,128)(2,1)}, bf16[1152,1024]{1,0:T(8,128)(2,1)S(1)}, f32[8,128]{1,0:T(8,128)S(1)}) custom-call(bf16[8,520,128]{2,1,0:T(8,128)(2,1)S(1)} %all-to-all-done.2.parts_ref, f32[512,1024]{1,0:T(8,128)S(1)} %copy-done.7, f32[512,128]{1,0:T(8,128)S(1)} %copy-done.11, f32[1,1024]{1,0:T(1,128)S(1)} %bitcast.43, ...), custom_call_target="tpu_custom_call" | custom-call | flops 1342177280 | bytes 7340032 | tf_op jit(solution)/shard_map/late_rows/pallas_call | solution.py:301
  107.0 0.1 dynamic-slice_bitcast_fusion
  107.1 0.0 copy-start.1
  107.1 1.6 collective-permute-start.1
  108.7 2.5 %collective-permute-done.1 = bf16[576,1024]{1,0:T(8,128)(2,1)S(1)} collective-permute-done((bf16[576,1024]{1,0:T(8,128)(2,1)S(1)}, bf16[576,1024]{1,0:T(8,128)(2,1)S(1)}, u32[]{:S(2)}, u32[]{:S(2)}) %collective-permute-start.1) | collective-permute-done | bytes 1179680 | tf_op jit(solution)/shard_map/ppermute | solution.py:381
  111.2 1.5 fusion
  112.7 4.3 %all-to-all-start.3 = ((bf16[8,72,1024]{2,1,0:T(8,128)(2,1)}), bf16[8,72,1024]{2,1,0:T(8,128)(2,1)}, u32[]{:S(2)}, u32[]{:S(2)}) async-start(bf16[8,72,1024]{2,1,0:T(8,128)(2,1)} %bitcast.11), calls=%async_computation.3 | async-start | bytes 2359296 | tf_op jit(solution)/shard_map/all_to_all | solution.py:319
  116.9 0.0 copy-done.1
  116.9 3.5 %convolution_convert_fusion = bf16[512,1024]{1,0:T(8,128)(2,1)} fusion(bf16[512,1024]{1,0:T(8,128)(2,1)} %get-tuple-element.27, bf16[1024,1024]{1,0:T(8,128)(2,1)S(1)} %copy-done.1), kind=kOutput, calls=%fused_computation.2 | convolution fusion | flops 1074266112 | bytes 4194304 | tf_op jit(solution)/shard_map/dot_general | solution.py:430
  120.4 13.4 %all-to-all-done.3 = bf16[8,72,1024]{2,1,0:T(8,128)(2,1)} async-done(((bf16[8,72,1024]{2,1,0:T(8,128)(2,1)}), bf16[8,72,1024]{2,1,0:T(8,128)(2,1)}, u32[]{:S(2)}, u32[]{:S(2)}) %all-to-all-start.3) | async-done | bytes 1179680 | tf_op jit(solution)/shard_map/all_to_all | solution.py:319
  133.9 1.5 reduce_sum.31
  135.4 11.2 %all_to_all.36 = bf16[8,200,128]{2,1,0:T(8,128)(2,1)S(1)} all-to-all(bf16[8,200,128]{2,1,0:T(8,128)(2,1)S(1)} %pad_maximum_fusion), channel_id=1, replica_groups=mesh['dp_0'=4,'dp_1'=2,'neg_0'=4,'neg_1'=2,'neg_2'=2] {'neg_0','neg_1'}, dimensions={0} | all-to-all | bytes 819200 | tf_op jit(solution)/shard_map/all_to_all | solution.py:319
  146.6 0.1 convert_reduce_fusion
  146.7 9.5 %all_to_all.37 = bf16[8,72,128]{2,1,0:T(8,128)(2,1)S(1)} all-to-all(bf16[8,72,128]{2,1,0:T(8,128)(2,1)S(1)} %broadcast_in_dim.67), channel_id=1, replica_groups=mesh['dp_0'=4,'dp_1'=2,'neg_0'=4,'neg_1'=2,'neg_2'=2] {'neg_0','neg_1'}, dimensions={0} | all-to-all | bytes 294912 | tf_op jit(solution)/shard_map/all_to_all | solution.py:319
  156.2 0.1 broadcast_in_dim.69
  156.3 17.8 %all_to_all.38 = bf16[8,72,1024]{2,1,0:T(8,128)(2,1)S(1)} all-to-all(bf16[8,72,1024]{2,1,0:T(8,128)(2,1)S(1)} %broadcast_in_dim.69), channel_id=1, replica_groups=mesh['dp_0'=4,'dp_1'=2,'neg_0'=4,'neg_1'=2,'neg_2'=2] {'dp_0','dp_1'}, dimensions={0} | all-to-all | bytes 2359296 | tf_op jit(solution)/shard_map/all_to_all | solution.py:319
  174.1 4.1 %collective-permute-start.2 = (bf16[576,1024]{1,0:T(8,128)(2,1)S(1)}, bf16[576,1024]{1,0:T(8,128)(2,1)S(1)}, u32[]{:S(2)}, u32[]{:S(2)}) collective-permute-start(bf16[576,1024]{1,0:T(8,128)(2,1)S(1)} %bitcast.37), channel_id=1, source_target_pairs={{0,1},{1,0},{2,3},{3,2},{4,5},{5,4},{6,7},{7,6},{8,9},{9,8},{10,11... | collective-permute-start | bytes 3538952 | tf_op jit(solution)/shard_map/ppermute | solution.py:441
  178.2 0.5 slice.10
  179.4 0.6 slice.13
  180.0 0.7 collective-permute-done.2.other_ref
  180.7 2.9 %finish.1 = (f32[1024,1024]{1,0:T(8,128)}, f32[1024,128]{1,0:T(8,128)}, f32[1,1024]{1,0:T(1,128)}) custom-call(s32[1]{0:T(128)} %bitcast.14.core_ref, bf16[576,1024]{1,0:T(8,128)(2,1)S(1)} %bitcast.38, bf16[576,1024]{1,0:T(8,128)(2,1)S(1)} %collective-permute-done.2.other_ref, bf16[1024,128]{1,0:T(8,128)(2,1)S(1)} %copy-done.4, f32[1,1024]{1,0:T(1,128)S(1)} %bitcast.44), custom_call_target="tpu_custom_call" | custom-call | flops 2359296 | bytes 9437184 | tf_op jit(solution)/shard_map/finish/pallas_call | solution.py:350
  (11 shorter events, 0.1 us)
Async XLA Ops:
  0.6 9.8 %copy-start.13 = (s32[4]{0:T(128)S(1)}, s32[4]{0:T(128)}, u32[]{:S(2)}) copy-start(s32[4]{0:T(128)} %param.10) | copy-start | bytes 52
  0.6 9.9 %copy-start = (bf16[1024,1024]{1,0:T(8,128)(2,1)S(1)}, bf16[1024,1024]{1,0:T(8,128)(2,1)}, u32[]{:S(2)}) copy-start(bf16[1024,1024]{1,0:T(8,128)(2,1)} %proj_ref.1) | copy-start | bytes 6291460
  3.5 41.7 %all-to-all-start = ((bf16[8,520,128]{2,1,0:T(8,128)(2,1)}), bf16[8,520,128]{2,1,0:T(8,128)(2,1)S(1)}, u32[]{:S(2)}, u32[]{:S(2)}) async-start(bf16[8,520,128]{2,1,0:T(8,128)(2,1)} %broadcast_in_dim.34), calls=%async_computation | async-start | bytes 2129920 | tf_op jit(solution)/shard_map/all_to_all | solution.py:319
  10.5 1.2 copy-start.2
  11.7 1.2 copy-start.3
  12.9 5.9 %copy-start.12 = (bf16[4,32,128]{2,1,0:T(8,128)(2,1)S(1)}, bf16[4,32,128]{2,1,0:T(8,128)(2,1)}, u32[]{:S(2)}) copy-start(bf16[4,32,128]{2,1,0:T(8,128)(2,1)} %param.9) | copy-start | bytes 98308
  15.8 1.3 copy-start.6
  17.2 1.0 copy-start.8
  18.1 0.7 copy-start.10
  81.6 20.2 %copy-start.4 = (bf16[1024,128]{1,0:T(8,128)(2,1)S(1)}, bf16[1024,128]{1,0:T(8,128)(2,1)}, u32[]{:S(2)}) copy-start(bf16[1024,128]{1,0:T(8,128)(2,1)} %colbert_ref.3) | copy-start | bytes 786436
  81.6 20.2 %copy-start.5 = (f32[1024]{0:T(1024)S(1)}, f32[1024]{0:T(1024)}, u32[]{:S(2)}) copy-start(f32[1024]{0:T(1024)} %param.16) | copy-start | bytes 12292
  81.6 20.2 %copy-start.11 = (f32[512,128]{1,0:T(8,128)S(1)}, f32[512,128]{1,0:T(8,128)}, u32[]{:S(2)}) copy-start(f32[512,128]{1,0:T(8,128)} %copy-done.10) | copy-start | bytes 786436
  81.6 20.2 %all-to-all-start.2 = ((bf16[8,520,128]{2,1,0:T(8,128)(2,1)}), bf16[8,520,128]{2,1,0:T(8,128)(2,1)S(1)}, u32[]{:S(2)}, u32[]{:S(2)}) async-start(bf16[8,520,128]{2,1,0:T(8,128)(2,1)} %get-tuple-element.42), calls=%async_computation.2 | async-start | bytes 2129920 | tf_op jit(solution)/shard_map/all_to_all | solution.py:319
  86.6 1.9 %collective-permute-start = (bf16[8,128,128]{2,1,0:T(8,128)(2,1)S(1)}, bf16[8,128,128]{2,1,0:T(8,128)(2,1)S(1)}, u32[]{:S(2)}, u32[]{:S(2)}) collective-permute-start(bf16[8,128,128]{2,1,0:T(8,128)(2,1)S(1)} %dynamic-slice_bitcast_fusion.1), channel_id=1, source_target_pairs={{0,1},{1,0},{2,3},{3,2},{4,5},{5,4},{6,7},{7,6},{8,9},{9,8},{10,11... | collective-permute-start | bytes 786440 | tf_op jit(solution)/shard_map/ppermute | solution.py:381
  101.9 1.6 copy-start.7
  103.5 1.2 copy-start.9
  107.1 9.8 %copy-start.1 = (bf16[1024,1024]{1,0:T(8,128)(2,1)S(1)}, bf16[1024,1024]{1,0:T(8,128)(2,1)}, u32[]{:S(2)}) copy-start(bf16[1024,1024]{1,0:T(8,128)(2,1)} %proj_ref.1) | copy-start | bytes 6291460
  107.1 4.1 %collective-permute-start.1 = (bf16[576,1024]{1,0:T(8,128)(2,1)S(1)}, bf16[576,1024]{1,0:T(8,128)(2,1)S(1)}, u32[]{:S(2)}, u32[]{:S(2)}) collective-permute-start(bf16[576,1024]{1,0:T(8,128)(2,1)S(1)} %dynamic-slice_bitcast_fusion), channel_id=1, source_target_pairs={{0,1},{1,0},{2,3},{3,2},{4,5},{5,4},{6,7},{7,6},{8,9},{9,8},{10,11... | collective-permute-start | bytes 3538952 | tf_op jit(solution)/shard_map/ppermute | solution.py:381
  112.7 21.2 %all-to-all-start.3 = ((bf16[8,72,1024]{2,1,0:T(8,128)(2,1)}), bf16[8,72,1024]{2,1,0:T(8,128)(2,1)}, u32[]{:S(2)}, u32[]{:S(2)}) async-start(bf16[8,72,1024]{2,1,0:T(8,128)(2,1)} %bitcast.11), calls=%async_computation.3 | async-start | bytes 2359296 | tf_op jit(solution)/shard_map/all_to_all | solution.py:319
  174.1 6.5 %collective-permute-start.2 = (bf16[576,1024]{1,0:T(8,128)(2,1)S(1)}, bf16[576,1024]{1,0:T(8,128)(2,1)S(1)}, u32[]{:S(2)}, u32[]{:S(2)}) collective-permute-start(bf16[576,1024]{1,0:T(8,128)(2,1)S(1)} %bitcast.37), channel_id=1, source_target_pairs={{0,1},{1,0},{2,3},{3,2},{4,5},{5,4},{6,7},{7,6},{8,9},{9,8},{10,11... | collective-permute-start | bytes 3538952 | tf_op jit(solution)/shard_map/ppermute | solution.py:441

commit v2 on v1

--- a/solution.py
+++ b/solution.py
@@ -37,13 +37,14 @@
 
 
 def forward_kernel(
-    query_len, group, q_ref, p_ref, ids_ref, exp_ref, mix_ref, inv_ref, sim_ref, stats_ref, lse_ref
+    query_len, group, flip_ref, q_ref, p_ref, ids_ref, exp_ref, mix_ref, inv_ref, sim_ref, stats_ref, lse_ref
 ):
     passage = pl.program_id(0)
     parts, q_rows, width = q_ref.shape[0], q_ref.shape[1] - EXTRA, q_ref.shape[2]
     slots = p_ref.shape[1] - EXTRA
     rows = parts * q_rows
     queries = rows // query_len
+    flip = flip_ref[0]
     tokens = p_ref[0, :slots, :]
     tokens_t = tokens.T
     length = p_ref[0, slots : slots + 1, :].astype(F32) + float(LEAST)
@@ -56,7 +57,7 @@
     steps = parts // group
 
     def scores(step):
-        block = jnp.concatenate([q_ref[step * group + k, :q_rows, :] for k in range(group)], axis=0)
+        block = jnp.concatenate([q_ref[(step * group + k) ^ flip, :q_rows, :] for k in range(group)], axis=0)
         return dot(tokens, block, ((1,), (1,)))
 
     ahead = scores(0)
@@ -99,7 +100,7 @@
         stats_ref[...] = jnp.broadcast_to(stats[None], stats_ref.shape)
 
 
-def forward_tile(query_pack, passage_pack, ids, query_len, group=2):
+def forward_tile(flip, query_pack, passage_pack, ids, query_len, group=4):
     parts, q_rows, width = query_pack.shape
     q_rows -= EXTRA
     count, slots = passage_pack.shape[0], passage_pack.shape[1] - EXTRA
@@ -111,6 +112,7 @@
         name="forward_tile",
         grid=(count,),
         in_specs=[
+            pl.BlockSpec(memory_space=pltpu.SMEM),
             whole(query_pack.shape),
             pl.BlockSpec((1, slots + EXTRA, width), lambda p: (p, 0, 0)),
             whole(ids.shape),
@@ -130,15 +132,15 @@
             jax.ShapeDtypeStruct((parts, 8, width), F32),
         ],
         scratch_shapes=[pltpu.VMEM((count, rows), F32)],
-        compiler_params=pltpu.CompilerParams(vmem_limit_bytes=20 * MIB),
+        compiler_params=pltpu.CompilerParams(vmem_limit_bytes=12 * MIB),
         cost_estimate=pl.CostEstimate(
             flops=4 * work * width, transcendentals=work, bytes_accessed=4 * work
         ),
-    )(query_pack, passage_pack, ids)
+    )(flip, query_pack, passage_pack, ids)
 
 
 def backward_kernel(
-    query_len, q_ref, exp_ref, mix_ref, inv_ref, sim_ref, stats_ref, pg_ref, qg_ref, qt, scale, sums
+    query_len, flip_ref, q_ref, exp_ref, mix_ref, inv_ref, sim_ref, stats_ref, pg_ref, qg_ref, qt, scale, sums
 ):
     passage = pl.program_id(0)
     parts, q_rows, width = q_ref.shape[0], q_ref.shape[1] - EXTRA, q_ref.shape[2]
@@ -174,7 +176,7 @@
         for k in range(pg_ref.shape[0]):
             pg_ref[k, slots:, :] = lines.astype(BF16)
         for k in range(parts):
-            qt[:, k * q_rows : (k + 1) * q_rows] = q_ref[k, :q_rows, :].T
+            qt[:, k * q_rows : (k + 1) * q_rows] = q_ref[k ^ flip_ref[0], :q_rows, :].T
         sums[...] = jnp.zeros_like(sums)
 
     factor = scale[pl.ds(passage, 1), :]
@@ -186,10 +188,10 @@
     @pl.when(passage == pl.num_programs(0) - 1)
     def _():
         for k in range(parts):
-            qg_ref[k % 2, k // 2] = sums[:, k * q_rows : (k + 1) * q_rows].T.astype(BF16)
-
-
-def backward_tile(query_pack, spread, mixed, inverse, similar, stats, query_len):
+            qg_ref[k % 2, k // 2 % 2, k // 4] = sums[:, k * q_rows : (k + 1) * q_rows].T.astype(BF16)
+
+
+def backward_tile(flip, query_pack, spread, mixed, inverse, similar, stats, query_len):
     parts, q_rows, width = query_pack.shape
     q_rows -= EXTRA
     count, slots, rows = spread.shape
@@ -199,6 +201,7 @@
         name="backward_tile",
         grid=(count,),
         in_specs=[
+            pl.BlockSpec(memory_space=pltpu.SMEM),
             whole(query_pack.shape),
             pl.BlockSpec(memory_space=pltpu.VMEM),
             pl.BlockSpec(memory_space=pltpu.VMEM),
@@ -206,21 +209,21 @@
             whole(similar.shape),
             whole(stats.shape),
         ],
-        out_specs=[whole((count, slots + EXTRA, width)), whole((2, parts // 2, q_rows, width))],
+        out_specs=[whole((count, slots + EXTRA, width)), whole((2, 2, parts // 4, q_rows, width))],
         out_shape=[
-            jax.ShapeDtypeStruct((count, slots + EXTRA, width), BF16),
-            jax.ShapeDtypeStruct((2, parts // 2, q_rows, width), BF16),
+            pltpu.HBM((count, slots + EXTRA, width), BF16),
+            pltpu.HBM((2, 2, parts // 4, q_rows, width), BF16),
         ],
         scratch_shapes=[
             pltpu.VMEM((width, rows), BF16),
             pltpu.VMEM((count, rows), F32),
             pltpu.VMEM((width, rows), F32),
         ],
-        compiler_params=pltpu.CompilerParams(vmem_limit_bytes=20 * MIB),
+        compiler_params=pltpu.CompilerParams(vmem_limit_bytes=12 * MIB),
         cost_estimate=pl.CostEstimate(
             flops=2 * work * width, transcendentals=0, bytes_accessed=3 * work
         ),
-    )(query_pack, spread, mixed, inverse, similar, stats)
+    )(flip, query_pack, spread, mixed, inverse, similar, stats)
 
 
 def early_kernel(resid_ref, context_ref, proj_ref, normed_ref, inv_ref, context_t_ref):
@@ -251,11 +254,11 @@
             pl.BlockSpec((width, block), lambda r: (0, r)),
         ],
         out_shape=[
-            jax.ShapeDtypeStruct((rows, width), F32),
-            jax.ShapeDtypeStruct((rows, 128), F32),
-            jax.ShapeDtypeStruct((width, rows), BF16),
-        ],
-        compiler_params=pltpu.CompilerParams(vmem_limit_bytes=24 * MIB),
+            pltpu.HBM((rows, width), F32),
+            pltpu.HBM((rows, 128), F32),
+            pltpu.HBM((width, rows), BF16),
+        ],
+        compiler_params=pltpu.CompilerParams(vmem_limit_bytes=10 * MIB),
         cost_estimate=pl.CostEstimate(
             flops=2 * rows * width * width, transcendentals=0, bytes_accessed=10 * rows * width
         ),
@@ -263,8 +266,28 @@
 
 
 def late_kernel(
-    parts_ref, normed_ref, inv_ref, gain_ref, colbert_ref, context_t_ref, resid_ref, sums_ref, loss_ref
+    parts_ref,
+    normed_far,
+    inv_far,
+    gain_ref,
+    colbert_ref,
+    context_far,
+    resid_ref,
+    sums_ref,
+    loss_ref,
+    normed_ref,
+    inv_ref,
+    context_t_ref,
+    sems,
 ):
+    loads = [
+        pltpu.make_async_copy(far, near, sems.at[k])
+        for k, (far, near) in enumerate(
+            ((normed_far, normed_ref), (inv_far, inv_ref), (context_far, context_t_ref))
+        )
+    ]
+    for load in loads:
+        load.start()
     slots = parts_ref.shape[1] - EXTRA
     count = parts_ref.shape[0]
     width = normed_ref.shape[1]
@@ -275,10 +298,13 @@
         jnp.sum(total[slots:], axis=0, keepdims=True), loss_ref.shape
     )
     grad = total[:slots].astype(BF16)
+    gain = gain_ref[...]
+    gained = dot(grad, colbert_ref[...], ((1,), (1,))) * gain
+    grad_t = grad.T
+    for load in loads[:2]:
+        load.wait()
     normed = normed_ref[...]
-    gain = gain_ref[...]
     inv_std = inv_ref[:, :1]
-    gained = dot(grad, colbert_ref[...], ((1,), (1,))) * gain
     resid = inv_std * (
         gained
         - jnp.mean(gained, axis=1, keepdims=True)
@@ -287,32 +313,67 @@
     resid = resid.astype(BF16)
     resid_ref[...] = resid
     scaled = (normed * gain).astype(BF16)
-    sums_ref[width:, :] = dot(grad.T, scaled, ((1,), (0,))).astype(BF16)
-    step = 256
-    for k in range(width // step):
-        sums_ref[k * step : (k + 1) * step, :] = dot(
-            context_t_ref[k * step : (k + 1) * step, :], resid, ((1,), (0,))
+    blocks, lines = sums_ref.shape[1], sums_ref.shape[3]
+    thin = grad.shape[1] // (2 * blocks)
+    thick = lines - thin
+    colbert = dot(grad_t, scaled, ((1,), (0,)))
+    for k in range(2 * blocks):
+        for j in range(width // 128):
+            sums_ref[k // blocks, k % blocks, j, thick:, :] = colbert[
+                k * thin : (k + 1) * thin, j * 128 : (j + 1) * 128
+            ].astype(BF16)
+    loads[2].wait()
+    group = 4
+    for first in range(0, 2 * blocks, group):
+        part = dot(
+            context_t_ref[first * thick : (first + group) * thick, :], resid, ((1,), (0,))
         ).astype(BF16)
-
-
-def late_rows(pieces, normed, inv_std, gain, colbert_proj, context_t):
+        for k in range(first, first + group):
+            at = (k - first) * thick
+            for j in range(width // 128):
+                sums_ref[k // blocks, k % blocks, j, :thick, :] = part[
+                    at : at + thick, j * 128 : (j + 1) * 128
+                ]
+
+
+def far(array):
+    return pltpu.with_memory_space_constraint(array, pltpu.HBM)
+
+
+def late_rows(blocks, pieces, normed, inv_std, gain, colbert_proj, context_t):
     rows, width = normed.shape
     emb = colbert_proj.shape[1]
     return pl.pallas_call(
         late_kernel,
         name="late_rows",
+        in_specs=[
+            whole(pieces.shape),
+            pl.BlockSpec(memory_space=pltpu.HBM),
+            pl.BlockSpec(memory_space=pltpu.HBM),
+            whole(gain.shape),
+            whole(colbert_proj.shape),
+            pl.BlockSpec(memory_space=pltpu.HBM),
+        ],
+        scratch_shapes=[
+            pltpu.VMEM(normed.shape, F32),
+            pltpu.VMEM(inv_std.shape, F32),
+            pltpu.VMEM(context_t.shape, BF16),
+            pltpu.SemaphoreType.DMA((3,)),
+        ],
         out_shape=[
             jax.ShapeDtypeStruct((rows, width), BF16),
-            jax.ShapeDtypeStruct((width + emb, width), BF16),
+            jax.ShapeDtypeStruct(
+                (2, blocks, width // 128, (width + emb) // (2 * blocks), 128), BF16
+            ),
             jax.ShapeDtypeStruct((8, emb), F32),
         ],
-        compiler_params=pltpu.CompilerParams(vmem_limit_bytes=40 * MIB),
+        compiler_params=pltpu.CompilerParams(vmem_limit_bytes=24 * MIB),
         cost_estimate=pl.CostEstimate(
             flops=2 * rows * width * (width + 2 * emb),
             transcendentals=0,
             bytes_accessed=14 * rows * width,
         ),
-    )(pieces, normed, inv_std, gain, colbert_proj, context_t)
+    )(pieces, far(normed), far(inv_std), gain, colbert_proj, far(context_t))
 
 
 def exchange(pieces, axis):
@@ -329,14 +390,18 @@
 
 
 def finish_kernel(core_ref, half_ref, other_ref, colbert_ref, gain_ref, proj_ref, grad_ref, gain_grad_ref):
-    rows = half_ref.shape[0]
-    top = proj_ref.shape[0] - rows
+    blocks, lines = half_ref.shape[0], half_ref.shape[2]
+    thick = proj_ref.shape[0] // (2 * blocks)
     even = core_ref[0] == 0
-    half, other = half_ref[...], other_ref[...]
-    proj_ref[:rows, :] = jnp.where(even, half, other).astype(F32)
-    second = jnp.where(even, other, half).astype(F32)
-    proj_ref[rows:, :] = second[:top]
-    colbert_grad = second[top:]
+    thin = []
+    for part in range(2):
+        for k in range(blocks):
+            half, other = half_ref[k, 0].astype(F32), other_ref[k, 0].astype(F32)
+            piece = jnp.where(even, half, other) if part == 0 else jnp.where(even, other, half)
+            at = (part * blocks + k) * thick
+            proj_ref[at : at + thick, :] = piece[:thick]
+            thin.append(piece[thick:])
+    colbert_grad = jnp.concatenate(thin, axis=0)
     colbert_t = colbert_ref[...].astype(F32).T
     gain_grad_ref[...] = (
         jnp.sum(colbert_grad * colbert_t, axis=0, keepdims=True) / gain_ref[...]
@@ -344,42 +409,59 @@
     grad_ref[...] = colbert_grad.T
 
 
-def finish(core, half, other, colbert_proj, gain, block=256):
-    rows, width = half.shape
-    emb = colbert_proj.shape[1]
+def finish(core, half, other, colbert_proj, gain):
+    blocks, columns, lines, block = half.shape
+    width, emb = colbert_proj.shape
     return pl.pallas_call(
         finish_kernel,
         name="finish",
-        grid=(width // block,),
+        grid=(columns,),
         in_specs=[
             pl.BlockSpec(memory_space=pltpu.SMEM),
-            pl.BlockSpec((rows, block), lambda k: (0, k)),
-            pl.BlockSpec((rows, block), lambda k: (0, k)),
+            pl.BlockSpec((blocks, 1, lines, block), lambda k: (0, k, 0, 0)),
+            pl.BlockSpec((blocks, 1, lines, block), lambda k: (0, k, 0, 0)),
             pl.BlockSpec((block, emb), lambda k: (k, 0)),
             pl.BlockSpec((1, block), lambda k: (0, k)),
         ],
         out_specs=[
-            pl.BlockSpec((2 * rows - emb, block), lambda k: (0, k)),
+            pl.BlockSpec((width, block), lambda k: (0, k)),
             pl.BlockSpec((block, emb), lambda k: (k, 0)),
             pl.BlockSpec((1, block), lambda k: (0, k)),
         ],
         out_shape=[
-            jax.ShapeDtypeStruct((2 * rows - emb, width), F32),
+            jax.ShapeDtypeStruct((width, width), F32),
             jax.ShapeDtypeStruct((width, emb), F32),
             jax.ShapeDtypeStruct((1, width), F32),
         ],
-        compiler_params=pltpu.CompilerParams(vmem_limit_bytes=24 * MIB),
+        compiler_params=pltpu.CompilerParams(vmem_limit_bytes=16 * MIB),
         cost_estimate=pl.CostEstimate(
-            flops=4 * rows * width, transcendentals=0, bytes_accessed=16 * rows * width
+            flops=4 * width * width, transcendentals=0, bytes_accessed=8 * width * width
         ),
-    )(core[None], half, other, colbert_proj, gain)
-
-
-def core_halves(halves, core):
-    given = lax.dynamic_index_in_dim(halves, 1 - core, 0, False)
-    kept = lax.dynamic_index_in_dim(halves, core, 0, False)
-    taken = lax.ppermute(given, CORE, [(0, 1), (1, 0)])
-    return (kept.astype(F32) + taken.astype(F32)).astype(BF16)
+    )(core, half, other, colbert_proj, gain)
+
+
+SWAP = [(0, 1), (1, 0)]
+
+
+def halves_summed(halves, axis, pairs, side, out_type):
+    given = lax.dynamic_index_in_dim(halves, 1 - side, 0, False)
+    kept = lax.dynamic_index_in_dim(halves, side, 0, False)
+    taken = lax.ppermute(given, axis, pairs)
+    return (kept.astype(F32) + taken.astype(F32)).astype(out_type)
+
+
+def crossed(parts, row, column):
+    parts = halves_summed(parts, "neg_1", SWAP, row, F32)
+    far, near = column // 2, column % 2
+    parts = parts.reshape(2, 2, *parts.shape[1:])
+    parts = halves_summed(parts, "neg_0", [(k, k ^ 2) for k in range(4)], far, F32)
+    return halves_summed(parts, "neg_0", [(k, k ^ 1) for k in range(4)], near, F32)
+
+
+def query_gathered(own):
+    pair = jnp.stack([own, lax.ppermute(own, CORE, SWAP)])
+    four = jnp.stack([pair, lax.ppermute(pair, "neg_1", SWAP)])
+    return lax.all_gather(four, "neg_0").reshape(-1, *own.shape)
 
 
 def body(
@@ -388,7 +470,6 @@
     query_dev, query_len, emb = query_emb.shape
     neg_size, dp_size, cross_size = lax.axis_size(NEG), lax.axis_size(DP), lax.axis_size(CROSS)
     place, core = lax.axis_index(NEG), lax.axis_index(CORE)
-    width = out_proj.shape[0]
     spot = jnp.arange(emb)[None] - place * query_dev
     wanted = jnp.sum(
         jnp.where(spot == jnp.arange(query_dev)[:, None], positive[:, None], 0), axis=0
@@ -405,42 +486,41 @@
             jnp.broadcast_to((lengths - LEAST).astype(BF16)[:, None], (EXTRA, emb)),
         ]
     )
-    query_pack = lax.all_gather(query_own, NEG)
+    query_pack = query_gathered(query_own)
     passage_pack = to_everyone(passage_own, DP)
     ids = jnp.broadcast_to(
         (jnp.arange(dp_size) * neg_size + place).astype(F32)[:, None], (dp_size, emb)
     )
-    early = early_rows(residual, context, out_proj)
-    (query_pack, passage_pack), early = lax.optimization_barrier(
-        ((query_pack, passage_pack), early)
-    )
-    normed, inv_std, context_t = early
-    spread, mixed, inverse, similar, stats = forward_tile(query_pack, passage_pack, ids, query_len)
+    row, column = lax.axis_index("neg_1"), lax.axis_index("neg_0")
+    flip = (2 * row + core)[None]
+    spread, mixed, inverse, similar, stats = forward_tile(
+        flip, query_pack, passage_pack, ids, query_len
+    )
     stats = exchange(stats, NEG)
     passage_parts, query_parts = backward_tile(
-        query_pack, spread, mixed, inverse, similar, stats, query_len
-    )
-    query_half = core_halves(query_parts, core)
+        flip, query_pack, spread, mixed, inverse, similar, stats, query_len
+    )
+    residual, query_parts = lax.optimization_barrier((residual, query_parts))
+    early = early_rows(residual, context, out_proj)
+    query_half = halves_summed(query_parts, CORE, SWAP, core, BF16)
     passage_parts = exchange(passage_parts, DP)
-    passage_parts, query_half = lax.optimization_barrier((passage_parts, query_half))
+    passage_parts, query_half, early = lax.optimization_barrier((passage_parts, query_half, early))
+    normed, inv_std, context_t = early
     residual_grad, partial, loss_sum = late_rows(
-        passage_parts, normed, inv_std, norm_gain[None], colbert_proj, context_t
-    )
-    half = core_halves(partial.reshape(2, -1, width), core)
+        dp_size, passage_parts, normed, inv_std, norm_gain[None], colbert_proj, context_t
+    )
+    half = halves_summed(partial, CORE, SWAP, core, BF16)
     context_grad = jnp.dot(residual_grad, out_proj.T, preferred_element_type=F32).astype(BF16)
-    slabs = exchange(half.reshape(dp_size, -1, width), DP)
-    slabs, context_grad = lax.optimization_barrier((slabs, context_grad))
-    slab = summed(slabs)
-    lines = slab.shape[0]
-    tiles = slab.reshape(lines, cross_size, -1).swapaxes(0, 1)
-    tiles = exchange(jnp.concatenate([tiles, query_half], axis=1), CROSS)
-    tile = jnp.sum(tiles.astype(F32), axis=0)
-    query_grad = tile[lines:].reshape(query_dev, query_len, emb)
-    slab = to_everyone(tile[:lines].astype(BF16), CROSS).swapaxes(0, 1).reshape(lines, width)
-    half = to_everyone(slab, DP).reshape(-1, width)
-    other = lax.ppermute(half, CORE, [(0, 1), (1, 0)])
+    slabs = exchange(half.reshape(dp_size * cross_size, *half.shape[2:]), DP + CROSS)
+    slabs, context_grad, query_half = lax.optimization_barrier((slabs, context_grad, query_half))
+    tile = summed(slabs)
+    half = to_everyone(tile, DP + CROSS).reshape(half.shape)
+    query_grad = crossed(query_half, row, column)
+    half, query_grad = lax.optimization_barrier((half, query_grad))
+    query_grad = query_grad.reshape(query_dev, query_len, emb)
+    other = lax.ppermute(half, CORE, SWAP)
     out_proj_grad, colbert_grad, gain_grad = finish(
-        core, half, other, colbert_proj, norm_gain[None]
+        core[None], half, other, colbert_proj, norm_gain[None]
     )
     loss = loss_sum[0, 0] / (query_dev * dp_size * neg_size)
     return (

time: 185 us -> 175 us (0.946)
  blocking collectives: 74.8 us -> 26.1 us
  waiting for transfers between devices: 31 us -> 53.5 us
  starting transfers between devices: 22.5 us -> 36.9 us
  local copies, waits for them, and re-layouts: 11.8 us -> 8.08 us
  Pallas kernels: 34.4 us -> 37.9 us
  other arithmetic: 3.22 us -> 5.33 us
    all_to_all x4 -> x1, blocking collectives: 48.5 us -> 14.7 us  [exchange(): return lax.all_to_all(pieces, axis, 0, 0, tiled=True)]
    ppermute x3 -> x8, waiting for transfers between devices: 4.31 us -> 32.8 us  [the longest x5 19.5 us: halves_summed(): taken = lax.ppermute(given, axis, pairs)]
    all_gather x1, blocking collectives: 26.4 us -> 11.4 us  [query_gathered(): return lax.all_gather(four, 'neg_0').reshape(-1, *own.shape)]
    ppermute x3 -> x8, starting transfers between devices: 6.46 us -> 14.1 us  [the longest x5 6.66 us: halves_summed(): taken = lax.ppermute(given, axis, pairs)]
    all_to_all x3 -> x4, starting transfers between devices: 16 us -> 22.8 us  [exchange(): return lax.all_to_all(pieces, axis, 0, 0, tiled=True)]
    all_to_all x3 -> x4, waiting for transfers between devices: 26.7 us -> 20.7 us  [exchange(): return lax.all_to_all(pieces, axis, 0, 0, tiled=True)]
    unnamed x28 -> x18, local copies, waits for them, and re-layouts: 8.27 us -> 2.48 us
    pallas_call x2, Pallas kernels: 5.19 us -> 7.83 us  [the longest x1 3.97 us: late_rows(): pl.pallas_call(late_kernel, name='late_rows', in_specs=[whole(pieces.shap...]
  transfers between devices with their start and end apart: 6 -> 12, of which waited for: 5 -> 8; matrix products, arithmetic and copies ran while one was open for 3% -> 6% of each run, Pallas kernels for 2% -> 2%
where the time goes in v2:
time: 175 us
  waiting for transfers between devices  53.5 us (31%)
  Pallas kernels  37.9 us (22%)
  starting transfers between devices  36.9 us (21%)
  blocking collectives  26.1 us (15%)
  local copies, waits for them, and re-layouts  8.08 us (5%)
  other arithmetic  5.33 us (3%)
  matrix products  3.53 us (2%)
  between operations  3.26 us (2%)
    all_to_all x4, starting transfers between devices, exchange(): return lax.all_to_all(pieces, axis, 0, 0, tiled=True)  22.8 us
    all_to_all x4, waiting for transfers between devices, exchange(): return lax.all_to_all(pieces, axis, 0, 0, tiled=True)  20.7 us
    ppermute x5, waiting for transfers between devices, halves_summed(): taken = lax.ppermute(given, axis, pairs)  19.5 us
    pallas_call x1, Pallas kernels, forward_tile(): pl.pallas_call(functools.partial(forward_kernel, query_len, group), name=...  16.5 us
    all_to_all x1, blocking collectives, exchange(): return lax.all_to_all(pieces, axis, 0, 0, tiled=True)  14.7 us
    all_gather x1, blocking collectives, query_gathered(): return lax.all_gather(four, 'neg_0').reshape(-1, *own.shape)  11.4 us
    ppermute x1, waiting for transfers between devices, query_gathered(): four = jnp.stack([pair, lax.ppermute(pair, 'neg_1', SWAP)])  11.1 us
    pallas_call x1, Pallas kernels, backward_tile(): pl.pallas_call(functools.partial(backward_kernel, query_len), name='backw...  9.66 us
  transfers between devices with their start and end apart: 12, of which 8 were waited for; matrix products, arithmetic and copies ran while one was open for 6% of the time, Pallas kernels for 2%

profile of v2, /device:TPU:1, one launch (start us, length us, event | category | flops | bytes accessed | tf_op | source)
XLA Modules:
  0.0 174.6 jit_solution(14720028140462841573)
XLA Ops:
  0.6 0.0 copy-start.8
  0.6 0.0 copy-start.7
  1.3 0.9 concatenate.7
  2.2 1.1 broadcast_in_dim.33
  3.3 6.9 %all-to-all-start = ((bf16[8,520,128]{2,1,0:T(8,128)(2,1)}), bf16[8,520,128]{2,1,0:T(8,128)(2,1)S(1)}, u32[]{:S(2)}, u32[]{:S(2)}) async-start(bf16[8,520,128]{2,1,0:T(8,128)(2,1)} %broadcast_in_dim.33), calls=%async_computation | async-start | bytes 2129920 | tf_op jit(solution)/shard_map/all_to_all | solution.py:380
  10.2 0.0 copy-done.8
  10.2 0.1 select_reduce_fusion
  10.3 0.0 copy-done.7
  10.4 1.0 collective-permute-start
  11.4 0.9 collective-permute-done
  12.3 2.7 %collective-permute-start.1 = (bf16[2,136,128]{2,1,0:T(8,128)(2,1)S(1)}, bf16[2,136,128]{2,1,0:T(8,128)(2,1)S(1)}, u32[]{:S(2)}, u32[]{:S(2)}) collective-permute-start(bf16[2,136,128]{2,1,0:T(8,128)(2,1)S(1)} %get-tuple-element.64), channel_id=1, source_target_pairs={{0,2},{2,0},{1,3},{3,1},{4,6},{6,4},{5,7},{7,5},{8,10},{10,8},{9,1... | collective-permute-start | bytes 208904 | tf_op jit(solution)/shard_map/ppermute | solution.py:463
  15.0 11.1 %collective-permute-done.1 = bf16[2,136,128]{2,1,0:T(8,128)(2,1)S(1)} collective-permute-done((bf16[2,136,128]{2,1,0:T(8,128)(2,1)S(1)}, bf16[2,136,128]{2,1,0:T(8,128)(2,1)S(1)}, u32[]{:S(2)}, u32[]{:S(2)}) %collective-permute-start.1) | collective-permute-done | bytes 69664 | tf_op jit(solution)/shard_map/ppermute | solution.py:463
  26.1 11.4 %all-gather = bf16[8,2,136,128]{3,2,1,0:T(8,128)(2,1)S(1)} all-gather(bf16[2,2,136,128]{3,2,1,0:T(8,128)(2,1)S(1)} %pad_maximum_fusion), channel_id=2, replica_groups=mesh['dp_0'=4,'dp_1'=2,'neg_0'=4,'neg_1'=2,'neg_2'=2] {'neg_0'}, dimensions={0}, use_global_device_ids=true | all-gather | bytes 696320 | tf_op jit(solution)/shard_map/all_gather | solution.py:464
  37.5 0.0 all-to-all-done.p_ref
  37.5 0.1 broadcast_in_dim.34.ids_ref
  37.6 16.5 %forward_tile.1 = (bf16[8,512,2048]{2,1,0:T(8,128)(2,1)S(1)}, f32[8,128,2048]{2,1,0:T(8,128)S(1)}, f32[8,2048]{1,0:T(8,128)S(1)}, f32[2,8,64]{2,1,0:T(8,128)S(1)}, f32[16,8,128]{2,1,0:T(8,128)S(1)}) custom-call(s32[1]{0:T(128)} %bitcast.flip_ref, bf16[16,136,128]{2,1,0:T(8,128)(2,1)S(1)} %bitcast.46, bf16[8,520,128]{2,1,0:T(8,128)(2,1)S(1)} %all-to-all-done.p_ref, ...), custom_call_target="tpu_custom_call" | custom-call | flops 4294967296 | bytes 33554432 | tf_op jit(solution)/shard_map/forward_tile/pallas_call | solution.py:110
  54.1 14.7 %all_to_all.25.stats_ref = f32[16,8,128]{2,1,0:T(8,128)S(1)} all-to-all(f32[16,8,128]{2,1,0:T(8,128)S(1)} %get-tuple-element.39), channel_id=1, replica_groups=mesh['dp_0'=4,'dp_1'=2,'neg_0'=4,'neg_1'=2,'neg_2'=2] {'neg_0','neg_1','..., dimensions={0} | all-to-all | bytes 131072 | tf_op jit(solution)/shard_map/all_to_all | solution.py:380
  68.8 9.7 %backward_tile.1 = (bf16[8,520,128]{2,1,0:T(8,128)(2,1)}, bf16[2,2,4,128,128]{4,3,2,1,0:T(8,128)(2,1)}) custom-call(s32[1]{0:T(128)} %bitcast.flip_ref, bf16[16,136,128]{2,1,0:T(8,128)(2,1)S(1)} %bitcast.47, bf16[8,512,2048]{2,1,0:T(8,128)(2,1)S(1)} %get-tuple-element.35.exp_ref, f32[8,128,2048]{2,1,0:T(8,128)S(1)} %get-tuple-element.36.mix_ref, ...), custom_call_target="tpu_custom_call" | custom-call | flops 2147483648 | bytes 25165824 | tf_op jit(solution)/shard_map/backward_tile/pallas_call | solution.py:199
  78.5 0.0 copy-start
  78.5 4.8 %all-to-all-start.2 = ((bf16[8,520,128]{2,1,0:T(8,128)(2,1)}), bf16[8,520,128]{2,1,0:T(8,128)(2,1)S(1)}, u32[]{:S(2)}, u32[]{:S(2)}) async-start(bf16[8,520,128]{2,1,0:T(8,128)(2,1)} %get-tuple-element.40), calls=%async_computation.2 | async-start | bytes 2129920 | tf_op jit(solution)/shard_map/all_to_all | solution.py:380
  83.3 1.7 dynamic-slice_bitcast_fusion.1
  85.0 0.7 collective-permute-start.2
  85.6 0.0 copy-done
  85.6 0.0 copy-start.1
  85.6 1.2 copy-done.1
  86.9 0.0 copy-start.2
  86.9 1.2 copy-done.2
  88.1 0.0 copy-start.6
  88.1 0.0 copy-start.3
  88.1 0.0 copy-start.4
  88.1 3.9 %early_rows.1 = (f32[512,1024]{1,0:T(8,128)}, f32[512,128]{1,0:T(8,128)}, bf16[1024,512]{1,0:T(8,128)(2,1)}) custom-call(bf16[512,1024]{1,0:T(8,128)(2,1)S(1)} %copy-done.1, bf16[512,1024]{1,0:T(8,128)(2,1)S(1)} %copy-done.2, bf16[1024,1024]{1,0:T(8,128)(2,1)S(1)} %copy-done), custom_call_target="tpu_custom_call" | custom-call | flops 1073741824 | bytes 5242880 | tf_op jit(solution)/shard_map/early_rows/pallas_call | solution.py:242
  92.0 0.0 collective-permute-done.2
  92.0 0.0 copy-done.6
  92.0 1.7 fusion.1
  93.7 4.9 %all-to-all-done.2.parts_ref = bf16[8,520,128]{2,1,0:T(8,128)(2,1)S(1)} async-done(((bf16[8,520,128]{2,1,0:T(8,128)(2,1)}), bf16[8,520,128]{2,1,0:T(8,128)(2,1)S(1)}, u32[]{:S(2)}, u32[]{:S(2)}) %all-to-all-start.2) | async-done | bytes 1064992 | tf_op jit(solution)/shard_map/all_to_all | solution.py:380
  98.6 0.0 copy-done.3
  98.6 0.0 copy-done.4
  98.6 4.0 %late_rows.1 = (bf16[512,1024]{1,0:T(8,128)(2,1)}, bf16[2,8,8,72,128]{4,3,2,1,0:T(8,128)(2,1)S(1)}, f32[8,128]{1,0:T(8,128)S(1)}) custom-call(bf16[8,520,128]{2,1,0:T(8,128)(2,1)S(1)} %all-to-all-done.2.parts_ref, f32[512,1024]{1,0:T(8,128)} %get-tuple-element.48.normed_far, f32[512,128]{1,0:T(8,128)} %get-tuple-element.49.inv_far, f32[1,1024]{1,0:T(1,128)S(1)} %bitcast.48, ...), custom_call_target="tpu_custom_call" | custom-call | flops 1342177280 | bytes 7340032 | tf_op jit(solution)/shard_map/late_rows/pallas_call | solution.py:346
  102.6 0.1 dynamic-slice_bitcast_fusion
  102.7 1.6 collective-permute-start.3
  104.3 2.5 %collective-permute-done.3 = bf16[8,8,72,128]{3,2,1,0:T(8,128)(2,1)S(1)} collective-permute-done((bf16[8,8,72,128]{3,2,1,0:T(8,128)(2,1)S(1)}, bf16[8,8,72,128]{3,2,1,0:T(8,128)(2,1)S(1)}, u32[]{:S(2)}, u32[]{:S(2)}) %collective-permute-start.3) | collective-permute-done | bytes 1179680 | tf_op jit(solution)/shard_map/ppermute | solution.py:449
  106.8 1.3 fusion
  108.1 5.5 %all-to-all-start.3 = ((bf16[64,72,128]{2,1,0:T(8,128)(2,1)}), bf16[64,72,128]{2,1,0:T(8,128)(2,1)}, u32[]{:S(2)}, u32[]{:S(2)}) async-start(bf16[64,72,128]{2,1,0:T(8,128)(2,1)} %bitcast.15), calls=%async_computation.3 | async-start | bytes 2359296 | tf_op jit(solution)/shard_map/all_to_all | solution.py:380
  113.6 0.0 copy-start.5
  113.6 3.5 %convolution_convert_fusion = bf16[512,1024]{1,0:T(8,128)(2,1)} fusion(bf16[512,1024]{1,0:T(8,128)(2,1)} %get-tuple-element.30, bf16[1024,1024]{1,0:T(8,128)(2,1)S(1)} %copy-done), kind=kOutput, calls=%fused_computation.2 | convolution fusion | flops 1074266112 | bytes 4194304 | tf_op jit(solution)/shard_map/dot_general | solution.py:513
  117.2 15.8 %all-to-all-done.3 = bf16[64,72,128]{2,1,0:T(8,128)(2,1)} async-done(((bf16[64,72,128]{2,1,0:T(8,128)(2,1)}), bf16[64,72,128]{2,1,0:T(8,128)(2,1)}, u32[]{:S(2)}, u32[]{:S(2)}) %all-to-all-start.3) | async-done | bytes 1179680 | tf_op jit(solution)/shard_map/all_to_all | solution.py:380
  132.9 0.0 copy-done.5
  133.0 1.4 collective-permute-start.4
  134.4 1.5 reduce_sum.22
  135.8 1.2 broadcast_in_dim.63
  137.0 5.6 %all-to-all-start.4 = ((bf16[64,72,128]{2,1,0:T(8,128)(2,1)}), bf16[64,72,128]{2,1,0:T(8,128)(2,1)S(1)}, u32[]{:S(2)}, u32[]{:S(2)}) async-start(bf16[64,72,128]{2,1,0:T(8,128)(2,1)} %broadcast_in_dim.63), calls=%async_computation.4 | async-start | bytes 2359296 | tf_op jit(solution)/shard_map/all_to_all | solution.py:380
  142.6 0.0 collective-permute-done.4
  142.7 2.6 %collective-permute-start.5 = (f32[2,128,128]{2,1,0:T(8,128)S(1)}, f32[2,128,128]{2,1,0:T(8,128)S(1)}, u32[]{:S(2)}, u32[]{:S(2)}) collective-permute-start(f32[2,128,128]{2,1,0:T(8,128)S(1)} %dynamic-slice_bitcast_fusion.2), channel_id=1, source_target_pairs={{0,8},{4,12},{8,0},{12,4},{1,9},{5,13},{9,1},{13,5},{2,10},{6,14},... | collective-permute-start | bytes 393224 | tf_op jit(solution)/shard_map/ppermute | solution.py:449
  145.3 13.9 %collective-permute-done.5 = f32[2,128,128]{2,1,0:T(8,128)S(1)} collective-permute-done((f32[2,128,128]{2,1,0:T(8,128)S(1)}, f32[2,128,128]{2,1,0:T(8,128)S(1)}, u32[]{:S(2)}, u32[]{:S(2)}) %collective-permute-start.5) | collective-permute-done | bytes 131104 | tf_op jit(solution)/shard_map/ppermute | solution.py:449
  159.2 0.4 collective-permute-start.6
  159.6 3.1 %collective-permute-done.6 = f32[128,128]{1,0:T(8,128)S(1)} collective-permute-done((f32[128,128]{1,0:T(8,128)S(1)}, f32[128,128]{1,0:T(8,128)S(1)}, u32[]{:S(2)}, u32[]{:S(2)}) %collective-permute-start.6) | collective-permute-done | bytes 65568 | tf_op jit(solution)/shard_map/ppermute | solution.py:449
  162.7 0.6 bitcast_add_fusion.1
  163.4 0.0 all-to-all-done.4
  163.4 3.7 %collective-permute-start.7 = (bf16[8,8,72,128]{3,2,1,0:T(8,128)(2,1)S(1)}, bf16[8,8,72,128]{3,2,1,0:T(8,128)(2,1)S(1)}, u32[]{:S(2)}, u32[]{:S(2)}) collective-permute-start(bf16[8,8,72,128]{3,2,1,0:T(8,128)(2,1)S(1)} %bitcast.44), channel_id=1, source_target_pairs={{0,1},{1,0},{2,3},{3,2},{4,5},{5,4},{6,7},{7,6},{8,9},{9,8},{10,11... | collective-permute-start | bytes 3538952 | tf_op jit(solution)/shard_map/ppermute | solution.py:521
  167.1 0.5 slice.3
  168.3 1.3 collective-permute-done.7.other_ref
  169.6 3.9 %finish.1 = (f32[1024,1024]{1,0:T(8,128)}, f32[1024,128]{1,0:T(8,128)}, f32[1,1024]{1,0:T(1,128)}) custom-call(s32[1]{0:T(128)} %bitcast.25.core_ref, bf16[8,8,72,128]{3,2,1,0:T(8,128)(2,1)S(1)} %bitcast.45, bf16[8,8,72,128]{3,2,1,0:T(8,128)(2,1)S(1)} %collective-permute-done.7.other_ref, bf16[1024,128]{1,0:T(8,128)(2,1)S(1)} %copy-done.3, ...), custom_call_target="tpu_custom_call" | custom-call | flops 4194304 | bytes 8388608 | tf_op jit(solution)/shard_map/finish/pallas_call | solution.py:415
  (12 shorter events, 0.1 us)
Async XLA Ops:
  0.6 9.6 %copy-start.8 = (s32[4]{0:T(128)S(1)}, s32[4]{0:T(128)}, u32[]{:S(2)}) copy-start(s32[4]{0:T(128)} %param.10) | copy-start | bytes 52
  0.6 9.7 %copy-start.7 = (bf16[4,32,128]{2,1,0:T(8,128)(2,1)S(1)}, bf16[4,32,128]{2,1,0:T(8,128)(2,1)}, u32[]{:S(2)}) copy-start(bf16[4,32,128]{2,1,0:T(8,128)(2,1)} %param.9) | copy-start | bytes 98308
  3.3 34.2 %all-to-all-start = ((bf16[8,520,128]{2,1,0:T(8,128)(2,1)}), bf16[8,520,128]{2,1,0:T(8,128)(2,1)S(1)}, u32[]{:S(2)}, u32[]{:S(2)}) async-start(bf16[8,520,128]{2,1,0:T(8,128)(2,1)} %broadcast_in_dim.33), calls=%async_computation | async-start | bytes 2129920 | tf_op jit(solution)/shard_map/all_to_all | solution.py:380
  10.4 1.9 %collective-permute-start = (bf16[136,128]{1,0:T(8,128)(2,1)S(1)}, bf16[136,128]{1,0:T(8,128)(2,1)S(1)}, u32[]{:S(2)}, u32[]{:S(2)}) collective-permute-start(bf16[136,128]{1,0:T(8,128)(2,1)S(1)} %get-tuple-element.66), channel_id=1, source_target_pairs={{0,1},{1,0},{2,3},{3,2},{4,5},{5,4},{6,7},{7,6},{8,9},{9,8},{10,11... | collective-permute-start | bytes 104456 | tf_op jit(solution)/shard_map/ppermute | solution.py:462
  12.3 13.8 %collective-permute-start.1 = (bf16[2,136,128]{2,1,0:T(8,128)(2,1)S(1)}, bf16[2,136,128]{2,1,0:T(8,128)(2,1)S(1)}, u32[]{:S(2)}, u32[]{:S(2)}) collective-permute-start(bf16[2,136,128]{2,1,0:T(8,128)(2,1)S(1)} %get-tuple-element.64), channel_id=1, source_target_pairs={{0,2},{2,0},{1,3},{3,1},{4,6},{6,4},{5,7},{7,5},{8,10},{10,8},{9,1... | collective-permute-start | bytes 208904 | tf_op jit(solution)/shard_map/ppermute | solution.py:463
  78.5 7.2 %copy-start = (bf16[1024,1024]{1,0:T(8,128)(2,1)S(1)}, bf16[1024,1024]{1,0:T(8,128)(2,1)}, u32[]{:S(2)}) copy-start(bf16[1024,1024]{1,0:T(8,128)(2,1)} %proj_ref.1) | copy-start | bytes 6291460
  78.5 20.1 %all-to-all-start.2 = ((bf16[8,520,128]{2,1,0:T(8,128)(2,1)}), bf16[8,520,128]{2,1,0:T(8,128)(2,1)S(1)}, u32[]{:S(2)}, u32[]{:S(2)}) async-start(bf16[8,520,128]{2,1,0:T(8,128)(2,1)} %get-tuple-element.40), calls=%async_computation.2 | async-start | bytes 2129920 | tf_op jit(solution)/shard_map/all_to_all | solution.py:380
  85.0 7.0 %collective-permute-start.2 = (bf16[2,4,128,128]{3,2,1,0:T(8,128)(2,1)}, bf16[2,4,128,128]{3,2,1,0:T(8,128)(2,1)}, u32[]{:S(2)}, u32[]{:S(2)}) collective-permute-start(bf16[2,4,128,128]{3,2,1,0:T(8,128)(2,1)} %dynamic-slice_bitcast_fusion.1), channel_id=1, source_target_pairs={{0,1},{1,0},{2,3},{3,2},{4,5},{5,4},{6,7},{7,6},{8,9},{9,8},{10,11... | collective-permute-start | bytes 786440 | tf_op jit(solution)/shard_map/ppermute | solution.py:449
  85.6 1.2 copy-start.1
  86.9 1.2 copy-start.2
  88.1 3.9 %copy-start.6 = (bf16[2,2,4,128,128]{4,3,2,1,0:T(8,128)(2,1)S(1)}, bf16[2,2,4,128,128]{4,3,2,1,0:T(8,128)(2,1)}, u32[]{:S(2)}) copy-start(bf16[2,2,4,128,128]{4,3,2,1,0:T(8,128)(2,1)} %get-tuple-element.42) | copy-start | bytes 1572868
  88.1 10.5 %copy-start.3 = (bf16[1024,128]{1,0:T(8,128)(2,1)S(1)}, bf16[1024,128]{1,0:T(8,128)(2,1)}, u32[]{:S(2)}) copy-start(bf16[1024,128]{1,0:T(8,128)(2,1)} %colbert_ref.3) | copy-start | bytes 786436
  88.1 10.5 %copy-start.4 = (f32[1024]{0:T(1024)S(1)}, f32[1024]{0:T(1024)}, u32[]{:S(2)}) copy-start(f32[1024]{0:T(1024)} %param.16) | copy-start | bytes 12292
  102.7 4.1 %collective-permute-start.3 = (bf16[8,8,72,128]{3,2,1,0:T(8,128)(2,1)S(1)}, bf16[8,8,72,128]{3,2,1,0:T(8,128)(2,1)S(1)}, u32[]{:S(2)}, u32[]{:S(2)}) collective-permute-start(bf16[8,8,72,128]{3,2,1,0:T(8,128)(2,1)S(1)} %dynamic-slice_bitcast_fusion), channel_id=1, source_target_pairs={{0,1},{1,0},{2,3},{3,2},{4,5},{5,4},{6,7},{7,6},{8,9},{9,8},{10,11... | collective-permute-start | bytes 3538952 | tf_op jit(solution)/shard_map/ppermute | solution.py:449
  108.1 24.8 %all-to-all-start.3 = ((bf16[64,72,128]{2,1,0:T(8,128)(2,1)}), bf16[64,72,128]{2,1,0:T(8,128)(2,1)}, u32[]{:S(2)}, u32[]{:S(2)}) async-start(bf16[64,72,128]{2,1,0:T(8,128)(2,1)} %bitcast.15), calls=%async_computation.3 | async-start | bytes 2359296 | tf_op jit(solution)/shard_map/all_to_all | solution.py:380
  113.6 19.3 %copy-start.5 = (bf16[2,4,128,128]{3,2,1,0:T(8,128)(2,1)S(1)}, bf16[2,4,128,128]{3,2,1,0:T(8,128)(2,1)}, u32[]{:S(2)}) copy-start(bf16[2,4,128,128]{3,2,1,0:T(8,128)(2,1)} %fusion.1) | copy-start | bytes 786436
  133.0 9.7 %collective-permute-start.4 = (bf16[4,128,128]{2,1,0:T(8,128)(2,1)S(1)}, bf16[4,128,128]{2,1,0:T(8,128)(2,1)S(1)}, u32[]{:S(2)}, u32[]{:S(2)}) collective-permute-start(bf16[4,128,128]{2,1,0:T(8,128)(2,1)S(1)} %dynamic-slice_bitcast_fusion.3), channel_id=1, source_target_pairs={{0,2},{2,0},{1,3},{3,1},{4,6},{6,4},{5,7},{7,5},{8,10},{10,8},{9,1... | collective-permute-start | bytes 393224 | tf_op jit(solution)/shard_map/ppermute | solution.py:449
  137.0 26.4 %all-to-all-start.4 = ((bf16[64,72,128]{2,1,0:T(8,128)(2,1)}), bf16[64,72,128]{2,1,0:T(8,128)(2,1)S(1)}, u32[]{:S(2)}, u32[]{:S(2)}) async-start(bf16[64,72,128]{2,1,0:T(8,128)(2,1)} %broadcast_in_dim.63), calls=%async_computation.4 | async-start | bytes 2359296 | tf_op jit(solution)/shard_map/all_to_all | solution.py:380
  142.7 16.5 %collective-permute-start.5 = (f32[2,128,128]{2,1,0:T(8,128)S(1)}, f32[2,128,128]{2,1,0:T(8,128)S(1)}, u32[]{:S(2)}, u32[]{:S(2)}) collective-permute-start(f32[2,128,128]{2,1,0:T(8,128)S(1)} %dynamic-slice_bitcast_fusion.2), channel_id=1, source_target_pairs={{0,8},{4,12},{8,0},{12,4},{1,9},{5,13},{9,1},{13,5},{2,10},{6,14},... | collective-permute-start | bytes 393224 | tf_op jit(solution)/shard_map/ppermute | solution.py:449
  159.2 3.5 %collective-permute-start.6 = (f32[128,128]{1,0:T(8,128)S(1)}, f32[128,128]{1,0:T(8,128)S(1)}, u32[]{:S(2)}, u32[]{:S(2)}) collective-permute-start(f32[128,128]{1,0:T(8,128)S(1)} %dynamic-slice_bitcast_fusion.4), channel_id=1, source_target_pairs={{0,4},{4,0},{8,12},{12,8},{1,5},{5,1},{9,13},{13,9},{2,6},{6,2},{1... | collective-permute-start | bytes 196616 | tf_op jit(solution)/shard_map/ppermute | solution.py:449
  163.4 6.2 %collective-permute-start.7 = (bf16[8,8,72,128]{3,2,1,0:T(8,128)(2,1)S(1)}, bf16[8,8,72,128]{3,2,1,0:T(8,128)(2,1)S(1)}, u32[]{:S(2)}, u32[]{:S(2)}) collective-permute-start(bf16[8,8,72,128]{3,2,1,0:T(8,128)(2,1)S(1)} %bitcast.44), channel_id=1, source_target_pairs={{0,1},{1,0},{2,3},{3,2},{4,5},{5,4},{6,7},{7,6},{8,9},{9,8},{10,11... | collective-permute-start | bytes 3538952 | tf_op jit(solution)/shard_map/ppermute | solution.py:521

commit v3 on v2

--- a/solution.py
+++ b/solution.py
@@ -36,29 +36,41 @@
     return pl.BlockSpec(shape, lambda *_: (0,) * len(shape))
 
 
+def stored(k, parts, flip_ref):
+    return ((k // 2 % 2) ^ flip_ref[0]) * (parts // 2) + k // 4 * 2 + ((k % 2) ^ flip_ref[1])
+
+
 def forward_kernel(
-    query_len, group, flip_ref, q_ref, p_ref, ids_ref, exp_ref, mix_ref, inv_ref, sim_ref, stats_ref, lse_ref
+    query_len, group, flip_ref, q_ref, p_ref, ids_ref, exp_ref, mix_ref, inv_ref, sim_ref, stats_ref, rows_ref
 ):
     passage = pl.program_id(0)
     parts, q_rows, width = q_ref.shape[0], q_ref.shape[1] - EXTRA, q_ref.shape[2]
     slots = p_ref.shape[1] - EXTRA
-    rows = parts * q_rows
+    count, rows = inv_ref.shape
     queries = rows // query_len
-    flip = flip_ref[0]
+    chunk = group * q_rows
+    steps = parts // group
     tokens = p_ref[0, :slots, :]
-    tokens_t = tokens.T
     length = p_ref[0, slots : slots + 1, :].astype(F32) + float(LEAST)
-    chunk = group * q_rows
-    wide = jnp.concatenate([length] * (chunk // width), axis=1)
-    position = lax.broadcasted_iota(jnp.int32, (slots - LEAST, chunk), 0).astype(F32) + float(LEAST)
-    usable = position < wide
-    log_length = jnp.log(wide)
-
-    steps = parts // group
+    log_length = jnp.log(length)[:, :1]
+    wide = jnp.concatenate([length] * ((slots - LEAST) // width), axis=1)
+    position = lax.broadcasted_iota(jnp.int32, wide.shape, 1).astype(F32) + float(LEAST)
+    bias = jnp.where(position < wide, 0.0, -1e30)
+    lane = lax.broadcasted_iota(jnp.int32, (chunk, width), 1)
+
+    @pl.when(passage == 0)
+    def _():
+        rows_ref[...] = jnp.zeros_like(rows_ref)
 
     def scores(step):
-        block = jnp.concatenate([q_ref[(step * group + k) ^ flip, :q_rows, :] for k in range(group)], axis=0)
-        return dot(tokens, block, ((1,), (1,)))
+        block = jnp.concatenate(
+            [
+                q_ref[stored(step * group + k, parts, flip_ref), :q_rows, :]
+                for k in range(group)
+            ],
+            axis=0,
+        )
+        return dot(block, tokens, ((1,), (1,)))
 
     ahead = scores(0)
     late = None
@@ -67,24 +79,31 @@
         if step + 1 < steps:
             ahead = scores(step + 1)
         if late is not None:
-            mix_ref[passage, :, pl.ds((step - 1) * chunk, chunk)] = dot(tokens_t, late, ((1,), (0,)))
-        sure, rest = now[:LEAST], jnp.where(usable, now[LEAST:], -1e30)
-        highest = jnp.max(sure, axis=0, keepdims=True)
-        highest = jnp.maximum(highest, jnp.max(rest, axis=0, keepdims=True))
+            mix_ref[passage, pl.ds((step - 1) * chunk, chunk), :] = dot(late, tokens, ((1,), (0,)))
+        sure, rest = now[:, :LEAST], now[:, LEAST:] + bias
+        highest = jnp.maximum(
+            jnp.max(sure, axis=1, keepdims=True), jnp.max(rest, axis=1, keepdims=True)
+        )
         sure = jnp.exp(sure - highest)
         rest = jnp.exp(rest - highest)
-        total = jnp.sum(sure, axis=0, keepdims=True) + jnp.sum(rest, axis=0, keepdims=True)
-        late = jnp.concatenate([sure.astype(BF16), rest.astype(BF16)], axis=0)
+        total = jnp.sum(sure, axis=1, keepdims=True) + jnp.sum(rest, axis=1, keepdims=True)
+        late = jnp.concatenate([sure.astype(BF16), rest.astype(BF16)], axis=1)
         at = pl.ds(step * chunk, chunk)
-        exp_ref[passage, :, at] = late
-        inv_ref[pl.ds(passage, 1), at] = 1.0 / total
-        lse_ref[pl.ds(passage, 1), at] = highest + jnp.log(total) - log_length
-    mix_ref[passage, :, pl.ds((steps - 1) * chunk, chunk)] = dot(tokens_t, late, ((1,), (0,)))
+        exp_ref[passage, at, :] = late
+        shifted = highest + jnp.log(total) - log_length
+        rows_ref[at, :] = jnp.where(
+            lane == passage,
+            shifted,
+            jnp.where(lane == passage + width // 2, total, rows_ref[at, :]),
+        )
+    mix_ref[passage, pl.ds((steps - 1) * chunk, chunk), :] = dot(late, tokens, ((1,), (0,)))
 
     @pl.when(passage == pl.num_programs(0) - 1)
     def _():
+        turned = rows_ref[...].T
+        inv_ref[...] = 1.0 / turned[width // 2 : width // 2 + count]
         similar = dot(
-            lse_ref[...], token_query(rows, queries, query_len), ((1,), (0,)), lax.Precision.HIGHEST
+            turned[:count], token_query(rows, queries, query_len), ((1,), (0,)), lax.Precision.HIGHEST
         )
         wanted = jnp.sum(q_ref[:, q_rows, :].astype(F32), axis=0, keepdims=True)[:, :queries]
         hit = (wanted == ids_ref[:, :queries]).astype(F32)
@@ -93,14 +112,12 @@
         positive = jnp.sum(jnp.where(hit > 0.0, similar, 0.0), axis=0, keepdims=True)
         sim_ref[0] = similar
         sim_ref[1] = hit
-        stats = jnp.concatenate(
-            [highest, total, positive, jnp.zeros((5, queries), F32)], axis=0
-        )
+        stats = jnp.concatenate([highest, total, positive, jnp.zeros((5, queries), F32)], axis=0)
         stats = jnp.concatenate([stats, jnp.zeros((8, width - queries), F32)], axis=1)
         stats_ref[...] = jnp.broadcast_to(stats[None], stats_ref.shape)
 
 
-def forward_tile(flip, query_pack, passage_pack, ids, query_len, group=4):
+def forward_tile(flip, query_pack, passage_pack, ids, query_len, group=8):
     parts, q_rows, width = query_pack.shape
     q_rows -= EXTRA
     count, slots = passage_pack.shape[0], passage_pack.shape[1] - EXTRA
@@ -125,14 +142,14 @@
             whole((parts, 8, width)),
         ],
         out_shape=[
-            pltpu.VMEM((count, slots, rows), BF16),
-            pltpu.VMEM((count, width, rows), F32),
+            pltpu.VMEM((count, rows, slots), BF16),
+            pltpu.VMEM((count, rows, width), F32),
             jax.ShapeDtypeStruct((count, rows), F32),
             jax.ShapeDtypeStruct((2, count, queries), F32),
             jax.ShapeDtypeStruct((parts, 8, width), F32),
         ],
-        scratch_shapes=[pltpu.VMEM((count, rows), F32)],
-        compiler_params=pltpu.CompilerParams(vmem_limit_bytes=12 * MIB),
+        scratch_shapes=[pltpu.VMEM((rows, width), F32)],
+        compiler_params=pltpu.CompilerParams(vmem_limit_bytes=16 * MIB),
         cost_estimate=pl.CostEstimate(
             flops=4 * work * width, transcendentals=work, bytes_accessed=4 * work
         ),
@@ -140,86 +157,63 @@
 
 
 def backward_kernel(
-    query_len, flip_ref, q_ref, exp_ref, mix_ref, inv_ref, sim_ref, stats_ref, pg_ref, qg_ref, qt, scale, sums
+    query_len, flip_ref, q_ref, exp_ref, mix_ref, inv_ref, sim_ref, stats_ref, pg_ref, qg_ref, qt
 ):
-    passage = pl.program_id(0)
     parts, q_rows, width = q_ref.shape[0], q_ref.shape[1] - EXTRA, q_ref.shape[2]
-    slots = exp_ref.shape[1]
-    rows = parts * q_rows
+    count, rows, slots = exp_ref.shape
     queries = rows // query_len
-
-    @pl.when(passage == 0)
-    def _():
-        highest_of = stats_ref[:, 0, :queries]
-        highest = jnp.max(highest_of, axis=0, keepdims=True)
-        total = jnp.sum(
-            stats_ref[:, 1, :queries] * jnp.exp(highest_of - highest), axis=0, keepdims=True
-        )
-        positive = jnp.sum(stats_ref[:, 2, :queries], axis=0, keepdims=True)
-        log_total = highest + jnp.log(total)
-        coefficient = jnp.exp(sim_ref[0] - log_total) - sim_ref[1]
-        spread = dot(
-            coefficient,
-            token_query(rows, queries, query_len, True),
-            ((1,), (0,)),
-            lax.Precision.HIGHEST,
-        )
-        scale[...] = spread * inv_ref[...]
-        loss = jnp.broadcast_to(
-            jnp.sum(log_total - positive, axis=1, keepdims=True), (EXTRA, width)
-        )
-        high = loss.astype(BF16).astype(F32)
-        low = (loss - high).astype(BF16).astype(F32)
-        last = loss - high - low
-        row = lax.broadcasted_iota(jnp.int32, (EXTRA, width), 0)
-        lines = jnp.where(row == 0, high, jnp.where(row == 1, low, jnp.where(row == 2, last, 0.0)))
-        for k in range(pg_ref.shape[0]):
-            pg_ref[k, slots:, :] = lines.astype(BF16)
-        for k in range(parts):
-            qt[:, k * q_rows : (k + 1) * q_rows] = q_ref[k ^ flip_ref[0], :q_rows, :].T
-        sums[...] = jnp.zeros_like(sums)
-
-    factor = scale[pl.ds(passage, 1), :]
-    weighted = (qt[...].astype(F32) * factor).astype(BF16)
-    grad_t = dot(weighted, exp_ref[passage], ((1,), (1,)))
-    pg_ref[passage, :slots, :] = grad_t.T.astype(BF16)
-    sums[...] += mix_ref[passage] * factor
-
-    @pl.when(passage == pl.num_programs(0) - 1)
-    def _():
-        for k in range(parts):
-            qg_ref[k % 2, k // 2 % 2, k // 4] = sums[:, k * q_rows : (k + 1) * q_rows].T.astype(BF16)
+    for k in range(parts):
+        qt[:, k * q_rows : (k + 1) * q_rows] = q_ref[stored(k, parts, flip_ref), :q_rows, :].T
+    highest_of = stats_ref[:, 0, :queries]
+    highest = jnp.max(highest_of, axis=0, keepdims=True)
+    total = jnp.sum(
+        stats_ref[:, 1, :queries] * jnp.exp(highest_of - highest), axis=0, keepdims=True
+    )
+    positive = jnp.sum(stats_ref[:, 2, :queries], axis=0, keepdims=True)
+    log_total = highest + jnp.log(total)
+    coefficient = jnp.exp(sim_ref[0] - log_total) - sim_ref[1]
+    scale = inv_ref[...] * dot(
+        coefficient,
+        token_query(rows, queries, query_len, True),
+        ((1,), (0,)),
+        lax.Precision.HIGHEST,
+    )
+    loss = jnp.broadcast_to(jnp.sum(log_total - positive, axis=1, keepdims=True), (EXTRA, width))
+    high = loss.astype(BF16).astype(F32)
+    low = (loss - high).astype(BF16).astype(F32)
+    last = loss - high - low
+    row = lax.broadcasted_iota(jnp.int32, (EXTRA, width), 0)
+    lines = jnp.where(row == 0, high, jnp.where(row == 1, low, jnp.where(row == 2, last, 0.0)))
+    for p in range(count):
+        weighted = (qt[...].astype(F32) * scale[p : p + 1]).astype(BF16)
+        pg_ref[p, :slots, :] = dot(weighted, exp_ref[p], ((1,), (0,))).T.astype(BF16)
+        pg_ref[p, slots:, :] = lines.astype(BF16)
+    turned = jnp.concatenate([scale, jnp.zeros((width - count, rows), F32)], axis=0).T
+    for k in range(parts):
+        at = slice(k * q_rows, (k + 1) * q_rows)
+        sums = mix_ref[0, at, :] * turned[at, :1]
+        for p in range(1, count):
+            sums += mix_ref[p, at, :] * turned[at, p : p + 1]
+        qg_ref[k % 2, k // 2 % 2, k // 4] = sums.astype(BF16)
 
 
 def backward_tile(flip, query_pack, spread, mixed, inverse, similar, stats, query_len):
     parts, q_rows, width = query_pack.shape
     q_rows -= EXTRA
-    count, slots, rows = spread.shape
+    count, rows, slots = spread.shape
     work = rows * slots * count
     return pl.pallas_call(
         functools.partial(backward_kernel, query_len),
         name="backward_tile",
-        grid=(count,),
-        in_specs=[
-            pl.BlockSpec(memory_space=pltpu.SMEM),
-            whole(query_pack.shape),
-            pl.BlockSpec(memory_space=pltpu.VMEM),
-            pl.BlockSpec(memory_space=pltpu.VMEM),
-            whole(inverse.shape),
-            whole(similar.shape),
-            whole(stats.shape),
-        ],
-        out_specs=[whole((count, slots + EXTRA, width)), whole((2, 2, parts // 4, q_rows, width))],
+        in_specs=[pl.BlockSpec(memory_space=pltpu.SMEM)]
+        + [pl.BlockSpec(memory_space=pltpu.VMEM)] * 6,
         out_shape=[
             pltpu.HBM((count, slots + EXTRA, width), BF16),
             pltpu.HBM((2, 2, parts // 4, q_rows, width), BF16),
         ],
-        scratch_shapes=[
-            pltpu.VMEM((width, rows), BF16),
-            pltpu.VMEM((count, rows), F32),
-            pltpu.VMEM((width, rows), F32),
-        ],
-        compiler_params=pltpu.CompilerParams(vmem_limit_bytes=12 * MIB),
+        out_specs=[whole((count, slots + EXTRA, width)), whole((2, 2, parts // 4, q_rows, width))],
+        scratch_shapes=[pltpu.VMEM((width, rows), BF16)],
+        compiler_params=pltpu.CompilerParams(vmem_limit_bytes=16 * MIB),
         cost_estimate=pl.CostEstimate(
             flops=2 * work * width, transcendentals=0, bytes_accessed=3 * work
         ),
@@ -380,15 +374,6 @@
     return lax.all_to_all(pieces, axis, 0, 0, tiled=True)
 
 
-def to_everyone(array, axis):
-    size = lax.axis_size(axis)
-    return exchange(jnp.broadcast_to(array[None], (size, *array.shape)), axis)
-
-
-def summed(pieces):
-    return jnp.sum(pieces.astype(F32), axis=0).astype(BF16)
-
-
 def finish_kernel(core_ref, half_ref, other_ref, colbert_ref, gain_ref, proj_ref, grad_ref, gain_grad_ref):
     blocks, lines = half_ref.shape[0], half_ref.shape[2]
     thick = proj_ref.shape[0] // (2 * blocks)
@@ -441,27 +426,62 @@
 
 
 SWAP = [(0, 1), (1, 0)]
+FAR = [(k, k ^ 2) for k in range(4)]
+NEAR = [(k, k ^ 1) for k in range(4)]
 
 
 def halves_summed(halves, axis, pairs, side, out_type):
-    given = lax.dynamic_index_in_dim(halves, 1 - side, 0, False)
-    kept = lax.dynamic_index_in_dim(halves, side, 0, False)
+    keep, give = side
+    given = lax.dynamic_index_in_dim(halves, give, 0, False)
+    kept = lax.dynamic_index_in_dim(halves, keep, 0, False)
     taken = lax.ppermute(given, axis, pairs)
     return (kept.astype(F32) + taken.astype(F32)).astype(out_type)
 
 
-def crossed(parts, row, column):
-    parts = halves_summed(parts, "neg_1", SWAP, row, F32)
-    far, near = column // 2, column % 2
-    parts = parts.reshape(2, 2, *parts.shape[1:])
-    parts = halves_summed(parts, "neg_0", [(k, k ^ 2) for k in range(4)], far, F32)
-    return halves_summed(parts, "neg_0", [(k, k ^ 1) for k in range(4)], near, F32)
-
-
 def query_gathered(own):
     pair = jnp.stack([own, lax.ppermute(own, CORE, SWAP)])
-    four = jnp.stack([pair, lax.ppermute(pair, "neg_1", SWAP)])
-    return lax.all_gather(four, "neg_0").reshape(-1, *own.shape)
+    line = lax.all_gather(pair, "neg_0")
+    both = jnp.stack([line, lax.ppermute(line, "neg_1", SWAP)])
+    return both.reshape(-1, *own.shape)
+
+
+def pack_kernel(length_ref, p_ref, out_ref):
+    slots = p_ref.shape[1]
+    extra = jnp.full((EXTRA, p_ref.shape[2]), (length_ref[0] - LEAST).astype(F32)).astype(BF16)
+    for k in range(out_ref.shape[0]):
+        out_ref[k, :slots, :] = p_ref[0]
+        out_ref[k, slots:, :] = extra
+
+
+def passage_copies(passage_emb, lengths, copies):
+    _, slots, width = passage_emb.shape
+    return pl.pallas_call(
+        pack_kernel,
+        name="passage_copies",
+        in_specs=[
+            pl.BlockSpec(memory_space=pltpu.SMEM),
+            pl.BlockSpec(memory_space=pltpu.VMEM),
+        ],
+        out_specs=whole((copies, slots + EXTRA, width)),
+        out_shape=pltpu.HBM((copies, slots + EXTRA, width), BF16),
+    )(lengths, passage_emb)
+
+
+def spread_kernel(parts_ref, out_ref):
+    total = parts_ref[0].astype(F32)
+    for k in range(1, parts_ref.shape[0]):
+        total += parts_ref[k].astype(F32)
+    out_ref[...] = jnp.broadcast_to(total.astype(BF16)[None], out_ref.shape)
+
+
+def summed_copies(parts):
+    return pl.pallas_call(
+        spread_kernel,
+        name="summed_copies",
+        in_specs=[pl.BlockSpec(memory_space=pltpu.VMEM)],
+        out_specs=whole(parts.shape),
+        out_shape=pltpu.HBM(parts.shape, BF16),
+    )(parts)
 
 
 def body(
@@ -480,19 +500,19 @@
             jnp.broadcast_to(wanted.astype(BF16)[None], (EXTRA, emb)),
         ]
     )
-    passage_own = jnp.concatenate(
-        [
-            passage_emb.reshape(-1, emb),
-            jnp.broadcast_to((lengths - LEAST).astype(BF16)[:, None], (EXTRA, emb)),
-        ]
-    )
     query_pack = query_gathered(query_own)
-    passage_pack = to_everyone(passage_own, DP)
+    passage_pack = exchange(passage_copies(passage_emb, lengths, dp_size), DP)
     ids = jnp.broadcast_to(
         (jnp.arange(dp_size) * neg_size + place).astype(F32)[:, None], (dp_size, emb)
     )
     row, column = lax.axis_index("neg_1"), lax.axis_index("neg_0")
-    flip = (2 * row + core)[None]
+    flip = jnp.stack([row, core])
+    sides = [
+        (own.astype(jnp.uint32), (1 - own).astype(jnp.uint32))
+        for own in (core, row, column // 2, column % 2)
+    ]
+    query_pack, sides = lax.optimization_barrier((query_pack, sides))
+    core_side, row_side, far_side, near_side = sides
     spread, mixed, inverse, similar, stats = forward_tile(
         flip, query_pack, passage_pack, ids, query_len
     )
@@ -502,20 +522,22 @@
     )
     residual, query_parts = lax.optimization_barrier((residual, query_parts))
     early = early_rows(residual, context, out_proj)
-    query_half = halves_summed(query_parts, CORE, SWAP, core, BF16)
+    query_part = halves_summed(query_parts, CORE, SWAP, core_side, BF16)
+    query_part = halves_summed(query_part, "neg_1", SWAP, row_side, F32)
     passage_parts = exchange(passage_parts, DP)
-    passage_parts, query_half, early = lax.optimization_barrier((passage_parts, query_half, early))
+    passage_parts, query_part, early = lax.optimization_barrier((passage_parts, query_part, early))
     normed, inv_std, context_t = early
     residual_grad, partial, loss_sum = late_rows(
         dp_size, passage_parts, normed, inv_std, norm_gain[None], colbert_proj, context_t
     )
-    half = halves_summed(partial, CORE, SWAP, core, BF16)
+    half = halves_summed(partial, CORE, SWAP, core_side, BF16)
     context_grad = jnp.dot(residual_grad, out_proj.T, preferred_element_type=F32).astype(BF16)
     slabs = exchange(half.reshape(dp_size * cross_size, *half.shape[2:]), DP + CROSS)
-    slabs, context_grad, query_half = lax.optimization_barrier((slabs, context_grad, query_half))
-    tile = summed(slabs)
-    half = to_everyone(tile, DP + CROSS).reshape(half.shape)
-    query_grad = crossed(query_half, row, column)
+    query_part = query_part.reshape(2, 2, *query_part.shape[1:])
+    query_part = halves_summed(query_part, "neg_0", FAR, far_side, F32)
+    slabs, context_grad, query_part = lax.optimization_barrier((slabs, context_grad, query_part))
+    half = exchange(summed_copies(slabs), DP + CROSS).reshape(half.shape)
+    query_grad = halves_summed(query_part, "neg_0", NEAR, near_side, F32)
     half, query_grad = lax.optimization_barrier((half, query_grad))
     query_grad = query_grad.reshape(query_dev, query_len, emb)
     other = lax.ppermute(half, CORE, SWAP)

time: 175 us -> 170 us (0.971)
  waiting for transfers between devices: 53.5 us -> 46.4 us
  starting transfers between devices: 36.9 us -> 40.8 us
  local copies, waits for them, and re-layouts: 8.08 us -> 4.33 us
  Pallas kernels: 37.9 us -> 40.4 us
    all_to_all x4, waiting for transfers between devices: 20.7 us -> 5.07 us  [exchange(): return lax.all_to_all(pieces, axis, 0, 0, tiled=True)]
    ppermute x5, waiting for transfers between devices: 19.5 us -> 34.5 us  [halves_summed(): taken = lax.ppermute(given, axis, pairs)]
    ppermute x1, waiting for transfers between devices: 11.1 us -> 4.6 us  [query_gathered(): both = jnp.stack([line, lax.ppermute(line, 'neg_1', SWAP)])]
    pallas_call x0 -> x2, Pallas kernels: none -> 4.52 us  [the longest x1 2.51 us: summed_copies(): pl.pallas_call(spread_kernel, name='summed_copies', in_specs=[pl.BlockSpe...]
    all_to_all x4, starting transfers between devices: 22.8 us -> 27.2 us  [exchange(): return lax.all_to_all(pieces, axis, 0, 0, tiled=True)]
    pallas_call x1, Pallas kernels: 9.66 us -> 6.74 us  [backward_tile(): pl.pallas_call(functools.partial(backward_kernel, query_len), name='backw...]
    broadcast_in_dim x2 -> x0, local copies, waits for them, and re-layouts: 2.28 us -> none  [to_everyone(): return exchange(jnp.broadcast_to(array[None], (size, *array.shape)), axis)]
  transfers between devices with their start and end apart: 12 -> 12, of which waited for: 8 -> 9; matrix products, arithmetic and copies ran while one was open for 6% -> 4% of each run, Pallas kernels for 2% -> 2%
where the time goes in v3:
time: 170 us
  waiting for transfers between devices  46.4 us (27%)
  starting transfers between devices  40.8 us (24%)
  Pallas kernels  40.4 us (24%)
  blocking collectives  27 us (16%)
  local copies, waits for them, and re-layouts  4.33 us (3%)
  other arithmetic  4.06 us (2%)
  matrix products  3.49 us (2%)
  between operations  3.24 us (2%)
    ppermute x5, waiting for transfers between devices, halves_summed(): taken = lax.ppermute(given, axis, pairs)  34.5 us
    all_to_all x4, starting transfers between devices, exchange(): return lax.all_to_all(pieces, axis, 0, 0, tiled=True)  27.2 us
    pallas_call x1, Pallas kernels, forward_tile(): pl.pallas_call(functools.partial(forward_kernel, query_len, group), name=...  17.5 us
    all_to_all x1, blocking collectives, exchange(): return lax.all_to_all(pieces, axis, 0, 0, tiled=True)  16.4 us
    all_gather x1, blocking collectives, query_gathered(): line = lax.all_gather(pair, 'neg_0')  10.6 us
    pallas_call x1, Pallas kernels, backward_tile(): pl.pallas_call(functools.partial(backward_kernel, query_len), name='backw...  6.74 us
    ppermute x5, starting transfers between devices, halves_summed(): taken = lax.ppermute(given, axis, pairs)  6.36 us
    all_to_all x4, waiting for transfers between devices, exchange(): return lax.all_to_all(pieces, axis, 0, 0, tiled=True)  5.07 us
  transfers between devices with their start and end apart: 12, of which 9 were waited for; matrix products, arithmetic and copies ran while one was open for 4% of the time, Pallas kernels for 2%

profile of v3, /device:TPU:1, one launch (start us, length us, event | category | flops | bytes accessed | tf_op | source)
XLA Modules:
  0.0 169.7 jit_solution(15613097233763048103)
XLA Ops:
  0.6 0.0 copy-start.7
  0.6 0.0 copy-start.6
  1.3 2.0 %passage_copies.1 = bf16[8,520,128]{2,1,0:T(8,128)(2,1)} custom-call(s32[1]{0:T(128)S(6)} %copy.16.length_ref, bf16[1,512,128]{2,1,0:T(8,128)(2,1)} %p_ref.1), custom_call_target="tpu_custom_call" | custom-call | tf_op jit(solution)/shard_map/passage_copies/pallas_call | solution.py:458
  3.3 6.9 %all-to-all-start = ((bf16[8,520,128]{2,1,0:T(8,128)(2,1)}), bf16[8,520,128]{2,1,0:T(8,128)(2,1)S(1)}, u32[]{:S(2)}, u32[]{:S(2)}) async-start(bf16[8,520,128]{2,1,0:T(8,128)(2,1)} %passage_copies.1), calls=%async_computation | async-start | bytes 2129920 | tf_op jit(solution)/shard_map/all_to_all | solution.py:374
  10.2 0.0 copy-done.7
  10.2 0.1 select_reduce_fusion
  10.3 0.0 copy-done.6
  10.3 1.0 collective-permute-start
  11.4 0.9 collective-permute-done
  12.2 10.6 %all-gather = bf16[8,136,128]{2,1,0:T(8,128)(2,1)S(1)} all-gather(bf16[2,136,128]{2,1,0:T(8,128)(2,1)S(1)} %pad_maximum_fusion.1), channel_id=2, replica_groups=mesh['dp_0'=4,'dp_1'=2,'neg_0'=4,'neg_1'=2,'neg_2'=2] {'neg_0'}, dimensions={0}, use_global_device_ids=true | all-gather | bytes 348160 | tf_op jit(solution)/shard_map/all_gather | solution.py:443
  22.9 2.6 %collective-permute-start.1 = (bf16[4,2,136,128]{3,2,1,0:T(8,128)(2,1)S(1)}, bf16[4,2,136,128]{3,2,1,0:T(8,128)(2,1)S(1)}, u32[]{:S(2)}, u32[]{:S(2)}) collective-permute-start(bf16[4,2,136,128]{3,2,1,0:T(8,128)(2,1)S(1)} %bitcast.48), channel_id=1, source_target_pairs={{0,2},{2,0},{1,3},{3,1},{4,6},{6,4},{5,7},{7,5},{8,10},{10,8},{9,1... | collective-permute-start | bytes 835592 | tf_op jit(solution)/shard_map/ppermute | solution.py:444
  25.5 0.1 pad_add_fusion.flip_ref
  25.6 4.6 %collective-permute-done.1 = bf16[4,2,136,128]{3,2,1,0:T(8,128)(2,1)S(1)} collective-permute-done((bf16[4,2,136,128]{3,2,1,0:T(8,128)(2,1)S(1)}, bf16[4,2,136,128]{3,2,1,0:T(8,128)(2,1)S(1)}, u32[]{:S(2)}, u32[]{:S(2)}) %collective-permute-start.1) | collective-permute-done | bytes 278560 | tf_op jit(solution)/shard_map/ppermute | solution.py:444
  30.2 0.1 pad_maximum_fusion
  30.2 0.0 all-to-all-done.p_ref
  30.3 0.1 broadcast_in_dim.21.ids_ref
  30.3 17.5 %forward_tile.1 = (bf16[8,2048,512]{2,1,0:T(8,128)(2,1)S(1)}, f32[8,2048,128]{2,1,0:T(8,128)S(1)}, f32[8,2048]{1,0:T(8,128)S(1)}, f32[2,8,64]{2,1,0:T(8,128)S(1)}, f32[16,8,128]{2,1,0:T(8,128)S(1)}) custom-call(s32[2]{0:T(128)S(1)} %pad_add_fusion.flip_ref, bf16[16,136,128]{2,1,0:T(8,128)(2,1)S(1)} %bitcast.44, bf16[8,520,128]{2,1,0:T(8,128)(2,1)S(1)} %all-to-all-done.p_ref, ...), custom_call_target="tpu_custom_call" | custom-call | flops 4294967296 | bytes 33554432 | tf_op jit(solution)/shard_map/forward_tile/pallas_call | solution.py:127
  47.8 16.4 %all_to_all.25.stats_ref = f32[16,8,128]{2,1,0:T(8,128)S(1)} all-to-all(f32[16,8,128]{2,1,0:T(8,128)S(1)} %get-tuple-element.49), channel_id=1, replica_groups=mesh['dp_0'=4,'dp_1'=2,'neg_0'=4,'neg_1'=2,'neg_2'=2] {'neg_0','neg_1','..., dimensions={0} | all-to-all | bytes 131072 | tf_op jit(solution)/shard_map/all_to_all | solution.py:374
  64.2 6.7 %backward_tile.1 = (bf16[8,520,128]{2,1,0:T(8,128)(2,1)}, bf16[2,2,4,128,128]{4,3,2,1,0:T(8,128)(2,1)}) custom-call(s32[2]{0:T(128)S(1)} %pad_add_fusion.flip_ref, bf16[16,136,128]{2,1,0:T(8,128)(2,1)S(1)} %bitcast.45, bf16[8,2048,512]{2,1,0:T(8,128)(2,1)S(1)} %get-tuple-element.45.exp_ref, f32[8,2048,128]{2,1,0:T(8,128)S(1)} %get-tuple-element.46.mix_ref, ...), custom_call_target="tpu_custom_call" | custom-call | flops 2147483648 | bytes 25165824 | tf_op jit(solution)/shard_map/backward_tile/pallas_call | solution.py:205
  71.0 0.0 copy-start
  71.0 1.1 dynamic-slice_bitcast_fusion.1
  72.1 0.5 collective-permute-start.2
  72.5 4.8 %all-to-all-start.2 = ((bf16[8,520,128]{2,1,0:T(8,128)(2,1)}), bf16[8,520,128]{2,1,0:T(8,128)(2,1)S(1)}, u32[]{:S(2)}, u32[]{:S(2)}) async-start(bf16[8,520,128]{2,1,0:T(8,128)(2,1)} %get-tuple-element.50), calls=%async_computation.2 | async-start | bytes 2129920 | tf_op jit(solution)/shard_map/all_to_all | solution.py:374
  77.3 0.0 collective-permute-done.2
  77.3 1.1 fusion.1
  78.4 1.2 collective-permute-start.3
  79.7 0.0 copy-done
  79.7 0.0 copy-start.1
  79.7 1.2 copy-done.1
  80.9 0.0 copy-start.2
  80.9 1.2 copy-done.2
  82.1 0.0 copy-start.3
  82.1 0.0 copy-start.4
  82.1 3.9 %early_rows.1 = (f32[512,1024]{1,0:T(8,128)}, f32[512,128]{1,0:T(8,128)}, bf16[1024,512]{1,0:T(8,128)(2,1)}) custom-call(bf16[512,1024]{1,0:T(8,128)(2,1)S(1)} %copy-done.1, bf16[512,1024]{1,0:T(8,128)(2,1)S(1)} %copy-done.2, bf16[1024,1024]{1,0:T(8,128)(2,1)S(1)} %copy-done), custom_call_target="tpu_custom_call" | custom-call | flops 1073741824 | bytes 5242880 | tf_op jit(solution)/shard_map/early_rows/pallas_call | solution.py:236
  86.0 7.5 %collective-permute-done.3 = bf16[4,128,128]{2,1,0:T(8,128)(2,1)S(1)} collective-permute-done((bf16[4,128,128]{2,1,0:T(8,128)(2,1)S(1)}, bf16[4,128,128]{2,1,0:T(8,128)(2,1)S(1)}, u32[]{:S(2)}, u32[]{:S(2)}) %collective-permute-start.3) | collective-permute-done | bytes 131104 | tf_op jit(solution)/shard_map/ppermute | solution.py:437
  93.5 0.7 convert_add_fusion.2
  94.2 0.0 all-to-all-done.2.parts_ref
  94.2 0.0 copy-done.3
  94.2 0.0 copy-done.4
  94.2 4.0 %late_rows.1 = (bf16[512,1024]{1,0:T(8,128)(2,1)}, bf16[2,8,8,72,128]{4,3,2,1,0:T(8,128)(2,1)S(1)}, f32[8,128]{1,0:T(8,128)S(1)}) custom-call(bf16[8,520,128]{2,1,0:T(8,128)(2,1)S(1)} %all-to-all-done.2.parts_ref, f32[512,1024]{1,0:T(8,128)} %get-tuple-element.62.normed_far, f32[512,128]{1,0:T(8,128)} %get-tuple-element.63.inv_far, f32[1,1024]{1,0:T(1,128)S(1)} %bitcast.46, ...), custom_call_target="tpu_custom_call" | custom-call | flops 1342177280 | bytes 7340032 | tf_op jit(solution)/shard_map/late_rows/pallas_call | solution.py:340
  98.2 0.1 dynamic-slice_bitcast_fusion
  98.3 0.0 copy-start.5
  98.3 1.0 collective-permute-start.4
  99.4 2.5 %collective-permute-done.4 = bf16[8,8,72,128]{3,2,1,0:T(8,128)(2,1)S(1)} collective-permute-done((bf16[8,8,72,128]{3,2,1,0:T(8,128)(2,1)S(1)}, bf16[8,8,72,128]{3,2,1,0:T(8,128)(2,1)S(1)}, u32[]{:S(2)}, u32[]{:S(2)}) %collective-permute-start.4) | collective-permute-done | bytes 1179680 | tf_op jit(solution)/shard_map/ppermute | solution.py:437
  101.8 1.3 fusion
  103.2 8.8 %all-to-all-start.3 = ((bf16[64,72,128]{2,1,0:T(8,128)(2,1)}), bf16[64,72,128]{2,1,0:T(8,128)(2,1)}, u32[]{:S(2)}, u32[]{:S(2)}) async-start(bf16[64,72,128]{2,1,0:T(8,128)(2,1)} %bitcast.17), calls=%async_computation.3 | async-start | bytes 2359296 | tf_op jit(solution)/shard_map/all_to_all | solution.py:374
  111.9 0.0 copy-done.5
  112.0 2.5 %collective-permute-start.5 = (f32[2,128,128]{2,1,0:T(8,128)S(1)}, f32[2,128,128]{2,1,0:T(8,128)S(1)}, u32[]{:S(2)}, u32[]{:S(2)}) collective-permute-start(f32[2,128,128]{2,1,0:T(8,128)S(1)} %dynamic-slice_bitcast_fusion.2), channel_id=1, source_target_pairs={{0,8},{4,12},{8,0},{12,4},{1,9},{5,13},{9,1},{13,5},{2,10},{6,14},... | collective-permute-start | bytes 393224 | tf_op jit(solution)/shard_map/ppermute | solution.py:437
  114.5 3.5 %convolution_convert_fusion = bf16[512,1024]{1,0:T(8,128)(2,1)} fusion(bf16[512,1024]{1,0:T(8,128)(2,1)} %get-tuple-element.39, bf16[1024,1024]{1,0:T(8,128)(2,1)S(1)} %copy-done), kind=kOutput, calls=%fused_computation.2 | convolution fusion | flops 1074266112 | bytes 4194304 | tf_op jit(solution)/shard_map/dot_general | solution.py:534
  118.0 11.7 %collective-permute-done.5 = f32[2,128,128]{2,1,0:T(8,128)S(1)} collective-permute-done((f32[2,128,128]{2,1,0:T(8,128)S(1)}, f32[2,128,128]{2,1,0:T(8,128)S(1)}, u32[]{:S(2)}, u32[]{:S(2)}) %collective-permute-start.5) | collective-permute-done | bytes 131104 | tf_op jit(solution)/shard_map/ppermute | solution.py:437
  129.8 1.3 all-to-all-done.3.parts_ref
  131.1 2.5 %summed_copies.1 = bf16[64,72,128]{2,1,0:T(8,128)(2,1)} custom-call(bf16[64,72,128]{2,1,0:T(8,128)(2,1)} %all-to-all-done.3.parts_ref), custom_call_target="tpu_custom_call" | custom-call | tf_op jit(solution)/shard_map/summed_copies/pallas_call | solution.py:478
  133.6 6.8 %all-to-all-start.4 = ((bf16[64,72,128]{2,1,0:T(8,128)(2,1)}), bf16[64,72,128]{2,1,0:T(8,128)(2,1)S(1)}, u32[]{:S(2)}, u32[]{:S(2)}) async-start(bf16[64,72,128]{2,1,0:T(8,128)(2,1)} %summed_copies.1), calls=%async_computation.4 | async-start | bytes 2359296 | tf_op jit(solution)/shard_map/all_to_all | solution.py:374
  140.4 1.1 collective-permute-start.6
  141.5 12.8 %collective-permute-done.6 = f32[128,128]{1,0:T(8,128)S(1)} collective-permute-done((f32[128,128]{1,0:T(8,128)S(1)}, f32[128,128]{1,0:T(8,128)S(1)}, u32[]{:S(2)}, u32[]{:S(2)}) %collective-permute-start.6) | collective-permute-done | bytes 65568 | tf_op jit(solution)/shard_map/ppermute | solution.py:437
  154.3 0.6 bitcast_add_fusion.1
  154.9 3.8 %all-to-all-done.4 = bf16[64,72,128]{2,1,0:T(8,128)(2,1)S(1)} async-done(((bf16[64,72,128]{2,1,0:T(8,128)(2,1)}), bf16[64,72,128]{2,1,0:T(8,128)(2,1)S(1)}, u32[]{:S(2)}, u32[]{:S(2)}) %all-to-all-start.4) | async-done | bytes 1179680 | tf_op jit(solution)/shard_map/all_to_all | solution.py:374
  158.7 3.5 %collective-permute-start.7 = (bf16[8,8,72,128]{3,2,1,0:T(8,128)(2,1)S(1)}, bf16[8,8,72,128]{3,2,1,0:T(8,128)(2,1)S(1)}, u32[]{:S(2)}, u32[]{:S(2)}) collective-permute-start(bf16[8,8,72,128]{3,2,1,0:T(8,128)(2,1)S(1)} %bitcast.42), channel_id=1, source_target_pairs={{0,1},{1,0},{2,3},{3,2},{4,5},{5,4},{6,7},{7,6},{8,9},{9,8},{10,11... | collective-permute-start | bytes 3538952 | tf_op jit(solution)/shard_map/ppermute | solution.py:543
  162.2 0.5 slice.3
  163.4 1.3 collective-permute-done.7.other_ref
  164.7 3.9 %finish.1 = (f32[1024,1024]{1,0:T(8,128)}, f32[1024,128]{1,0:T(8,128)}, f32[1,1024]{1,0:T(1,128)}) custom-call(s32[1]{0:T(128)} %bitcast.1.core_ref, bf16[8,8,72,128]{3,2,1,0:T(8,128)(2,1)S(1)} %bitcast.43, bf16[8,8,72,128]{3,2,1,0:T(8,128)(2,1)S(1)} %collective-permute-done.7.other_ref, bf16[1024,128]{1,0:T(8,128)(2,1)S(1)} %copy-done.3, f32[1,1024]{1,0:T(1,128)S(1)} %bitcast.47), custom_call_target="tpu_custom_call" | custom-call | flops 4194304 | bytes 8388608 | tf_op jit(solution)/shard_map/finish/pallas_call | solution.py:400
  (10 shorter events, 0.1 us)
Async XLA Ops:
  0.6 9.6 %copy-start.7 = (s32[4]{0:T(128)S(1)}, s32[4]{0:T(128)}, u32[]{:S(2)}) copy-start(s32[4]{0:T(128)} %param.10) | copy-start | bytes 52
  0.6 9.7 %copy-start.6 = (bf16[4,32,128]{2,1,0:T(8,128)(2,1)S(1)}, bf16[4,32,128]{2,1,0:T(8,128)(2,1)}, u32[]{:S(2)}) copy-start(bf16[4,32,128]{2,1,0:T(8,128)(2,1)} %param.9) | copy-start | bytes 98308
  3.3 26.9 %all-to-all-start = ((bf16[8,520,128]{2,1,0:T(8,128)(2,1)}), bf16[8,520,128]{2,1,0:T(8,128)(2,1)S(1)}, u32[]{:S(2)}, u32[]{:S(2)}) async-start(bf16[8,520,128]{2,1,0:T(8,128)(2,1)} %passage_copies.1), calls=%async_computation | async-start | bytes 2129920 | tf_op jit(solution)/shard_map/all_to_all | solution.py:374
  10.3 1.9 %collective-permute-start = (bf16[136,128]{1,0:T(8,128)(2,1)S(1)}, bf16[136,128]{1,0:T(8,128)(2,1)S(1)}, u32[]{:S(2)}, u32[]{:S(2)}) collective-permute-start(bf16[136,128]{1,0:T(8,128)(2,1)S(1)} %get-tuple-element.82), channel_id=1, source_target_pairs={{0,1},{1,0},{2,3},{3,2},{4,5},{5,4},{6,7},{7,6},{8,9},{9,8},{10,11... | collective-permute-start | bytes 104456 | tf_op jit(solution)/shard_map/ppermute | solution.py:442
  22.9 7.3 %collective-permute-start.1 = (bf16[4,2,136,128]{3,2,1,0:T(8,128)(2,1)S(1)}, bf16[4,2,136,128]{3,2,1,0:T(8,128)(2,1)S(1)}, u32[]{:S(2)}, u32[]{:S(2)}) collective-permute-start(bf16[4,2,136,128]{3,2,1,0:T(8,128)(2,1)S(1)} %bitcast.48), channel_id=1, source_target_pairs={{0,2},{2,0},{1,3},{3,1},{4,6},{6,4},{5,7},{7,5},{8,10},{10,8},{9,1... | collective-permute-start | bytes 835592 | tf_op jit(solution)/shard_map/ppermute | solution.py:444
  71.0 8.7 %copy-start = (bf16[1024,1024]{1,0:T(8,128)(2,1)S(1)}, bf16[1024,1024]{1,0:T(8,128)(2,1)}, u32[]{:S(2)}) copy-start(bf16[1024,1024]{1,0:T(8,128)(2,1)} %proj_ref.1) | copy-start | bytes 6291460
  72.1 5.2 %collective-permute-start.2 = (bf16[2,4,128,128]{3,2,1,0:T(8,128)(2,1)S(1)}, bf16[2,4,128,128]{3,2,1,0:T(8,128)(2,1)}, u32[]{:S(2)}, u32[]{:S(2)}) collective-permute-start(bf16[2,4,128,128]{3,2,1,0:T(8,128)(2,1)S(1)} %dynamic-slice_bitcast_fusion.1), channel_id=1, source_target_pairs={{0,1},{1,0},{2,3},{3,2},{4,5},{5,4},{6,7},{7,6},{8,9},{9,8},{10,11... | collective-permute-start | bytes 786440 | tf_op jit(solution)/shard_map/ppermute | solution.py:437
  72.5 21.7 %all-to-all-start.2 = ((bf16[8,520,128]{2,1,0:T(8,128)(2,1)}), bf16[8,520,128]{2,1,0:T(8,128)(2,1)S(1)}, u32[]{:S(2)}, u32[]{:S(2)}) async-start(bf16[8,520,128]{2,1,0:T(8,128)(2,1)} %get-tuple-element.50), calls=%async_computation.2 | async-start | bytes 2129920 | tf_op jit(solution)/shard_map/all_to_all | solution.py:374
  78.4 15.0 %collective-permute-start.3 = (bf16[4,128,128]{2,1,0:T(8,128)(2,1)S(1)}, bf16[4,128,128]{2,1,0:T(8,128)(2,1)S(1)}, u32[]{:S(2)}, u32[]{:S(2)}) collective-permute-start(bf16[4,128,128]{2,1,0:T(8,128)(2,1)S(1)} %dynamic-slice_bitcast_fusion.3), channel_id=1, source_target_pairs={{0,2},{2,0},{1,3},{3,1},{4,6},{6,4},{5,7},{7,5},{8,10},{10,8},{9,1... | collective-permute-start | bytes 393224 | tf_op jit(solution)/shard_map/ppermute | solution.py:437
  79.7 1.2 copy-start.1
  80.9 1.2 copy-start.2
  82.1 12.1 %copy-start.3 = (bf16[1024,128]{1,0:T(8,128)(2,1)S(1)}, bf16[1024,128]{1,0:T(8,128)(2,1)}, u32[]{:S(2)}) copy-start(bf16[1024,128]{1,0:T(8,128)(2,1)} %colbert_ref.3) | copy-start | bytes 786436
  82.1 12.1 %copy-start.4 = (f32[1024]{0:T(1024)S(1)}, f32[1024]{0:T(1024)}, u32[]{:S(2)}) copy-start(f32[1024]{0:T(1024)} %param.16) | copy-start | bytes 12292
  98.3 13.6 %copy-start.5 = (f32[4,128,128]{2,1,0:T(8,128)S(1)}, f32[4,128,128]{2,1,0:T(8,128)}, u32[]{:S(2)}) copy-start(f32[4,128,128]{2,1,0:T(8,128)} %convert_add_fusion.2) | copy-start | bytes 786436
  98.3 3.5 %collective-permute-start.4 = (bf16[8,8,72,128]{3,2,1,0:T(8,128)(2,1)S(1)}, bf16[8,8,72,128]{3,2,1,0:T(8,128)(2,1)S(1)}, u32[]{:S(2)}, u32[]{:S(2)}) collective-permute-start(bf16[8,8,72,128]{3,2,1,0:T(8,128)(2,1)S(1)} %dynamic-slice_bitcast_fusion), channel_id=1, source_target_pairs={{0,1},{1,0},{2,3},{3,2},{4,5},{5,4},{6,7},{7,6},{8,9},{9,8},{10,11... | collective-permute-start | bytes 3538952 | tf_op jit(solution)/shard_map/ppermute | solution.py:437
  103.2 27.9 %all-to-all-start.3 = ((bf16[64,72,128]{2,1,0:T(8,128)(2,1)}), bf16[64,72,128]{2,1,0:T(8,128)(2,1)}, u32[]{:S(2)}, u32[]{:S(2)}) async-start(bf16[64,72,128]{2,1,0:T(8,128)(2,1)} %bitcast.17), calls=%async_computation.3 | async-start | bytes 2359296 | tf_op jit(solution)/shard_map/all_to_all | solution.py:374
  112.0 17.8 %collective-permute-start.5 = (f32[2,128,128]{2,1,0:T(8,128)S(1)}, f32[2,128,128]{2,1,0:T(8,128)S(1)}, u32[]{:S(2)}, u32[]{:S(2)}) collective-permute-start(f32[2,128,128]{2,1,0:T(8,128)S(1)} %dynamic-slice_bitcast_fusion.2), channel_id=1, source_target_pairs={{0,8},{4,12},{8,0},{12,4},{1,9},{5,13},{9,1},{13,5},{2,10},{6,14},... | collective-permute-start | bytes 393224 | tf_op jit(solution)/shard_map/ppermute | solution.py:437
  133.6 25.1 %all-to-all-start.4 = ((bf16[64,72,128]{2,1,0:T(8,128)(2,1)}), bf16[64,72,128]{2,1,0:T(8,128)(2,1)S(1)}, u32[]{:S(2)}, u32[]{:S(2)}) async-start(bf16[64,72,128]{2,1,0:T(8,128)(2,1)} %summed_copies.1), calls=%async_computation.4 | async-start | bytes 2359296 | tf_op jit(solution)/shard_map/all_to_all | solution.py:374
  140.4 13.9 %collective-permute-start.6 = (f32[128,128]{1,0:T(8,128)S(1)}, f32[128,128]{1,0:T(8,128)S(1)}, u32[]{:S(2)}, u32[]{:S(2)}) collective-permute-start(f32[128,128]{1,0:T(8,128)S(1)} %dynamic-slice_bitcast_fusion.4), channel_id=1, source_target_pairs={{0,4},{4,0},{8,12},{12,8},{1,5},{5,1},{9,13},{13,9},{2,6},{6,2},{1... | collective-permute-start | bytes 196616 | tf_op jit(solution)/shard_map/ppermute | solution.py:437
  158.7 6.0 %collective-permute-start.7 = (bf16[8,8,72,128]{3,2,1,0:T(8,128)(2,1)S(1)}, bf16[8,8,72,128]{3,2,1,0:T(8,128)(2,1)S(1)}, u32[]{:S(2)}, u32[]{:S(2)}) collective-permute-start(bf16[8,8,72,128]{3,2,1,0:T(8,128)(2,1)S(1)} %bitcast.42), channel_id=1, source_target_pairs={{0,1},{1,0},{2,3},{3,2},{4,5},{5,4},{6,7},{7,6},{8,9},{9,8},{10,11... | collective-permute-start | bytes 3538952 | tf_op jit(solution)/shard_map/ppermute | solution.py:543

commit v4 on v3

--- a/solution.py
+++ b/solution.py
@@ -36,15 +36,31 @@
     return pl.BlockSpec(shape, lambda *_: (0,) * len(shape))
 
 
-def stored(k, parts, flip_ref):
-    return ((k // 2 % 2) ^ flip_ref[0]) * (parts // 2) + k // 4 * 2 + ((k % 2) ^ flip_ref[1])
+def stored(k):
+    core, row, near, far = k % 2, k // 2 % 2, k // 4 % 2, k // 8
+    return row * 8 + far * 4 + near * 2 + core
 
 
 def forward_kernel(
-    query_len, group, flip_ref, q_ref, p_ref, ids_ref, exp_ref, mix_ref, inv_ref, sim_ref, stats_ref, rows_ref
+    query_len,
+    group,
+    flip_ref,
+    near_ref,
+    far_ref,
+    p_ref,
+    ids_ref,
+    exp_ref,
+    mix_ref,
+    own_ref,
+    inv_ref,
+    sim_ref,
+    stats_ref,
+    rows_ref,
+    length_ref,
 ):
     passage = pl.program_id(0)
-    parts, q_rows, width = q_ref.shape[0], q_ref.shape[1] - EXTRA, q_ref.shape[2]
+    half, q_rows, width = near_ref.shape[0], near_ref.shape[1] - EXTRA, near_ref.shape[2]
+    parts = 2 * half
     slots = p_ref.shape[1] - EXTRA
     count, rows = inv_ref.shape
     queries = rows // query_len
@@ -52,7 +68,7 @@
     steps = parts // group
     tokens = p_ref[0, :slots, :]
     length = p_ref[0, slots : slots + 1, :].astype(F32) + float(LEAST)
-    log_length = jnp.log(length)[:, :1]
+    length_ref[pl.ds(passage, 1), :] = length
     wide = jnp.concatenate([length] * ((slots - LEAST) // width), axis=1)
     position = lax.broadcasted_iota(jnp.int32, wide.shape, 1).astype(F32) + float(LEAST)
     bias = jnp.where(position < wide, 0.0, -1e30)
@@ -61,15 +77,15 @@
     @pl.when(passage == 0)
     def _():
         rows_ref[...] = jnp.zeros_like(rows_ref)
+        for k in range(parts):
+            at = stored(k) ^ flip_ref[0]
+            spot = at % half
+            own_ref[k * q_rows : (k + 1) * q_rows, :] = jnp.where(
+                at < half, near_ref[spot, :q_rows, :], far_ref[spot, :q_rows, :]
+            )
 
     def scores(step):
-        block = jnp.concatenate(
-            [
-                q_ref[stored(step * group + k, parts, flip_ref), :q_rows, :]
-                for k in range(group)
-            ],
-            axis=0,
-        )
+        block = own_ref[step * chunk : (step + 1) * chunk, :]
         return dot(block, tokens, ((1,), (1,)))
 
     ahead = scores(0)
@@ -90,10 +106,9 @@
         late = jnp.concatenate([sure.astype(BF16), rest.astype(BF16)], axis=1)
         at = pl.ds(step * chunk, chunk)
         exp_ref[passage, at, :] = late
-        shifted = highest + jnp.log(total) - log_length
         rows_ref[at, :] = jnp.where(
             lane == passage,
-            shifted,
+            highest + jnp.log(total),
             jnp.where(lane == passage + width // 2, total, rows_ref[at, :]),
         )
     mix_ref[passage, pl.ds((steps - 1) * chunk, chunk), :] = dot(late, tokens, ((1,), (0,)))
@@ -105,7 +120,12 @@
         similar = dot(
             turned[:count], token_query(rows, queries, query_len), ((1,), (0,)), lax.Precision.HIGHEST
         )
-        wanted = jnp.sum(q_ref[:, q_rows, :].astype(F32), axis=0, keepdims=True)[:, :queries]
+        similar = similar - float(query_len) * jnp.log(length_ref[...])[:, :queries]
+        wanted = jnp.sum(
+            near_ref[:, q_rows, :].astype(F32) + far_ref[:, q_rows, :].astype(F32),
+            axis=0,
+            keepdims=True,
+        )[:, :queries]
         hit = (wanted == ids_ref[:, :queries]).astype(F32)
         highest = jnp.max(similar, axis=0, keepdims=True)
         total = jnp.sum(jnp.exp(similar - highest), axis=0, keepdims=True)
@@ -117,9 +137,9 @@
         stats_ref[...] = jnp.broadcast_to(stats[None], stats_ref.shape)
 
 
-def forward_tile(flip, query_pack, passage_pack, ids, query_len, group=8):
-    parts, q_rows, width = query_pack.shape
-    q_rows -= EXTRA
+def forward_tile(flip, near, far, passage_pack, ids, query_len, group=8):
+    half, q_rows, width = near.shape
+    parts, q_rows = 2 * half, q_rows - EXTRA
     count, slots = passage_pack.shape[0], passage_pack.shape[1] - EXTRA
     rows = parts * q_rows
     queries = rows // query_len
@@ -130,11 +150,13 @@
         grid=(count,),
         in_specs=[
             pl.BlockSpec(memory_space=pltpu.SMEM),
-            whole(query_pack.shape),
+            whole(near.shape),
+            whole(far.shape),
             pl.BlockSpec((1, slots + EXTRA, width), lambda p: (p, 0, 0)),
             whole(ids.shape),
         ],
         out_specs=[
+            pl.BlockSpec(memory_space=pltpu.VMEM),
             pl.BlockSpec(memory_space=pltpu.VMEM),
             pl.BlockSpec(memory_space=pltpu.VMEM),
             whole((count, rows)),
@@ -144,26 +166,27 @@
         out_shape=[
             pltpu.VMEM((count, rows, slots), BF16),
             pltpu.VMEM((count, rows, width), F32),
+            pltpu.VMEM((rows, width), BF16),
             jax.ShapeDtypeStruct((count, rows), F32),
             jax.ShapeDtypeStruct((2, count, queries), F32),
             jax.ShapeDtypeStruct((parts, 8, width), F32),
         ],
-        scratch_shapes=[pltpu.VMEM((rows, width), F32)],
+        scratch_shapes=[pltpu.VMEM((rows, width), F32), pltpu.VMEM((count, width), F32)],
         compiler_params=pltpu.CompilerParams(vmem_limit_bytes=16 * MIB),
         cost_estimate=pl.CostEstimate(
             flops=4 * work * width, transcendentals=work, bytes_accessed=4 * work
         ),
-    )(flip, query_pack, passage_pack, ids)
+    )(flip, near, far, passage_pack, ids)
 
 
 def backward_kernel(
-    query_len, flip_ref, q_ref, exp_ref, mix_ref, inv_ref, sim_ref, stats_ref, pg_ref, qg_ref, qt
+    query_len, parts, own_ref, exp_ref, mix_ref, inv_ref, sim_ref, stats_ref, pg_ref, qg_ref, qt
 ):
-    parts, q_rows, width = q_ref.shape[0], q_ref.shape[1] - EXTRA, q_ref.shape[2]
     count, rows, slots = exp_ref.shape
+    width, q_rows = own_ref.shape[1], rows // parts
     queries = rows // query_len
     for k in range(parts):
-        qt[:, k * q_rows : (k + 1) * q_rows] = q_ref[stored(k, parts, flip_ref), :q_rows, :].T
+        qt[:, k * q_rows : (k + 1) * q_rows] = own_ref[k * q_rows : (k + 1) * q_rows, :].T
     highest_of = stats_ref[:, 0, :queries]
     highest = jnp.max(highest_of, axis=0, keepdims=True)
     total = jnp.sum(
@@ -197,16 +220,14 @@
         qg_ref[k % 2, k // 2 % 2, k // 4] = sums.astype(BF16)
 
 
-def backward_tile(flip, query_pack, spread, mixed, inverse, similar, stats, query_len):
-    parts, q_rows, width = query_pack.shape
-    q_rows -= EXTRA
+def backward_tile(parts, own, spread, mixed, inverse, similar, stats, query_len):
     count, rows, slots = spread.shape
+    q_rows, width = rows // parts, own.shape[1]
     work = rows * slots * count
     return pl.pallas_call(
-        functools.partial(backward_kernel, query_len),
+        functools.partial(backward_kernel, query_len, parts),
         name="backward_tile",
-        in_specs=[pl.BlockSpec(memory_space=pltpu.SMEM)]
-        + [pl.BlockSpec(memory_space=pltpu.VMEM)] * 6,
+        in_specs=[pl.BlockSpec(memory_space=pltpu.VMEM)] * 6,
         out_shape=[
             pltpu.HBM((count, slots + EXTRA, width), BF16),
             pltpu.HBM((2, 2, parts // 4, q_rows, width), BF16),
@@ -217,7 +238,7 @@
         cost_estimate=pl.CostEstimate(
             flops=2 * work * width, transcendentals=0, bytes_accessed=3 * work
         ),
-    )(flip, query_pack, spread, mixed, inverse, similar, stats)
+    )(own, spread, mixed, inverse, similar, stats)
 
 
 def early_kernel(resid_ref, context_ref, proj_ref, normed_ref, inv_ref, context_t_ref):
@@ -439,10 +460,10 @@
 
 
 def query_gathered(own):
-    pair = jnp.stack([own, lax.ppermute(own, CORE, SWAP)])
-    line = lax.all_gather(pair, "neg_0")
-    both = jnp.stack([line, lax.ppermute(line, "neg_1", SWAP)])
-    return both.reshape(-1, *own.shape)
+    held = own[None]
+    for axis, pairs in ((CORE, SWAP), ("neg_0", NEAR), ("neg_0", FAR)):
+        held = jnp.concatenate([held, lax.ppermute(held, axis, pairs)])
+    return held, lax.ppermute(held, "neg_1", SWAP)
 
 
 def pack_kernel(length_ref, p_ref, out_ref):
@@ -500,25 +521,28 @@
             jnp.broadcast_to(wanted.astype(BF16)[None], (EXTRA, emb)),
         ]
     )
-    query_pack = query_gathered(query_own)
-    passage_pack = exchange(passage_copies(passage_emb, lengths, dp_size), DP)
+    copies, query_own = lax.optimization_barrier(
+        (passage_copies(passage_emb, lengths, dp_size), query_own)
+    )
+    passage_pack = exchange(copies, DP)
+    queries = query_gathered(query_own)
     ids = jnp.broadcast_to(
         (jnp.arange(dp_size) * neg_size + place).astype(F32)[:, None], (dp_size, emb)
     )
     row, column = lax.axis_index("neg_1"), lax.axis_index("neg_0")
-    flip = jnp.stack([row, core])
+    flip = (row * 8 + column * 2 + core)[None]
     sides = [
         (own.astype(jnp.uint32), (1 - own).astype(jnp.uint32))
         for own in (core, row, column // 2, column % 2)
     ]
-    query_pack, sides = lax.optimization_barrier((query_pack, sides))
+    queries, sides = lax.optimization_barrier((queries, sides))
     core_side, row_side, far_side, near_side = sides
-    spread, mixed, inverse, similar, stats = forward_tile(
-        flip, query_pack, passage_pack, ids, query_len
+    spread, mixed, query_rows, inverse, similar, stats = forward_tile(
+        flip, *queries, passage_pack, ids, query_len
     )
     stats = exchange(stats, NEG)
     passage_parts, query_parts = backward_tile(
-        flip, query_pack, spread, mixed, inverse, similar, stats, query_len
+        neg_size, query_rows, spread, mixed, inverse, similar, stats, query_len
     )
     residual, query_parts = lax.optimization_barrier((residual, query_parts))
     early = early_rows(residual, context, out_proj)
@@ -532,13 +556,13 @@
     )
     half = halves_summed(partial, CORE, SWAP, core_side, BF16)
     context_grad = jnp.dot(residual_grad, out_proj.T, preferred_element_type=F32).astype(BF16)
-    slabs = exchange(half.reshape(dp_size * cross_size, *half.shape[2:]), DP + CROSS)
     query_part = query_part.reshape(2, 2, *query_part.shape[1:])
     query_part = halves_summed(query_part, "neg_0", FAR, far_side, F32)
-    slabs, context_grad, query_part = lax.optimization_barrier((slabs, context_grad, query_part))
+    half, context_grad, query_part = lax.optimization_barrier((half, context_grad, query_part))
+    slabs = exchange(half.reshape(dp_size * cross_size, *half.shape[2:]), DP + CROSS)
     half = exchange(summed_copies(slabs), DP + CROSS).reshape(half.shape)
+    half, query_part = lax.optimization_barrier((half, query_part))
     query_grad = halves_summed(query_part, "neg_0", NEAR, near_side, F32)
-    half, query_grad = lax.optimization_barrier((half, query_grad))
     query_grad = query_grad.reshape(query_dev, query_len, emb)
     other = lax.ppermute(half, CORE, SWAP)
     out_proj_grad, colbert_grad, gain_grad = finish(

time: 170 us -> 167 us (0.982)
  blocking collectives: 27 us -> 65.4 us
  waiting for transfers between devices: 46.4 us -> 23.2 us
  starting transfers between devices: 40.8 us -> 27.5 us
  Pallas kernels: 40.4 us -> 36.5 us
    all_to_all x1 -> x3, blocking collectives: 16.4 us -> 65.4 us  [exchange(): return lax.all_to_all(pieces, axis, 0, 0, tiled=True)]
    ppermute x5, waiting for transfers between devices: 34.5 us -> 12.1 us  [halves_summed(): taken = lax.ppermute(given, axis, pairs)]
    all_to_all x4 -> x2, starting transfers between devices: 27.2 us -> 11.5 us  [exchange(): return lax.all_to_all(pieces, axis, 0, 0, tiled=True)]
    all_gather x1 -> x0, blocking collectives: 10.6 us -> none  [query_gathered(): line = lax.all_gather(pair, 'neg_0')]
    ppermute x2 -> x4, waiting for transfers between devices: 5.46 us -> 11.1 us  [the longest x3 6.07 us: query_gathered(): held = jnp.concatenate([held, lax.ppermute(held, axis, pairs)])]
    all_to_all x4 -> x2, waiting for transfers between devices: 5.07 us -> 0.01 us  [exchange(): return lax.all_to_all(pieces, axis, 0, 0, tiled=True)]
    ppermute x2 -> x4, starting transfers between devices: 3.66 us -> 7.77 us  [the longest x3 5.07 us: query_gathered(): held = jnp.concatenate([held, lax.ppermute(held, axis, pairs)])]
    pallas_call x1, Pallas kernels: 17.5 us -> 14.1 us  [forward_tile(): pl.pallas_call(functools.partial(forward_kernel, query_len, group), name=...]
  transfers between devices with their start and end apart: 12 -> 12, of which waited for: 9 -> 7; matrix products, arithmetic and copies ran while one was open for 4% -> 3% of each run, Pallas kernels for 2% -> 2%
where the time goes in v4:
time: 167 us
  blocking collectives  65.4 us (39%)
  Pallas kernels  36.5 us (22%)
  starting transfers between devices  27.5 us (16%)
  waiting for transfers between devices  23.2 us (14%)
  other arithmetic  4.38 us (3%)
  local copies, waits for them, and re-layouts  4.31 us (3%)
  between operations  3.2 us (2%)
  matrix products  2.29 us (1%)
    all_to_all x3, blocking collectives, exchange(): return lax.all_to_all(pieces, axis, 0, 0, tiled=True)  65.4 us
    pallas_call x1, Pallas kernels, forward_tile(): pl.pallas_call(functools.partial(forward_kernel, query_len, group), name=...  14.1 us
    ppermute x5, waiting for transfers between devices, halves_summed(): taken = lax.ppermute(given, axis, pairs)  12.1 us
    all_to_all x2, starting transfers between devices, exchange(): return lax.all_to_all(pieces, axis, 0, 0, tiled=True)  11.5 us
    pallas_call x1, Pallas kernels, backward_tile(): pl.pallas_call(functools.partial(backward_kernel, query_len, parts), name...  6.18 us
    ppermute x3, waiting for transfers between devices, query_gathered(): held = jnp.concatenate([held, lax.ppermute(held, axis, pairs)])  6.07 us
    ppermute x3, starting transfers between devices, query_gathered(): held = jnp.concatenate([held, lax.ppermute(held, axis, pairs)])  5.07 us
    ppermute x1, waiting for transfers between devices, query_gathered(): return (held, lax.ppermute(held, 'neg_1', SWAP))  5.03 us
  transfers between devices with their start and end apart: 12, of which 7 were waited for; matrix products, arithmetic and copies ran while one was open for 3% of the time, Pallas kernels for 2%

profile of v4, /device:TPU:1, one launch (start us, length us, event | category | flops | bytes accessed | tf_op | source)
XLA Modules:
  0.0 166.8 jit_solution(6571384196795223386)
XLA Ops:
  1.3 0.7 select_reduce_fusion
  2.1 0.8 pad_maximum_fusion.3
  2.8 2.0 %passage_copies.1 = bf16[8,520,128]{2,1,0:T(8,128)(2,1)} custom-call(s32[1]{0:T(128)S(6)} %copy.16.length_ref, bf16[1,512,128]{2,1,0:T(8,128)(2,1)} %p_ref.1), custom_call_target="tpu_custom_call" | custom-call | tf_op jit(solution)/shard_map/passage_copies/pallas_call | solution.py:479
  4.8 6.9 %all-to-all-start = ((bf16[8,520,128]{2,1,0:T(8,128)(2,1)}), bf16[8,520,128]{2,1,0:T(8,128)(2,1)S(1)}, u32[]{:S(2)}, u32[]{:S(2)}) async-start(bf16[8,520,128]{2,1,0:T(8,128)(2,1)} %passage_copies.1), calls=%async_computation | async-start | bytes 2129920 | tf_op jit(solution)/shard_map/all_to_all | solution.py:395
  11.7 1.0 collective-permute-start
  12.7 0.9 collective-permute-done
  13.5 1.3 collective-permute-start.1
  14.8 2.2 %collective-permute-done.1 = bf16[2,136,128]{2,1,0:T(8,128)(2,1)S(1)} collective-permute-done((bf16[2,136,128]{2,1,0:T(8,128)(2,1)S(1)}, bf16[2,136,128]{2,1,0:T(8,128)(2,1)S(1)}, u32[]{:S(2)}, u32[]{:S(2)}) %collective-permute-start.1) | collective-permute-done | bytes 69664 | tf_op jit(solution)/shard_map/ppermute | solution.py:465
  17.1 2.8 %collective-permute-start.2 = (bf16[4,136,128]{2,1,0:T(8,128)(2,1)S(1)}, bf16[4,136,128]{2,1,0:T(8,128)(2,1)S(1)}, u32[]{:S(2)}, u32[]{:S(2)}) collective-permute-start(bf16[4,136,128]{2,1,0:T(8,128)(2,1)S(1)} %pad_maximum_fusion.1), channel_id=1, source_target_pairs={{0,8},{4,12},{8,0},{12,4},{1,9},{5,13},{9,1},{13,5},{2,10},{6,14},... | collective-permute-start | bytes 417800 | tf_op jit(solution)/shard_map/ppermute | solution.py:465
  19.9 3.0 %collective-permute-done.2 = bf16[4,136,128]{2,1,0:T(8,128)(2,1)S(1)} collective-permute-done((bf16[4,136,128]{2,1,0:T(8,128)(2,1)S(1)}, bf16[4,136,128]{2,1,0:T(8,128)(2,1)S(1)}, u32[]{:S(2)}, u32[]{:S(2)}) %collective-permute-start.2) | collective-permute-done | bytes 139296 | tf_op jit(solution)/shard_map/ppermute | solution.py:465
  22.9 2.7 %collective-permute-start.3 = (bf16[8,136,128]{2,1,0:T(8,128)(2,1)S(1)}, bf16[8,136,128]{2,1,0:T(8,128)(2,1)S(1)}, u32[]{:S(2)}, u32[]{:S(2)}) collective-permute-start(bf16[8,136,128]{2,1,0:T(8,128)(2,1)S(1)} %pad_maximum_fusion.near_ref), channel_id=1, source_target_pairs={{0,2},{2,0},{1,3},{3,1},{4,6},{6,4},{5,7},{7,5},{8,10},{10,8},{9,1... | collective-permute-start | bytes 835592 | tf_op jit(solution)/shard_map/ppermute | solution.py:466
  25.6 5.0 %collective-permute-done.3.far_ref = bf16[8,136,128]{2,1,0:T(8,128)(2,1)S(1)} collective-permute-done((bf16[8,136,128]{2,1,0:T(8,128)(2,1)S(1)}, bf16[8,136,128]{2,1,0:T(8,128)(2,1)S(1)}, u32[]{:S(2)}, u32[]{:S(2)}) %collective-permute-start.3) | collective-permute-done | bytes 278560 | tf_op jit(solution)/shard_map/ppermute | solution.py:466
  30.7 0.0 all-to-all-done.p_ref
  30.7 0.1 broadcast_in_dim.45.ids_ref
  30.7 14.1 %forward_tile.1 = (bf16[8,2048,512]{2,1,0:T(8,128)(2,1)S(1)}, f32[8,2048,128]{2,1,0:T(8,128)S(1)}, bf16[2048,128]{1,0:T(8,128)(2,1)S(1)}, f32[8,2048]{1,0:T(8,12...) custom-call(s32[1]{0:T(128)} %bitcast.flip_ref, bf16[8,136,128]{2,1,0:T(8,128)(2,1)S(1)} %pad_maximum_fusion.near_ref, ...), custom_call_target="tpu_custom_call" | custom-call | flops 4294967296 | bytes 33554432 | tf_op jit(solution)/shard_map/forward_tile/pallas_call | solution.py:147
  44.8 16.7 %all_to_all.25.stats_ref = f32[16,8,128]{2,1,0:T(8,128)S(1)} all-to-all(f32[16,8,128]{2,1,0:T(8,128)S(1)} %get-tuple-element.57), channel_id=1, replica_groups=mesh['dp_0'=4,'dp_1'=2,'neg_0'=4,'neg_1'=2,'neg_2'=2] {'neg_0','neg_1','..., dimensions={0} | all-to-all | bytes 131072 | tf_op jit(solution)/shard_map/all_to_all | solution.py:395
  61.6 6.2 %backward_tile.1 = (bf16[8,520,128]{2,1,0:T(8,128)(2,1)}, bf16[2,2,4,128,128]{4,3,2,1,0:T(8,128)(2,1)}) custom-call(bf16[2048,128]{1,0:T(8,128)(2,1)S(1)} %get-tuple-element.52.own_ref, bf16[8,2048,512]{2,1,0:T(8,128)(2,1)S(1)} %get-tuple-element.53.exp_ref, f32[8,2048,128]{2,1,0:T(8,128)S(1)} %get-tuple-element.54.mix_ref, ...), custom_call_target="tpu_custom_call" | custom-call | flops 2147483648 | bytes 25165824 | tf_op jit(solution)/shard_map/backward_tile/pallas_call | solution.py:227
  67.7 0.0 copy-start
  67.7 1.1 dynamic-slice_bitcast_fusion.1
  68.9 0.5 collective-permute-start.4
  69.3 4.6 %all-to-all-start.2 = ((bf16[8,520,128]{2,1,0:T(8,128)(2,1)}), bf16[8,520,128]{2,1,0:T(8,128)(2,1)S(1)}, u32[]{:S(2)}, u32[]{:S(2)}) async-start(bf16[8,520,128]{2,1,0:T(8,128)(2,1)} %get-tuple-element.58), calls=%async_computation.2 | async-start | bytes 2129920 | tf_op jit(solution)/shard_map/all_to_all | solution.py:395
  73.9 0.0 collective-permute-done.4
  74.0 1.1 fusion.1
  75.1 1.2 collective-permute-start.5
  76.3 0.0 copy-done
  76.3 0.0 copy-start.1
  76.3 1.2 copy-done.1
  77.5 0.0 copy-start.2
  77.5 1.2 copy-done.2
  78.7 0.0 copy-start.3
  78.7 0.0 copy-start.4
  78.7 3.8 %early_rows.1 = (f32[512,1024]{1,0:T(8,128)}, f32[512,128]{1,0:T(8,128)}, bf16[1024,512]{1,0:T(8,128)(2,1)}) custom-call(bf16[512,1024]{1,0:T(8,128)(2,1)S(1)} %copy-done.1, bf16[512,1024]{1,0:T(8,128)(2,1)S(1)} %copy-done.2, bf16[1024,1024]{1,0:T(8,128)(2,1)S(1)} %copy-done), custom_call_target="tpu_custom_call" | custom-call | flops 1073741824 | bytes 5242880 | tf_op jit(solution)/shard_map/early_rows/pallas_call | solution.py:257
  82.6 7.5 %collective-permute-done.5 = bf16[4,128,128]{2,1,0:T(8,128)(2,1)S(1)} collective-permute-done((bf16[4,128,128]{2,1,0:T(8,128)(2,1)S(1)}, bf16[4,128,128]{2,1,0:T(8,128)(2,1)S(1)}, u32[]{:S(2)}, u32[]{:S(2)}) %collective-permute-start.5) | collective-permute-done | bytes 131104 | tf_op jit(solution)/shard_map/ppermute | solution.py:458
  90.1 0.7 convert_add_fusion.2
  90.8 0.0 all-to-all-done.2.parts_ref
  90.8 0.0 copy-done.3
  90.8 0.0 copy-done.4
  90.8 4.0 %late_rows.1 = (bf16[512,1024]{1,0:T(8,128)(2,1)}, bf16[2,8,8,72,128]{4,3,2,1,0:T(8,128)(2,1)S(1)}, f32[8,128]{1,0:T(8,128)S(1)}) custom-call(bf16[8,520,128]{2,1,0:T(8,128)(2,1)S(1)} %all-to-all-done.2.parts_ref, f32[512,1024]{1,0:T(8,128)} %get-tuple-element.70.normed_far, f32[512,128]{1,0:T(8,128)} %get-tuple-element.71.inv_far, f32[1,1024]{1,0:T(1,128)S(1)} %bitcast.38, ...), custom_call_target="tpu_custom_call" | custom-call | flops 1342177280 | bytes 7340032 | tf_op jit(solution)/shard_map/late_rows/pallas_call | solution.py:361
  94.8 0.0 copy-start.5
  94.8 0.0 copy-start.6
  94.8 0.1 dynamic-slice_bitcast_fusion
  94.9 1.0 collective-permute-start.6
  96.0 0.0 copy-done.5
  96.0 1.0 collective-permute-start.7
  97.0 0.0 copy-done.6
  97.0 2.3 %convolution_convert_fusion = bf16[512,1024]{1,0:T(8,128)(2,1)} fusion(bf16[512,1024]{1,0:T(8,128)(2,1)S(1)} %copy-done.6, bf16[1024,1024]{1,0:T(8,128)(2,1)S(1)} %copy-done), kind=kOutput, calls=%fused_computation.2 | convolution fusion | flops 1074266112 | bytes 4194304 | tf_op jit(solution)/shard_map/dot_general | solution.py:558
  99.3 2.6 %collective-permute-done.7 = f32[2,128,128]{2,1,0:T(8,128)S(1)} collective-permute-done((f32[2,128,128]{2,1,0:T(8,128)S(1)}, f32[2,128,128]{2,1,0:T(8,128)S(1)}, u32[]{:S(2)}, u32[]{:S(2)}) %collective-permute-start.7) | collective-permute-done | bytes 131104 | tf_op jit(solution)/shard_map/ppermute | solution.py:458
  101.9 0.0 collective-permute-done.6
  101.9 0.3 fusion
  102.2 26.4 %all_to_all.26.parts_ref = bf16[64,72,128]{2,1,0:T(8,128)(2,1)} all-to-all(bf16[64,72,128]{2,1,0:T(8,128)(2,1)S(1)} %bitcast.40), channel_id=1, replica_groups=mesh['dp_0'=4,'dp_1'=2,'neg_0'=4,'neg_1'=2,'neg_2'=2] {'dp_0','dp_1','ne..., dimensions={0} | all-to-all | bytes 2359296 | tf_op jit(solution)/shard_map/all_to_all | solution.py:395
  128.7 2.5 %summed_copies.1 = bf16[64,72,128]{2,1,0:T(8,128)(2,1)} custom-call(bf16[64,72,128]{2,1,0:T(8,128)(2,1)} %all_to_all.26.parts_ref), custom_call_target="tpu_custom_call" | custom-call | tf_op jit(solution)/shard_map/summed_copies/pallas_call | solution.py:499
  131.2 22.3 %all_to_all.27 = bf16[64,72,128]{2,1,0:T(8,128)(2,1)S(1)} all-to-all(bf16[64,72,128]{2,1,0:T(8,128)(2,1)} %summed_copies.1), channel_id=1, replica_groups=mesh['dp_0'=4,'dp_1'=2,'neg_0'=4,'neg_1'=2,'neg_2'=2] {'dp_0','dp_1','ne..., dimensions={0} | all-to-all | bytes 2359296 | tf_op jit(solution)/shard_map/all_to_all | solution.py:395
  153.4 4.0 %collective-permute-start.9 = (bf16[8,8,72,128]{3,2,1,0:T(8,128)(2,1)S(1)}, bf16[8,8,72,128]{3,2,1,0:T(8,128)(2,1)S(1)}, u32[]{:S(2)}, u32[]{:S(2)}) collective-permute-start(bf16[8,8,72,128]{3,2,1,0:T(8,128)(2,1)S(1)} %bitcast.36), channel_id=1, source_target_pairs={{0,1},{1,0},{2,3},{3,2},{4,5},{5,4},{6,7},{7,6},{8,9},{9,8},{10,11... | collective-permute-start | bytes 3538952 | tf_op jit(solution)/shard_map/ppermute | solution.py:567
  157.5 0.5 collective-permute-start.8
  158.0 0.5 slice.3
  159.1 2.0 %collective-permute-done.8 = f32[128,128]{1,0:T(8,128)S(1)} collective-permute-done((f32[128,128]{1,0:T(8,128)S(1)}, f32[128,128]{1,0:T(8,128)S(1)}, u32[]{:S(2)}, u32[]{:S(2)}) %collective-permute-start.8) | collective-permute-done | bytes 65568 | tf_op jit(solution)/shard_map/ppermute | solution.py:458
  161.1 0.6 bitcast_add_fusion.1
  161.8 0.0 collective-permute-done.9.other_ref
  161.8 3.9 %finish.1 = (f32[1024,1024]{1,0:T(8,128)}, f32[1024,128]{1,0:T(8,128)}, f32[1,1024]{1,0:T(1,128)}) custom-call(s32[1]{0:T(128)} %bitcast.19.core_ref, bf16[8,8,72,128]{3,2,1,0:T(8,128)(2,1)S(1)} %bitcast.37, bf16[8,8,72,128]{3,2,1,0:T(8,128)(2,1)S(1)} %collective-permute-done.9.other_ref, bf16[1024,128]{1,0:T(8,128)(2,1)S(1)} %copy-done.3, ...), custom_call_target="tpu_custom_call" | custom-call | flops 4194304 | bytes 8388608 | tf_op jit(solution)/shard_map/finish/pallas_call | solution.py:421
  (11 shorter events, 0.1 us)
Async XLA Ops:
  4.8 25.8 %all-to-all-start = ((bf16[8,520,128]{2,1,0:T(8,128)(2,1)}), bf16[8,520,128]{2,1,0:T(8,128)(2,1)S(1)}, u32[]{:S(2)}, u32[]{:S(2)}) async-start(bf16[8,520,128]{2,1,0:T(8,128)(2,1)} %passage_copies.1), calls=%async_computation | async-start | bytes 2129920 | tf_op jit(solution)/shard_map/all_to_all | solution.py:395
  11.7 1.8 %collective-permute-start = (bf16[1,136,128]{2,1,0:T(8,128)(2,1)S(1)}, bf16[1,136,128]{2,1,0:T(8,128)(2,1)S(1)}, u32[]{:S(2)}, u32[]{:S(2)}) collective-permute-start(bf16[1,136,128]{2,1,0:T(8,128)(2,1)S(1)} %bitcast.43), channel_id=1, source_target_pairs={{0,1},{1,0},{2,3},{3,2},{4,5},{5,4},{6,7},{7,6},{8,9},{9,8},{10,11... | collective-permute-start | bytes 104456 | tf_op jit(solution)/shard_map/ppermute | solution.py:465
  13.5 3.5 %collective-permute-start.1 = (bf16[2,136,128]{2,1,0:T(8,128)(2,1)S(1)}, bf16[2,136,128]{2,1,0:T(8,128)(2,1)S(1)}, u32[]{:S(2)}, u32[]{:S(2)}) collective-permute-start(bf16[2,136,128]{2,1,0:T(8,128)(2,1)S(1)} %pad_maximum_fusion.2), channel_id=1, source_target_pairs={{0,4},{4,0},{8,12},{12,8},{1,5},{5,1},{9,13},{13,9},{2,6},{6,2},{1... | collective-permute-start | bytes 208904 | tf_op jit(solution)/shard_map/ppermute | solution.py:465
  17.1 5.8 %collective-permute-start.2 = (bf16[4,136,128]{2,1,0:T(8,128)(2,1)S(1)}, bf16[4,136,128]{2,1,0:T(8,128)(2,1)S(1)}, u32[]{:S(2)}, u32[]{:S(2)}) collective-permute-start(bf16[4,136,128]{2,1,0:T(8,128)(2,1)S(1)} %pad_maximum_fusion.1), channel_id=1, source_target_pairs={{0,8},{4,12},{8,0},{12,4},{1,9},{5,13},{9,1},{13,5},{2,10},{6,14},... | collective-permute-start | bytes 417800 | tf_op jit(solution)/shard_map/ppermute | solution.py:465
  22.9 7.7 %collective-permute-start.3 = (bf16[8,136,128]{2,1,0:T(8,128)(2,1)S(1)}, bf16[8,136,128]{2,1,0:T(8,128)(2,1)S(1)}, u32[]{:S(2)}, u32[]{:S(2)}) collective-permute-start(bf16[8,136,128]{2,1,0:T(8,128)(2,1)S(1)} %pad_maximum_fusion.near_ref), channel_id=1, source_target_pairs={{0,2},{2,0},{1,3},{3,1},{4,6},{6,4},{5,7},{7,5},{8,10},{10,8},{9,1... | collective-permute-start | bytes 835592 | tf_op jit(solution)/shard_map/ppermute | solution.py:466
  67.7 8.5 %copy-start = (bf16[1024,1024]{1,0:T(8,128)(2,1)S(1)}, bf16[1024,1024]{1,0:T(8,128)(2,1)}, u32[]{:S(2)}) copy-start(bf16[1024,1024]{1,0:T(8,128)(2,1)} %proj_ref.1) | copy-start | bytes 6291460
  68.9 5.1 %collective-permute-start.4 = (bf16[2,4,128,128]{3,2,1,0:T(8,128)(2,1)S(1)}, bf16[2,4,128,128]{3,2,1,0:T(8,128)(2,1)}, u32[]{:S(2)}, u32[]{:S(2)}) collective-permute-start(bf16[2,4,128,128]{3,2,1,0:T(8,128)(2,1)S(1)} %dynamic-slice_bitcast_fusion.1), channel_id=1, source_target_pairs={{0,1},{1,0},{2,3},{3,2},{4,5},{5,4},{6,7},{7,6},{8,9},{9,8},{10,11... | collective-permute-start | bytes 786440 | tf_op jit(solution)/shard_map/ppermute | solution.py:458
  69.3 21.5 %all-to-all-start.2 = ((bf16[8,520,128]{2,1,0:T(8,128)(2,1)}), bf16[8,520,128]{2,1,0:T(8,128)(2,1)S(1)}, u32[]{:S(2)}, u32[]{:S(2)}) async-start(bf16[8,520,128]{2,1,0:T(8,128)(2,1)} %get-tuple-element.58), calls=%async_computation.2 | async-start | bytes 2129920 | tf_op jit(solution)/shard_map/all_to_all | solution.py:395
  75.1 15.0 %collective-permute-start.5 = (bf16[4,128,128]{2,1,0:T(8,128)(2,1)S(1)}, bf16[4,128,128]{2,1,0:T(8,128)(2,1)S(1)}, u32[]{:S(2)}, u32[]{:S(2)}) collective-permute-start(bf16[4,128,128]{2,1,0:T(8,128)(2,1)S(1)} %dynamic-slice_bitcast_fusion.3), channel_id=1, source_target_pairs={{0,2},{2,0},{1,3},{3,1},{4,6},{6,4},{5,7},{7,5},{8,10},{10,8},{9,1... | collective-permute-start | bytes 393224 | tf_op jit(solution)/shard_map/ppermute | solution.py:458
  76.3 1.2 copy-start.1
  77.5 1.2 copy-start.2
  78.7 12.1 %copy-start.3 = (bf16[1024,128]{1,0:T(8,128)(2,1)S(1)}, bf16[1024,128]{1,0:T(8,128)(2,1)}, u32[]{:S(2)}) copy-start(bf16[1024,128]{1,0:T(8,128)(2,1)} %colbert_ref.3) | copy-start | bytes 786436
  78.7 12.1 %copy-start.4 = (f32[1024]{0:T(1024)S(1)}, f32[1024]{0:T(1024)}, u32[]{:S(2)}) copy-start(f32[1024]{0:T(1024)} %param.16) | copy-start | bytes 12292
  94.8 1.2 copy-start.5
  94.8 2.2 %copy-start.6 = (bf16[512,1024]{1,0:T(8,128)(2,1)S(1)}, bf16[512,1024]{1,0:T(8,128)(2,1)}, u32[]{:S(2)}) copy-start(bf16[512,1024]{1,0:T(8,128)(2,1)} %get-tuple-element.43) | copy-start | bytes 3145732
  94.9 6.9 %collective-permute-start.6 = (bf16[8,8,72,128]{3,2,1,0:T(8,128)(2,1)S(1)}, bf16[8,8,72,128]{3,2,1,0:T(8,128)(2,1)S(1)}, u32[]{:S(2)}, u32[]{:S(2)}) collective-permute-start(bf16[8,8,72,128]{3,2,1,0:T(8,128)(2,1)S(1)} %dynamic-slice_bitcast_fusion), channel_id=1, source_target_pairs={{0,1},{1,0},{2,3},{3,2},{4,5},{5,4},{6,7},{7,6},{8,9},{9,8},{10,11... | collective-permute-start | bytes 3538952 | tf_op jit(solution)/shard_map/ppermute | solution.py:458
  96.0 5.9 %collective-permute-start.7 = (f32[2,128,128]{2,1,0:T(8,128)S(1)}, f32[2,128,128]{2,1,0:T(8,128)S(1)}, u32[]{:S(2)}, u32[]{:S(2)}) collective-permute-start(f32[2,128,128]{2,1,0:T(8,128)S(1)} %dynamic-slice_bitcast_fusion.2), channel_id=1, source_target_pairs={{0,8},{4,12},{8,0},{12,4},{1,9},{5,13},{9,1},{13,5},{2,10},{6,14},... | collective-permute-start | bytes 393224 | tf_op jit(solution)/shard_map/ppermute | solution.py:458
  153.4 8.3 %collective-permute-start.9 = (bf16[8,8,72,128]{3,2,1,0:T(8,128)(2,1)S(1)}, bf16[8,8,72,128]{3,2,1,0:T(8,128)(2,1)S(1)}, u32[]{:S(2)}, u32[]{:S(2)}) collective-permute-start(bf16[8,8,72,128]{3,2,1,0:T(8,128)(2,1)S(1)} %bitcast.36), channel_id=1, source_target_pairs={{0,1},{1,0},{2,3},{3,2},{4,5},{5,4},{6,7},{7,6},{8,9},{9,8},{10,11... | collective-permute-start | bytes 3538952 | tf_op jit(solution)/shard_map/ppermute | solution.py:567
  157.5 3.7 %collective-permute-start.8 = (f32[128,128]{1,0:T(8,128)S(1)}, f32[128,128]{1,0:T(8,128)S(1)}, u32[]{:S(2)}, u32[]{:S(2)}) collective-permute-start(f32[128,128]{1,0:T(8,128)S(1)} %dynamic-slice_bitcast_fusion.4), channel_id=1, source_target_pairs={{0,4},{4,0},{8,12},{12,8},{1,5},{5,1},{9,13},{13,9},{2,6},{6,2},{1... | collective-permute-start | bytes 196616 | tf_op jit(solution)/shard_map/ppermute | solution.py:458

commit v5 on v4

--- a/solution.py
+++ b/solution.py
@@ -179,8 +179,30 @@
     )(flip, near, far, passage_pack, ids)
 
 
+def split_lines(value):
+    high = value.astype(BF16).astype(F32)
+    low = (value - high).astype(BF16).astype(F32)
+    last = value - high - low
+    row = lax.broadcasted_iota(jnp.int32, value.shape, 0)
+    lines = jnp.where(row == 0, high, jnp.where(row == 1, low, jnp.where(row == 2, last, 0.0)))
+    return lines.astype(BF16)
+
+
 def backward_kernel(
-    query_len, parts, own_ref, exp_ref, mix_ref, inv_ref, sim_ref, stats_ref, pg_ref, qg_ref, qt
+    query_len,
+    parts,
+    core_ref,
+    own_ref,
+    exp_ref,
+    mix_ref,
+    inv_ref,
+    sim_ref,
+    stats_ref,
+    pg_ref,
+    kept_ref,
+    given_ref,
+    qt,
+    halves,
 ):
     count, rows, slots = exp_ref.shape
     width, q_rows = own_ref.shape[1], rows // parts
@@ -201,44 +223,49 @@
         ((1,), (0,)),
         lax.Precision.HIGHEST,
     )
-    loss = jnp.broadcast_to(jnp.sum(log_total - positive, axis=1, keepdims=True), (EXTRA, width))
-    high = loss.astype(BF16).astype(F32)
-    low = (loss - high).astype(BF16).astype(F32)
-    last = loss - high - low
-    row = lax.broadcasted_iota(jnp.int32, (EXTRA, width), 0)
-    lines = jnp.where(row == 0, high, jnp.where(row == 1, low, jnp.where(row == 2, last, 0.0)))
+    lines = split_lines(
+        jnp.broadcast_to(jnp.sum(log_total - positive, axis=1, keepdims=True), (EXTRA, width))
+    )
     for p in range(count):
         weighted = (qt[...].astype(F32) * scale[p : p + 1]).astype(BF16)
         pg_ref[p, :slots, :] = dot(weighted, exp_ref[p], ((1,), (0,))).T.astype(BF16)
-        pg_ref[p, slots:, :] = lines.astype(BF16)
+        pg_ref[p, slots:, :] = lines
     turned = jnp.concatenate([scale, jnp.zeros((width - count, rows), F32)], axis=0).T
     for k in range(parts):
         at = slice(k * q_rows, (k + 1) * q_rows)
         sums = mix_ref[0, at, :] * turned[at, :1]
         for p in range(1, count):
             sums += mix_ref[p, at, :] * turned[at, p : p + 1]
-        qg_ref[k % 2, k // 2 % 2, k // 4] = sums.astype(BF16)
-
-
-def backward_tile(parts, own, spread, mixed, inverse, similar, stats, query_len):
+        halves[k % 2, k // 2 % 2, k // 4] = sums.astype(BF16)
+    kept_ref[...] = halves[core_ref[0]]
+    given_ref[...] = halves[1 - core_ref[0]]
+
+
+def backward_tile(core, parts, own, spread, mixed, inverse, similar, stats, query_len):
     count, rows, slots = spread.shape
     q_rows, width = rows // parts, own.shape[1]
     work = rows * slots * count
     return pl.pallas_call(
         functools.partial(backward_kernel, query_len, parts),
         name="backward_tile",
-        in_specs=[pl.BlockSpec(memory_space=pltpu.VMEM)] * 6,
+        in_specs=[pl.BlockSpec(memory_space=pltpu.SMEM)]
+        + [pl.BlockSpec(memory_space=pltpu.VMEM)] * 6,
         out_shape=[
             pltpu.HBM((count, slots + EXTRA, width), BF16),
-            pltpu.HBM((2, 2, parts // 4, q_rows, width), BF16),
-        ],
-        out_specs=[whole((count, slots + EXTRA, width)), whole((2, 2, parts // 4, q_rows, width))],
-        scratch_shapes=[pltpu.VMEM((width, rows), BF16)],
+            jax.ShapeDtypeStruct((2, parts // 4, q_rows, width), BF16),
+            jax.ShapeDtypeStruct((2, parts // 4, q_rows, width), BF16),
+        ],
+        out_specs=[whole((count, slots + EXTRA, width))]
+        + [whole((2, parts // 4, q_rows, width))] * 2,
+        scratch_shapes=[
+            pltpu.VMEM((width, rows), BF16),
+            pltpu.VMEM((2, 2, parts // 4, q_rows, width), BF16),
+        ],
         compiler_params=pltpu.CompilerParams(vmem_limit_bytes=16 * MIB),
         cost_estimate=pl.CostEstimate(
             flops=2 * work * width, transcendentals=0, bytes_accessed=3 * work
         ),
-    )(own, spread, mixed, inverse, similar, stats)
+    )(core, own, spread, mixed, inverse, similar, stats)
 
 
 def early_kernel(resid_ref, context_ref, proj_ref, normed_ref, inv_ref, context_t_ref):
@@ -281,18 +308,22 @@
 
 
 def late_kernel(
-    parts_ref,
+    core_ref,
+    own_ref,
+    taken_ref,
     normed_far,
     inv_far,
     gain_ref,
     colbert_ref,
     context_far,
     resid_ref,
-    sums_ref,
+    kept_ref,
+    given_ref,
     loss_ref,
     normed_ref,
     inv_ref,
     context_t_ref,
+    sums_ref,
     sems,
 ):
     loads = [
@@ -303,12 +334,9 @@
     ]
     for load in loads:
         load.start()
-    slots = parts_ref.shape[1] - EXTRA
-    count = parts_ref.shape[0]
+    slots = own_ref.shape[0] - EXTRA
     width = normed_ref.shape[1]
-    total = parts_ref[0].astype(F32)
-    for k in range(1, count):
-        total = total + parts_ref[k].astype(F32)
+    total = own_ref[...] + taken_ref[...].astype(F32)
     loss_ref[...] = jnp.broadcast_to(
         jnp.sum(total[slots:], axis=0, keepdims=True), loss_ref.shape
     )
@@ -349,20 +377,48 @@
                 sums_ref[k // blocks, k % blocks, j, :thick, :] = part[
                     at : at + thick, j * 128 : (j + 1) * 128
                 ]
+    kept_ref[...] = sums_ref[core_ref[0]]
+    given_ref[...] = sums_ref[1 - core_ref[0]]
+
+
+def fold_kernel(parts_ref, kept_ref, given_ref):
+    slots = parts_ref.shape[2] - EXTRA
+    for side, out_ref in enumerate((kept_ref, given_ref)):
+        total = parts_ref[0, side].astype(F32)
+        for k in range(1, parts_ref.shape[0]):
+            total += parts_ref[k, side].astype(F32)
+        if side == 0:
+            out_ref[...] = total
+        else:
+            out_ref[:slots, :] = total[:slots].astype(BF16)
+            loss = jnp.sum(total[slots:], axis=0, keepdims=True)
+            out_ref[slots:, :] = split_lines(jnp.broadcast_to(loss, (EXTRA, loss.shape[1])))
+
+
+def folded(parts):
+    shape = parts.shape[2:]
+    return pl.pallas_call(
+        fold_kernel,
+        name="folded",
+        out_shape=[jax.ShapeDtypeStruct(shape, F32), jax.ShapeDtypeStruct(shape, BF16)],
+    )(parts)
 
 
 def far(array):
     return pltpu.with_memory_space_constraint(array, pltpu.HBM)
 
 
-def late_rows(blocks, pieces, normed, inv_std, gain, colbert_proj, context_t):
+def late_rows(core, blocks, own, taken, normed, inv_std, gain, colbert_proj, context_t):
     rows, width = normed.shape
     emb = colbert_proj.shape[1]
+    shape = (blocks, width // 128, (width + emb) // (2 * blocks), 128)
     return pl.pallas_call(
         late_kernel,
         name="late_rows",
         in_specs=[
-            whole(pieces.shape),
+            pl.BlockSpec(memory_space=pltpu.SMEM),
+            whole(own.shape),
+            whole(taken.shape),
             pl.BlockSpec(memory_space=pltpu.HBM),
             pl.BlockSpec(memory_space=pltpu.HBM),
             whole(gain.shape),
@@ -373,13 +429,13 @@
             pltpu.VMEM(normed.shape, F32),
             pltpu.VMEM(inv_std.shape, F32),
             pltpu.VMEM(context_t.shape, BF16),
+            pltpu.VMEM((2, *shape), BF16),
             pltpu.SemaphoreType.DMA((3,)),
         ],
         out_shape=[
             jax.ShapeDtypeStruct((rows, width), BF16),
-            jax.ShapeDtypeStruct(
-                (2, blocks, width // 128, (width + emb) // (2 * blocks), 128), BF16
-            ),
+            jax.ShapeDtypeStruct(shape, BF16),
+            jax.ShapeDtypeStruct(shape, BF16),
             jax.ShapeDtypeStruct((8, emb), F32),
         ],
         compiler_params=pltpu.CompilerParams(vmem_limit_bytes=24 * MIB),
@@ -388,26 +444,54 @@
             transcendentals=0,
             bytes_accessed=14 * rows * width,
         ),
-    )(pieces, far(normed), far(inv_std), gain, colbert_proj, far(context_t))
+    )(core, own, taken, far(normed), far(inv_std), gain, colbert_proj, far(context_t))
 
 
 def exchange(pieces, axis):
     return lax.all_to_all(pieces, axis, 0, 0, tiled=True)
 
 
-def finish_kernel(core_ref, half_ref, other_ref, colbert_ref, gain_ref, proj_ref, grad_ref, gain_grad_ref):
-    blocks, lines = half_ref.shape[0], half_ref.shape[2]
-    thick = proj_ref.shape[0] // (2 * blocks)
+def own_kernel(core_ref, half_ref, proj_ref):
+    thick = proj_ref.shape[0] // half_ref.shape[0]
+    for k in range(half_ref.shape[0]):
+        proj_ref[k * thick : (k + 1) * thick, :] = half_ref[k, 0, :thick, :].astype(F32)
+
+
+def own_rows(core, half, width):
+    blocks, columns, lines, block = half.shape
+    return pl.pallas_call(
+        own_kernel,
+        name="own_rows",
+        grid_spec=pltpu.PrefetchScalarGridSpec(
+            num_scalar_prefetch=1,
+            grid=(columns,),
+            in_specs=[pl.BlockSpec((blocks, 1, lines, block), lambda k, core: (0, k, 0, 0))],
+            out_specs=pl.BlockSpec((width // 2, block), lambda k, core: (core[0], k)),
+        ),
+        out_shape=pltpu.HBM((width, width), F32),
+        compiler_params=pltpu.CompilerParams(vmem_limit_bytes=8 * MIB),
+        cost_estimate=pl.CostEstimate(
+            flops=width * width, transcendentals=0, bytes_accessed=4 * width * width
+        ),
+    )(core, half)
+
+
+def finish_kernel(
+    core_ref, half_ref, other_ref, colbert_ref, gain_ref, _, proj_ref, grad_ref, gain_grad_ref
+):
+    blocks = half_ref.shape[0]
+    thick = proj_ref.shape[0] // blocks
     even = core_ref[0] == 0
-    thin = []
-    for part in range(2):
-        for k in range(blocks):
-            half, other = half_ref[k, 0].astype(F32), other_ref[k, 0].astype(F32)
-            piece = jnp.where(even, half, other) if part == 0 else jnp.where(even, other, half)
-            at = (part * blocks + k) * thick
-            proj_ref[at : at + thick, :] = piece[:thick]
-            thin.append(piece[thick:])
-    colbert_grad = jnp.concatenate(thin, axis=0)
+    own, others = [], []
+    for k in range(blocks):
+        piece = other_ref[k, 0].astype(F32)
+        proj_ref[k * thick : (k + 1) * thick, :] = piece[:thick]
+        others.append(piece[thick:])
+        own.append(half_ref[k, 0].astype(F32)[thick:])
+    own, others = jnp.concatenate(own, axis=0), jnp.concatenate(others, axis=0)
+    colbert_grad = jnp.concatenate(
+        [jnp.where(even, own, others), jnp.where(even, others, own)], axis=0
+    )
     colbert_t = colbert_ref[...].astype(F32).T
     gain_grad_ref[...] = (
         jnp.sum(colbert_grad * colbert_t, axis=0, keepdims=True) / gain_ref[...]
@@ -415,48 +499,57 @@
     grad_ref[...] = colbert_grad.T
 
 
-def finish(core, half, other, colbert_proj, gain):
+def finish(core, half, other, colbert_proj, gain, proj):
     blocks, columns, lines, block = half.shape
     width, emb = colbert_proj.shape
+    piece = pl.BlockSpec((blocks, 1, lines, block), lambda k, core: (0, k, 0, 0))
     return pl.pallas_call(
         finish_kernel,
         name="finish",
-        grid=(columns,),
-        in_specs=[
-            pl.BlockSpec(memory_space=pltpu.SMEM),
-            pl.BlockSpec((blocks, 1, lines, block), lambda k: (0, k, 0, 0)),
-            pl.BlockSpec((blocks, 1, lines, block), lambda k: (0, k, 0, 0)),
-            pl.BlockSpec((block, emb), lambda k: (k, 0)),
-            pl.BlockSpec((1, block), lambda k: (0, k)),
-        ],
-        out_specs=[
-            pl.BlockSpec((width, block), lambda k: (0, k)),
-            pl.BlockSpec((block, emb), lambda k: (k, 0)),
-            pl.BlockSpec((1, block), lambda k: (0, k)),
-        ],
+        grid_spec=pltpu.PrefetchScalarGridSpec(
+            num_scalar_prefetch=1,
+            grid=(columns,),
+            in_specs=[
+                piece,
+                piece,
+                pl.BlockSpec((block, emb), lambda k, core: (k, 0)),
+                pl.BlockSpec((1, block), lambda k, core: (0, k)),
+                pl.BlockSpec(memory_space=pl.ANY),
+            ],
+            out_specs=[
+                pl.BlockSpec((width // 2, block), lambda k, core: (1 - core[0], k)),
+                pl.BlockSpec((block, emb), lambda k, core: (k, 0)),
+                pl.BlockSpec((1, block), lambda k, core: (0, k)),
+            ],
+        ),
         out_shape=[
             jax.ShapeDtypeStruct((width, width), F32),
             jax.ShapeDtypeStruct((width, emb), F32),
             jax.ShapeDtypeStruct((1, width), F32),
         ],
-        compiler_params=pltpu.CompilerParams(vmem_limit_bytes=16 * MIB),
+        input_output_aliases={5: 0},
+        compiler_params=pltpu.CompilerParams(vmem_limit_bytes=8 * MIB),
         cost_estimate=pl.CostEstimate(
-            flops=4 * width * width, transcendentals=0, bytes_accessed=8 * width * width
-        ),
-    )(core, half, other, colbert_proj, gain)
+            flops=2 * width * width, transcendentals=0, bytes_accessed=4 * width * width
+        ),
+    )(core, half, other, colbert_proj, gain, proj)
 
 
 SWAP = [(0, 1), (1, 0)]
 FAR = [(k, k ^ 2) for k in range(4)]
 NEAR = [(k, k ^ 1) for k in range(4)]
+
+
+def pair_summed(kept, given, axis, pairs, out_type):
+    taken = lax.ppermute(given, axis, pairs)
+    return (kept.astype(F32) + taken.astype(F32)).astype(out_type)
 
 
 def halves_summed(halves, axis, pairs, side, out_type):
     keep, give = side
     given = lax.dynamic_index_in_dim(halves, give, 0, False)
     kept = lax.dynamic_index_in_dim(halves, keep, 0, False)
-    taken = lax.ppermute(given, axis, pairs)
-    return (kept.astype(F32) + taken.astype(F32)).astype(out_type)
+    return pair_summed(kept, given, axis, pairs, out_type)
 
 
 def query_gathered(own):
@@ -466,26 +559,21 @@
     return held, lax.ppermute(held, "neg_1", SWAP)
 
 
-def pack_kernel(length_ref, p_ref, out_ref):
-    slots = p_ref.shape[1]
-    extra = jnp.full((EXTRA, p_ref.shape[2]), (length_ref[0] - LEAST).astype(F32)).astype(BF16)
+def pack_kernel(own_ref, taken_ref, out_ref):
     for k in range(out_ref.shape[0]):
-        out_ref[k, :slots, :] = p_ref[0]
-        out_ref[k, slots:, :] = extra
-
-
-def passage_copies(passage_emb, lengths, copies):
-    _, slots, width = passage_emb.shape
+        out_ref[k, 0] = own_ref[...]
+        out_ref[k, 1] = taken_ref[...]
+
+
+def passage_copies(own, taken, copies):
+    shape = (copies, 2, *own.shape)
     return pl.pallas_call(
         pack_kernel,
         name="passage_copies",
-        in_specs=[
-            pl.BlockSpec(memory_space=pltpu.SMEM),
-            pl.BlockSpec(memory_space=pltpu.VMEM),
-        ],
-        out_specs=whole((copies, slots + EXTRA, width)),
-        out_shape=pltpu.HBM((copies, slots + EXTRA, width), BF16),
-    )(lengths, passage_emb)
+        compiler_params=pltpu.CompilerParams(vmem_limit_bytes=8 * MIB),
+        out_specs=whole(shape),
+        out_shape=pltpu.HBM(shape, BF16),
+    )(own, taken)
 
 
 def spread_kernel(parts_ref, out_ref):
@@ -521,52 +609,60 @@
             jnp.broadcast_to(wanted.astype(BF16)[None], (EXTRA, emb)),
         ]
     )
-    copies, query_own = lax.optimization_barrier(
-        (passage_copies(passage_emb, lengths, dp_size), query_own)
-    )
-    passage_pack = exchange(copies, DP)
+    passage_own = jnp.concatenate(
+        [
+            passage_emb.reshape(-1, emb),
+            jnp.broadcast_to((lengths - LEAST).astype(BF16)[:, None], (EXTRA, emb)),
+        ]
+    )
+    passage_pair = passage_copies(
+        passage_own, lax.ppermute(passage_own, "dp_1", SWAP), lax.axis_size("dp_0")
+    )
+    passage_pack = exchange(passage_pair, "dp_0").reshape(dp_size, *passage_own.shape)
     queries = query_gathered(query_own)
-    ids = jnp.broadcast_to(
-        (jnp.arange(dp_size) * neg_size + place).astype(F32)[:, None], (dp_size, emb)
-    )
+    group = jnp.arange(dp_size) ^ lax.axis_index("dp_1")
+    ids = jnp.broadcast_to((group * neg_size + place).astype(F32)[:, None], (dp_size, emb))
     row, column = lax.axis_index("neg_1"), lax.axis_index("neg_0")
     flip = (row * 8 + column * 2 + core)[None]
     sides = [
         (own.astype(jnp.uint32), (1 - own).astype(jnp.uint32))
-        for own in (core, row, column // 2, column % 2)
+        for own in (row, column // 2, column % 2)
     ]
     queries, sides = lax.optimization_barrier((queries, sides))
-    core_side, row_side, far_side, near_side = sides
+    row_side, far_side, near_side = sides
     spread, mixed, query_rows, inverse, similar, stats = forward_tile(
         flip, *queries, passage_pack, ids, query_len
     )
     stats = exchange(stats, NEG)
-    passage_parts, query_parts = backward_tile(
-        neg_size, query_rows, spread, mixed, inverse, similar, stats, query_len
-    )
-    residual, query_parts = lax.optimization_barrier((residual, query_parts))
+    passage_parts, kept, given = backward_tile(
+        core[None], neg_size, query_rows, spread, mixed, inverse, similar, stats, query_len
+    )
+    residual, kept, given = lax.optimization_barrier((residual, kept, given))
     early = early_rows(residual, context, out_proj)
-    query_part = halves_summed(query_parts, CORE, SWAP, core_side, BF16)
+    query_part = pair_summed(kept, given, CORE, SWAP, BF16)
     query_part = halves_summed(query_part, "neg_1", SWAP, row_side, F32)
-    passage_parts = exchange(passage_parts, DP)
+    passage_parts = exchange(passage_parts.reshape(passage_pair.shape), "dp_0")
     passage_parts, query_part, early = lax.optimization_barrier((passage_parts, query_part, early))
     normed, inv_std, context_t = early
-    residual_grad, partial, loss_sum = late_rows(
-        dp_size, passage_parts, normed, inv_std, norm_gain[None], colbert_proj, context_t
-    )
-    half = halves_summed(partial, CORE, SWAP, core_side, BF16)
-    context_grad = jnp.dot(residual_grad, out_proj.T, preferred_element_type=F32).astype(BF16)
+    own_part, given_part = folded(passage_parts)
+    taken_part = lax.ppermute(given_part, "dp_1", SWAP)
     query_part = query_part.reshape(2, 2, *query_part.shape[1:])
     query_part = halves_summed(query_part, "neg_0", FAR, far_side, F32)
-    half, context_grad, query_part = lax.optimization_barrier((half, context_grad, query_part))
+    taken_part, query_part = lax.optimization_barrier((taken_part, query_part))
+    residual_grad, kept, given, loss_sum = late_rows(
+        core[None], dp_size, own_part, taken_part, normed, inv_std, norm_gain[None], colbert_proj, context_t
+    )
+    half = pair_summed(kept, given, CORE, SWAP, BF16)
+    context_grad = jnp.dot(residual_grad, out_proj.T, preferred_element_type=F32).astype(BF16)
+    query_grad = halves_summed(query_part, "neg_0", NEAR, near_side, F32)
+    half, context_grad, query_grad = lax.optimization_barrier((half, context_grad, query_grad))
+    query_grad = query_grad.reshape(query_dev, query_len, emb)
     slabs = exchange(half.reshape(dp_size * cross_size, *half.shape[2:]), DP + CROSS)
     half = exchange(summed_copies(slabs), DP + CROSS).reshape(half.shape)
-    half, query_part = lax.optimization_barrier((half, query_part))
-    query_grad = halves_summed(query_part, "neg_0", NEAR, near_side, F32)
-    query_grad = query_grad.reshape(query_dev, query_len, emb)
     other = lax.ppermute(half, CORE, SWAP)
+    proj = own_rows(core[None], half, out_proj.shape[0])
     out_proj_grad, colbert_grad, gain_grad = finish(
-        core[None], half, other, colbert_proj, norm_gain[None]
+        core[None], half, other, colbert_proj, norm_gain[None], proj
     )
     loss = loss_sum[0, 0] / (query_dev * dp_size * neg_size)
     return (

time: 167 us -> 172 us (1.030)
  Pallas kernels: 36.5 us -> 40.2 us
  starting transfers between devices: 27.5 us -> 29.4 us
    all_to_all x2, waiting for transfers between devices: 0.01 us -> 7.75 us  [exchange(): return lax.all_to_all(pieces, axis, 0, 0, tiled=True)]
    ppermute x5 -> x7, waiting for transfers between devices: 12.1 us -> 4.86 us  [the longest x5 2.5 us: pair_summed(): taken = lax.ppermute(given, axis, pairs)]
    pallas_call x3 -> x5, Pallas kernels: 9.85 us -> 13.6 us  [the longest x1 4.11 us: late_rows(): pl.pallas_call(late_kernel, name='late_rows', in_specs=[pl.BlockSpec(memo...]
    ppermute x5 -> x7, starting transfers between devices: 4.21 us -> 7.64 us  [the longest x5 4.92 us: pair_summed(): taken = lax.ppermute(given, axis, pairs)]
  transfers between devices with their start and end apart: 12 -> 14, of which waited for: 7 -> 8; matrix products, arithmetic and copies ran while one was open for 3% -> 4% of each run, Pallas kernels for 2% -> 6%
where the time goes in v5:
time: 172 us; the launch traced here: 171 us
  blocking collectives  66.3 us (39%)
  Pallas kernels  40.2 us (23%)
  starting transfers between devices  29.4 us (17%)
  waiting for transfers between devices  21.7 us (13%)
  local copies, waits for them, and re-layouts  3.73 us (2%)
  other arithmetic  3.59 us (2%)
  matrix products  3.49 us (2%)
  between operations  3.16 us (2%)
    all_to_all x3, blocking collectives, exchange(): return lax.all_to_all(pieces, axis, 0, 0, tiled=True)  66.3 us
    pallas_call x1, Pallas kernels, forward_tile(): pl.pallas_call(functools.partial(forward_kernel, query_len, group), name=...  14.1 us
    all_to_all x2, starting transfers between devices, exchange(): return lax.all_to_all(pieces, axis, 0, 0, tiled=True)  10.3 us
    all_to_all x2, waiting for transfers between devices, exchange(): return lax.all_to_all(pieces, axis, 0, 0, tiled=True)  7.75 us
    pallas_call x1, Pallas kernels, backward_tile(): pl.pallas_call(functools.partial(backward_kernel, query_len, parts), name...  6.12 us
    ppermute x3, waiting for transfers between devices, query_gathered(): held = jnp.concatenate([held, lax.ppermute(held, axis, pairs)])  5.08 us
    ppermute x3, starting transfers between devices, query_gathered(): held = jnp.concatenate([held, lax.ppermute(held, axis, pairs)])  5.07 us
    ppermute x5, starting transfers between devices, pair_summed(): taken = lax.ppermute(given, axis, pairs)  4.92 us
  transfers between devices with their start and end apart: 14, of which 8 were waited for; matrix products, arithmetic and copies ran while one was open for 4% of the time, Pallas kernels for 6%

profile of v5, /device:TPU:1, one launch (start us, length us, event | category | flops | bytes accessed | tf_op | source)
XLA Modules:
  0.0 171.5 jit_solution(12773120347551864594)
XLA Ops:
  1.3 0.9 concatenate.21.own_ref
  2.2 2.2 %collective-permute-start.4 = (bf16[520,128]{1,0:T(8,128)(2,1)S(1)}, bf16[520,128]{1,0:T(8,128)(2,1)S(1)}, u32[]{:S(2)}, u32[]{:S(2)}) collective-permute-start(bf16[520,128]{1,0:T(8,128)(2,1)S(1)} %concatenate.21.own_ref), channel_id=1, source_target_pairs={{0,16},{16,0},{1,17},{17,1},{2,18},{18,2},{3,19},{19,3},{4,20},{20... | collective-permute-start | bytes 399368 | tf_op jit(solution)/shard_map/ppermute | solution.py:619
  4.4 0.7 select_reduce_fusion
  5.2 0.8 maximum_bitcast_fusion
  5.9 1.0 collective-permute-start
  6.9 0.4 collective-permute-done.4.taken_ref
  7.3 1.1 passage_copies.1
  8.4 5.3 %all-to-all-start = ((bf16[4,2,520,128]{3,2,1,0:T(8,128)(2,1)}), bf16[4,2,520,128]{3,2,1,0:T(8,128)(2,1)S(1)}, u32[]{:S(2)}, u32[]{:S(2)}) async-start(bf16[4,2,520,128]{3,2,1,0:T(8,128)(2,1)} %passage_copies.1), calls=%async_computation | async-start | bytes 2129920 | tf_op jit(solution)/shard_map/all_to_all | solution.py:451
  13.7 0.0 collective-permute-done
  13.7 1.3 collective-permute-start.1
  15.0 1.9 %collective-permute-done.1 = bf16[2,136,128]{2,1,0:T(8,128)(2,1)S(1)} collective-permute-done((bf16[2,136,128]{2,1,0:T(8,128)(2,1)S(1)}, bf16[2,136,128]{2,1,0:T(8,128)(2,1)S(1)}, u32[]{:S(2)}, u32[]{:S(2)}) %collective-permute-start.1) | collective-permute-done | bytes 69664 | tf_op jit(solution)/shard_map/ppermute | solution.py:558
  16.9 2.8 %collective-permute-start.2 = (bf16[4,136,128]{2,1,0:T(8,128)(2,1)S(1)}, bf16[4,136,128]{2,1,0:T(8,128)(2,1)S(1)}, u32[]{:S(2)}, u32[]{:S(2)}) collective-permute-start(bf16[4,136,128]{2,1,0:T(8,128)(2,1)S(1)} %pad_maximum_fusion.1), channel_id=1, source_target_pairs={{0,8},{4,12},{8,0},{12,4},{1,9},{5,13},{9,1},{13,5},{2,10},{6,14},... | collective-permute-start | bytes 417800 | tf_op jit(solution)/shard_map/ppermute | solution.py:558
  19.8 3.1 %collective-permute-done.2 = bf16[4,136,128]{2,1,0:T(8,128)(2,1)S(1)} collective-permute-done((bf16[4,136,128]{2,1,0:T(8,128)(2,1)S(1)}, bf16[4,136,128]{2,1,0:T(8,128)(2,1)S(1)}, u32[]{:S(2)}, u32[]{:S(2)}) %collective-permute-start.2) | collective-permute-done | bytes 139296 | tf_op jit(solution)/shard_map/ppermute | solution.py:558
  22.9 3.0 %collective-permute-start.3 = (bf16[8,136,128]{2,1,0:T(8,128)(2,1)S(1)}, bf16[8,136,128]{2,1,0:T(8,128)(2,1)S(1)}, u32[]{:S(2)}, u32[]{:S(2)}) collective-permute-start(bf16[8,136,128]{2,1,0:T(8,128)(2,1)S(1)} %pad_maximum_fusion.near_ref), channel_id=1, source_target_pairs={{0,2},{2,0},{1,3},{3,1},{4,6},{6,4},{5,7},{7,5},{8,10},{10,8},{9,1... | collective-permute-start | bytes 835592 | tf_op jit(solution)/shard_map/ppermute | solution.py:559
  25.9 4.0 %collective-permute-done.3.far_ref = bf16[8,136,128]{2,1,0:T(8,128)(2,1)S(1)} collective-permute-done((bf16[8,136,128]{2,1,0:T(8,128)(2,1)S(1)}, bf16[8,136,128]{2,1,0:T(8,128)(2,1)S(1)}, u32[]{:S(2)}, u32[]{:S(2)}) %collective-permute-start.3) | collective-permute-done | bytes 278560 | tf_op jit(solution)/shard_map/ppermute | solution.py:559
  29.9 0.0 all-to-all-done
  29.9 0.1 broadcast_in_dim.56.ids_ref
  30.0 14.1 %forward_tile.1 = (bf16[8,2048,512]{2,1,0:T(8,128)(2,1)S(1)}, f32[8,2048,128]{2,1,0:T(8,128)S(1)}, bf16[2048,128]{1,0:T(8,128)(2,1)S(1)}, f32[8,2048]{1,0:T(8,12...) custom-call(s32[1]{0:T(128)} %bitcast.1.flip_ref, bf16[8,136,128]{2,1,0:T(8,128)(2,1)S(1)} %pad_maximum_fusion.near_ref, ...), custom_call_target="tpu_custom_call" | custom-call | flops 4294967296 | bytes 33554432 | tf_op jit(solution)/shard_map/forward_tile/pallas_call | solution.py:147
  44.1 19.1 %all_to_all.25.stats_ref = f32[16,8,128]{2,1,0:T(8,128)S(1)} all-to-all(f32[16,8,128]{2,1,0:T(8,128)S(1)} %get-tuple-element.56), channel_id=1, replica_groups=mesh['dp_0'=4,'dp_1'=2,'neg_0'=4,'neg_1'=2,'neg_2'=2] {'neg_0','neg_1','..., dimensions={0} | all-to-all | bytes 131072 | tf_op jit(solution)/shard_map/all_to_all | solution.py:451
  63.2 6.1 %backward_tile.1 = (bf16[8,520,128]{2,1,0:T(8,128)(2,1)}, bf16[2,4,128,128]{3,2,1,0:T(8,128)(2,1)S(1)}, bf16[2,4,128,128]{3,2,1,0:T(8,128)(2,1)}) custom-call(s32[1]{0:T(128)} %bitcast.core_ref, bf16[2048,128]{1,0:T(8,128)(2,1)S(1)} %get-tuple-element.51.own_ref, bf16[8,2048,512]{2,1,0:T(8,128)(2,1)S(1)} %get-tuple-element.52.exp_ref, ...), custom_call_target="tpu_custom_call" | custom-call | flops 2147483648 | bytes 25165824 | tf_op jit(solution)/shard_map/backward_tile/pallas_call | solution.py:248
  69.3 0.4 collective-permute-start.5
  69.7 0.0 copy-start
  69.7 0.0 copy-start.1
  69.7 5.1 %all-to-all-start.2 = ((bf16[4,2,520,128]{3,2,1,0:T(8,128)(2,1)}), bf16[4,2,520,128]{3,2,1,0:T(8,128)(2,1)}, u32[]{:S(2)}, u32[]{:S(2)}) async-start(bf16[4,2,520,128]{3,2,1,0:T(8,128)(2,1)} %bitcast.38), calls=%async_computation.2 | async-start | bytes 2129920 | tf_op jit(solution)/shard_map/all_to_all | solution.py:451
  74.8 0.0 collective-permute-done.5
  74.8 1.0 add_convert_fusion.1
  75.8 0.5 collective-permute-start.6
  76.3 0.0 copy-done
  76.3 0.0 copy-done.1
  76.3 0.0 copy-start.2
  76.3 1.2 copy-done.2
  77.6 3.9 %early_rows.1 = (f32[512,1024]{1,0:T(8,128)}, f32[512,128]{1,0:T(8,128)}, bf16[1024,512]{1,0:T(8,128)(2,1)}) custom-call(bf16[512,1024]{1,0:T(8,128)(2,1)S(1)} %copy-done.1, bf16[512,1024]{1,0:T(8,128)(2,1)S(1)} %copy-done.2, bf16[1024,1024]{1,0:T(8,128)(2,1)S(1)} %copy-done), custom_call_target="tpu_custom_call" | custom-call | flops 1073741824 | bytes 5242880 | tf_op jit(solution)/shard_map/early_rows/pallas_call | solution.py:284
  81.4 0.0 copy-start.3
  81.4 0.0 copy-start.4
  81.4 0.7 collective-permute-done.6
  82.1 7.7 %all-to-all-done.2.parts_ref = bf16[4,2,520,128]{3,2,1,0:T(8,128)(2,1)} async-done(((bf16[4,2,520,128]{3,2,1,0:T(8,128)(2,1)}), bf16[4,2,520,128]{3,2,1,0:T(8,128)(2,1)}, u32[]{:S(2)}, u32[]{:S(2)}) %all-to-all-start.2) | async-done | bytes 1064992 | tf_op jit(solution)/shard_map/all_to_all | solution.py:451
  89.9 1.0 collective-permute-start.8
  90.9 2.0 %folded.1 = (f32[520,128]{1,0:T(8,128)}, bf16[520,128]{1,0:T(8,128)(2,1)}) custom-call(bf16[4,2,520,128]{3,2,1,0:T(8,128)(2,1)} %all-to-all-done.2.parts_ref), custom_call_target="tpu_custom_call" | custom-call | tf_op jit(solution)/shard_map/folded/pallas_call | solution.py:400
  92.9 0.5 collective-permute-start.7
  93.4 1.8 %collective-permute-done.8 = f32[2,128,128]{2,1,0:T(8,128)S(1)} collective-permute-done((f32[2,128,128]{2,1,0:T(8,128)S(1)}, f32[2,128,128]{2,1,0:T(8,128)S(1)}, u32[]{:S(2)}, u32[]{:S(2)}) %collective-permute-start.8) | collective-permute-done | bytes 131104 | tf_op jit(solution)/shard_map/ppermute | solution.py:544
  95.3 2.0 %collective-permute-done.7.taken_ref = bf16[520,128]{1,0:T(8,128)(2,1)S(1)} collective-permute-done((bf16[520,128]{1,0:T(8,128)(2,1)}, bf16[520,128]{1,0:T(8,128)(2,1)S(1)}, u32[]{:S(2)}, u32[]{:S(2)}) %collective-permute-start.7) | collective-permute-done | bytes 133152 | tf_op jit(solution)/shard_map/ppermute | solution.py:648
  97.3 0.0 copy-done.3
  97.3 0.0 copy-done.4
  97.3 0.0 copy-start.5
  97.3 1.0 copy-done.5
  98.2 4.1 %late_rows.1 = (bf16[512,1024]{1,0:T(8,128)(2,1)}, bf16[8,8,72,128]{3,2,1,0:T(8,128)(2,1)S(1)}, bf16[8,8,72,128]{3,2,1,0:T(8,128)(2,1)S(1)}, f32[8,128]{1,0:T(8,128)S(1)}) custom-call(s32[1]{0:T(128)} %bitcast.core_ref, f32[520,128]{1,0:T(8,128)S(1)} %copy-done.5, bf16[520,128]{1,0:T(8,128)(2,1)S(1)} %collective-permute-done.7.taken_ref, ...), custom_call_target="tpu_custom_call" | custom-call | flops 1342177280 | bytes 7340032 | tf_op jit(solution)/shard_map/late_rows/pallas_call | solution.py:415
  102.3 2.5 %collective-permute-start.9 = (bf16[8,8,72,128]{3,2,1,0:T(8,128)(2,1)S(1)}, bf16[8,8,72,128]{3,2,1,0:T(8,128)(2,1)S(1)}, u32[]{:S(2)}, u32[]{:S(2)}) collective-permute-start(bf16[8,8,72,128]{3,2,1,0:T(8,128)(2,1)S(1)} %get-tuple-element.80), channel_id=1, source_target_pairs={{0,1},{1,0},{2,3},{3,2},{4,5},{5,4},{6,7},{7,6},{8,9},{9,8},{10,11... | collective-permute-start | bytes 3538952 | tf_op jit(solution)/shard_map/ppermute | solution.py:544
  104.8 0.5 collective-permute-start.10
  105.4 3.5 %convolution_convert_fusion = bf16[512,1024]{1,0:T(8,128)(2,1)} fusion(bf16[512,1024]{1,0:T(8,128)(2,1)} %get-tuple-element.44, bf16[1024,1024]{1,0:T(8,128)(2,1)S(1)} %copy-done), kind=kOutput, calls=%fused_computation.1 | convolution fusion | flops 1074266112 | bytes 4194304 | tf_op jit(solution)/shard_map/dot_general | solution.py:656
  108.9 0.0 collective-permute-done.10
  108.9 0.6 bitcast_add_fusion.1
  109.5 0.0 collective-permute-done.9
  109.5 0.3 add_convert_fusion
  109.8 24.6 %all_to_all.26.parts_ref = bf16[64,72,128]{2,1,0:T(8,128)(2,1)} all-to-all(bf16[64,72,128]{2,1,0:T(8,128)(2,1)S(1)} %bitcast.37), channel_id=1, replica_groups=mesh['dp_0'=4,'dp_1'=2,'neg_0'=4,'neg_1'=2,'neg_2'=2] {'dp_0','dp_1','ne..., dimensions={0} | all-to-all | bytes 2359296 | tf_op jit(solution)/shard_map/all_to_all | solution.py:451
  134.4 2.5 %summed_copies.1 = bf16[64,72,128]{2,1,0:T(8,128)(2,1)} custom-call(bf16[64,72,128]{2,1,0:T(8,128)(2,1)} %all_to_all.26.parts_ref), custom_call_target="tpu_custom_call" | custom-call | tf_op jit(solution)/shard_map/summed_copies/pallas_call | solution.py:587
  136.9 22.6 %all_to_all.27 = bf16[64,72,128]{2,1,0:T(8,128)(2,1)S(1)} all-to-all(bf16[64,72,128]{2,1,0:T(8,128)(2,1)} %summed_copies.1), channel_id=1, replica_groups=mesh['dp_0'=4,'dp_1'=2,'neg_0'=4,'neg_1'=2,'neg_2'=2] {'dp_0','dp_1','ne..., dimensions={0} | all-to-all | bytes 2359296 | tf_op jit(solution)/shard_map/all_to_all | solution.py:451
  159.5 3.3 %collective-permute-start.11 = (bf16[8,8,72,128]{3,2,1,0:T(8,128)(2,1)S(1)}, bf16[8,8,72,128]{3,2,1,0:T(8,128)(2,1)S(1)}, u32[]{:S(2)}, u32[]{:S(2)}) collective-permute-start(bf16[8,8,72,128]{3,2,1,0:T(8,128)(2,1)S(1)} %bitcast.31), channel_id=1, source_target_pairs={{0,1},{1,0},{2,3},{3,2},{4,5},{5,4},{6,7},{7,6},{8,9},{9,8},{10,11... | collective-permute-start | bytes 3538952 | tf_op jit(solution)/shard_map/ppermute | solution.py:662
  162.8 0.5 slice.3
  164.0 3.1 %own_rows.1._ = f32[1024,1024]{1,0:T(8,128)} custom-call(s32[1]{0:T(128)} %bitcast.core_ref, bf16[8,8,72,128]{3,2,1,0:T(8,128)(2,1)S(1)} %bitcast.32), custom_call_target="tpu_custom_call" | custom-call | flops 1048576 | bytes 4194304 | tf_op jit(solution)/shard_map/own_rows/pallas_call | solution.py:462
  167.0 0.0 collective-permute-done.11.other_ref
  167.0 3.3 %finish.1 = (f32[1024,1024]{1,0:T(8,128)}, f32[1024,128]{1,0:T(8,128)}, f32[1,1024]{1,0:T(1,128)}) custom-call(s32[1]{0:T(128)} %bitcast.core_ref, bf16[8,8,72,128]{3,2,1,0:T(8,128)(2,1)S(1)} %bitcast.33, bf16[8,8,72,128]{3,2,1,0:T(8,128)(2,1)S(1)} %collective-permute-done.11.other_ref, ...), custom_call_target="tpu_custom_call", output_to_operand_aliasing={{0}: (5, {})} | custom-call | flops 2097152 | bytes 4194304 | tf_op jit(solution)/shard_map/finish/pallas_call | solution.py:506
  (12 shorter events, 0.2 us)
Async XLA Ops:
  2.2 5.1 %collective-permute-start.4 = (bf16[520,128]{1,0:T(8,128)(2,1)S(1)}, bf16[520,128]{1,0:T(8,128)(2,1)S(1)}, u32[]{:S(2)}, u32[]{:S(2)}) collective-permute-start(bf16[520,128]{1,0:T(8,128)(2,1)S(1)} %concatenate.21.own_ref), channel_id=1, source_target_pairs={{0,16},{16,0},{1,17},{17,1},{2,18},{18,2},{3,19},{19,3},{4,20},{20... | collective-permute-start | bytes 399368 | tf_op jit(solution)/shard_map/ppermute | solution.py:619
  5.9 7.7 %collective-permute-start = (bf16[1,136,128]{2,1,0:T(8,128)(2,1)S(1)}, bf16[1,136,128]{2,1,0:T(8,128)(2,1)S(1)}, u32[]{:S(2)}, u32[]{:S(2)}) collective-permute-start(bf16[1,136,128]{2,1,0:T(8,128)(2,1)S(1)} %maximum_bitcast_fusion), channel_id=1, source_target_pairs={{0,1},{1,0},{2,3},{3,2},{4,5},{5,4},{6,7},{7,6},{8,9},{9,8},{10,11... | collective-permute-start | bytes 104456 | tf_op jit(solution)/shard_map/ppermute | solution.py:558
  8.4 21.5 %all-to-all-start = ((bf16[4,2,520,128]{3,2,1,0:T(8,128)(2,1)}), bf16[4,2,520,128]{3,2,1,0:T(8,128)(2,1)S(1)}, u32[]{:S(2)}, u32[]{:S(2)}) async-start(bf16[4,2,520,128]{3,2,1,0:T(8,128)(2,1)} %passage_copies.1), calls=%async_computation | async-start | bytes 2129920 | tf_op jit(solution)/shard_map/all_to_all | solution.py:451
  13.7 3.2 %collective-permute-start.1 = (bf16[2,136,128]{2,1,0:T(8,128)(2,1)S(1)}, bf16[2,136,128]{2,1,0:T(8,128)(2,1)S(1)}, u32[]{:S(2)}, u32[]{:S(2)}) collective-permute-start(bf16[2,136,128]{2,1,0:T(8,128)(2,1)S(1)} %pad_maximum_fusion.2), channel_id=1, source_target_pairs={{0,4},{4,0},{8,12},{12,8},{1,5},{5,1},{9,13},{13,9},{2,6},{6,2},{1... | collective-permute-start | bytes 208904 | tf_op jit(solution)/shard_map/ppermute | solution.py:558
  16.9 6.0 %collective-permute-start.2 = (bf16[4,136,128]{2,1,0:T(8,128)(2,1)S(1)}, bf16[4,136,128]{2,1,0:T(8,128)(2,1)S(1)}, u32[]{:S(2)}, u32[]{:S(2)}) collective-permute-start(bf16[4,136,128]{2,1,0:T(8,128)(2,1)S(1)} %pad_maximum_fusion.1), channel_id=1, source_target_pairs={{0,8},{4,12},{8,0},{12,4},{1,9},{5,13},{9,1},{13,5},{2,10},{6,14},... | collective-permute-start | bytes 417800 | tf_op jit(solution)/shard_map/ppermute | solution.py:558
  22.9 7.0 %collective-permute-start.3 = (bf16[8,136,128]{2,1,0:T(8,128)(2,1)S(1)}, bf16[8,136,128]{2,1,0:T(8,128)(2,1)S(1)}, u32[]{:S(2)}, u32[]{:S(2)}) collective-permute-start(bf16[8,136,128]{2,1,0:T(8,128)(2,1)S(1)} %pad_maximum_fusion.near_ref), channel_id=1, source_target_pairs={{0,2},{2,0},{1,3},{3,1},{4,6},{6,4},{5,7},{7,5},{8,10},{10,8},{9,1... | collective-permute-start | bytes 835592 | tf_op jit(solution)/shard_map/ppermute | solution.py:559
  69.3 5.5 %collective-permute-start.5 = (bf16[2,4,128,128]{3,2,1,0:T(8,128)(2,1)}, bf16[2,4,128,128]{3,2,1,0:T(8,128)(2,1)}, u32[]{:S(2)}, u32[]{:S(2)}) collective-permute-start(bf16[2,4,128,128]{3,2,1,0:T(8,128)(2,1)} %get-tuple-element.61), channel_id=1, source_target_pairs={{0,1},{1,0},{2,3},{3,2},{4,5},{5,4},{6,7},{7,6},{8,9},{9,8},{10,11... | collective-permute-start | bytes 786440 | tf_op jit(solution)/shard_map/ppermute | solution.py:544
  69.7 6.6 %copy-start = (bf16[1024,1024]{1,0:T(8,128)(2,1)S(1)}, bf16[1024,1024]{1,0:T(8,128)(2,1)}, u32[]{:S(2)}) copy-start(bf16[1024,1024]{1,0:T(8,128)(2,1)} %proj_ref.1) | copy-start | bytes 6291460
  69.7 6.6 %copy-start.1 = (bf16[512,1024]{1,0:T(8,128)(2,1)S(1)}, bf16[512,1024]{1,0:T(8,128)(2,1)}, u32[]{:S(2)}) copy-start(bf16[512,1024]{1,0:T(8,128)(2,1)} %resid_ref) | copy-start | bytes 3145732
  69.7 20.1 %all-to-all-start.2 = ((bf16[4,2,520,128]{3,2,1,0:T(8,128)(2,1)}), bf16[4,2,520,128]{3,2,1,0:T(8,128)(2,1)}, u32[]{:S(2)}, u32[]{:S(2)}) async-start(bf16[4,2,520,128]{3,2,1,0:T(8,128)(2,1)} %bitcast.38), calls=%async_computation.2 | async-start | bytes 2129920 | tf_op jit(solution)/shard_map/all_to_all | solution.py:451
  75.8 6.2 %collective-permute-start.6 = (bf16[4,128,128]{2,1,0:T(8,128)(2,1)S(1)}, bf16[4,128,128]{2,1,0:T(8,128)(2,1)S(1)}, u32[]{:S(2)}, u32[]{:S(2)}) collective-permute-start(bf16[4,128,128]{2,1,0:T(8,128)(2,1)S(1)} %dynamic-slice_bitcast_fusion.1), channel_id=1, source_target_pairs={{0,2},{2,0},{1,3},{3,1},{4,6},{6,4},{5,7},{7,5},{8,10},{10,8},{9,1... | collective-permute-start | bytes 393224 | tf_op jit(solution)/shard_map/ppermute | solution.py:544
  76.3 1.2 copy-start.2
  81.4 15.9 %copy-start.3 = (bf16[1024,128]{1,0:T(8,128)(2,1)S(1)}, bf16[1024,128]{1,0:T(8,128)(2,1)}, u32[]{:S(2)}) copy-start(bf16[1024,128]{1,0:T(8,128)(2,1)} %colbert_ref.3) | copy-start | bytes 786436
  81.4 15.9 %copy-start.4 = (f32[1024]{0:T(1024)S(1)}, f32[1024]{0:T(1024)}, u32[]{:S(2)}) copy-start(f32[1024]{0:T(1024)} %param.16) | copy-start | bytes 12292
  89.9 5.4 %collective-permute-start.8 = (f32[2,128,128]{2,1,0:T(8,128)S(1)}, f32[2,128,128]{2,1,0:T(8,128)S(1)}, u32[]{:S(2)}, u32[]{:S(2)}) collective-permute-start(f32[2,128,128]{2,1,0:T(8,128)S(1)} %dynamic-slice_bitcast_fusion), channel_id=1, source_target_pairs={{0,8},{4,12},{8,0},{12,4},{1,9},{5,13},{9,1},{13,5},{2,10},{6,14},... | collective-permute-start | bytes 393224 | tf_op jit(solution)/shard_map/ppermute | solution.py:544
  92.9 4.3 %collective-permute-start.7 = (bf16[520,128]{1,0:T(8,128)(2,1)}, bf16[520,128]{1,0:T(8,128)(2,1)S(1)}, u32[]{:S(2)}, u32[]{:S(2)}) collective-permute-start(bf16[520,128]{1,0:T(8,128)(2,1)} %get-tuple-element.70), channel_id=1, source_target_pairs={{0,16},{16,0},{1,17},{17,1},{2,18},{18,2},{3,19},{19,3},{4,20},{20... | collective-permute-start | bytes 399368 | tf_op jit(solution)/shard_map/ppermute | solution.py:648
  97.3 1.0 copy-start.5
  102.3 7.2 %collective-permute-start.9 = (bf16[8,8,72,128]{3,2,1,0:T(8,128)(2,1)S(1)}, bf16[8,8,72,128]{3,2,1,0:T(8,128)(2,1)S(1)}, u32[]{:S(2)}, u32[]{:S(2)}) collective-permute-start(bf16[8,8,72,128]{3,2,1,0:T(8,128)(2,1)S(1)} %get-tuple-element.80), channel_id=1, source_target_pairs={{0,1},{1,0},{2,3},{3,2},{4,5},{5,4},{6,7},{7,6},{8,9},{9,8},{10,11... | collective-permute-start | bytes 3538952 | tf_op jit(solution)/shard_map/ppermute | solution.py:544
  104.8 4.0 %collective-permute-start.10 = (f32[128,128]{1,0:T(8,128)S(1)}, f32[128,128]{1,0:T(8,128)S(1)}, u32[]{:S(2)}, u32[]{:S(2)}) collective-permute-start(f32[128,128]{1,0:T(8,128)S(1)} %dynamic-slice_bitcast_fusion.2), channel_id=1, source_target_pairs={{0,4},{4,0},{8,12},{12,8},{1,5},{5,1},{9,13},{13,9},{2,6},{6,2},{1... | collective-permute-start | bytes 196616 | tf_op jit(solution)/shard_map/ppermute | solution.py:544
  159.5 7.6 %collective-permute-start.11 = (bf16[8,8,72,128]{3,2,1,0:T(8,128)(2,1)S(1)}, bf16[8,8,72,128]{3,2,1,0:T(8,128)(2,1)S(1)}, u32[]{:S(2)}, u32[]{:S(2)}) collective-permute-start(bf16[8,8,72,128]{3,2,1,0:T(8,128)(2,1)S(1)} %bitcast.31), channel_id=1, source_target_pairs={{0,1},{1,0},{2,3},{3,2},{4,5},{5,4},{6,7},{7,6},{8,9},{9,8},{10,11... | collective-permute-start | bytes 3538952 | tf_op jit(solution)/shard_map/ppermute | solution.py:662

commit v6 on v5

--- a/solution.py
+++ b/solution.py
@@ -134,7 +134,7 @@
         sim_ref[1] = hit
         stats = jnp.concatenate([highest, total, positive, jnp.zeros((5, queries), F32)], axis=0)
         stats = jnp.concatenate([stats, jnp.zeros((8, width - queries), F32)], axis=1)
-        stats_ref[...] = jnp.broadcast_to(stats[None], stats_ref.shape)
+        stats_ref[...] = stats
 
 
 def forward_tile(flip, near, far, passage_pack, ids, query_len, group=8):
@@ -161,7 +161,7 @@
             pl.BlockSpec(memory_space=pltpu.VMEM),
             whole((count, rows)),
             whole((2, count, queries)),
-            whole((parts, 8, width)),
+            whole((8, width)),
         ],
         out_shape=[
             pltpu.VMEM((count, rows, slots), BF16),
@@ -169,7 +169,7 @@
             pltpu.VMEM((rows, width), BF16),
             jax.ShapeDtypeStruct((count, rows), F32),
             jax.ShapeDtypeStruct((2, count, queries), F32),
-            jax.ShapeDtypeStruct((parts, 8, width), F32),
+            jax.ShapeDtypeStruct((8, width), F32),
         ],
         scratch_shapes=[pltpu.VMEM((rows, width), F32), pltpu.VMEM((count, width), F32)],
         compiler_params=pltpu.CompilerParams(vmem_limit_bytes=16 * MIB),
@@ -192,12 +192,14 @@
     query_len,
     parts,
     core_ref,
+    flip_ref,
     own_ref,
     exp_ref,
     mix_ref,
     inv_ref,
     sim_ref,
-    stats_ref,
+    near_ref,
+    far_ref,
     pg_ref,
     kept_ref,
     given_ref,
@@ -209,12 +211,18 @@
     queries = rows // query_len
     for k in range(parts):
         qt[:, k * q_rows : (k + 1) * q_rows] = own_ref[k * q_rows : (k + 1) * q_rows, :].T
-    highest_of = stats_ref[:, 0, :queries]
+    stats = []
+    for k in range(parts):
+        at = stored(k) ^ flip_ref[0]
+        spot = at % (parts // 2)
+        stats.append(jnp.where(at < parts // 2, near_ref[spot], far_ref[spot]))
+    stats = jnp.stack(stats)
+    highest_of = stats[:, 0, :queries]
     highest = jnp.max(highest_of, axis=0, keepdims=True)
     total = jnp.sum(
-        stats_ref[:, 1, :queries] * jnp.exp(highest_of - highest), axis=0, keepdims=True
-    )
-    positive = jnp.sum(stats_ref[:, 2, :queries], axis=0, keepdims=True)
+        stats[:, 1, :queries] * jnp.exp(highest_of - highest), axis=0, keepdims=True
+    )
+    positive = jnp.sum(stats[:, 2, :queries], axis=0, keepdims=True)
     log_total = highest + jnp.log(total)
     coefficient = jnp.exp(sim_ref[0] - log_total) - sim_ref[1]
     scale = inv_ref[...] * dot(
@@ -241,15 +249,15 @@
     given_ref[...] = halves[1 - core_ref[0]]
 
 
-def backward_tile(core, parts, own, spread, mixed, inverse, similar, stats, query_len):
+def backward_tile(core, flip, parts, own, spread, mixed, inverse, similar, near, far, query_len):
     count, rows, slots = spread.shape
     q_rows, width = rows // parts, own.shape[1]
     work = rows * slots * count
     return pl.pallas_call(
         functools.partial(backward_kernel, query_len, parts),
         name="backward_tile",
-        in_specs=[pl.BlockSpec(memory_space=pltpu.SMEM)]
-        + [pl.BlockSpec(memory_space=pltpu.VMEM)] * 6,
+        in_specs=[pl.BlockSpec(memory_space=pltpu.SMEM)] * 2
+        + [pl.BlockSpec(memory_space=pltpu.VMEM)] * 7,
         out_shape=[
             pltpu.HBM((count, slots + EXTRA, width), BF16),
             jax.ShapeDtypeStruct((2, parts // 4, q_rows, width), BF16),
@@ -265,7 +273,7 @@
         cost_estimate=pl.CostEstimate(
             flops=2 * work * width, transcendentals=0, bytes_accessed=3 * work
         ),
-    )(core, own, spread, mixed, inverse, similar, stats)
+    )(core, flip, own, spread, mixed, inverse, similar, near, far)
 
 
 def early_kernel(resid_ref, context_ref, proj_ref, normed_ref, inv_ref, context_t_ref):
@@ -309,8 +317,7 @@
 
 def late_kernel(
     core_ref,
-    own_ref,
-    taken_ref,
+    parts_ref,
     normed_far,
     inv_far,
     gain_ref,
@@ -334,9 +341,11 @@
     ]
     for load in loads:
         load.start()
-    slots = own_ref.shape[0] - EXTRA
+    slots = parts_ref.shape[1] - EXTRA
     width = normed_ref.shape[1]
-    total = own_ref[...] + taken_ref[...].astype(F32)
+    total = parts_ref[0].astype(F32)
+    for k in range(1, parts_ref.shape[0]):
+        total = total + parts_ref[k].astype(F32)
     loss_ref[...] = jnp.broadcast_to(
         jnp.sum(total[slots:], axis=0, keepdims=True), loss_ref.shape
     )
@@ -381,34 +390,11 @@
     given_ref[...] = sums_ref[1 - core_ref[0]]
 
 
-def fold_kernel(parts_ref, kept_ref, given_ref):
-    slots = parts_ref.shape[2] - EXTRA
-    for side, out_ref in enumerate((kept_ref, given_ref)):
-        total = parts_ref[0, side].astype(F32)
-        for k in range(1, parts_ref.shape[0]):
-            total += parts_ref[k, side].astype(F32)
-        if side == 0:
-            out_ref[...] = total
-        else:
-            out_ref[:slots, :] = total[:slots].astype(BF16)
-            loss = jnp.sum(total[slots:], axis=0, keepdims=True)
-            out_ref[slots:, :] = split_lines(jnp.broadcast_to(loss, (EXTRA, loss.shape[1])))
-
-
-def folded(parts):
-    shape = parts.shape[2:]
-    return pl.pallas_call(
-        fold_kernel,
-        name="folded",
-        out_shape=[jax.ShapeDtypeStruct(shape, F32), jax.ShapeDtypeStruct(shape, BF16)],
-    )(parts)
-
-
 def far(array):
     return pltpu.with_memory_space_constraint(array, pltpu.HBM)
 
 
-def late_rows(core, blocks, own, taken, normed, inv_std, gain, colbert_proj, context_t):
+def late_rows(core, blocks, pieces, normed, inv_std, gain, colbert_proj, context_t):
     rows, width = normed.shape
     emb = colbert_proj.shape[1]
     shape = (blocks, width // 128, (width + emb) // (2 * blocks), 128)
@@ -417,8 +403,7 @@
         name="late_rows",
         in_specs=[
             pl.BlockSpec(memory_space=pltpu.SMEM),
-            whole(own.shape),
-            whole(taken.shape),
+            whole(pieces.shape),
             pl.BlockSpec(memory_space=pltpu.HBM),
             pl.BlockSpec(memory_space=pltpu.HBM),
             whole(gain.shape),
@@ -444,7 +429,7 @@
             transcendentals=0,
             bytes_accessed=14 * rows * width,
         ),
-    )(core, own, taken, far(normed), far(inv_std), gain, colbert_proj, far(context_t))
+    )(core, pieces, far(normed), far(inv_std), gain, colbert_proj, far(context_t))
 
 
 def exchange(pieces, axis):
@@ -452,24 +437,28 @@
 
 
 def own_kernel(core_ref, half_ref, proj_ref):
-    thick = proj_ref.shape[0] // half_ref.shape[0]
-    for k in range(half_ref.shape[0]):
-        proj_ref[k * thick : (k + 1) * thick, :] = half_ref[k, 0, :thick, :].astype(F32)
-
-
-def own_rows(core, half, width):
+    blocks, columns, _, block = half_ref.shape
+    thick = proj_ref.shape[0] // blocks
+    for k in range(blocks):
+        for j in range(columns):
+            proj_ref[k * thick : (k + 1) * thick, j * block : (j + 1) * block] = half_ref[
+                k, j, :thick, :
+            ].astype(F32)
+
+
+def own_rows(core, half, width, group=4):
     blocks, columns, lines, block = half.shape
     return pl.pallas_call(
         own_kernel,
         name="own_rows",
         grid_spec=pltpu.PrefetchScalarGridSpec(
             num_scalar_prefetch=1,
-            grid=(columns,),
-            in_specs=[pl.BlockSpec((blocks, 1, lines, block), lambda k, core: (0, k, 0, 0))],
-            out_specs=pl.BlockSpec((width // 2, block), lambda k, core: (core[0], k)),
+            grid=(columns // group,),
+            in_specs=[pl.BlockSpec((blocks, group, lines, block), lambda k, core: (0, k, 0, 0))],
+            out_specs=pl.BlockSpec((width // 2, group * block), lambda k, core: (core[0], k)),
         ),
         out_shape=pltpu.HBM((width, width), F32),
-        compiler_params=pltpu.CompilerParams(vmem_limit_bytes=8 * MIB),
+        compiler_params=pltpu.CompilerParams(vmem_limit_bytes=12 * MIB),
         cost_estimate=pl.CostEstimate(
             flops=width * width, transcendentals=0, bytes_accessed=4 * width * width
         ),
@@ -479,47 +468,50 @@
 def finish_kernel(
     core_ref, half_ref, other_ref, colbert_ref, gain_ref, _, proj_ref, grad_ref, gain_grad_ref
 ):
-    blocks = half_ref.shape[0]
+    blocks, columns, _, block = half_ref.shape
     thick = proj_ref.shape[0] // blocks
     even = core_ref[0] == 0
-    own, others = [], []
-    for k in range(blocks):
-        piece = other_ref[k, 0].astype(F32)
-        proj_ref[k * thick : (k + 1) * thick, :] = piece[:thick]
-        others.append(piece[thick:])
-        own.append(half_ref[k, 0].astype(F32)[thick:])
-    own, others = jnp.concatenate(own, axis=0), jnp.concatenate(others, axis=0)
-    colbert_grad = jnp.concatenate(
-        [jnp.where(even, own, others), jnp.where(even, others, own)], axis=0
-    )
-    colbert_t = colbert_ref[...].astype(F32).T
-    gain_grad_ref[...] = (
-        jnp.sum(colbert_grad * colbert_t, axis=0, keepdims=True) / gain_ref[...]
-    )
-    grad_ref[...] = colbert_grad.T
-
-
-def finish(core, half, other, colbert_proj, gain, proj):
+    for j in range(columns):
+        at = slice(j * block, (j + 1) * block)
+        own, others = [], []
+        for k in range(blocks):
+            piece = other_ref[k, j].astype(F32)
+            proj_ref[k * thick : (k + 1) * thick, at] = piece[:thick]
+            others.append(piece[thick:])
+            own.append(half_ref[k, j].astype(F32)[thick:])
+        own, others = jnp.concatenate(own, axis=0), jnp.concatenate(others, axis=0)
+        colbert_grad = jnp.concatenate(
+            [jnp.where(even, own, others), jnp.where(even, others, own)], axis=0
+        )
+        colbert_t = colbert_ref[at, :].astype(F32).T
+        gain_grad_ref[:, at] = (
+            jnp.sum(colbert_grad * colbert_t, axis=0, keepdims=True) / gain_ref[:, at]
+        )
+        grad_ref[at, :] = colbert_grad.T
+
+
+def finish(core, half, other, colbert_proj, gain, proj, group=4):
     blocks, columns, lines, block = half.shape
     width, emb = colbert_proj.shape
-    piece = pl.BlockSpec((blocks, 1, lines, block), lambda k, core: (0, k, 0, 0))
+    piece = pl.BlockSpec((blocks, group, lines, block), lambda k, core: (0, k, 0, 0))
+    span = group * block
     return pl.pallas_call(
         finish_kernel,
         name="finish",
         grid_spec=pltpu.PrefetchScalarGridSpec(
             num_scalar_prefetch=1,
-            grid=(columns,),
+            grid=(columns // group,),
             in_specs=[
                 piece,
                 piece,
-                pl.BlockSpec((block, emb), lambda k, core: (k, 0)),
-                pl.BlockSpec((1, block), lambda k, core: (0, k)),
+                pl.BlockSpec((span, emb), lambda k, core: (k, 0)),
+                pl.BlockSpec((1, span), lambda k, core: (0, k)),
                 pl.BlockSpec(memory_space=pl.ANY),
             ],
             out_specs=[
-                pl.BlockSpec((width // 2, block), lambda k, core: (1 - core[0], k)),
-                pl.BlockSpec((block, emb), lambda k, core: (k, 0)),
-                pl.BlockSpec((1, block), lambda k, core: (0, k)),
+                pl.BlockSpec((width // 2, span), lambda k, core: (1 - core[0], k)),
+                pl.BlockSpec((span, emb), lambda k, core: (k, 0)),
+                pl.BlockSpec((1, span), lambda k, core: (0, k)),
             ],
         ),
         out_shape=[
@@ -528,7 +520,7 @@
             jax.ShapeDtypeStruct((1, width), F32),
         ],
         input_output_aliases={5: 0},
-        compiler_params=pltpu.CompilerParams(vmem_limit_bytes=8 * MIB),
+        compiler_params=pltpu.CompilerParams(vmem_limit_bytes=12 * MIB),
         cost_estimate=pl.CostEstimate(
             flops=2 * width * width, transcendentals=0, bytes_accessed=4 * width * width
         ),
@@ -552,28 +544,35 @@
     return pair_summed(kept, given, axis, pairs, out_type)
 
 
-def query_gathered(own):
-    held = own[None]
-    for axis, pairs in ((CORE, SWAP), ("neg_0", NEAR), ("neg_0", FAR)):
-        held = jnp.concatenate([held, lax.ppermute(held, axis, pairs)])
+def doubled(held, axis, pairs):
+    return jnp.concatenate([held, lax.ppermute(held, axis, pairs)])
+
+
+def fours_gathered(four):
+    held = doubled(four, "neg_0", FAR)
     return held, lax.ppermute(held, "neg_1", SWAP)
 
 
-def pack_kernel(own_ref, taken_ref, out_ref):
+def pack_kernel(length_ref, p_ref, out_ref):
+    slots = p_ref.shape[1]
+    extra = jnp.full((EXTRA, p_ref.shape[2]), (length_ref[0] - LEAST).astype(F32)).astype(BF16)
     for k in range(out_ref.shape[0]):
-        out_ref[k, 0] = own_ref[...]
-        out_ref[k, 1] = taken_ref[...]
-
-
-def passage_copies(own, taken, copies):
-    shape = (copies, 2, *own.shape)
+        out_ref[k, :slots, :] = p_ref[0]
+        out_ref[k, slots:, :] = extra
+
+
+def passage_copies(passage_emb, lengths, copies):
+    _, slots, width = passage_emb.shape
     return pl.pallas_call(
         pack_kernel,
         name="passage_copies",
-        compiler_params=pltpu.CompilerParams(vmem_limit_bytes=8 * MIB),
-        out_specs=whole(shape),
-        out_shape=pltpu.HBM(shape, BF16),
-    )(own, taken)
+        in_specs=[
+            pl.BlockSpec(memory_space=pltpu.SMEM),
+            pl.BlockSpec(memory_space=pltpu.VMEM),
+        ],
+        out_specs=whole((copies, slots + EXTRA, width)),
+        out_shape=pltpu.HBM((copies, slots + EXTRA, width), BF16),
+    )(lengths, passage_emb)
 
 
 def spread_kernel(parts_ref, out_ref):
@@ -609,19 +608,13 @@
             jnp.broadcast_to(wanted.astype(BF16)[None], (EXTRA, emb)),
         ]
     )
-    passage_own = jnp.concatenate(
-        [
-            passage_emb.reshape(-1, emb),
-            jnp.broadcast_to((lengths - LEAST).astype(BF16)[:, None], (EXTRA, emb)),
-        ]
-    )
-    passage_pair = passage_copies(
-        passage_own, lax.ppermute(passage_own, "dp_1", SWAP), lax.axis_size("dp_0")
-    )
-    passage_pack = exchange(passage_pair, "dp_0").reshape(dp_size, *passage_own.shape)
-    queries = query_gathered(query_own)
-    group = jnp.arange(dp_size) ^ lax.axis_index("dp_1")
-    ids = jnp.broadcast_to((group * neg_size + place).astype(F32)[:, None], (dp_size, emb))
+    query_four = doubled(doubled(query_own[None], CORE, SWAP), "neg_0", NEAR)
+    copies, query_four = lax.optimization_barrier(
+        (passage_copies(passage_emb, lengths, dp_size), query_four)
+    )
+    passage_pack = exchange(copies, DP)
+    queries = fours_gathered(query_four)
+    ids = jnp.broadcast_to((jnp.arange(dp_size) * neg_size + place).astype(F32)[:, None], (dp_size, emb))
     row, column = lax.axis_index("neg_1"), lax.axis_index("neg_0")
     flip = (row * 8 + column * 2 + core)[None]
     sides = [
@@ -633,32 +626,39 @@
     spread, mixed, query_rows, inverse, similar, stats = forward_tile(
         flip, *queries, passage_pack, ids, query_len
     )
-    stats = exchange(stats, NEG)
+    stats = fours_gathered(doubled(doubled(stats[None], CORE, SWAP), "neg_0", NEAR))
     passage_parts, kept, given = backward_tile(
-        core[None], neg_size, query_rows, spread, mixed, inverse, similar, stats, query_len
+        core[None],
+        flip,
+        neg_size,
+        query_rows,
+        spread,
+        mixed,
+        inverse,
+        similar,
+        *stats,
+        query_len,
     )
     residual, kept, given = lax.optimization_barrier((residual, kept, given))
     early = early_rows(residual, context, out_proj)
     query_part = pair_summed(kept, given, CORE, SWAP, BF16)
     query_part = halves_summed(query_part, "neg_1", SWAP, row_side, F32)
-    passage_parts = exchange(passage_parts.reshape(passage_pair.shape), "dp_0")
+    passage_parts = exchange(passage_parts, DP)
     passage_parts, query_part, early = lax.optimization_barrier((passage_parts, query_part, early))
     normed, inv_std, context_t = early
-    own_part, given_part = folded(passage_parts)
-    taken_part = lax.ppermute(given_part, "dp_1", SWAP)
+    residual_grad, kept, given, loss_sum = late_rows(
+        core[None], dp_size, passage_parts, normed, inv_std, norm_gain[None], colbert_proj, context_t
+    )
+    half = pair_summed(kept, given, CORE, SWAP, BF16)
+    context_grad = jnp.dot(residual_grad, out_proj.T, preferred_element_type=F32).astype(BF16)
     query_part = query_part.reshape(2, 2, *query_part.shape[1:])
     query_part = halves_summed(query_part, "neg_0", FAR, far_side, F32)
-    taken_part, query_part = lax.optimization_barrier((taken_part, query_part))
-    residual_grad, kept, given, loss_sum = late_rows(
-        core[None], dp_size, own_part, taken_part, normed, inv_std, norm_gain[None], colbert_proj, context_t
-    )
-    half = pair_summed(kept, given, CORE, SWAP, BF16)
-    context_grad = jnp.dot(residual_grad, out_proj.T, preferred_element_type=F32).astype(BF16)
-    query_grad = halves_summed(query_part, "neg_0", NEAR, near_side, F32)
-    half, context_grad, query_grad = lax.optimization_barrier((half, context_grad, query_grad))
-    query_grad = query_grad.reshape(query_dev, query_len, emb)
+    half, context_grad, query_part = lax.optimization_barrier((half, context_grad, query_part))
     slabs = exchange(half.reshape(dp_size * cross_size, *half.shape[2:]), DP + CROSS)
     half = exchange(summed_copies(slabs), DP + CROSS).reshape(half.shape)
+    half, query_part = lax.optimization_barrier((half, query_part))
+    query_grad = halves_summed(query_part, "neg_0", NEAR, near_side, F32)
+    query_grad = query_grad.reshape(query_dev, query_len, emb)
     other = lax.ppermute(half, CORE, SWAP)
     proj = own_rows(core[None], half, out_proj.shape[0])
     out_proj_grad, colbert_grad, gain_grad = finish(

time: 172 us -> 172 us (level)
  blocking collectives: 66.3 us -> 51.1 us
  waiting for transfers between devices: 21.7 us -> 34.5 us
  starting transfers between devices: 29.4 us -> 36.4 us
  Pallas kernels: 40.2 us -> 36.1 us
  local copies, waits for them, and re-layouts: 3.73 us -> 1.89 us
    all_to_all x3 -> x2, blocking collectives: 66.3 us -> 51.1 us  [exchange(): return lax.all_to_all(pieces, axis, 0, 0, tiled=True)]
    ppermute x6 -> x8, waiting for transfers between devices: 11.4 us -> 24.4 us  [the longest x2 16 us: fours_gathered(): return (held, lax.ppermute(held, 'neg_1', SWAP))]
    all_to_all x2, waiting for transfers between devices: 7.75 us -> 0.01 us  [exchange(): return lax.all_to_all(pieces, axis, 0, 0, tiled=True)]
    ppermute x5, waiting for transfers between devices: 2.5 us -> 10.1 us  [pair_summed(): taken = lax.ppermute(given, axis, pairs)]
    ppermute x5, starting transfers between devices: 4.92 us -> 9.51 us  [pair_summed(): taken = lax.ppermute(given, axis, pairs)]
    ppermute x6 -> x8, starting transfers between devices: 10.8 us -> 12.9 us  [the longest x6 9.83 us: doubled(): return jnp.concatenate([held, lax.ppermute(held, axis, pairs)])]
  transfers between devices with their start and end apart: 14 -> 16, of which waited for: 8 -> 10; matrix products, arithmetic and copies ran while one was open for 4% -> 4% of each run, Pallas kernels for 6% -> 4%
where the time goes in v6:
time: 172 us; the launch traced here: 171 us
  blocking collectives  51.1 us (30%)
  starting transfers between devices  36.4 us (21%)
  Pallas kernels  36.1 us (21%)
  waiting for transfers between devices  34.5 us (20%)
  other arithmetic  4.35 us (3%)
  matrix products  3.49 us (2%)
  between operations  3.2 us (2%)
  local copies, waits for them, and re-layouts  1.89 us (1%)
    all_to_all x2, blocking collectives, exchange(): return lax.all_to_all(pieces, axis, 0, 0, tiled=True)  51.1 us
    ppermute x2, waiting for transfers between devices, fours_gathered(): return (held, lax.ppermute(held, 'neg_1', SWAP))  16 us
    pallas_call x1, Pallas kernels, forward_tile(): pl.pallas_call(functools.partial(forward_kernel, query_len, group), name=...  14.1 us
    all_to_all x2, starting transfers between devices, exchange(): return lax.all_to_all(pieces, axis, 0, 0, tiled=True)  10.7 us
    ppermute x5, waiting for transfers between devices, pair_summed(): taken = lax.ppermute(given, axis, pairs)  10.1 us
    ppermute x6, starting transfers between devices, doubled(): return jnp.concatenate([held, lax.ppermute(held, axis, pairs)])  9.83 us
    ppermute x5, starting transfers between devices, pair_summed(): taken = lax.ppermute(given, axis, pairs)  9.51 us
    ppermute x6, waiting for transfers between devices, doubled(): return jnp.concatenate([held, lax.ppermute(held, axis, pairs)])  8.38 us
  transfers between devices with their start and end apart: 16, of which 10 were waited for; matrix products, arithmetic and copies ran while one was open for 4% of the time, Pallas kernels for 4%

profile of v6, /device:TPU:1, one launch (start us, length us, event | category | flops | bytes accessed | tf_op | source)
XLA Modules:
  0.0 171.1 jit_solution(16263311615247397518)
XLA Ops:
  0.7 0.7 select_reduce_fusion
  1.4 0.8 maximum_bitcast_fusion
  2.2 1.4 collective-permute-start
  3.6 0.9 collective-permute-done
  4.5 1.4 collective-permute-start.1
  6.5 2.0 %passage_copies.1 = bf16[8,520,128]{2,1,0:T(8,128)(2,1)} custom-call(s32[1]{0:T(128)S(6)} %copy.19.length_ref, bf16[1,512,128]{2,1,0:T(8,128)(2,1)} %p_ref.1), custom_call_target="tpu_custom_call" | custom-call | tf_op jit(solution)/shard_map/passage_copies/pallas_call | solution.py:566
  8.5 0.0 collective-permute-done.1
  8.5 6.1 %all-to-all-start = ((bf16[8,520,128]{2,1,0:T(8,128)(2,1)}), bf16[8,520,128]{2,1,0:T(8,128)(2,1)S(1)}, u32[]{:S(2)}, u32[]{:S(2)}) async-start(bf16[8,520,128]{2,1,0:T(8,128)(2,1)} %passage_copies.1), calls=%async_computation | async-start | bytes 2129920 | tf_op jit(solution)/shard_map/all_to_all | solution.py:436
  14.6 2.5 %collective-permute-start.2 = (bf16[4,136,128]{2,1,0:T(8,128)(2,1)S(1)}, bf16[4,136,128]{2,1,0:T(8,128)(2,1)S(1)}, u32[]{:S(2)}, u32[]{:S(2)}) collective-permute-start(bf16[4,136,128]{2,1,0:T(8,128)(2,1)S(1)} %pad_maximum_fusion), channel_id=1, source_target_pairs={{0,8},{4,12},{8,0},{12,4},{1,9},{5,13},{9,1},{13,5},{2,10},{6,14},... | collective-permute-start | bytes 417800 | tf_op jit(solution)/shard_map/ppermute | solution.py:548
  17.1 2.9 %collective-permute-done.2 = bf16[4,136,128]{2,1,0:T(8,128)(2,1)S(1)} collective-permute-done((bf16[4,136,128]{2,1,0:T(8,128)(2,1)S(1)}, bf16[4,136,128]{2,1,0:T(8,128)(2,1)S(1)}, u32[]{:S(2)}, u32[]{:S(2)}) %collective-permute-start.2) | collective-permute-done | bytes 139296 | tf_op jit(solution)/shard_map/ppermute | solution.py:548
  20.0 2.7 %collective-permute-start.3 = (bf16[8,136,128]{2,1,0:T(8,128)(2,1)S(1)}, bf16[8,136,128]{2,1,0:T(8,128)(2,1)S(1)}, u32[]{:S(2)}, u32[]{:S(2)}) collective-permute-start(bf16[8,136,128]{2,1,0:T(8,128)(2,1)S(1)} %constant_dynamic-update-slice_fusion.near_ref), channel_id=1, source_target_pairs={{0,2},{2,0},{1,3},{3,1},{4,6},{6,4},{5,7},{7,5},{8,10},{10,8},{9,1... | collective-permute-start | bytes 835592 | tf_op jit(solution)/shard_map/ppermute | solution.py:553
  22.7 12.1 %collective-permute-done.3.far_ref = bf16[8,136,128]{2,1,0:T(8,128)(2,1)S(1)} collective-permute-done((bf16[8,136,128]{2,1,0:T(8,128)(2,1)S(1)}, bf16[8,136,128]{2,1,0:T(8,128)(2,1)S(1)}, u32[]{:S(2)}, u32[]{:S(2)}) %collective-permute-start.3) | collective-permute-done | bytes 278560 | tf_op jit(solution)/shard_map/ppermute | solution.py:553
  34.8 0.0 all-to-all-done.p_ref
  34.8 0.1 broadcast_in_dim.52.ids_ref
  34.9 14.1 %forward_tile.1 = (bf16[8,2048,512]{2,1,0:T(8,128)(2,1)S(1)}, f32[8,2048,128]{2,1,0:T(8,128)S(1)}, bf16[2048,128]{1,0:T(8,128)(2,1)S(1)}, f32[8,2048]{1,0:T(8,12...) custom-call(s32[1]{0:T(128)} %bitcast.1.flip_ref, ...), custom_call_target="tpu_custom_call" | custom-call | flops 4294967296 | bytes 33554432 | tf_op jit(solution)/shard_map/forward_tile/pallas_call | solution.py:147
  49.0 1.7 %collective-permute-start.4 = (f32[1,8,128]{2,1,0:T(8,128)S(1)}, f32[1,8,128]{2,1,0:T(8,128)S(1)}, u32[]{:S(2)}, u32[]{:S(2)}) collective-permute-start(f32[1,8,128]{2,1,0:T(8,128)S(1)} %bitcast.31), channel_id=1, source_target_pairs={{0,1},{1,0},{2,3},{3,2},{4,5},{5,4},{6,7},{7,6},{8,9},{9,8},{10,11... | collective-permute-start | bytes 12296 | tf_op jit(solution)/shard_map/ppermute | solution.py:548
  50.7 0.8 collective-permute-done.4
  51.6 0.4 collective-permute-start.5
  52.0 2.1 %collective-permute-done.5 = f32[2,8,128]{2,1,0:T(8,128)S(1)} collective-permute-done((f32[2,8,128]{2,1,0:T(8,128)S(1)}, f32[2,8,128]{2,1,0:T(8,128)S(1)}, u32[]{:S(2)}, u32[]{:S(2)}) %collective-permute-start.5) | collective-permute-done | bytes 8224 | tf_op jit(solution)/shard_map/ppermute | solution.py:548
  54.1 2.4 %collective-permute-start.6 = (f32[4,8,128]{2,1,0:T(8,128)S(1)}, f32[4,8,128]{2,1,0:T(8,128)S(1)}, u32[]{:S(2)}, u32[]{:S(2)}) collective-permute-start(f32[4,8,128]{2,1,0:T(8,128)S(1)} %pad_maximum_fusion.3), channel_id=1, source_target_pairs={{0,8},{4,12},{8,0},{12,4},{1,9},{5,13},{9,1},{13,5},{2,10},{6,14},... | collective-permute-start | bytes 49160 | tf_op jit(solution)/shard_map/ppermute | solution.py:548
  56.5 1.7 collective-permute-done.6
  58.2 0.3 collective-permute-start.7
  58.5 3.9 %collective-permute-done.7.far_ref = f32[8,8,128]{2,1,0:T(8,128)S(1)} collective-permute-done((f32[8,8,128]{2,1,0:T(8,128)S(1)}, f32[8,8,128]{2,1,0:T(8,128)S(1)}, u32[]{:S(2)}, u32[]{:S(2)}) %collective-permute-start.7) | collective-permute-done | bytes 32800 | tf_op jit(solution)/shard_map/ppermute | solution.py:553
  62.4 6.2 %backward_tile.1 = (bf16[8,520,128]{2,1,0:T(8,128)(2,1)}, bf16[2,4,128,128]{3,2,1,0:T(8,128)(2,1)S(1)}, bf16[2,4,128,128]{3,2,1,0:T(8,128)(2,1)}) custom-call(s32[1]{0:T(128)} %bitcast.core_ref, s32[1]{0:T(128)} %bitcast.1.flip_ref, bf16[2048,128]{1,0:T(8,128)(2,1)S(1)} %get-tuple-element.53.own_ref, bf16[8,2048,512]{2,1,0:T(8,128)(2,1)S(1)} %get-tuple-element.54.exp_ref, ...), custom_call_target="tpu_custom_call" | custom-call | flops 2147483648 | bytes 25165824 | tf_op jit(solution)/shard_map/backward_tile/pallas_call | solution.py:256
  68.6 3.8 %collective-permute-start.8 = (bf16[2,4,128,128]{3,2,1,0:T(8,128)(2,1)}, bf16[2,4,128,128]{3,2,1,0:T(8,128)(2,1)}, u32[]{:S(2)}, u32[]{:S(2)}) collective-permute-start(bf16[2,4,128,128]{3,2,1,0:T(8,128)(2,1)} %get-tuple-element.63), channel_id=1, source_target_pairs={{0,1},{1,0},{2,3},{3,2},{4,5},{5,4},{6,7},{7,6},{8,9},{9,8},{10,11... | collective-permute-start | bytes 786440 | tf_op jit(solution)/shard_map/ppermute | solution.py:536
  72.4 0.0 copy-start
  72.4 4.6 %all-to-all-start.1 = ((bf16[8,520,128]{2,1,0:T(8,128)(2,1)}), bf16[8,520,128]{2,1,0:T(8,128)(2,1)S(1)}, u32[]{:S(2)}, u32[]{:S(2)}) async-start(bf16[8,520,128]{2,1,0:T(8,128)(2,1)} %get-tuple-element.59), calls=%async_computation.1 | async-start | bytes 2129920 | tf_op jit(solution)/shard_map/all_to_all | solution.py:436
  77.0 0.0 copy-start.1
  77.0 0.0 collective-permute-done.8
  77.0 1.1 add_convert_fusion.1
  78.2 1.8 %collective-permute-start.9 = (bf16[4,128,128]{2,1,0:T(8,128)(2,1)S(1)}, bf16[4,128,128]{2,1,0:T(8,128)(2,1)S(1)}, u32[]{:S(2)}, u32[]{:S(2)}) collective-permute-start(bf16[4,128,128]{2,1,0:T(8,128)(2,1)S(1)} %dynamic-slice_bitcast_fusion.1), channel_id=1, source_target_pairs={{0,2},{2,0},{1,3},{3,1},{4,6},{6,4},{5,7},{7,5},{8,10},{10,8},{9,1... | collective-permute-start | bytes 393224 | tf_op jit(solution)/shard_map/ppermute | solution.py:536
  80.0 0.0 copy-done
  80.0 0.0 copy-done.1
  80.0 0.0 copy-start.2
  80.0 1.2 copy-done.2
  81.2 0.0 copy-start.3
  81.2 0.0 copy-start.4
  81.2 3.9 %early_rows.1 = (f32[512,1024]{1,0:T(8,128)}, f32[512,128]{1,0:T(8,128)}, bf16[1024,512]{1,0:T(8,128)(2,1)}) custom-call(bf16[512,1024]{1,0:T(8,128)(2,1)S(1)} %copy-done.1, bf16[512,1024]{1,0:T(8,128)(2,1)S(1)} %copy-done.2, bf16[1024,1024]{1,0:T(8,128)(2,1)S(1)} %copy-done), custom_call_target="tpu_custom_call" | custom-call | flops 1073741824 | bytes 5242880 | tf_op jit(solution)/shard_map/early_rows/pallas_call | solution.py:292
  85.1 8.9 %collective-permute-done.9 = bf16[4,128,128]{2,1,0:T(8,128)(2,1)S(1)} collective-permute-done((bf16[4,128,128]{2,1,0:T(8,128)(2,1)S(1)}, bf16[4,128,128]{2,1,0:T(8,128)(2,1)S(1)}, u32[]{:S(2)}, u32[]{:S(2)}) %collective-permute-start.9) | collective-permute-done | bytes 131104 | tf_op jit(solution)/shard_map/ppermute | solution.py:536
  94.0 0.7 convert_add_fusion
  94.7 0.0 all-to-all-done.1.parts_ref
  94.7 0.0 copy-done.3
  94.7 0.0 copy-done.4
  94.8 0.0 copy-start.5
  94.8 4.1 %late_rows.1 = (bf16[512,1024]{1,0:T(8,128)(2,1)}, bf16[8,8,72,128]{3,2,1,0:T(8,128)(2,1)S(1)}, bf16[8,8,72,128]{3,2,1,0:T(8,128)(2,1)S(1)}, f32[8,128]{1,0:T(8,128)S(1)}) custom-call(s32[1]{0:T(128)} %bitcast.core_ref, bf16[8,520,128]{2,1,0:T(8,128)(2,1)S(1)} %all-to-all-done.1.parts_ref, f32[512,1024]{1,0:T(8,128)} %get-tuple-element.71.normed_far, ...), custom_call_target="tpu_custom_call" | custom-call | flops 1342177280 | bytes 7340032 | tf_op jit(solution)/shard_map/late_rows/pallas_call | solution.py:401
  98.9 0.9 collective-permute-start.10
  99.8 0.0 copy-done.5
  99.8 2.5 %collective-permute-start.11 = (f32[2,128,128]{2,1,0:T(8,128)S(1)}, f32[2,128,128]{2,1,0:T(8,128)S(1)}, u32[]{:S(2)}, u32[]{:S(2)}) collective-permute-start(f32[2,128,128]{2,1,0:T(8,128)S(1)} %dynamic-slice_bitcast_fusion), channel_id=1, source_target_pairs={{0,8},{4,12},{8,0},{12,4},{1,9},{5,13},{9,1},{13,5},{2,10},{6,14},... | collective-permute-start | bytes 393224 | tf_op jit(solution)/shard_map/ppermute | solution.py:536
  102.3 3.5 %convolution_convert_fusion = bf16[512,1024]{1,0:T(8,128)(2,1)} fusion(bf16[512,1024]{1,0:T(8,128)(2,1)} %get-tuple-element.44, bf16[1024,1024]{1,0:T(8,128)(2,1)S(1)} %copy-done), kind=kOutput, calls=%fused_computation.1 | convolution fusion | flops 1074266112 | bytes 4194304 | tf_op jit(solution)/shard_map/dot_general | solution.py:653
  105.8 0.7 collective-permute-done.11
  106.5 0.0 collective-permute-done.10
  106.5 0.3 add_convert_fusion
  106.8 28.6 %all_to_all.20.parts_ref = bf16[64,72,128]{2,1,0:T(8,128)(2,1)} all-to-all(bf16[64,72,128]{2,1,0:T(8,128)(2,1)S(1)} %bitcast.37), channel_id=1, replica_groups=mesh['dp_0'=4,'dp_1'=2,'neg_0'=4,'neg_1'=2,'neg_2'=2] {'dp_0','dp_1','ne..., dimensions={0} | all-to-all | bytes 2359296 | tf_op jit(solution)/shard_map/all_to_all | solution.py:436
  135.4 2.5 %summed_copies.1 = bf16[64,72,128]{2,1,0:T(8,128)(2,1)} custom-call(bf16[64,72,128]{2,1,0:T(8,128)(2,1)} %all_to_all.20.parts_ref), custom_call_target="tpu_custom_call" | custom-call | tf_op jit(solution)/shard_map/summed_copies/pallas_call | solution.py:586
  137.9 22.5 %all_to_all.21 = bf16[64,72,128]{2,1,0:T(8,128)(2,1)S(1)} all-to-all(bf16[64,72,128]{2,1,0:T(8,128)(2,1)} %summed_copies.1), channel_id=1, replica_groups=mesh['dp_0'=4,'dp_1'=2,'neg_0'=4,'neg_1'=2,'neg_2'=2] {'dp_0','dp_1','ne..., dimensions={0} | all-to-all | bytes 2359296 | tf_op jit(solution)/shard_map/all_to_all | solution.py:436
  160.5 3.3 %collective-permute-start.13 = (bf16[8,8,72,128]{3,2,1,0:T(8,128)(2,1)S(1)}, bf16[8,8,72,128]{3,2,1,0:T(8,128)(2,1)S(1)}, u32[]{:S(2)}, u32[]{:S(2)}) collective-permute-start(bf16[8,8,72,128]{3,2,1,0:T(8,128)(2,1)S(1)} %bitcast.28), channel_id=1, source_target_pairs={{0,1},{1,0},{2,3},{3,2},{4,5},{5,4},{6,7},{7,6},{8,9},{9,8},{10,11... | collective-permute-start | bytes 3538952 | tf_op jit(solution)/shard_map/ppermute | solution.py:662
  163.8 0.5 collective-permute-start.12
  164.3 0.5 slice.3
  165.5 1.5 own_rows.1._
  167.0 0.5 collective-permute-done.12
  167.5 0.6 bitcast_add_fusion.1
  168.1 0.0 collective-permute-done.13.other_ref
  168.1 1.9 %finish.1 = (f32[1024,1024]{1,0:T(8,128)}, f32[1024,128]{1,0:T(8,128)}, f32[1,1024]{1,0:T(1,128)}) custom-call(s32[1]{0:T(128)} %bitcast.core_ref, bf16[8,8,72,128]{3,2,1,0:T(8,128)(2,1)S(1)} %bitcast.30, bf16[8,8,72,128]{3,2,1,0:T(8,128)(2,1)S(1)} %collective-permute-done.13.other_ref, ...), custom_call_target="tpu_custom_call", output_to_operand_aliasing={{0}: (5, {})} | custom-call | flops 2097152 | bytes 4194304 | tf_op jit(solution)/shard_map/finish/pallas_call | solution.py:498
  (15 shorter events, 0.1 us)
Async XLA Ops:
  2.2 2.3 %collective-permute-start = (bf16[1,136,128]{2,1,0:T(8,128)(2,1)S(1)}, bf16[1,136,128]{2,1,0:T(8,128)(2,1)S(1)}, u32[]{:S(2)}, u32[]{:S(2)}) collective-permute-start(bf16[1,136,128]{2,1,0:T(8,128)(2,1)S(1)} %maximum_bitcast_fusion), channel_id=1, source_target_pairs={{0,1},{1,0},{2,3},{3,2},{4,5},{5,4},{6,7},{7,6},{8,9},{9,8},{10,11... | collective-permute-start | bytes 104456 | tf_op jit(solution)/shard_map/ppermute | solution.py:548
  4.5 4.0 %collective-permute-start.1 = (bf16[2,136,128]{2,1,0:T(8,128)(2,1)S(1)}, bf16[2,136,128]{2,1,0:T(8,128)(2,1)S(1)}, u32[]{:S(2)}, u32[]{:S(2)}) collective-permute-start(bf16[2,136,128]{2,1,0:T(8,128)(2,1)S(1)} %pad_maximum_fusion.1), channel_id=1, source_target_pairs={{0,4},{4,0},{8,12},{12,8},{1,5},{5,1},{9,13},{13,9},{2,6},{6,2},{1... | collective-permute-start | bytes 208904 | tf_op jit(solution)/shard_map/ppermute | solution.py:548
  8.5 26.3 %all-to-all-start = ((bf16[8,520,128]{2,1,0:T(8,128)(2,1)}), bf16[8,520,128]{2,1,0:T(8,128)(2,1)S(1)}, u32[]{:S(2)}, u32[]{:S(2)}) async-start(bf16[8,520,128]{2,1,0:T(8,128)(2,1)} %passage_copies.1), calls=%async_computation | async-start | bytes 2129920 | tf_op jit(solution)/shard_map/all_to_all | solution.py:436
  14.6 5.4 %collective-permute-start.2 = (bf16[4,136,128]{2,1,0:T(8,128)(2,1)S(1)}, bf16[4,136,128]{2,1,0:T(8,128)(2,1)S(1)}, u32[]{:S(2)}, u32[]{:S(2)}) collective-permute-start(bf16[4,136,128]{2,1,0:T(8,128)(2,1)S(1)} %pad_maximum_fusion), channel_id=1, source_target_pairs={{0,8},{4,12},{8,0},{12,4},{1,9},{5,13},{9,1},{13,5},{2,10},{6,14},... | collective-permute-start | bytes 417800 | tf_op jit(solution)/shard_map/ppermute | solution.py:548
  20.0 14.8 %collective-permute-start.3 = (bf16[8,136,128]{2,1,0:T(8,128)(2,1)S(1)}, bf16[8,136,128]{2,1,0:T(8,128)(2,1)S(1)}, u32[]{:S(2)}, u32[]{:S(2)}) collective-permute-start(bf16[8,136,128]{2,1,0:T(8,128)(2,1)S(1)} %constant_dynamic-update-slice_fusion.near_ref), channel_id=1, source_target_pairs={{0,2},{2,0},{1,3},{3,1},{4,6},{6,4},{5,7},{7,5},{8,10},{10,8},{9,1... | collective-permute-start | bytes 835592 | tf_op jit(solution)/shard_map/ppermute | solution.py:553
  49.0 2.6 %collective-permute-start.4 = (f32[1,8,128]{2,1,0:T(8,128)S(1)}, f32[1,8,128]{2,1,0:T(8,128)S(1)}, u32[]{:S(2)}, u32[]{:S(2)}) collective-permute-start(f32[1,8,128]{2,1,0:T(8,128)S(1)} %bitcast.31), channel_id=1, source_target_pairs={{0,1},{1,0},{2,3},{3,2},{4,5},{5,4},{6,7},{7,6},{8,9},{9,8},{10,11... | collective-permute-start | bytes 12296 | tf_op jit(solution)/shard_map/ppermute | solution.py:548
  51.6 2.5 %collective-permute-start.5 = (f32[2,8,128]{2,1,0:T(8,128)S(1)}, f32[2,8,128]{2,1,0:T(8,128)S(1)}, u32[]{:S(2)}, u32[]{:S(2)}) collective-permute-start(f32[2,8,128]{2,1,0:T(8,128)S(1)} %pad_maximum_fusion.4), channel_id=1, source_target_pairs={{0,4},{4,0},{8,12},{12,8},{1,5},{5,1},{9,13},{13,9},{2,6},{6,2},{1... | collective-permute-start | bytes 24584 | tf_op jit(solution)/shard_map/ppermute | solution.py:548
  54.1 4.1 %collective-permute-start.6 = (f32[4,8,128]{2,1,0:T(8,128)S(1)}, f32[4,8,128]{2,1,0:T(8,128)S(1)}, u32[]{:S(2)}, u32[]{:S(2)}) collective-permute-start(f32[4,8,128]{2,1,0:T(8,128)S(1)} %pad_maximum_fusion.3), channel_id=1, source_target_pairs={{0,8},{4,12},{8,0},{12,4},{1,9},{5,13},{9,1},{13,5},{2,10},{6,14},... | collective-permute-start | bytes 49160 | tf_op jit(solution)/shard_map/ppermute | solution.py:548
  58.2 4.3 %collective-permute-start.7 = (f32[8,8,128]{2,1,0:T(8,128)S(1)}, f32[8,8,128]{2,1,0:T(8,128)S(1)}, u32[]{:S(2)}, u32[]{:S(2)}) collective-permute-start(f32[8,8,128]{2,1,0:T(8,128)S(1)} %pad_maximum_fusion.2.near_ref), channel_id=1, source_target_pairs={{0,2},{2,0},{1,3},{3,1},{4,6},{6,4},{5,7},{7,5},{8,10},{10,8},{9,1... | collective-permute-start | bytes 98312 | tf_op jit(solution)/shard_map/ppermute | solution.py:553
  68.6 8.4 %collective-permute-start.8 = (bf16[2,4,128,128]{3,2,1,0:T(8,128)(2,1)}, bf16[2,4,128,128]{3,2,1,0:T(8,128)(2,1)}, u32[]{:S(2)}, u32[]{:S(2)}) collective-permute-start(bf16[2,4,128,128]{3,2,1,0:T(8,128)(2,1)} %get-tuple-element.63), channel_id=1, source_target_pairs={{0,1},{1,0},{2,3},{3,2},{4,5},{5,4},{6,7},{7,6},{8,9},{9,8},{10,11... | collective-permute-start | bytes 786440 | tf_op jit(solution)/shard_map/ppermute | solution.py:536
  72.4 7.6 %copy-start = (bf16[1024,1024]{1,0:T(8,128)(2,1)S(1)}, bf16[1024,1024]{1,0:T(8,128)(2,1)}, u32[]{:S(2)}) copy-start(bf16[1024,1024]{1,0:T(8,128)(2,1)} %proj_ref.1) | copy-start | bytes 6291460
  72.4 22.3 %all-to-all-start.1 = ((bf16[8,520,128]{2,1,0:T(8,128)(2,1)}), bf16[8,520,128]{2,1,0:T(8,128)(2,1)S(1)}, u32[]{:S(2)}, u32[]{:S(2)}) async-start(bf16[8,520,128]{2,1,0:T(8,128)(2,1)} %get-tuple-element.59), calls=%async_computation.1 | async-start | bytes 2129920 | tf_op jit(solution)/shard_map/all_to_all | solution.py:436
  77.0 3.0 %copy-start.1 = (bf16[512,1024]{1,0:T(8,128)(2,1)S(1)}, bf16[512,1024]{1,0:T(8,128)(2,1)}, u32[]{:S(2)}) copy-start(bf16[512,1024]{1,0:T(8,128)(2,1)} %resid_ref) | copy-start | bytes 3145732
  78.2 15.8 %collective-permute-start.9 = (bf16[4,128,128]{2,1,0:T(8,128)(2,1)S(1)}, bf16[4,128,128]{2,1,0:T(8,128)(2,1)S(1)}, u32[]{:S(2)}, u32[]{:S(2)}) collective-permute-start(bf16[4,128,128]{2,1,0:T(8,128)(2,1)S(1)} %dynamic-slice_bitcast_fusion.1), channel_id=1, source_target_pairs={{0,2},{2,0},{1,3},{3,1},{4,6},{6,4},{5,7},{7,5},{8,10},{10,8},{9,1... | collective-permute-start | bytes 393224 | tf_op jit(solution)/shard_map/ppermute | solution.py:536
  80.0 1.2 copy-start.2
  81.2 13.5 %copy-start.3 = (bf16[1024,128]{1,0:T(8,128)(2,1)S(1)}, bf16[1024,128]{1,0:T(8,128)(2,1)}, u32[]{:S(2)}) copy-start(bf16[1024,128]{1,0:T(8,128)(2,1)} %colbert_ref.3) | copy-start | bytes 786436
  81.2 13.5 %copy-start.4 = (f32[1024]{0:T(1024)S(1)}, f32[1024]{0:T(1024)}, u32[]{:S(2)}) copy-start(f32[1024]{0:T(1024)} %param.16) | copy-start | bytes 12292
  94.8 5.0 %copy-start.5 = (f32[4,128,128]{2,1,0:T(8,128)S(1)}, f32[4,128,128]{2,1,0:T(8,128)}, u32[]{:S(2)}) copy-start(f32[4,128,128]{2,1,0:T(8,128)} %convert_add_fusion) | copy-start | bytes 786436
  98.9 7.6 %collective-permute-start.10 = (bf16[8,8,72,128]{3,2,1,0:T(8,128)(2,1)S(1)}, bf16[8,8,72,128]{3,2,1,0:T(8,128)(2,1)S(1)}, u32[]{:S(2)}, u32[]{:S(2)}) collective-permute-start(bf16[8,8,72,128]{3,2,1,0:T(8,128)(2,1)S(1)} %get-tuple-element.76), channel_id=1, source_target_pairs={{0,1},{1,0},{2,3},{3,2},{4,5},{5,4},{6,7},{7,6},{8,9},{9,8},{10,11... | collective-permute-start | bytes 3538952 | tf_op jit(solution)/shard_map/ppermute | solution.py:536
  99.8 6.7 %collective-permute-start.11 = (f32[2,128,128]{2,1,0:T(8,128)S(1)}, f32[2,128,128]{2,1,0:T(8,128)S(1)}, u32[]{:S(2)}, u32[]{:S(2)}) collective-permute-start(f32[2,128,128]{2,1,0:T(8,128)S(1)} %dynamic-slice_bitcast_fusion), channel_id=1, source_target_pairs={{0,8},{4,12},{8,0},{12,4},{1,9},{5,13},{9,1},{13,5},{2,10},{6,14},... | collective-permute-start | bytes 393224 | tf_op jit(solution)/shard_map/ppermute | solution.py:536
  160.5 7.6 %collective-permute-start.13 = (bf16[8,8,72,128]{3,2,1,0:T(8,128)(2,1)S(1)}, bf16[8,8,72,128]{3,2,1,0:T(8,128)(2,1)S(1)}, u32[]{:S(2)}, u32[]{:S(2)}) collective-permute-start(bf16[8,8,72,128]{3,2,1,0:T(8,128)(2,1)S(1)} %bitcast.28), channel_id=1, source_target_pairs={{0,1},{1,0},{2,3},{3,2},{4,5},{5,4},{6,7},{7,6},{8,9},{9,8},{10,11... | collective-permute-start | bytes 3538952 | tf_op jit(solution)/shard_map/ppermute | solution.py:662
  163.8 3.7 %collective-permute-start.12 = (f32[128,128]{1,0:T(8,128)S(1)}, f32[128,128]{1,0:T(8,128)S(1)}, u32[]{:S(2)}, u32[]{:S(2)}) collective-permute-start(f32[128,128]{1,0:T(8,128)S(1)} %dynamic-slice_bitcast_fusion.2), channel_id=1, source_target_pairs={{0,4},{4,0},{8,12},{12,8},{1,5},{5,1},{9,13},{13,9},{2,6},{6,2},{1... | collective-permute-start | bytes 196616 | tf_op jit(solution)/shard_map/ppermute | solution.py:536

commit v7 on v6

--- a/solution.py
+++ b/solution.py
@@ -134,7 +134,7 @@
         sim_ref[1] = hit
         stats = jnp.concatenate([highest, total, positive, jnp.zeros((5, queries), F32)], axis=0)
         stats = jnp.concatenate([stats, jnp.zeros((8, width - queries), F32)], axis=1)
-        stats_ref[...] = stats
+        stats_ref[...] = jnp.broadcast_to(stats[None], stats_ref.shape)
 
 
 def forward_tile(flip, near, far, passage_pack, ids, query_len, group=8):
@@ -161,7 +161,7 @@
             pl.BlockSpec(memory_space=pltpu.VMEM),
             whole((count, rows)),
             whole((2, count, queries)),
-            whole((8, width)),
+            whole((parts, 8, width)),
         ],
         out_shape=[
             pltpu.VMEM((count, rows, slots), BF16),
@@ -169,7 +169,7 @@
             pltpu.VMEM((rows, width), BF16),
             jax.ShapeDtypeStruct((count, rows), F32),
             jax.ShapeDtypeStruct((2, count, queries), F32),
-            jax.ShapeDtypeStruct((8, width), F32),
+            jax.ShapeDtypeStruct((parts, 8, width), F32),
         ],
         scratch_shapes=[pltpu.VMEM((rows, width), F32), pltpu.VMEM((count, width), F32)],
         compiler_params=pltpu.CompilerParams(vmem_limit_bytes=16 * MIB),
@@ -192,14 +192,12 @@
     query_len,
     parts,
     core_ref,
-    flip_ref,
     own_ref,
     exp_ref,
     mix_ref,
     inv_ref,
     sim_ref,
-    near_ref,
-    far_ref,
+    stats_ref,
     pg_ref,
     kept_ref,
     given_ref,
@@ -211,18 +209,12 @@
     queries = rows // query_len
     for k in range(parts):
         qt[:, k * q_rows : (k + 1) * q_rows] = own_ref[k * q_rows : (k + 1) * q_rows, :].T
-    stats = []
-    for k in range(parts):
-        at = stored(k) ^ flip_ref[0]
-        spot = at % (parts // 2)
-        stats.append(jnp.where(at < parts // 2, near_ref[spot], far_ref[spot]))
-    stats = jnp.stack(stats)
-    highest_of = stats[:, 0, :queries]
+    highest_of = stats_ref[:, 0, :queries]
     highest = jnp.max(highest_of, axis=0, keepdims=True)
     total = jnp.sum(
-        stats[:, 1, :queries] * jnp.exp(highest_of - highest), axis=0, keepdims=True
-    )
-    positive = jnp.sum(stats[:, 2, :queries], axis=0, keepdims=True)
+        stats_ref[:, 1, :queries] * jnp.exp(highest_of - highest), axis=0, keepdims=True
+    )
+    positive = jnp.sum(stats_ref[:, 2, :queries], axis=0, keepdims=True)
     log_total = highest + jnp.log(total)
     coefficient = jnp.exp(sim_ref[0] - log_total) - sim_ref[1]
     scale = inv_ref[...] * dot(
@@ -249,15 +241,15 @@
     given_ref[...] = halves[1 - core_ref[0]]
 
 
-def backward_tile(core, flip, parts, own, spread, mixed, inverse, similar, near, far, query_len):
+def backward_tile(core, parts, own, spread, mixed, inverse, similar, stats, query_len):
     count, rows, slots = spread.shape
     q_rows, width = rows // parts, own.shape[1]
     work = rows * slots * count
     return pl.pallas_call(
         functools.partial(backward_kernel, query_len, parts),
         name="backward_tile",
-        in_specs=[pl.BlockSpec(memory_space=pltpu.SMEM)] * 2
-        + [pl.BlockSpec(memory_space=pltpu.VMEM)] * 7,
+        in_specs=[pl.BlockSpec(memory_space=pltpu.SMEM)]
+        + [pl.BlockSpec(memory_space=pltpu.VMEM)] * 6,
         out_shape=[
             pltpu.HBM((count, slots + EXTRA, width), BF16),
             jax.ShapeDtypeStruct((2, parts // 4, q_rows, width), BF16),
@@ -273,7 +265,7 @@
         cost_estimate=pl.CostEstimate(
             flops=2 * work * width, transcendentals=0, bytes_accessed=3 * work
         ),
-    )(core, flip, own, spread, mixed, inverse, similar, near, far)
+    )(core, own, spread, mixed, inverse, similar, stats)
 
 
 def early_kernel(resid_ref, context_ref, proj_ref, normed_ref, inv_ref, context_t_ref):
@@ -544,25 +536,35 @@
     return pair_summed(kept, given, axis, pairs, out_type)
 
 
-def doubled(held, axis, pairs):
-    return jnp.concatenate([held, lax.ppermute(held, axis, pairs)])
-
-
-def fours_gathered(four):
-    held = doubled(four, "neg_0", FAR)
+def query_gathered(own):
+    held = own[None]
+    for axis, pairs in ((CORE, SWAP), ("neg_0", NEAR), ("neg_0", FAR)):
+        held = jnp.concatenate([held, lax.ppermute(held, axis, pairs)])
     return held, lax.ppermute(held, "neg_1", SWAP)
 
 
-def pack_kernel(length_ref, p_ref, out_ref):
+def sent_out(tile_ref, out_ref, sems):
+    copies = [
+        pltpu.make_async_copy(tile_ref, out_ref.at[k], sems.at[k]) for k in range(out_ref.shape[0])
+    ]
+    for copy in copies:
+        copy.start()
+    for copy in copies:
+        copy.wait()
+
+
+def pack_kernel(length_ref, p_ref, out_ref, tile_ref, sems):
     slots = p_ref.shape[1]
-    extra = jnp.full((EXTRA, p_ref.shape[2]), (length_ref[0] - LEAST).astype(F32)).astype(BF16)
-    for k in range(out_ref.shape[0]):
-        out_ref[k, :slots, :] = p_ref[0]
-        out_ref[k, slots:, :] = extra
+    tile_ref[:slots, :] = p_ref[0]
+    tile_ref[slots:, :] = jnp.full(
+        (EXTRA, p_ref.shape[2]), (length_ref[0] - LEAST).astype(F32)
+    ).astype(BF16)
+    sent_out(tile_ref, out_ref, sems)
 
 
 def passage_copies(passage_emb, lengths, copies):
     _, slots, width = passage_emb.shape
+    tile = (slots + EXTRA, width)
     return pl.pallas_call(
         pack_kernel,
         name="passage_copies",
@@ -570,16 +572,18 @@
             pl.BlockSpec(memory_space=pltpu.SMEM),
             pl.BlockSpec(memory_space=pltpu.VMEM),
         ],
-        out_specs=whole((copies, slots + EXTRA, width)),
-        out_shape=pltpu.HBM((copies, slots + EXTRA, width), BF16),
+        out_specs=pl.BlockSpec(memory_space=pltpu.HBM),
+        out_shape=pltpu.HBM((copies, *tile), BF16),
+        scratch_shapes=[pltpu.VMEM(tile, BF16), pltpu.SemaphoreType.DMA((copies,))],
     )(lengths, passage_emb)
 
 
-def spread_kernel(parts_ref, out_ref):
+def spread_kernel(parts_ref, out_ref, tile_ref, sems):
     total = parts_ref[0].astype(F32)
     for k in range(1, parts_ref.shape[0]):
         total += parts_ref[k].astype(F32)
-    out_ref[...] = jnp.broadcast_to(total.astype(BF16)[None], out_ref.shape)
+    tile_ref[...] = total.astype(BF16)
+    sent_out(tile_ref, out_ref, sems)
 
 
 def summed_copies(parts):
@@ -587,8 +591,12 @@
         spread_kernel,
         name="summed_copies",
         in_specs=[pl.BlockSpec(memory_space=pltpu.VMEM)],
-        out_specs=whole(parts.shape),
+        out_specs=pl.BlockSpec(memory_space=pltpu.HBM),
         out_shape=pltpu.HBM(parts.shape, BF16),
+        scratch_shapes=[
+            pltpu.VMEM(parts.shape[1:], BF16),
+            pltpu.SemaphoreType.DMA((parts.shape[0],)),
+        ],
     )(parts)
 
 
@@ -608,12 +616,11 @@
             jnp.broadcast_to(wanted.astype(BF16)[None], (EXTRA, emb)),
         ]
     )
-    query_four = doubled(doubled(query_own[None], CORE, SWAP), "neg_0", NEAR)
-    copies, query_four = lax.optimization_barrier(
-        (passage_copies(passage_emb, lengths, dp_size), query_four)
+    copies, query_own = lax.optimization_barrier(
+        (passage_copies(passage_emb, lengths, dp_size), query_own)
     )
     passage_pack = exchange(copies, DP)
-    queries = fours_gathered(query_four)
+    queries = query_gathered(query_own)
     ids = jnp.broadcast_to((jnp.arange(dp_size) * neg_size + place).astype(F32)[:, None], (dp_size, emb))
     row, column = lax.axis_index("neg_1"), lax.axis_index("neg_0")
     flip = (row * 8 + column * 2 + core)[None]
@@ -626,18 +633,9 @@
     spread, mixed, query_rows, inverse, similar, stats = forward_tile(
         flip, *queries, passage_pack, ids, query_len
     )
-    stats = fours_gathered(doubled(doubled(stats[None], CORE, SWAP), "neg_0", NEAR))
+    stats = exchange(stats, NEG)
     passage_parts, kept, given = backward_tile(
-        core[None],
-        flip,
-        neg_size,
-        query_rows,
-        spread,
-        mixed,
-        inverse,
-        similar,
-        *stats,
-        query_len,
+        core[None], neg_size, query_rows, spread, mixed, inverse, similar, stats, query_len
     )
     residual, kept, given = lax.optimization_barrier((residual, kept, given))
     early = early_rows(residual, context, out_proj)

time: 172 us -> 166 us (0.965)
  blocking collectives: 51.1 us -> 66.8 us
  waiting for transfers between devices: 34.5 us -> 22.6 us
  starting transfers between devices: 36.4 us -> 26.8 us
    all_to_all x2 -> x3, blocking collectives: 51.1 us -> 66.8 us  [exchange(): return lax.all_to_all(pieces, axis, 0, 0, tiled=True)]
    ppermute x8 -> x4, waiting for transfers between devices: 24.4 us -> 11.1 us  [the longest x3 6.07 us: query_gathered(): held = jnp.concatenate([held, lax.ppermute(held, axis, pairs)])]
    ppermute x5, starting transfers between devices: 9.51 us -> 4.06 us  [pair_summed(): taken = lax.ppermute(given, axis, pairs)]
    ppermute x8 -> x4, starting transfers between devices: 12.9 us -> 7.77 us  [the longest x3 5.07 us: query_gathered(): held = jnp.concatenate([held, lax.ppermute(held, axis, pairs)])]
  transfers between devices with their start and end apart: 16 -> 12, of which waited for: 10 -> 7; matrix products, arithmetic and copies ran while one was open for 4% -> 4% of each run, Pallas kernels for 4% -> 3%
where the time goes in v7:
time: 166 us
  blocking collectives  66.8 us (40%)
  Pallas kernels  36.5 us (22%)
  starting transfers between devices  26.8 us (16%)
  waiting for transfers between devices  22.6 us (14%)
  other arithmetic  4.37 us (3%)
  matrix products  3.49 us (2%)
  between operations  3.2 us (2%)
  local copies, waits for them, and re-layouts  1.86 us (1%)
    all_to_all x3, blocking collectives, exchange(): return lax.all_to_all(pieces, axis, 0, 0, tiled=True)  66.8 us
    pallas_call x1, Pallas kernels, forward_tile(): pl.pallas_call(functools.partial(forward_kernel, query_len, group), name=...  14.1 us
    all_to_all x2, starting transfers between devices, exchange(): return lax.all_to_all(pieces, axis, 0, 0, tiled=True)  11.6 us
    ppermute x5, waiting for transfers between devices, pair_summed(): taken = lax.ppermute(given, axis, pairs)  11.5 us
    pallas_call x1, Pallas kernels, backward_tile(): pl.pallas_call(functools.partial(backward_kernel, query_len, parts), name...  6.12 us
    ppermute x3, waiting for transfers between devices, query_gathered(): held = jnp.concatenate([held, lax.ppermute(held, axis, pairs)])  6.07 us
    ppermute x3, starting transfers between devices, query_gathered(): held = jnp.concatenate([held, lax.ppermute(held, axis, pairs)])  5.07 us
    ppermute x1, waiting for transfers between devices, query_gathered(): return (held, lax.ppermute(held, 'neg_1', SWAP))  5.03 us
  transfers between devices with their start and end apart: 12, of which 7 were waited for; matrix products, arithmetic and copies ran while one was open for 4% of the time, Pallas kernels for 3%

profile of v7, /device:TPU:1, one launch (start us, length us, event | category | flops | bytes accessed | tf_op | source)
XLA Modules:
  0.0 165.6 jit_solution(7616937038000606223)
XLA Ops:
  1.3 0.7 select_reduce_fusion
  2.1 0.8 pad_maximum_fusion.3
  2.8 1.9 %passage_copies.1 = bf16[8,520,128]{2,1,0:T(8,128)(2,1)} custom-call(s32[1]{0:T(128)S(6)} %copy.18.length_ref, bf16[1,512,128]{2,1,0:T(8,128)(2,1)} %p_ref.1), custom_call_target="tpu_custom_call" | custom-call | tf_op jit(solution)/shard_map/passage_copies/pallas_call | solution.py:568
  4.8 6.9 %all-to-all-start = ((bf16[8,520,128]{2,1,0:T(8,128)(2,1)}), bf16[8,520,128]{2,1,0:T(8,128)(2,1)S(1)}, u32[]{:S(2)}, u32[]{:S(2)}) async-start(bf16[8,520,128]{2,1,0:T(8,128)(2,1)} %passage_copies.1), calls=%async_computation | async-start | bytes 2129920 | tf_op jit(solution)/shard_map/all_to_all | solution.py:428
  11.7 1.0 collective-permute-start
  12.6 0.9 collective-permute-done
  13.5 1.3 collective-permute-start.1
  14.8 2.2 %collective-permute-done.1 = bf16[2,136,128]{2,1,0:T(8,128)(2,1)S(1)} collective-permute-done((bf16[2,136,128]{2,1,0:T(8,128)(2,1)S(1)}, bf16[2,136,128]{2,1,0:T(8,128)(2,1)S(1)}, u32[]{:S(2)}, u32[]{:S(2)}) %collective-permute-start.1) | collective-permute-done | bytes 69664 | tf_op jit(solution)/shard_map/ppermute | solution.py:542
  17.0 2.8 %collective-permute-start.2 = (bf16[4,136,128]{2,1,0:T(8,128)(2,1)S(1)}, bf16[4,136,128]{2,1,0:T(8,128)(2,1)S(1)}, u32[]{:S(2)}, u32[]{:S(2)}) collective-permute-start(bf16[4,136,128]{2,1,0:T(8,128)(2,1)S(1)} %pad_maximum_fusion.1), channel_id=1, source_target_pairs={{0,8},{4,12},{8,0},{12,4},{1,9},{5,13},{9,1},{13,5},{2,10},{6,14},... | collective-permute-start | bytes 417800 | tf_op jit(solution)/shard_map/ppermute | solution.py:542
  19.9 3.0 %collective-permute-done.2 = bf16[4,136,128]{2,1,0:T(8,128)(2,1)S(1)} collective-permute-done((bf16[4,136,128]{2,1,0:T(8,128)(2,1)S(1)}, bf16[4,136,128]{2,1,0:T(8,128)(2,1)S(1)}, u32[]{:S(2)}, u32[]{:S(2)}) %collective-permute-start.2) | collective-permute-done | bytes 139296 | tf_op jit(solution)/shard_map/ppermute | solution.py:542
  22.9 2.7 %collective-permute-start.3 = (bf16[8,136,128]{2,1,0:T(8,128)(2,1)S(1)}, bf16[8,136,128]{2,1,0:T(8,128)(2,1)S(1)}, u32[]{:S(2)}, u32[]{:S(2)}) collective-permute-start(bf16[8,136,128]{2,1,0:T(8,128)(2,1)S(1)} %pad_maximum_fusion.near_ref), channel_id=1, source_target_pairs={{0,2},{2,0},{1,3},{3,1},{4,6},{6,4},{5,7},{7,5},{8,10},{10,8},{9,1... | collective-permute-start | bytes 835592 | tf_op jit(solution)/shard_map/ppermute | solution.py:543
  25.6 5.0 %collective-permute-done.3.far_ref = bf16[8,136,128]{2,1,0:T(8,128)(2,1)S(1)} collective-permute-done((bf16[8,136,128]{2,1,0:T(8,128)(2,1)S(1)}, bf16[8,136,128]{2,1,0:T(8,128)(2,1)S(1)}, u32[]{:S(2)}, u32[]{:S(2)}) %collective-permute-start.3) | collective-permute-done | bytes 278560 | tf_op jit(solution)/shard_map/ppermute | solution.py:543
  30.6 0.0 all-to-all-done.p_ref
  30.6 0.1 broadcast_in_dim.49.ids_ref
  30.7 14.1 %forward_tile.1 = (bf16[8,2048,512]{2,1,0:T(8,128)(2,1)S(1)}, f32[8,2048,128]{2,1,0:T(8,128)S(1)}, bf16[2048,128]{1,0:T(8,128)(2,1)S(1)}, f32[8,2048]{1,0:T(8,12...) custom-call(s32[1]{0:T(128)} %bitcast.1.flip_ref, bf16[8,136,128]{2,1,0:T(8,128)(2,1)S(1)} %pad_maximum_fusion.near_ref, ...), custom_call_target="tpu_custom_call" | custom-call | flops 4294967296 | bytes 33554432 | tf_op jit(solution)/shard_map/forward_tile/pallas_call | solution.py:147
  44.8 16.7 %all_to_all.25.stats_ref = f32[16,8,128]{2,1,0:T(8,128)S(1)} all-to-all(f32[16,8,128]{2,1,0:T(8,128)S(1)} %get-tuple-element.58), channel_id=1, replica_groups=mesh['dp_0'=4,'dp_1'=2,'neg_0'=4,'neg_1'=2,'neg_2'=2] {'neg_0','neg_1','..., dimensions={0} | all-to-all | bytes 131072 | tf_op jit(solution)/shard_map/all_to_all | solution.py:428
  61.5 6.1 %backward_tile.1 = (bf16[8,520,128]{2,1,0:T(8,128)(2,1)}, bf16[2,4,128,128]{3,2,1,0:T(8,128)(2,1)S(1)}, bf16[2,4,128,128]{3,2,1,0:T(8,128)(2,1)}) custom-call(s32[1]{0:T(128)} %bitcast.core_ref, bf16[2048,128]{1,0:T(8,128)(2,1)S(1)} %get-tuple-element.53.own_ref, bf16[8,2048,512]{2,1,0:T(8,128)(2,1)S(1)} %get-tuple-element.54.exp_ref, ...), custom_call_target="tpu_custom_call" | custom-call | flops 2147483648 | bytes 25165824 | tf_op jit(solution)/shard_map/backward_tile/pallas_call | solution.py:248
  67.6 0.4 collective-permute-start.4
  68.0 0.0 copy-start
  68.0 4.7 %all-to-all-start.2 = ((bf16[8,520,128]{2,1,0:T(8,128)(2,1)}), bf16[8,520,128]{2,1,0:T(8,128)(2,1)S(1)}, u32[]{:S(2)}, u32[]{:S(2)}) async-start(bf16[8,520,128]{2,1,0:T(8,128)(2,1)} %get-tuple-element.59), calls=%async_computation.2 | async-start | bytes 2129920 | tf_op jit(solution)/shard_map/all_to_all | solution.py:428
  72.7 0.0 copy-start.1
  72.7 0.0 collective-permute-done.4
  72.7 1.1 add_convert_fusion.1
  73.9 1.3 collective-permute-start.5
  75.2 0.0 copy-done
  75.2 0.0 copy-done.1
  75.2 0.0 copy-start.2
  75.2 1.2 copy-done.2
  76.4 0.0 copy-start.3
  76.4 0.0 copy-start.4
  76.4 3.9 %early_rows.1 = (f32[512,1024]{1,0:T(8,128)}, f32[512,128]{1,0:T(8,128)}, bf16[1024,512]{1,0:T(8,128)(2,1)}) custom-call(bf16[512,1024]{1,0:T(8,128)(2,1)S(1)} %copy-done.1, bf16[512,1024]{1,0:T(8,128)(2,1)S(1)} %copy-done.2, bf16[1024,1024]{1,0:T(8,128)(2,1)S(1)} %copy-done), custom_call_target="tpu_custom_call" | custom-call | flops 1073741824 | bytes 5242880 | tf_op jit(solution)/shard_map/early_rows/pallas_call | solution.py:284
  80.2 8.8 %collective-permute-done.5 = bf16[4,128,128]{2,1,0:T(8,128)(2,1)S(1)} collective-permute-done((bf16[4,128,128]{2,1,0:T(8,128)(2,1)S(1)}, bf16[4,128,128]{2,1,0:T(8,128)(2,1)S(1)}, u32[]{:S(2)}, u32[]{:S(2)}) %collective-permute-start.5) | collective-permute-done | bytes 131104 | tf_op jit(solution)/shard_map/ppermute | solution.py:528
  89.0 0.7 convert_add_fusion
  89.7 0.0 all-to-all-done.2.parts_ref
  89.7 0.0 copy-done.3
  89.7 0.0 copy-done.4
  89.8 0.0 copy-start.5
  89.8 4.1 %late_rows.1 = (bf16[512,1024]{1,0:T(8,128)(2,1)}, bf16[8,8,72,128]{3,2,1,0:T(8,128)(2,1)S(1)}, bf16[8,8,72,128]{3,2,1,0:T(8,128)(2,1)S(1)}, f32[8,128]{1,0:T(8,128)S(1)}) custom-call(s32[1]{0:T(128)} %bitcast.core_ref, bf16[8,520,128]{2,1,0:T(8,128)(2,1)S(1)} %all-to-all-done.2.parts_ref, f32[512,1024]{1,0:T(8,128)} %get-tuple-element.71.normed_far, ...), custom_call_target="tpu_custom_call" | custom-call | flops 1342177280 | bytes 7340032 | tf_op jit(solution)/shard_map/late_rows/pallas_call | solution.py:393
  93.9 1.0 collective-permute-start.6
  94.8 0.0 copy-done.5
  94.9 0.9 collective-permute-start.7
  95.8 3.5 %convolution_convert_fusion = bf16[512,1024]{1,0:T(8,128)(2,1)} fusion(bf16[512,1024]{1,0:T(8,128)(2,1)} %get-tuple-element.44, bf16[1024,1024]{1,0:T(8,128)(2,1)S(1)} %copy-done), kind=kOutput, calls=%fused_computation.1 | convolution fusion | flops 1074266112 | bytes 4194304 | tf_op jit(solution)/shard_map/dot_general | solution.py:651
  99.3 2.3 %collective-permute-done.7 = f32[2,128,128]{2,1,0:T(8,128)S(1)} collective-permute-done((f32[2,128,128]{2,1,0:T(8,128)S(1)}, f32[2,128,128]{2,1,0:T(8,128)S(1)}, u32[]{:S(2)}, u32[]{:S(2)}) %collective-permute-start.7) | collective-permute-done | bytes 131104 | tf_op jit(solution)/shard_map/ppermute | solution.py:528
  101.6 0.0 collective-permute-done.6
  101.6 0.3 add_convert_fusion
  101.9 27.6 %all_to_all.26.parts_ref = bf16[64,72,128]{2,1,0:T(8,128)(2,1)} all-to-all(bf16[64,72,128]{2,1,0:T(8,128)(2,1)S(1)} %bitcast.31), channel_id=1, replica_groups=mesh['dp_0'=4,'dp_1'=2,'neg_0'=4,'neg_1'=2,'neg_2'=2] {'dp_0','dp_1','ne..., dimensions={0} | all-to-all | bytes 2359296 | tf_op jit(solution)/shard_map/all_to_all | solution.py:428
  129.5 3.0 %summed_copies.1 = bf16[64,72,128]{2,1,0:T(8,128)(2,1)} custom-call(bf16[64,72,128]{2,1,0:T(8,128)(2,1)} %all_to_all.26.parts_ref), custom_call_target="tpu_custom_call" | custom-call | tf_op jit(solution)/shard_map/summed_copies/pallas_call | solution.py:590
  132.5 22.5 %all_to_all.27 = bf16[64,72,128]{2,1,0:T(8,128)(2,1)S(1)} all-to-all(bf16[64,72,128]{2,1,0:T(8,128)(2,1)} %summed_copies.1), channel_id=1, replica_groups=mesh['dp_0'=4,'dp_1'=2,'neg_0'=4,'neg_1'=2,'neg_2'=2] {'dp_0','dp_1','ne..., dimensions={0} | all-to-all | bytes 2359296 | tf_op jit(solution)/shard_map/all_to_all | solution.py:428
  155.0 3.3 %collective-permute-start.9 = (bf16[8,8,72,128]{3,2,1,0:T(8,128)(2,1)S(1)}, bf16[8,8,72,128]{3,2,1,0:T(8,128)(2,1)S(1)}, u32[]{:S(2)}, u32[]{:S(2)}) collective-permute-start(bf16[8,8,72,128]{3,2,1,0:T(8,128)(2,1)S(1)} %bitcast.26), channel_id=1, source_target_pairs={{0,1},{1,0},{2,3},{3,2},{4,5},{5,4},{6,7},{7,6},{8,9},{9,8},{10,11... | collective-permute-start | bytes 3538952 | tf_op jit(solution)/shard_map/ppermute | solution.py:660
  158.4 0.5 collective-permute-start.8
  158.9 0.5 slice.3
  160.0 1.5 own_rows.1._
  161.5 0.5 collective-permute-done.8
  162.0 0.6 bitcast_add_fusion.1
  162.7 0.0 collective-permute-done.9.other_ref
  162.7 1.9 %finish.1 = (f32[1024,1024]{1,0:T(8,128)}, f32[1024,128]{1,0:T(8,128)}, f32[1,1024]{1,0:T(1,128)}) custom-call(s32[1]{0:T(128)} %bitcast.core_ref, bf16[8,8,72,128]{3,2,1,0:T(8,128)(2,1)S(1)} %bitcast.28, bf16[8,8,72,128]{3,2,1,0:T(8,128)(2,1)S(1)} %collective-permute-done.9.other_ref, ...), custom_call_target="tpu_custom_call", output_to_operand_aliasing={{0}: (5, {})} | custom-call | flops 2097152 | bytes 4194304 | tf_op jit(solution)/shard_map/finish/pallas_call | solution.py:490
  (11 shorter events, 0.1 us)
Async XLA Ops:
  4.8 25.8 %all-to-all-start = ((bf16[8,520,128]{2,1,0:T(8,128)(2,1)}), bf16[8,520,128]{2,1,0:T(8,128)(2,1)S(1)}, u32[]{:S(2)}, u32[]{:S(2)}) async-start(bf16[8,520,128]{2,1,0:T(8,128)(2,1)} %passage_copies.1), calls=%async_computation | async-start | bytes 2129920 | tf_op jit(solution)/shard_map/all_to_all | solution.py:428
  11.7 1.8 %collective-permute-start = (bf16[1,136,128]{2,1,0:T(8,128)(2,1)S(1)}, bf16[1,136,128]{2,1,0:T(8,128)(2,1)S(1)}, u32[]{:S(2)}, u32[]{:S(2)}) collective-permute-start(bf16[1,136,128]{2,1,0:T(8,128)(2,1)S(1)} %bitcast.34), channel_id=1, source_target_pairs={{0,1},{1,0},{2,3},{3,2},{4,5},{5,4},{6,7},{7,6},{8,9},{9,8},{10,11... | collective-permute-start | bytes 104456 | tf_op jit(solution)/shard_map/ppermute | solution.py:542
  13.5 3.5 %collective-permute-start.1 = (bf16[2,136,128]{2,1,0:T(8,128)(2,1)S(1)}, bf16[2,136,128]{2,1,0:T(8,128)(2,1)S(1)}, u32[]{:S(2)}, u32[]{:S(2)}) collective-permute-start(bf16[2,136,128]{2,1,0:T(8,128)(2,1)S(1)} %pad_maximum_fusion.2), channel_id=1, source_target_pairs={{0,4},{4,0},{8,12},{12,8},{1,5},{5,1},{9,13},{13,9},{2,6},{6,2},{1... | collective-permute-start | bytes 208904 | tf_op jit(solution)/shard_map/ppermute | solution.py:542
  17.0 5.8 %collective-permute-start.2 = (bf16[4,136,128]{2,1,0:T(8,128)(2,1)S(1)}, bf16[4,136,128]{2,1,0:T(8,128)(2,1)S(1)}, u32[]{:S(2)}, u32[]{:S(2)}) collective-permute-start(bf16[4,136,128]{2,1,0:T(8,128)(2,1)S(1)} %pad_maximum_fusion.1), channel_id=1, source_target_pairs={{0,8},{4,12},{8,0},{12,4},{1,9},{5,13},{9,1},{13,5},{2,10},{6,14},... | collective-permute-start | bytes 417800 | tf_op jit(solution)/shard_map/ppermute | solution.py:542
  22.9 7.7 %collective-permute-start.3 = (bf16[8,136,128]{2,1,0:T(8,128)(2,1)S(1)}, bf16[8,136,128]{2,1,0:T(8,128)(2,1)S(1)}, u32[]{:S(2)}, u32[]{:S(2)}) collective-permute-start(bf16[8,136,128]{2,1,0:T(8,128)(2,1)S(1)} %pad_maximum_fusion.near_ref), channel_id=1, source_target_pairs={{0,2},{2,0},{1,3},{3,1},{4,6},{6,4},{5,7},{7,5},{8,10},{10,8},{9,1... | collective-permute-start | bytes 835592 | tf_op jit(solution)/shard_map/ppermute | solution.py:543
  67.6 5.1 %collective-permute-start.4 = (bf16[2,4,128,128]{3,2,1,0:T(8,128)(2,1)}, bf16[2,4,128,128]{3,2,1,0:T(8,128)(2,1)}, u32[]{:S(2)}, u32[]{:S(2)}) collective-permute-start(bf16[2,4,128,128]{3,2,1,0:T(8,128)(2,1)} %get-tuple-element.63), channel_id=1, source_target_pairs={{0,1},{1,0},{2,3},{3,2},{4,5},{5,4},{6,7},{7,6},{8,9},{9,8},{10,11... | collective-permute-start | bytes 786440 | tf_op jit(solution)/shard_map/ppermute | solution.py:528
  68.0 7.1 %copy-start = (bf16[1024,1024]{1,0:T(8,128)(2,1)S(1)}, bf16[1024,1024]{1,0:T(8,128)(2,1)}, u32[]{:S(2)}) copy-start(bf16[1024,1024]{1,0:T(8,128)(2,1)} %proj_ref.1) | copy-start | bytes 6291460
  68.0 21.7 %all-to-all-start.2 = ((bf16[8,520,128]{2,1,0:T(8,128)(2,1)}), bf16[8,520,128]{2,1,0:T(8,128)(2,1)S(1)}, u32[]{:S(2)}, u32[]{:S(2)}) async-start(bf16[8,520,128]{2,1,0:T(8,128)(2,1)} %get-tuple-element.59), calls=%async_computation.2 | async-start | bytes 2129920 | tf_op jit(solution)/shard_map/all_to_all | solution.py:428
  72.7 2.4 %copy-start.1 = (bf16[512,1024]{1,0:T(8,128)(2,1)S(1)}, bf16[512,1024]{1,0:T(8,128)(2,1)}, u32[]{:S(2)}) copy-start(bf16[512,1024]{1,0:T(8,128)(2,1)} %resid_ref) | copy-start | bytes 3145732
  73.9 15.1 %collective-permute-start.5 = (bf16[4,128,128]{2,1,0:T(8,128)(2,1)S(1)}, bf16[4,128,128]{2,1,0:T(8,128)(2,1)S(1)}, u32[]{:S(2)}, u32[]{:S(2)}) collective-permute-start(bf16[4,128,128]{2,1,0:T(8,128)(2,1)S(1)} %dynamic-slice_bitcast_fusion.1), channel_id=1, source_target_pairs={{0,2},{2,0},{1,3},{3,1},{4,6},{6,4},{5,7},{7,5},{8,10},{10,8},{9,1... | collective-permute-start | bytes 393224 | tf_op jit(solution)/shard_map/ppermute | solution.py:528
  75.2 1.2 copy-start.2
  76.4 13.4 %copy-start.3 = (bf16[1024,128]{1,0:T(8,128)(2,1)S(1)}, bf16[1024,128]{1,0:T(8,128)(2,1)}, u32[]{:S(2)}) copy-start(bf16[1024,128]{1,0:T(8,128)(2,1)} %colbert_ref.3) | copy-start | bytes 786436
  76.4 13.4 %copy-start.4 = (f32[1024]{0:T(1024)S(1)}, f32[1024]{0:T(1024)}, u32[]{:S(2)}) copy-start(f32[1024]{0:T(1024)} %param.16) | copy-start | bytes 12292
  89.8 5.1 %copy-start.5 = (f32[4,128,128]{2,1,0:T(8,128)S(1)}, f32[4,128,128]{2,1,0:T(8,128)}, u32[]{:S(2)}) copy-start(f32[4,128,128]{2,1,0:T(8,128)} %convert_add_fusion) | copy-start | bytes 786436
  93.9 7.7 %collective-permute-start.6 = (bf16[8,8,72,128]{3,2,1,0:T(8,128)(2,1)S(1)}, bf16[8,8,72,128]{3,2,1,0:T(8,128)(2,1)S(1)}, u32[]{:S(2)}, u32[]{:S(2)}) collective-permute-start(bf16[8,8,72,128]{3,2,1,0:T(8,128)(2,1)S(1)} %get-tuple-element.76), channel_id=1, source_target_pairs={{0,1},{1,0},{2,3},{3,2},{4,5},{5,4},{6,7},{7,6},{8,9},{9,8},{10,11... | collective-permute-start | bytes 3538952 | tf_op jit(solution)/shard_map/ppermute | solution.py:528
  94.9 6.7 %collective-permute-start.7 = (f32[2,128,128]{2,1,0:T(8,128)S(1)}, f32[2,128,128]{2,1,0:T(8,128)S(1)}, u32[]{:S(2)}, u32[]{:S(2)}) collective-permute-start(f32[2,128,128]{2,1,0:T(8,128)S(1)} %dynamic-slice_bitcast_fusion), channel_id=1, source_target_pairs={{0,8},{4,12},{8,0},{12,4},{1,9},{5,13},{9,1},{13,5},{2,10},{6,14},... | collective-permute-start | bytes 393224 | tf_op jit(solution)/shard_map/ppermute | solution.py:528
  155.0 7.6 %collective-permute-start.9 = (bf16[8,8,72,128]{3,2,1,0:T(8,128)(2,1)S(1)}, bf16[8,8,72,128]{3,2,1,0:T(8,128)(2,1)S(1)}, u32[]{:S(2)}, u32[]{:S(2)}) collective-permute-start(bf16[8,8,72,128]{3,2,1,0:T(8,128)(2,1)S(1)} %bitcast.26), channel_id=1, source_target_pairs={{0,1},{1,0},{2,3},{3,2},{4,5},{5,4},{6,7},{7,6},{8,9},{9,8},{10,11... | collective-permute-start | bytes 3538952 | tf_op jit(solution)/shard_map/ppermute | solution.py:660
  158.4 3.7 %collective-permute-start.8 = (f32[128,128]{1,0:T(8,128)S(1)}, f32[128,128]{1,0:T(8,128)S(1)}, u32[]{:S(2)}, u32[]{:S(2)}) collective-permute-start(f32[128,128]{1,0:T(8,128)S(1)} %dynamic-slice_bitcast_fusion.2), channel_id=1, source_target_pairs={{0,4},{4,0},{8,12},{12,8},{1,5},{5,1},{9,13},{13,9},{2,6},{6,2},{1... | collective-permute-start | bytes 196616 | tf_op jit(solution)/shard_map/ppermute | solution.py:528

commit v8 on v7

--- a/solution.py
+++ b/solution.py
@@ -578,12 +578,11 @@
     )(lengths, passage_emb)
 
 
-def spread_kernel(parts_ref, out_ref, tile_ref, sems):
+def spread_kernel(parts_ref, out_ref):
     total = parts_ref[0].astype(F32)
     for k in range(1, parts_ref.shape[0]):
         total += parts_ref[k].astype(F32)
-    tile_ref[...] = total.astype(BF16)
-    sent_out(tile_ref, out_ref, sems)
+    out_ref[...] = jnp.broadcast_to(total.astype(BF16)[None], out_ref.shape)
 
 
 def summed_copies(parts):
@@ -591,12 +590,9 @@
         spread_kernel,
         name="summed_copies",
         in_specs=[pl.BlockSpec(memory_space=pltpu.VMEM)],
-        out_specs=pl.BlockSpec(memory_space=pltpu.HBM),
-        out_shape=pltpu.HBM(parts.shape, BF16),
-        scratch_shapes=[
-            pltpu.VMEM(parts.shape[1:], BF16),
-            pltpu.SemaphoreType.DMA((parts.shape[0],)),
-        ],
+        out_specs=pl.BlockSpec(memory_space=pltpu.VMEM),
+        out_shape=pltpu.VMEM(parts.shape, BF16),
+        compiler_params=pltpu.CompilerParams(vmem_limit_bytes=6 * MIB),
     )(parts)
 
 

time: 166 us -> 163 us (0.982)
  Pallas kernels: 36.5 us -> 33.7 us
    pallas_call x1, Pallas kernels: 3.01 us -> 0.23 us  [summed_copies(): pl.pallas_call(spread_kernel, name='summed_copies', in_specs=[pl.BlockSpe...]
where the time goes in v8:
time: 163 us; the launch traced here: 162 us
  blocking collectives  66.1 us (41%)
  Pallas kernels  33.7 us (21%)
  starting transfers between devices  27 us (17%)
  waiting for transfers between devices  22.6 us (14%)
  other arithmetic  4.37 us (3%)
  matrix products  3.49 us (2%)
  between operations  3.2 us (2%)
  local copies, waits for them, and re-layouts  1.86 us (1%)
    all_to_all x3, blocking collectives, exchange(): return lax.all_to_all(pieces, axis, 0, 0, tiled=True)  66.1 us
    pallas_call x1, Pallas kernels, forward_tile(): pl.pallas_call(functools.partial(forward_kernel, query_len, group), name=...  14.1 us
    all_to_all x2, starting transfers between devices, exchange(): return lax.all_to_all(pieces, axis, 0, 0, tiled=True)  11.6 us
    ppermute x5, waiting for transfers between devices, pair_summed(): taken = lax.ppermute(given, axis, pairs)  11.5 us
    pallas_call x1, Pallas kernels, backward_tile(): pl.pallas_call(functools.partial(backward_kernel, query_len, parts), name...  6.12 us
    ppermute x3, waiting for transfers between devices, query_gathered(): held = jnp.concatenate([held, lax.ppermute(held, axis, pairs)])  6.07 us
    ppermute x3, starting transfers between devices, query_gathered(): held = jnp.concatenate([held, lax.ppermute(held, axis, pairs)])  5.07 us
    ppermute x1, waiting for transfers between devices, query_gathered(): return (held, lax.ppermute(held, 'neg_1', SWAP))  5.03 us
  transfers between devices with their start and end apart: 12, of which 7 were waited for; matrix products, arithmetic and copies ran while one was open for 4% of the time, Pallas kernels for 3%

profile of v8, /device:TPU:1, one launch (start us, length us, event | category | flops | bytes accessed | tf_op | source)
XLA Modules:
  0.0 162.4 jit_solution(5529187699302730)
XLA Ops:
  1.3 0.7 select_reduce_fusion
  2.1 0.8 pad_maximum_fusion.3
  2.8 1.9 %passage_copies.1 = bf16[8,520,128]{2,1,0:T(8,128)(2,1)} custom-call(s32[1]{0:T(128)S(6)} %copy.18.length_ref, bf16[1,512,128]{2,1,0:T(8,128)(2,1)} %p_ref.1), custom_call_target="tpu_custom_call" | custom-call | tf_op jit(solution)/shard_map/passage_copies/pallas_call | solution.py:568
  4.8 6.9 %all-to-all-start = ((bf16[8,520,128]{2,1,0:T(8,128)(2,1)}), bf16[8,520,128]{2,1,0:T(8,128)(2,1)S(1)}, u32[]{:S(2)}, u32[]{:S(2)}) async-start(bf16[8,520,128]{2,1,0:T(8,128)(2,1)} %passage_copies.1), calls=%async_computation | async-start | bytes 2129920 | tf_op jit(solution)/shard_map/all_to_all | solution.py:428
  11.7 1.0 collective-permute-start
  12.6 0.9 collective-permute-done
  13.5 1.3 collective-permute-start.1
  14.8 2.2 %collective-permute-done.1 = bf16[2,136,128]{2,1,0:T(8,128)(2,1)S(1)} collective-permute-done((bf16[2,136,128]{2,1,0:T(8,128)(2,1)S(1)}, bf16[2,136,128]{2,1,0:T(8,128)(2,1)S(1)}, u32[]{:S(2)}, u32[]{:S(2)}) %collective-permute-start.1) | collective-permute-done | bytes 69664 | tf_op jit(solution)/shard_map/ppermute | solution.py:542
  17.0 2.8 %collective-permute-start.2 = (bf16[4,136,128]{2,1,0:T(8,128)(2,1)S(1)}, bf16[4,136,128]{2,1,0:T(8,128)(2,1)S(1)}, u32[]{:S(2)}, u32[]{:S(2)}) collective-permute-start(bf16[4,136,128]{2,1,0:T(8,128)(2,1)S(1)} %pad_maximum_fusion.1), channel_id=1, source_target_pairs={{0,8},{4,12},{8,0},{12,4},{1,9},{5,13},{9,1},{13,5},{2,10},{6,14},... | collective-permute-start | bytes 417800 | tf_op jit(solution)/shard_map/ppermute | solution.py:542
  19.9 3.0 %collective-permute-done.2 = bf16[4,136,128]{2,1,0:T(8,128)(2,1)S(1)} collective-permute-done((bf16[4,136,128]{2,1,0:T(8,128)(2,1)S(1)}, bf16[4,136,128]{2,1,0:T(8,128)(2,1)S(1)}, u32[]{:S(2)}, u32[]{:S(2)}) %collective-permute-start.2) | collective-permute-done | bytes 139296 | tf_op jit(solution)/shard_map/ppermute | solution.py:542
  22.9 2.7 %collective-permute-start.3 = (bf16[8,136,128]{2,1,0:T(8,128)(2,1)S(1)}, bf16[8,136,128]{2,1,0:T(8,128)(2,1)S(1)}, u32[]{:S(2)}, u32[]{:S(2)}) collective-permute-start(bf16[8,136,128]{2,1,0:T(8,128)(2,1)S(1)} %pad_maximum_fusion.near_ref), channel_id=1, source_target_pairs={{0,2},{2,0},{1,3},{3,1},{4,6},{6,4},{5,7},{7,5},{8,10},{10,8},{9,1... | collective-permute-start | bytes 835592 | tf_op jit(solution)/shard_map/ppermute | solution.py:543
  25.6 5.0 %collective-permute-done.3.far_ref = bf16[8,136,128]{2,1,0:T(8,128)(2,1)S(1)} collective-permute-done((bf16[8,136,128]{2,1,0:T(8,128)(2,1)S(1)}, bf16[8,136,128]{2,1,0:T(8,128)(2,1)S(1)}, u32[]{:S(2)}, u32[]{:S(2)}) %collective-permute-start.3) | collective-permute-done | bytes 278560 | tf_op jit(solution)/shard_map/ppermute | solution.py:543
  30.6 0.0 all-to-all-done.p_ref
  30.6 0.1 broadcast_in_dim.49.ids_ref
  30.7 14.1 %forward_tile.1 = (bf16[8,2048,512]{2,1,0:T(8,128)(2,1)S(1)}, f32[8,2048,128]{2,1,0:T(8,128)S(1)}, bf16[2048,128]{1,0:T(8,128)(2,1)S(1)}, f32[8,2048]{1,0:T(8,12...) custom-call(s32[1]{0:T(128)} %bitcast.1.flip_ref, bf16[8,136,128]{2,1,0:T(8,128)(2,1)S(1)} %pad_maximum_fusion.near_ref, ...), custom_call_target="tpu_custom_call" | custom-call | flops 4294967296 | bytes 33554432 | tf_op jit(solution)/shard_map/forward_tile/pallas_call | solution.py:147
  44.8 16.7 %all_to_all.25.stats_ref = f32[16,8,128]{2,1,0:T(8,128)S(1)} all-to-all(f32[16,8,128]{2,1,0:T(8,128)S(1)} %get-tuple-element.58), channel_id=1, replica_groups=mesh['dp_0'=4,'dp_1'=2,'neg_0'=4,'neg_1'=2,'neg_2'=2] {'neg_0','neg_1','..., dimensions={0} | all-to-all | bytes 131072 | tf_op jit(solution)/shard_map/all_to_all | solution.py:428
  61.5 6.1 %backward_tile.1 = (bf16[8,520,128]{2,1,0:T(8,128)(2,1)}, bf16[2,4,128,128]{3,2,1,0:T(8,128)(2,1)S(1)}, bf16[2,4,128,128]{3,2,1,0:T(8,128)(2,1)}) custom-call(s32[1]{0:T(128)} %bitcast.core_ref, bf16[2048,128]{1,0:T(8,128)(2,1)S(1)} %get-tuple-element.53.own_ref, bf16[8,2048,512]{2,1,0:T(8,128)(2,1)S(1)} %get-tuple-element.54.exp_ref, ...), custom_call_target="tpu_custom_call" | custom-call | flops 2147483648 | bytes 25165824 | tf_op jit(solution)/shard_map/backward_tile/pallas_call | solution.py:248
  67.6 0.4 collective-permute-start.4
  68.0 0.0 copy-start
  68.0 4.7 %all-to-all-start.2 = ((bf16[8,520,128]{2,1,0:T(8,128)(2,1)}), bf16[8,520,128]{2,1,0:T(8,128)(2,1)S(1)}, u32[]{:S(2)}, u32[]{:S(2)}) async-start(bf16[8,520,128]{2,1,0:T(8,128)(2,1)} %get-tuple-element.59), calls=%async_computation.2 | async-start | bytes 2129920 | tf_op jit(solution)/shard_map/all_to_all | solution.py:428
  72.7 0.0 copy-start.1
  72.7 0.0 collective-permute-done.4
  72.7 1.1 add_convert_fusion.1
  73.9 1.3 collective-permute-start.5
  75.2 0.0 copy-done
  75.2 0.0 copy-done.1
  75.2 0.0 copy-start.2
  75.2 1.2 copy-done.2
  76.4 0.0 copy-start.3
  76.4 0.0 copy-start.4
  76.4 3.9 %early_rows.1 = (f32[512,1024]{1,0:T(8,128)}, f32[512,128]{1,0:T(8,128)}, bf16[1024,512]{1,0:T(8,128)(2,1)}) custom-call(bf16[512,1024]{1,0:T(8,128)(2,1)S(1)} %copy-done.1, bf16[512,1024]{1,0:T(8,128)(2,1)S(1)} %copy-done.2, bf16[1024,1024]{1,0:T(8,128)(2,1)S(1)} %copy-done), custom_call_target="tpu_custom_call" | custom-call | flops 1073741824 | bytes 5242880 | tf_op jit(solution)/shard_map/early_rows/pallas_call | solution.py:284
  80.2 8.8 %collective-permute-done.5 = bf16[4,128,128]{2,1,0:T(8,128)(2,1)S(1)} collective-permute-done((bf16[4,128,128]{2,1,0:T(8,128)(2,1)S(1)}, bf16[4,128,128]{2,1,0:T(8,128)(2,1)S(1)}, u32[]{:S(2)}, u32[]{:S(2)}) %collective-permute-start.5) | collective-permute-done | bytes 131104 | tf_op jit(solution)/shard_map/ppermute | solution.py:528
  89.0 0.7 convert_add_fusion
  89.7 0.0 all-to-all-done.2.parts_ref
  89.7 0.0 copy-done.3
  89.7 0.0 copy-done.4
  89.8 0.0 copy-start.5
  89.8 4.1 %late_rows.1 = (bf16[512,1024]{1,0:T(8,128)(2,1)}, bf16[8,8,72,128]{3,2,1,0:T(8,128)(2,1)S(1)}, bf16[8,8,72,128]{3,2,1,0:T(8,128)(2,1)S(1)}, f32[8,128]{1,0:T(8,128)S(1)}) custom-call(s32[1]{0:T(128)} %bitcast.core_ref, bf16[8,520,128]{2,1,0:T(8,128)(2,1)S(1)} %all-to-all-done.2.parts_ref, f32[512,1024]{1,0:T(8,128)} %get-tuple-element.71.normed_far, ...), custom_call_target="tpu_custom_call" | custom-call | flops 1342177280 | bytes 7340032 | tf_op jit(solution)/shard_map/late_rows/pallas_call | solution.py:393
  93.9 1.0 collective-permute-start.6
  94.8 0.0 copy-done.5
  94.9 0.9 collective-permute-start.7
  95.8 3.5 %convolution_convert_fusion = bf16[512,1024]{1,0:T(8,128)(2,1)} fusion(bf16[512,1024]{1,0:T(8,128)(2,1)} %get-tuple-element.44, bf16[1024,1024]{1,0:T(8,128)(2,1)S(1)} %copy-done), kind=kOutput, calls=%fused_computation.1 | convolution fusion | flops 1074266112 | bytes 4194304 | tf_op jit(solution)/shard_map/dot_general | solution.py:647
  99.3 2.3 %collective-permute-done.7 = f32[2,128,128]{2,1,0:T(8,128)S(1)} collective-permute-done((f32[2,128,128]{2,1,0:T(8,128)S(1)}, f32[2,128,128]{2,1,0:T(8,128)S(1)}, u32[]{:S(2)}, u32[]{:S(2)}) %collective-permute-start.7) | collective-permute-done | bytes 131104 | tf_op jit(solution)/shard_map/ppermute | solution.py:528
  101.6 0.0 collective-permute-done.6
  101.6 0.3 add_convert_fusion
  101.9 27.5 %all_to_all.26.parts_ref = bf16[64,72,128]{2,1,0:T(8,128)(2,1)S(1)} all-to-all(bf16[64,72,128]{2,1,0:T(8,128)(2,1)S(1)} %bitcast.31), channel_id=1, replica_groups=mesh['dp_0'=4,'dp_1'=2,'neg_0'=4,'neg_1'=2,'neg_2'=2] {'dp_0','dp_1','ne..., dimensions={0} | all-to-all | bytes 2359296 | tf_op jit(solution)/shard_map/all_to_all | solution.py:428
  129.4 0.2 summed_copies.1
  129.6 21.9 %all_to_all.27 = bf16[64,72,128]{2,1,0:T(8,128)(2,1)S(1)} all-to-all(bf16[64,72,128]{2,1,0:T(8,128)(2,1)S(1)} %summed_copies.1), channel_id=1, replica_groups=mesh['dp_0'=4,'dp_1'=2,'neg_0'=4,'neg_1'=2,'neg_2'=2] {'dp_0','dp_1','ne..., dimensions={0} | all-to-all | bytes 2359296 | tf_op jit(solution)/shard_map/all_to_all | solution.py:428
  151.5 3.6 %collective-permute-start.9 = (bf16[8,8,72,128]{3,2,1,0:T(8,128)(2,1)S(1)}, bf16[8,8,72,128]{3,2,1,0:T(8,128)(2,1)S(1)}, u32[]{:S(2)}, u32[]{:S(2)}) collective-permute-start(bf16[8,8,72,128]{3,2,1,0:T(8,128)(2,1)S(1)} %bitcast.26), channel_id=1, source_target_pairs={{0,1},{1,0},{2,3},{3,2},{4,5},{5,4},{6,7},{7,6},{8,9},{9,8},{10,11... | collective-permute-start | bytes 3538952 | tf_op jit(solution)/shard_map/ppermute | solution.py:656
  155.1 0.5 collective-permute-start.8
  155.6 0.5 slice.3
  156.8 1.5 own_rows.1._
  158.3 0.5 collective-permute-done.8
  158.8 0.6 bitcast_add_fusion.1
  159.4 0.0 collective-permute-done.9.other_ref
  159.4 1.9 %finish.1 = (f32[1024,1024]{1,0:T(8,128)}, f32[1024,128]{1,0:T(8,128)}, f32[1,1024]{1,0:T(1,128)}) custom-call(s32[1]{0:T(128)} %bitcast.core_ref, bf16[8,8,72,128]{3,2,1,0:T(8,128)(2,1)S(1)} %bitcast.28, bf16[8,8,72,128]{3,2,1,0:T(8,128)(2,1)S(1)} %collective-permute-done.9.other_ref, ...), custom_call_target="tpu_custom_call", output_to_operand_aliasing={{0}: (5, {})} | custom-call | flops 2097152 | bytes 4194304 | tf_op jit(solution)/shard_map/finish/pallas_call | solution.py:490
  (11 shorter events, 0.1 us)
Async XLA Ops:
  4.8 25.8 %all-to-all-start = ((bf16[8,520,128]{2,1,0:T(8,128)(2,1)}), bf16[8,520,128]{2,1,0:T(8,128)(2,1)S(1)}, u32[]{:S(2)}, u32[]{:S(2)}) async-start(bf16[8,520,128]{2,1,0:T(8,128)(2,1)} %passage_copies.1), calls=%async_computation | async-start | bytes 2129920 | tf_op jit(solution)/shard_map/all_to_all | solution.py:428
  11.7 1.8 %collective-permute-start = (bf16[1,136,128]{2,1,0:T(8,128)(2,1)S(1)}, bf16[1,136,128]{2,1,0:T(8,128)(2,1)S(1)}, u32[]{:S(2)}, u32[]{:S(2)}) collective-permute-start(bf16[1,136,128]{2,1,0:T(8,128)(2,1)S(1)} %bitcast.34), channel_id=1, source_target_pairs={{0,1},{1,0},{2,3},{3,2},{4,5},{5,4},{6,7},{7,6},{8,9},{9,8},{10,11... | collective-permute-start | bytes 104456 | tf_op jit(solution)/shard_map/ppermute | solution.py:542
  13.5 3.5 %collective-permute-start.1 = (bf16[2,136,128]{2,1,0:T(8,128)(2,1)S(1)}, bf16[2,136,128]{2,1,0:T(8,128)(2,1)S(1)}, u32[]{:S(2)}, u32[]{:S(2)}) collective-permute-start(bf16[2,136,128]{2,1,0:T(8,128)(2,1)S(1)} %pad_maximum_fusion.2), channel_id=1, source_target_pairs={{0,4},{4,0},{8,12},{12,8},{1,5},{5,1},{9,13},{13,9},{2,6},{6,2},{1... | collective-permute-start | bytes 208904 | tf_op jit(solution)/shard_map/ppermute | solution.py:542
  17.0 5.8 %collective-permute-start.2 = (bf16[4,136,128]{2,1,0:T(8,128)(2,1)S(1)}, bf16[4,136,128]{2,1,0:T(8,128)(2,1)S(1)}, u32[]{:S(2)}, u32[]{:S(2)}) collective-permute-start(bf16[4,136,128]{2,1,0:T(8,128)(2,1)S(1)} %pad_maximum_fusion.1), channel_id=1, source_target_pairs={{0,8},{4,12},{8,0},{12,4},{1,9},{5,13},{9,1},{13,5},{2,10},{6,14},... | collective-permute-start | bytes 417800 | tf_op jit(solution)/shard_map/ppermute | solution.py:542
  22.9 7.7 %collective-permute-start.3 = (bf16[8,136,128]{2,1,0:T(8,128)(2,1)S(1)}, bf16[8,136,128]{2,1,0:T(8,128)(2,1)S(1)}, u32[]{:S(2)}, u32[]{:S(2)}) collective-permute-start(bf16[8,136,128]{2,1,0:T(8,128)(2,1)S(1)} %pad_maximum_fusion.near_ref), channel_id=1, source_target_pairs={{0,2},{2,0},{1,3},{3,1},{4,6},{6,4},{5,7},{7,5},{8,10},{10,8},{9,1... | collective-permute-start | bytes 835592 | tf_op jit(solution)/shard_map/ppermute | solution.py:543
  67.6 5.1 %collective-permute-start.4 = (bf16[2,4,128,128]{3,2,1,0:T(8,128)(2,1)}, bf16[2,4,128,128]{3,2,1,0:T(8,128)(2,1)}, u32[]{:S(2)}, u32[]{:S(2)}) collective-permute-start(bf16[2,4,128,128]{3,2,1,0:T(8,128)(2,1)} %get-tuple-element.63), channel_id=1, source_target_pairs={{0,1},{1,0},{2,3},{3,2},{4,5},{5,4},{6,7},{7,6},{8,9},{9,8},{10,11... | collective-permute-start | bytes 786440 | tf_op jit(solution)/shard_map/ppermute | solution.py:528
  68.0 7.1 %copy-start = (bf16[1024,1024]{1,0:T(8,128)(2,1)S(1)}, bf16[1024,1024]{1,0:T(8,128)(2,1)}, u32[]{:S(2)}) copy-start(bf16[1024,1024]{1,0:T(8,128)(2,1)} %proj_ref.1) | copy-start | bytes 6291460
  68.0 21.7 %all-to-all-start.2 = ((bf16[8,520,128]{2,1,0:T(8,128)(2,1)}), bf16[8,520,128]{2,1,0:T(8,128)(2,1)S(1)}, u32[]{:S(2)}, u32[]{:S(2)}) async-start(bf16[8,520,128]{2,1,0:T(8,128)(2,1)} %get-tuple-element.59), calls=%async_computation.2 | async-start | bytes 2129920 | tf_op jit(solution)/shard_map/all_to_all | solution.py:428
  72.7 2.4 %copy-start.1 = (bf16[512,1024]{1,0:T(8,128)(2,1)S(1)}, bf16[512,1024]{1,0:T(8,128)(2,1)}, u32[]{:S(2)}) copy-start(bf16[512,1024]{1,0:T(8,128)(2,1)} %resid_ref) | copy-start | bytes 3145732
  73.9 15.1 %collective-permute-start.5 = (bf16[4,128,128]{2,1,0:T(8,128)(2,1)S(1)}, bf16[4,128,128]{2,1,0:T(8,128)(2,1)S(1)}, u32[]{:S(2)}, u32[]{:S(2)}) collective-permute-start(bf16[4,128,128]{2,1,0:T(8,128)(2,1)S(1)} %dynamic-slice_bitcast_fusion.1), channel_id=1, source_target_pairs={{0,2},{2,0},{1,3},{3,1},{4,6},{6,4},{5,7},{7,5},{8,10},{10,8},{9,1... | collective-permute-start | bytes 393224 | tf_op jit(solution)/shard_map/ppermute | solution.py:528
  75.2 1.2 copy-start.2
  76.4 13.4 %copy-start.3 = (bf16[1024,128]{1,0:T(8,128)(2,1)S(1)}, bf16[1024,128]{1,0:T(8,128)(2,1)}, u32[]{:S(2)}) copy-start(bf16[1024,128]{1,0:T(8,128)(2,1)} %colbert_ref.3) | copy-start | bytes 786436
  76.4 13.4 %copy-start.4 = (f32[1024]{0:T(1024)S(1)}, f32[1024]{0:T(1024)}, u32[]{:S(2)}) copy-start(f32[1024]{0:T(1024)} %param.16) | copy-start | bytes 12292
  89.8 5.1 %copy-start.5 = (f32[4,128,128]{2,1,0:T(8,128)S(1)}, f32[4,128,128]{2,1,0:T(8,128)}, u32[]{:S(2)}) copy-start(f32[4,128,128]{2,1,0:T(8,128)} %convert_add_fusion) | copy-start | bytes 786436
  93.9 7.7 %collective-permute-start.6 = (bf16[8,8,72,128]{3,2,1,0:T(8,128)(2,1)S(1)}, bf16[8,8,72,128]{3,2,1,0:T(8,128)(2,1)S(1)}, u32[]{:S(2)}, u32[]{:S(2)}) collective-permute-start(bf16[8,8,72,128]{3,2,1,0:T(8,128)(2,1)S(1)} %get-tuple-element.76), channel_id=1, source_target_pairs={{0,1},{1,0},{2,3},{3,2},{4,5},{5,4},{6,7},{7,6},{8,9},{9,8},{10,11... | collective-permute-start | bytes 3538952 | tf_op jit(solution)/shard_map/ppermute | solution.py:528
  94.9 6.7 %collective-permute-start.7 = (f32[2,128,128]{2,1,0:T(8,128)S(1)}, f32[2,128,128]{2,1,0:T(8,128)S(1)}, u32[]{:S(2)}, u32[]{:S(2)}) collective-permute-start(f32[2,128,128]{2,1,0:T(8,128)S(1)} %dynamic-slice_bitcast_fusion), channel_id=1, source_target_pairs={{0,8},{4,12},{8,0},{12,4},{1,9},{5,13},{9,1},{13,5},{2,10},{6,14},... | collective-permute-start | bytes 393224 | tf_op jit(solution)/shard_map/ppermute | solution.py:528
  151.5 7.9 %collective-permute-start.9 = (bf16[8,8,72,128]{3,2,1,0:T(8,128)(2,1)S(1)}, bf16[8,8,72,128]{3,2,1,0:T(8,128)(2,1)S(1)}, u32[]{:S(2)}, u32[]{:S(2)}) collective-permute-start(bf16[8,8,72,128]{3,2,1,0:T(8,128)(2,1)S(1)} %bitcast.26), channel_id=1, source_target_pairs={{0,1},{1,0},{2,3},{3,2},{4,5},{5,4},{6,7},{7,6},{8,9},{9,8},{10,11... | collective-permute-start | bytes 3538952 | tf_op jit(solution)/shard_map/ppermute | solution.py:656
  155.1 3.7 %collective-permute-start.8 = (f32[128,128]{1,0:T(8,128)S(1)}, f32[128,128]{1,0:T(8,128)S(1)}, u32[]{:S(2)}, u32[]{:S(2)}) collective-permute-start(f32[128,128]{1,0:T(8,128)S(1)} %dynamic-slice_bitcast_fusion.2), channel_id=1, source_target_pairs={{0,4},{4,0},{8,12},{12,8},{1,5},{5,1},{9,13},{13,9},{2,6},{6,2},{1... | collective-permute-start | bytes 196616 | tf_op jit(solution)/shard_map/ppermute | solution.py:528

commit v9 on v8

--- a/solution.py
+++ b/solution.py
@@ -647,8 +647,8 @@
     context_grad = jnp.dot(residual_grad, out_proj.T, preferred_element_type=F32).astype(BF16)
     query_part = query_part.reshape(2, 2, *query_part.shape[1:])
     query_part = halves_summed(query_part, "neg_0", FAR, far_side, F32)
-    half, context_grad, query_part = lax.optimization_barrier((half, context_grad, query_part))
     slabs = exchange(half.reshape(dp_size * cross_size, *half.shape[2:]), DP + CROSS)
+    slabs, context_grad, query_part = lax.optimization_barrier((slabs, context_grad, query_part))
     half = exchange(summed_copies(slabs), DP + CROSS).reshape(half.shape)
     half, query_part = lax.optimization_barrier((half, query_part))
     query_grad = halves_summed(query_part, "neg_0", NEAR, near_side, F32)

time: 163 us -> 162 us (level)
  blocking collectives: 66.1 us -> 41.4 us
  waiting for transfers between devices: 22.6 us -> 35 us
  starting transfers between devices: 27 us -> 36.7 us
    all_to_all x3 -> x2, blocking collectives: 66.1 us -> 41.4 us  [exchange(): return lax.all_to_all(pieces, axis, 0, 0, tiled=True)]
    ppermute x5, waiting for transfers between devices: 11.5 us -> 22.6 us  [pair_summed(): taken = lax.ppermute(given, axis, pairs)]
    all_to_all x2 -> x3, starting transfers between devices: 11.6 us -> 20.1 us  [exchange(): return lax.all_to_all(pieces, axis, 0, 0, tiled=True)]
    ppermute x5, starting transfers between devices: 4.06 us -> 5.72 us  [pair_summed(): taken = lax.ppermute(given, axis, pairs)]
  transfers between devices with their start and end apart: 12 -> 13, of which waited for: 7 -> 9; matrix products, arithmetic and copies ran while one was open for 4% -> 5% of each run, Pallas kernels for 3% -> 3%
where the time goes in v9:
time: 162 us
  blocking collectives  41.4 us (26%)
  starting transfers between devices  36.7 us (23%)
  waiting for transfers between devices  35 us (22%)
  Pallas kernels  33.7 us (21%)
  other arithmetic  5.38 us (3%)
  matrix products  3.53 us (2%)
  between operations  3.19 us (2%)
  local copies, waits for them, and re-layouts  2.77 us (2%)
    all_to_all x2, blocking collectives, exchange(): return lax.all_to_all(pieces, axis, 0, 0, tiled=True)  41.4 us
    ppermute x5, waiting for transfers between devices, pair_summed(): taken = lax.ppermute(given, axis, pairs)  22.6 us
    all_to_all x3, starting transfers between devices, exchange(): return lax.all_to_all(pieces, axis, 0, 0, tiled=True)  20.1 us
    pallas_call x1, Pallas kernels, forward_tile(): pl.pallas_call(functools.partial(forward_kernel, query_len, group), name=...  14.1 us
    pallas_call x1, Pallas kernels, backward_tile(): pl.pallas_call(functools.partial(backward_kernel, query_len, parts), name...  6.12 us
    ppermute x3, waiting for transfers between devices, query_gathered(): held = jnp.concatenate([held, lax.ppermute(held, axis, pairs)])  6.07 us
    ppermute x5, starting transfers between devices, pair_summed(): taken = lax.ppermute(given, axis, pairs)  5.72 us
    ppermute x3, starting transfers between devices, query_gathered(): held = jnp.concatenate([held, lax.ppermute(held, axis, pairs)])  5.07 us
  transfers between devices with their start and end apart: 13, of which 9 were waited for; matrix products, arithmetic and copies ran while one was open for 5% of the time, Pallas kernels for 3%

profile of v9, /device:TPU:1, one launch (start us, length us, event | category | flops | bytes accessed | tf_op | source)
XLA Modules:
  0.0 161.7 jit_solution(9387386356583942459)
XLA Ops:
  1.3 0.7 select_reduce_fusion
  2.1 0.8 pad_maximum_fusion.3
  2.8 1.9 %passage_copies.1 = bf16[8,520,128]{2,1,0:T(8,128)(2,1)} custom-call(s32[1]{0:T(128)S(6)} %copy.18.length_ref, bf16[1,512,128]{2,1,0:T(8,128)(2,1)} %p_ref.1), custom_call_target="tpu_custom_call" | custom-call | tf_op jit(solution)/shard_map/passage_copies/pallas_call | solution.py:568
  4.8 6.9 %all-to-all-start = ((bf16[8,520,128]{2,1,0:T(8,128)(2,1)}), bf16[8,520,128]{2,1,0:T(8,128)(2,1)S(1)}, u32[]{:S(2)}, u32[]{:S(2)}) async-start(bf16[8,520,128]{2,1,0:T(8,128)(2,1)} %passage_copies.1), calls=%async_computation | async-start | bytes 2129920 | tf_op jit(solution)/shard_map/all_to_all | solution.py:428
  11.7 1.0 collective-permute-start
  12.6 0.9 collective-permute-done
  13.5 1.3 collective-permute-start.1
  14.8 2.2 %collective-permute-done.1 = bf16[2,136,128]{2,1,0:T(8,128)(2,1)S(1)} collective-permute-done((bf16[2,136,128]{2,1,0:T(8,128)(2,1)S(1)}, bf16[2,136,128]{2,1,0:T(8,128)(2,1)S(1)}, u32[]{:S(2)}, u32[]{:S(2)}) %collective-permute-start.1) | collective-permute-done | bytes 69664 | tf_op jit(solution)/shard_map/ppermute | solution.py:542
  17.0 2.8 %collective-permute-start.2 = (bf16[4,136,128]{2,1,0:T(8,128)(2,1)S(1)}, bf16[4,136,128]{2,1,0:T(8,128)(2,1)S(1)}, u32[]{:S(2)}, u32[]{:S(2)}) collective-permute-start(bf16[4,136,128]{2,1,0:T(8,128)(2,1)S(1)} %pad_maximum_fusion.1), channel_id=1, source_target_pairs={{0,8},{4,12},{8,0},{12,4},{1,9},{5,13},{9,1},{13,5},{2,10},{6,14},... | collective-permute-start | bytes 417800 | tf_op jit(solution)/shard_map/ppermute | solution.py:542
  19.9 3.0 %collective-permute-done.2 = bf16[4,136,128]{2,1,0:T(8,128)(2,1)S(1)} collective-permute-done((bf16[4,136,128]{2,1,0:T(8,128)(2,1)S(1)}, bf16[4,136,128]{2,1,0:T(8,128)(2,1)S(1)}, u32[]{:S(2)}, u32[]{:S(2)}) %collective-permute-start.2) | collective-permute-done | bytes 139296 | tf_op jit(solution)/shard_map/ppermute | solution.py:542
  22.9 2.7 %collective-permute-start.3 = (bf16[8,136,128]{2,1,0:T(8,128)(2,1)S(1)}, bf16[8,136,128]{2,1,0:T(8,128)(2,1)S(1)}, u32[]{:S(2)}, u32[]{:S(2)}) collective-permute-start(bf16[8,136,128]{2,1,0:T(8,128)(2,1)S(1)} %pad_maximum_fusion.near_ref), channel_id=1, source_target_pairs={{0,2},{2,0},{1,3},{3,1},{4,6},{6,4},{5,7},{7,5},{8,10},{10,8},{9,1... | collective-permute-start | bytes 835592 | tf_op jit(solution)/shard_map/ppermute | solution.py:543
  25.6 5.0 %collective-permute-done.3.far_ref = bf16[8,136,128]{2,1,0:T(8,128)(2,1)S(1)} collective-permute-done((bf16[8,136,128]{2,1,0:T(8,128)(2,1)S(1)}, bf16[8,136,128]{2,1,0:T(8,128)(2,1)S(1)}, u32[]{:S(2)}, u32[]{:S(2)}) %collective-permute-start.3) | collective-permute-done | bytes 278560 | tf_op jit(solution)/shard_map/ppermute | solution.py:543
  30.6 0.0 all-to-all-done.p_ref
  30.6 0.1 broadcast_in_dim.49.ids_ref
  30.7 14.1 %forward_tile.1 = (bf16[8,2048,512]{2,1,0:T(8,128)(2,1)S(1)}, f32[8,2048,128]{2,1,0:T(8,128)S(1)}, bf16[2048,128]{1,0:T(8,128)(2,1)S(1)}, f32[8,2048]{1,0:T(8,12...) custom-call(s32[1]{0:T(128)} %bitcast.1.flip_ref, bf16[8,136,128]{2,1,0:T(8,128)(2,1)S(1)} %pad_maximum_fusion.near_ref, ...), custom_call_target="tpu_custom_call" | custom-call | flops 4294967296 | bytes 33554432 | tf_op jit(solution)/shard_map/forward_tile/pallas_call | solution.py:147
  44.8 16.7 %all_to_all.25.stats_ref = f32[16,8,128]{2,1,0:T(8,128)S(1)} all-to-all(f32[16,8,128]{2,1,0:T(8,128)S(1)} %get-tuple-element.58), channel_id=1, replica_groups=mesh['dp_0'=4,'dp_1'=2,'neg_0'=4,'neg_1'=2,'neg_2'=2] {'neg_0','neg_1','..., dimensions={0} | all-to-all | bytes 131072 | tf_op jit(solution)/shard_map/all_to_all | solution.py:428
  61.5 6.1 %backward_tile.1 = (bf16[8,520,128]{2,1,0:T(8,128)(2,1)}, bf16[2,4,128,128]{3,2,1,0:T(8,128)(2,1)S(1)}, bf16[2,4,128,128]{3,2,1,0:T(8,128)(2,1)}) custom-call(s32[1]{0:T(128)} %bitcast.core_ref, bf16[2048,128]{1,0:T(8,128)(2,1)S(1)} %get-tuple-element.53.own_ref, bf16[8,2048,512]{2,1,0:T(8,128)(2,1)S(1)} %get-tuple-element.54.exp_ref, ...), custom_call_target="tpu_custom_call" | custom-call | flops 2147483648 | bytes 25165824 | tf_op jit(solution)/shard_map/backward_tile/pallas_call | solution.py:248
  67.6 0.4 collective-permute-start.4
  68.0 0.0 copy-start
  68.0 4.7 %all-to-all-start.2 = ((bf16[8,520,128]{2,1,0:T(8,128)(2,1)}), bf16[8,520,128]{2,1,0:T(8,128)(2,1)S(1)}, u32[]{:S(2)}, u32[]{:S(2)}) async-start(bf16[8,520,128]{2,1,0:T(8,128)(2,1)} %get-tuple-element.59), calls=%async_computation.2 | async-start | bytes 2129920 | tf_op jit(solution)/shard_map/all_to_all | solution.py:428
  72.7 0.0 copy-start.1
  72.7 0.0 collective-permute-done.4
  72.7 1.1 add_convert_fusion.1
  73.9 1.3 collective-permute-start.5
  75.2 0.0 copy-done
  75.2 0.0 copy-done.1
  75.2 0.0 copy-start.2
  75.2 1.2 copy-done.2
  76.4 0.0 copy-start.3
  76.4 0.0 copy-start.4
  76.4 3.9 %early_rows.1 = (f32[512,1024]{1,0:T(8,128)}, f32[512,128]{1,0:T(8,128)}, bf16[1024,512]{1,0:T(8,128)(2,1)}) custom-call(bf16[512,1024]{1,0:T(8,128)(2,1)S(1)} %copy-done.1, bf16[512,1024]{1,0:T(8,128)(2,1)S(1)} %copy-done.2, bf16[1024,1024]{1,0:T(8,128)(2,1)S(1)} %copy-done), custom_call_target="tpu_custom_call" | custom-call | flops 1073741824 | bytes 5242880 | tf_op jit(solution)/shard_map/early_rows/pallas_call | solution.py:284
  80.2 8.8 %collective-permute-done.5 = bf16[4,128,128]{2,1,0:T(8,128)(2,1)S(1)} collective-permute-done((bf16[4,128,128]{2,1,0:T(8,128)(2,1)S(1)}, bf16[4,128,128]{2,1,0:T(8,128)(2,1)S(1)}, u32[]{:S(2)}, u32[]{:S(2)}) %collective-permute-start.5) | collective-permute-done | bytes 131104 | tf_op jit(solution)/shard_map/ppermute | solution.py:528
  89.0 0.7 convert_add_fusion
  89.7 0.0 all-to-all-done.2.parts_ref
  89.7 0.0 copy-done.3
  89.8 0.0 copy-done.4
  89.8 4.1 %late_rows.1 = (bf16[512,1024]{1,0:T(8,128)(2,1)}, bf16[8,8,72,128]{3,2,1,0:T(8,128)(2,1)S(1)}, bf16[8,8,72,128]{3,2,1,0:T(8,128)(2,1)S(1)}, f32[8,128]{1,0:T(8,128)S(1)}) custom-call(s32[1]{0:T(128)} %bitcast.core_ref, bf16[8,520,128]{2,1,0:T(8,128)(2,1)S(1)} %all-to-all-done.2.parts_ref, f32[512,1024]{1,0:T(8,128)} %get-tuple-element.71.normed_far, ...), custom_call_target="tpu_custom_call" | custom-call | flops 1342177280 | bytes 7340032 | tf_op jit(solution)/shard_map/late_rows/pallas_call | solution.py:393
  93.9 1.0 collective-permute-start.6
  94.8 2.5 %collective-permute-done.6 = bf16[8,8,72,128]{3,2,1,0:T(8,128)(2,1)S(1)} collective-permute-done((bf16[8,8,72,128]{3,2,1,0:T(8,128)(2,1)S(1)}, bf16[8,8,72,128]{3,2,1,0:T(8,128)(2,1)S(1)}, u32[]{:S(2)}, u32[]{:S(2)}) %collective-permute-start.6) | collective-permute-done | bytes 1179680 | tf_op jit(solution)/shard_map/ppermute | solution.py:528
  97.3 1.3 add_convert_fusion
  98.6 8.5 %all-to-all-start.3 = ((bf16[64,72,128]{2,1,0:T(8,128)(2,1)}), bf16[64,72,128]{2,1,0:T(8,128)(2,1)S(1)}, u32[]{:S(2)}, u32[]{:S(2)}) async-start(bf16[64,72,128]{2,1,0:T(8,128)(2,1)} %bitcast.31), calls=%async_computation.3 | async-start | bytes 2359296 | tf_op jit(solution)/shard_map/all_to_all | solution.py:428
  107.2 0.9 dynamic-slice_bitcast_fusion
  108.1 2.6 %collective-permute-start.7 = (f32[2,128,128]{2,1,0:T(8,128)S(1)}, f32[2,128,128]{2,1,0:T(8,128)S(1)}, u32[]{:S(2)}, u32[]{:S(2)}) collective-permute-start(f32[2,128,128]{2,1,0:T(8,128)S(1)} %dynamic-slice_bitcast_fusion), channel_id=1, source_target_pairs={{0,8},{4,12},{8,0},{12,4},{1,9},{5,13},{9,1},{13,5},{2,10},{6,14},... | collective-permute-start | bytes 393224 | tf_op jit(solution)/shard_map/ppermute | solution.py:528
  110.7 0.0 copy-start.5
  110.7 3.5 %convolution_convert_fusion = bf16[512,1024]{1,0:T(8,128)(2,1)} fusion(bf16[512,1024]{1,0:T(8,128)(2,1)} %get-tuple-element.44, bf16[1024,1024]{1,0:T(8,128)(2,1)S(1)} %copy-done), kind=kOutput, calls=%fused_computation.1 | convolution fusion | flops 1074266112 | bytes 4194304 | tf_op jit(solution)/shard_map/dot_general | solution.py:647
  114.2 10.9 %collective-permute-done.7 = f32[2,128,128]{2,1,0:T(8,128)S(1)} collective-permute-done((f32[2,128,128]{2,1,0:T(8,128)S(1)}, f32[2,128,128]{2,1,0:T(8,128)S(1)}, u32[]{:S(2)}, u32[]{:S(2)}) %collective-permute-start.7) | collective-permute-done | bytes 131104 | tf_op jit(solution)/shard_map/ppermute | solution.py:528
  125.1 0.0 copy-done.5
  125.1 1.3 all-to-all-done.3.parts_ref
  126.4 0.2 summed_copies.1
  126.7 24.6 %all_to_all.26 = bf16[64,72,128]{2,1,0:T(8,128)(2,1)S(1)} all-to-all(bf16[64,72,128]{2,1,0:T(8,128)(2,1)S(1)} %summed_copies.1), channel_id=1, replica_groups=mesh['dp_0'=4,'dp_1'=2,'neg_0'=4,'neg_1'=2,'neg_2'=2] {'dp_0','dp_1','ne..., dimensions={0} | all-to-all | bytes 2359296 | tf_op jit(solution)/shard_map/all_to_all | solution.py:428
  151.3 3.1 %collective-permute-start.9 = (bf16[8,8,72,128]{3,2,1,0:T(8,128)(2,1)S(1)}, bf16[8,8,72,128]{3,2,1,0:T(8,128)(2,1)S(1)}, u32[]{:S(2)}, u32[]{:S(2)}) collective-permute-start(bf16[8,8,72,128]{3,2,1,0:T(8,128)(2,1)S(1)} %bitcast.26), channel_id=1, source_target_pairs={{0,1},{1,0},{2,3},{3,2},{4,5},{5,4},{6,7},{7,6},{8,9},{9,8},{10,11... | collective-permute-start | bytes 3538952 | tf_op jit(solution)/shard_map/ppermute | solution.py:656
  154.4 0.5 collective-permute-start.8
  154.9 0.5 slice.3
  156.1 1.5 own_rows.1._
  157.6 0.5 collective-permute-done.8
  158.1 0.6 bitcast_add_fusion.1
  158.7 0.0 collective-permute-done.9.other_ref
  158.7 1.9 %finish.1 = (f32[1024,1024]{1,0:T(8,128)}, f32[1024,128]{1,0:T(8,128)}, f32[1,1024]{1,0:T(1,128)}) custom-call(s32[1]{0:T(128)} %bitcast.core_ref, bf16[8,8,72,128]{3,2,1,0:T(8,128)(2,1)S(1)} %bitcast.28, bf16[8,8,72,128]{3,2,1,0:T(8,128)(2,1)S(1)} %collective-permute-done.9.other_ref, ...), custom_call_target="tpu_custom_call", output_to_operand_aliasing={{0}: (5, {})} | custom-call | flops 2097152 | bytes 4194304 | tf_op jit(solution)/shard_map/finish/pallas_call | solution.py:490
  (10 shorter events, 0.1 us)
Async XLA Ops:
  4.8 25.8 %all-to-all-start = ((bf16[8,520,128]{2,1,0:T(8,128)(2,1)}), bf16[8,520,128]{2,1,0:T(8,128)(2,1)S(1)}, u32[]{:S(2)}, u32[]{:S(2)}) async-start(bf16[8,520,128]{2,1,0:T(8,128)(2,1)} %passage_copies.1), calls=%async_computation | async-start | bytes 2129920 | tf_op jit(solution)/shard_map/all_to_all | solution.py:428
  11.7 1.8 %collective-permute-start = (bf16[1,136,128]{2,1,0:T(8,128)(2,1)S(1)}, bf16[1,136,128]{2,1,0:T(8,128)(2,1)S(1)}, u32[]{:S(2)}, u32[]{:S(2)}) collective-permute-start(bf16[1,136,128]{2,1,0:T(8,128)(2,1)S(1)} %bitcast.34), channel_id=1, source_target_pairs={{0,1},{1,0},{2,3},{3,2},{4,5},{5,4},{6,7},{7,6},{8,9},{9,8},{10,11... | collective-permute-start | bytes 104456 | tf_op jit(solution)/shard_map/ppermute | solution.py:542
  13.5 3.5 %collective-permute-start.1 = (bf16[2,136,128]{2,1,0:T(8,128)(2,1)S(1)}, bf16[2,136,128]{2,1,0:T(8,128)(2,1)S(1)}, u32[]{:S(2)}, u32[]{:S(2)}) collective-permute-start(bf16[2,136,128]{2,1,0:T(8,128)(2,1)S(1)} %pad_maximum_fusion.2), channel_id=1, source_target_pairs={{0,4},{4,0},{8,12},{12,8},{1,5},{5,1},{9,13},{13,9},{2,6},{6,2},{1... | collective-permute-start | bytes 208904 | tf_op jit(solution)/shard_map/ppermute | solution.py:542
  17.0 5.8 %collective-permute-start.2 = (bf16[4,136,128]{2,1,0:T(8,128)(2,1)S(1)}, bf16[4,136,128]{2,1,0:T(8,128)(2,1)S(1)}, u32[]{:S(2)}, u32[]{:S(2)}) collective-permute-start(bf16[4,136,128]{2,1,0:T(8,128)(2,1)S(1)} %pad_maximum_fusion.1), channel_id=1, source_target_pairs={{0,8},{4,12},{8,0},{12,4},{1,9},{5,13},{9,1},{13,5},{2,10},{6,14},... | collective-permute-start | bytes 417800 | tf_op jit(solution)/shard_map/ppermute | solution.py:542
  22.9 7.7 %collective-permute-start.3 = (bf16[8,136,128]{2,1,0:T(8,128)(2,1)S(1)}, bf16[8,136,128]{2,1,0:T(8,128)(2,1)S(1)}, u32[]{:S(2)}, u32[]{:S(2)}) collective-permute-start(bf16[8,136,128]{2,1,0:T(8,128)(2,1)S(1)} %pad_maximum_fusion.near_ref), channel_id=1, source_target_pairs={{0,2},{2,0},{1,3},{3,1},{4,6},{6,4},{5,7},{7,5},{8,10},{10,8},{9,1... | collective-permute-start | bytes 835592 | tf_op jit(solution)/shard_map/ppermute | solution.py:543
  67.6 5.1 %collective-permute-start.4 = (bf16[2,4,128,128]{3,2,1,0:T(8,128)(2,1)}, bf16[2,4,128,128]{3,2,1,0:T(8,128)(2,1)}, u32[]{:S(2)}, u32[]{:S(2)}) collective-permute-start(bf16[2,4,128,128]{3,2,1,0:T(8,128)(2,1)} %get-tuple-element.63), channel_id=1, source_target_pairs={{0,1},{1,0},{2,3},{3,2},{4,5},{5,4},{6,7},{7,6},{8,9},{9,8},{10,11... | collective-permute-start | bytes 786440 | tf_op jit(solution)/shard_map/ppermute | solution.py:528
  68.0 7.1 %copy-start = (bf16[1024,1024]{1,0:T(8,128)(2,1)S(1)}, bf16[1024,1024]{1,0:T(8,128)(2,1)}, u32[]{:S(2)}) copy-start(bf16[1024,1024]{1,0:T(8,128)(2,1)} %proj_ref.1) | copy-start | bytes 6291460
  68.0 21.7 %all-to-all-start.2 = ((bf16[8,520,128]{2,1,0:T(8,128)(2,1)}), bf16[8,520,128]{2,1,0:T(8,128)(2,1)S(1)}, u32[]{:S(2)}, u32[]{:S(2)}) async-start(bf16[8,520,128]{2,1,0:T(8,128)(2,1)} %get-tuple-element.59), calls=%async_computation.2 | async-start | bytes 2129920 | tf_op jit(solution)/shard_map/all_to_all | solution.py:428
  72.7 2.4 %copy-start.1 = (bf16[512,1024]{1,0:T(8,128)(2,1)S(1)}, bf16[512,1024]{1,0:T(8,128)(2,1)}, u32[]{:S(2)}) copy-start(bf16[512,1024]{1,0:T(8,128)(2,1)} %resid_ref) | copy-start | bytes 3145732
  73.9 15.1 %collective-permute-start.5 = (bf16[4,128,128]{2,1,0:T(8,128)(2,1)S(1)}, bf16[4,128,128]{2,1,0:T(8,128)(2,1)S(1)}, u32[]{:S(2)}, u32[]{:S(2)}) collective-permute-start(bf16[4,128,128]{2,1,0:T(8,128)(2,1)S(1)} %dynamic-slice_bitcast_fusion.1), channel_id=1, source_target_pairs={{0,2},{2,0},{1,3},{3,1},{4,6},{6,4},{5,7},{7,5},{8,10},{10,8},{9,1... | collective-permute-start | bytes 393224 | tf_op jit(solution)/shard_map/ppermute | solution.py:528
  75.2 1.2 copy-start.2
  76.4 13.4 %copy-start.3 = (bf16[1024,128]{1,0:T(8,128)(2,1)S(1)}, bf16[1024,128]{1,0:T(8,128)(2,1)}, u32[]{:S(2)}) copy-start(bf16[1024,128]{1,0:T(8,128)(2,1)} %colbert_ref.3) | copy-start | bytes 786436
  76.4 13.4 %copy-start.4 = (f32[1024]{0:T(1024)S(1)}, f32[1024]{0:T(1024)}, u32[]{:S(2)}) copy-start(f32[1024]{0:T(1024)} %param.16) | copy-start | bytes 12292
  93.9 3.4 %collective-permute-start.6 = (bf16[8,8,72,128]{3,2,1,0:T(8,128)(2,1)S(1)}, bf16[8,8,72,128]{3,2,1,0:T(8,128)(2,1)S(1)}, u32[]{:S(2)}, u32[]{:S(2)}) collective-permute-start(bf16[8,8,72,128]{3,2,1,0:T(8,128)(2,1)S(1)} %get-tuple-element.76), channel_id=1, source_target_pairs={{0,1},{1,0},{2,3},{3,2},{4,5},{5,4},{6,7},{7,6},{8,9},{9,8},{10,11... | collective-permute-start | bytes 3538952 | tf_op jit(solution)/shard_map/ppermute | solution.py:528
  98.6 27.8 %all-to-all-start.3 = ((bf16[64,72,128]{2,1,0:T(8,128)(2,1)}), bf16[64,72,128]{2,1,0:T(8,128)(2,1)S(1)}, u32[]{:S(2)}, u32[]{:S(2)}) async-start(bf16[64,72,128]{2,1,0:T(8,128)(2,1)} %bitcast.31), calls=%async_computation.3 | async-start | bytes 2359296 | tf_op jit(solution)/shard_map/all_to_all | solution.py:428
  108.1 17.0 %collective-permute-start.7 = (f32[2,128,128]{2,1,0:T(8,128)S(1)}, f32[2,128,128]{2,1,0:T(8,128)S(1)}, u32[]{:S(2)}, u32[]{:S(2)}) collective-permute-start(f32[2,128,128]{2,1,0:T(8,128)S(1)} %dynamic-slice_bitcast_fusion), channel_id=1, source_target_pairs={{0,8},{4,12},{8,0},{12,4},{1,9},{5,13},{9,1},{13,5},{2,10},{6,14},... | collective-permute-start | bytes 393224 | tf_op jit(solution)/shard_map/ppermute | solution.py:528
  110.7 14.4 %copy-start.5 = (f32[4,128,128]{2,1,0:T(8,128)S(1)}, f32[4,128,128]{2,1,0:T(8,128)}, u32[]{:S(2)}) copy-start(f32[4,128,128]{2,1,0:T(8,128)} %convert_add_fusion) | copy-start | bytes 786436
  151.3 7.4 %collective-permute-start.9 = (bf16[8,8,72,128]{3,2,1,0:T(8,128)(2,1)S(1)}, bf16[8,8,72,128]{3,2,1,0:T(8,128)(2,1)S(1)}, u32[]{:S(2)}, u32[]{:S(2)}) collective-permute-start(bf16[8,8,72,128]{3,2,1,0:T(8,128)(2,1)S(1)} %bitcast.26), channel_id=1, source_target_pairs={{0,1},{1,0},{2,3},{3,2},{4,5},{5,4},{6,7},{7,6},{8,9},{9,8},{10,11... | collective-permute-start | bytes 3538952 | tf_op jit(solution)/shard_map/ppermute | solution.py:656
  154.4 3.7 %collective-permute-start.8 = (f32[128,128]{1,0:T(8,128)S(1)}, f32[128,128]{1,0:T(8,128)S(1)}, u32[]{:S(2)}, u32[]{:S(2)}) collective-permute-start(f32[128,128]{1,0:T(8,128)S(1)} %dynamic-slice_bitcast_fusion.2), channel_id=1, source_target_pairs={{0,4},{4,0},{8,12},{12,8},{1,5},{5,1},{9,13},{13,9},{2,6},{6,2},{1... | collective-permute-start | bytes 196616 | tf_op jit(solution)/shard_map/ppermute | solution.py:528

commit v10 on v9

--- a/solution.py
+++ b/solution.py
@@ -636,7 +636,6 @@
     residual, kept, given = lax.optimization_barrier((residual, kept, given))
     early = early_rows(residual, context, out_proj)
     query_part = pair_summed(kept, given, CORE, SWAP, BF16)
-    query_part = halves_summed(query_part, "neg_1", SWAP, row_side, F32)
     passage_parts = exchange(passage_parts, DP)
     passage_parts, query_part, early = lax.optimization_barrier((passage_parts, query_part, early))
     normed, inv_std, context_t = early
@@ -645,12 +644,14 @@
     )
     half = pair_summed(kept, given, CORE, SWAP, BF16)
     context_grad = jnp.dot(residual_grad, out_proj.T, preferred_element_type=F32).astype(BF16)
+    query_part = halves_summed(query_part, "neg_1", SWAP, row_side, F32)
+    half, query_part = lax.optimization_barrier((half, query_part))
+    slabs = exchange(half.reshape(dp_size * cross_size, *half.shape[2:]), DP + CROSS)
+    slabs, context_grad = lax.optimization_barrier((slabs, context_grad))
+    half = exchange(summed_copies(slabs), DP + CROSS).reshape(half.shape)
+    half, query_part = lax.optimization_barrier((half, query_part))
     query_part = query_part.reshape(2, 2, *query_part.shape[1:])
     query_part = halves_summed(query_part, "neg_0", FAR, far_side, F32)
-    slabs = exchange(half.reshape(dp_size * cross_size, *half.shape[2:]), DP + CROSS)
-    slabs, context_grad, query_part = lax.optimization_barrier((slabs, context_grad, query_part))
-    half = exchange(summed_copies(slabs), DP + CROSS).reshape(half.shape)
-    half, query_part = lax.optimization_barrier((half, query_part))
     query_grad = halves_summed(query_part, "neg_0", NEAR, near_side, F32)
     query_grad = query_grad.reshape(query_dev, query_len, emb)
     other = lax.ppermute(half, CORE, SWAP)

time: 162 us -> 168 us (1.037)
  waiting for transfers between devices: 35 us -> 45.9 us
  starting transfers between devices: 36.7 us -> 32.1 us
  blocking collectives: 41.4 us -> 39.3 us
    all_to_all x3, waiting for transfers between devices: 1.3 us -> 23.3 us  [exchange(): return lax.all_to_all(pieces, axis, 0, 0, tiled=True)]
    ppermute x5, waiting for transfers between devices: 22.6 us -> 11.5 us  [pair_summed(): taken = lax.ppermute(given, axis, pairs)]
    all_to_all x3, starting transfers between devices: 20.1 us -> 16.2 us  [exchange(): return lax.all_to_all(pieces, axis, 0, 0, tiled=True)]
    all_to_all x2, blocking collectives: 41.4 us -> 39.3 us  [exchange(): return lax.all_to_all(pieces, axis, 0, 0, tiled=True)]
    unnamed x12 -> x18, local copies, waits for them, and re-layouts: 1.24 us -> 3.18 us
  transfers between devices with their start and end apart: 13 -> 13, of which waited for: 9 -> 8; matrix products, arithmetic and copies ran while one was open for 5% -> 4% of each run, Pallas kernels for 3% -> 3%
where the time goes in v10:
time: 168 us; the launch traced here: 167 us
  waiting for transfers between devices  45.9 us (27%)
  blocking collectives  39.3 us (23%)
  Pallas kernels  33.7 us (20%)
  starting transfers between devices  32.1 us (19%)
  other arithmetic  5.06 us (3%)
  local copies, waits for them, and re-layouts  3.79 us (2%)
  matrix products  3.49 us (2%)
  between operations  3.19 us (2%)
    all_to_all x2, blocking collectives, exchange(): return lax.all_to_all(pieces, axis, 0, 0, tiled=True)  39.3 us
    all_to_all x3, waiting for transfers between devices, exchange(): return lax.all_to_all(pieces, axis, 0, 0, tiled=True)  23.3 us
    all_to_all x3, starting transfers between devices, exchange(): return lax.all_to_all(pieces, axis, 0, 0, tiled=True)  16.2 us
    pallas_call x1, Pallas kernels, forward_tile(): pl.pallas_call(functools.partial(forward_kernel, query_len, group), name=...  14.1 us
    ppermute x5, waiting for transfers between devices, pair_summed(): taken = lax.ppermute(given, axis, pairs)  11.5 us
    pallas_call x1, Pallas kernels, backward_tile(): pl.pallas_call(functools.partial(backward_kernel, query_len, parts), name...  6.12 us
    ppermute x3, waiting for transfers between devices, query_gathered(): held = jnp.concatenate([held, lax.ppermute(held, axis, pairs)])  6.07 us
    ppermute x3, starting transfers between devices, query_gathered(): held = jnp.concatenate([held, lax.ppermute(held, axis, pairs)])  5.07 us
  transfers between devices with their start and end apart: 13, of which 8 were waited for; matrix products, arithmetic and copies ran while one was open for 4% of the time, Pallas kernels for 3%

profile of v10, /device:TPU:1, one launch (start us, length us, event | category | flops | bytes accessed | tf_op | source)
XLA Modules:
  0.0 166.5 jit_solution(16534550235328216215)
XLA Ops:
  1.3 0.7 select_reduce_fusion
  2.1 0.8 pad_maximum_fusion.3
  2.8 1.9 %passage_copies.1 = bf16[8,520,128]{2,1,0:T(8,128)(2,1)} custom-call(s32[1]{0:T(128)S(6)} %copy.18.length_ref, bf16[1,512,128]{2,1,0:T(8,128)(2,1)} %p_ref.1), custom_call_target="tpu_custom_call" | custom-call | tf_op jit(solution)/shard_map/passage_copies/pallas_call | solution.py:568
  4.8 6.9 %all-to-all-start = ((bf16[8,520,128]{2,1,0:T(8,128)(2,1)}), bf16[8,520,128]{2,1,0:T(8,128)(2,1)S(1)}, u32[]{:S(2)}, u32[]{:S(2)}) async-start(bf16[8,520,128]{2,1,0:T(8,128)(2,1)} %passage_copies.1), calls=%async_computation | async-start | bytes 2129920 | tf_op jit(solution)/shard_map/all_to_all | solution.py:428
  11.7 1.0 collective-permute-start
  12.6 0.9 collective-permute-done
  13.5 1.3 collective-permute-start.1
  14.8 2.2 %collective-permute-done.1 = bf16[2,136,128]{2,1,0:T(8,128)(2,1)S(1)} collective-permute-done((bf16[2,136,128]{2,1,0:T(8,128)(2,1)S(1)}, bf16[2,136,128]{2,1,0:T(8,128)(2,1)S(1)}, u32[]{:S(2)}, u32[]{:S(2)}) %collective-permute-start.1) | collective-permute-done | bytes 69664 | tf_op jit(solution)/shard_map/ppermute | solution.py:542
  17.0 2.8 %collective-permute-start.2 = (bf16[4,136,128]{2,1,0:T(8,128)(2,1)S(1)}, bf16[4,136,128]{2,1,0:T(8,128)(2,1)S(1)}, u32[]{:S(2)}, u32[]{:S(2)}) collective-permute-start(bf16[4,136,128]{2,1,0:T(8,128)(2,1)S(1)} %pad_maximum_fusion.1), channel_id=1, source_target_pairs={{0,8},{4,12},{8,0},{12,4},{1,9},{5,13},{9,1},{13,5},{2,10},{6,14},... | collective-permute-start | bytes 417800 | tf_op jit(solution)/shard_map/ppermute | solution.py:542
  19.9 3.0 %collective-permute-done.2 = bf16[4,136,128]{2,1,0:T(8,128)(2,1)S(1)} collective-permute-done((bf16[4,136,128]{2,1,0:T(8,128)(2,1)S(1)}, bf16[4,136,128]{2,1,0:T(8,128)(2,1)S(1)}, u32[]{:S(2)}, u32[]{:S(2)}) %collective-permute-start.2) | collective-permute-done | bytes 139296 | tf_op jit(solution)/shard_map/ppermute | solution.py:542
  22.9 2.7 %collective-permute-start.3 = (bf16[8,136,128]{2,1,0:T(8,128)(2,1)S(1)}, bf16[8,136,128]{2,1,0:T(8,128)(2,1)S(1)}, u32[]{:S(2)}, u32[]{:S(2)}) collective-permute-start(bf16[8,136,128]{2,1,0:T(8,128)(2,1)S(1)} %pad_maximum_fusion.near_ref), channel_id=1, source_target_pairs={{0,2},{2,0},{1,3},{3,1},{4,6},{6,4},{5,7},{7,5},{8,10},{10,8},{9,1... | collective-permute-start | bytes 835592 | tf_op jit(solution)/shard_map/ppermute | solution.py:543
  25.6 5.0 %collective-permute-done.3.far_ref = bf16[8,136,128]{2,1,0:T(8,128)(2,1)S(1)} collective-permute-done((bf16[8,136,128]{2,1,0:T(8,128)(2,1)S(1)}, bf16[8,136,128]{2,1,0:T(8,128)(2,1)S(1)}, u32[]{:S(2)}, u32[]{:S(2)}) %collective-permute-start.3) | collective-permute-done | bytes 278560 | tf_op jit(solution)/shard_map/ppermute | solution.py:543
  30.6 0.0 all-to-all-done.p_ref
  30.6 0.1 broadcast_in_dim.49.ids_ref
  30.7 14.1 %forward_tile.1 = (bf16[8,2048,512]{2,1,0:T(8,128)(2,1)S(1)}, f32[8,2048,128]{2,1,0:T(8,128)S(1)}, bf16[2048,128]{1,0:T(8,128)(2,1)S(1)}, f32[8,2048]{1,0:T(8,12...) custom-call(s32[1]{0:T(128)} %bitcast.1.flip_ref, bf16[8,136,128]{2,1,0:T(8,128)(2,1)S(1)} %pad_maximum_fusion.near_ref, ...), custom_call_target="tpu_custom_call" | custom-call | flops 4294967296 | bytes 33554432 | tf_op jit(solution)/shard_map/forward_tile/pallas_call | solution.py:147
  44.8 16.7 %all_to_all.25.stats_ref = f32[16,8,128]{2,1,0:T(8,128)S(1)} all-to-all(f32[16,8,128]{2,1,0:T(8,128)S(1)} %get-tuple-element.59), channel_id=1, replica_groups=mesh['dp_0'=4,'dp_1'=2,'neg_0'=4,'neg_1'=2,'neg_2'=2] {'neg_0','neg_1','..., dimensions={0} | all-to-all | bytes 131072 | tf_op jit(solution)/shard_map/all_to_all | solution.py:428
  61.5 6.1 %backward_tile.1 = (bf16[8,520,128]{2,1,0:T(8,128)(2,1)}, bf16[2,4,128,128]{3,2,1,0:T(8,128)(2,1)S(1)}, bf16[2,4,128,128]{3,2,1,0:T(8,128)(2,1)}) custom-call(s32[1]{0:T(128)} %bitcast.core_ref, bf16[2048,128]{1,0:T(8,128)(2,1)S(1)} %get-tuple-element.54.own_ref, bf16[8,2048,512]{2,1,0:T(8,128)(2,1)S(1)} %get-tuple-element.55.exp_ref, ...), custom_call_target="tpu_custom_call" | custom-call | flops 2147483648 | bytes 25165824 | tf_op jit(solution)/shard_map/backward_tile/pallas_call | solution.py:248
  67.6 0.0 copy-start.4
  67.6 0.7 copy-done.4
  68.3 0.0 copy-start
  68.3 4.7 %all-to-all-start.2 = ((bf16[8,520,128]{2,1,0:T(8,128)(2,1)}), bf16[8,520,128]{2,1,0:T(8,128)(2,1)S(1)}, u32[]{:S(2)}, u32[]{:S(2)}) async-start(bf16[8,520,128]{2,1,0:T(8,128)(2,1)} %get-tuple-element.60), calls=%async_computation.2 | async-start | bytes 2129920 | tf_op jit(solution)/shard_map/all_to_all | solution.py:428
  73.0 0.7 collective-permute-start.4
  73.7 0.0 copy-done
  73.7 0.0 copy-start.1
  73.7 1.2 copy-done.1
  74.9 0.0 copy-start.2
  74.9 1.2 copy-done.2
  76.2 0.0 copy-start.5
  76.2 0.0 copy-start.3
  76.2 0.0 copy-start.6
  76.2 3.9 %early_rows.1 = (f32[512,1024]{1,0:T(8,128)}, f32[512,128]{1,0:T(8,128)}, bf16[1024,512]{1,0:T(8,128)(2,1)}) custom-call(bf16[512,1024]{1,0:T(8,128)(2,1)S(1)} %copy-done.1, bf16[512,1024]{1,0:T(8,128)(2,1)S(1)} %copy-done.2, bf16[1024,1024]{1,0:T(8,128)(2,1)S(1)} %copy-done), custom_call_target="tpu_custom_call" | custom-call | flops 1073741824 | bytes 5242880 | tf_op jit(solution)/shard_map/early_rows/pallas_call | solution.py:284
  80.0 0.0 collective-permute-done.4
  80.1 0.0 copy-done.5
  80.1 0.8 add_convert_fusion.1
  80.8 7.5 %all-to-all-done.2.parts_ref = bf16[8,520,128]{2,1,0:T(8,128)(2,1)S(1)} async-done(((bf16[8,520,128]{2,1,0:T(8,128)(2,1)}), bf16[8,520,128]{2,1,0:T(8,128)(2,1)S(1)}, u32[]{:S(2)}, u32[]{:S(2)}) %all-to-all-start.2) | async-done | bytes 1064992 | tf_op jit(solution)/shard_map/all_to_all | solution.py:428
  88.4 0.0 copy-done.3
  88.4 0.0 copy-done.6
  88.4 0.0 copy-start.7
  88.4 4.1 %late_rows.1 = (bf16[512,1024]{1,0:T(8,128)(2,1)}, bf16[8,8,72,128]{3,2,1,0:T(8,128)(2,1)S(1)}, bf16[8,8,72,128]{3,2,1,0:T(8,128)(2,1)S(1)}, f32[8,128]{1,0:T(8,128)S(1)}) custom-call(s32[1]{0:T(128)} %bitcast.core_ref, bf16[8,520,128]{2,1,0:T(8,128)(2,1)S(1)} %all-to-all-done.2.parts_ref, f32[512,1024]{1,0:T(8,128)} %get-tuple-element.70.normed_far, ...), custom_call_target="tpu_custom_call" | custom-call | flops 1342177280 | bytes 7340032 | tf_op jit(solution)/shard_map/late_rows/pallas_call | solution.py:393
  92.5 1.6 collective-permute-start.5
  94.1 0.0 copy-done.7
  94.1 1.1 collective-permute-start.6
  95.2 5.6 %collective-permute-done.6 = bf16[4,128,128]{2,1,0:T(8,128)(2,1)S(1)} collective-permute-done((bf16[4,128,128]{2,1,0:T(8,128)(2,1)S(1)}, bf16[4,128,128]{2,1,0:T(8,128)(2,1)S(1)}, u32[]{:S(2)}, u32[]{:S(2)}) %collective-permute-start.6) | collective-permute-done | bytes 131104 | tf_op jit(solution)/shard_map/ppermute | solution.py:528
  100.8 0.7 convert_add_fusion
  101.6 0.0 collective-permute-done.5
  101.6 1.3 add_convert_fusion
  102.9 4.7 %all-to-all-start.3 = ((bf16[64,72,128]{2,1,0:T(8,128)(2,1)}), bf16[64,72,128]{2,1,0:T(8,128)(2,1)S(1)}, u32[]{:S(2)}, u32[]{:S(2)}) async-start(bf16[64,72,128]{2,1,0:T(8,128)(2,1)} %bitcast.31), calls=%async_computation.3 | async-start | bytes 2359296 | tf_op jit(solution)/shard_map/all_to_all | solution.py:428
  107.5 3.5 %convolution_convert_fusion = bf16[512,1024]{1,0:T(8,128)(2,1)} fusion(bf16[512,1024]{1,0:T(8,128)(2,1)} %get-tuple-element.45, bf16[1024,1024]{1,0:T(8,128)(2,1)S(1)} %copy-done), kind=kOutput, calls=%fused_computation.1 | convolution fusion | flops 1074266112 | bytes 4194304 | tf_op jit(solution)/shard_map/dot_general | solution.py:646
  111.0 15.8 %all-to-all-done.3.parts_ref = bf16[64,72,128]{2,1,0:T(8,128)(2,1)S(1)} async-done(((bf16[64,72,128]{2,1,0:T(8,128)(2,1)}), bf16[64,72,128]{2,1,0:T(8,128)(2,1)S(1)}, u32[]{:S(2)}, u32[]{:S(2)}) %all-to-all-start.3) | async-done | bytes 1179680 | tf_op jit(solution)/shard_map/all_to_all | solution.py:428
  126.8 0.2 summed_copies.1
  127.0 0.0 copy-start.8
  127.0 22.5 %all_to_all.26 = bf16[64,72,128]{2,1,0:T(8,128)(2,1)S(1)} all-to-all(bf16[64,72,128]{2,1,0:T(8,128)(2,1)S(1)} %summed_copies.1), channel_id=1, replica_groups=mesh['dp_0'=4,'dp_1'=2,'neg_0'=4,'neg_1'=2,'neg_2'=2] {'dp_0','dp_1','ne..., dimensions={0} | all-to-all | bytes 2359296 | tf_op jit(solution)/shard_map/all_to_all | solution.py:428
  149.6 3.3 %collective-permute-start.9 = (bf16[8,8,72,128]{3,2,1,0:T(8,128)(2,1)S(1)}, bf16[8,8,72,128]{3,2,1,0:T(8,128)(2,1)S(1)}, u32[]{:S(2)}, u32[]{:S(2)}) collective-permute-start(bf16[8,8,72,128]{3,2,1,0:T(8,128)(2,1)S(1)} %bitcast.26), channel_id=1, source_target_pairs={{0,1},{1,0},{2,3},{3,2},{4,5},{5,4},{6,7},{7,6},{8,9},{9,8},{10,11... | collective-permute-start | bytes 3538952 | tf_op jit(solution)/shard_map/ppermute | solution.py:657
  152.9 0.0 copy-done.8
  152.9 0.8 collective-permute-start.7
  153.7 5.9 %collective-permute-done.7 = f32[2,128,128]{2,1,0:T(8,128)S(1)} collective-permute-done((f32[2,128,128]{2,1,0:T(8,128)S(1)}, f32[2,128,128]{2,1,0:T(8,128)S(1)}, u32[]{:S(2)}, u32[]{:S(2)}) %collective-permute-start.7) | collective-permute-done | bytes 131104 | tf_op jit(solution)/shard_map/ppermute | solution.py:528
  159.7 0.6 collective-permute-start.8
  160.2 0.5 slice.3
  161.4 1.5 own_rows.1._
  162.9 0.0 collective-permute-done.8
  162.9 0.6 bitcast_add_fusion.1
  163.5 0.0 collective-permute-done.9.other_ref
  163.5 1.9 %finish.1 = (f32[1024,1024]{1,0:T(8,128)}, f32[1024,128]{1,0:T(8,128)}, f32[1,1024]{1,0:T(1,128)}) custom-call(s32[1]{0:T(128)} %bitcast.core_ref, bf16[8,8,72,128]{3,2,1,0:T(8,128)(2,1)S(1)} %bitcast.28, bf16[8,8,72,128]{3,2,1,0:T(8,128)(2,1)S(1)} %collective-permute-done.9.other_ref, ...), custom_call_target="tpu_custom_call", output_to_operand_aliasing={{0}: (5, {})} | custom-call | flops 2097152 | bytes 4194304 | tf_op jit(solution)/shard_map/finish/pallas_call | solution.py:490
  (11 shorter events, 0.1 us)
Async XLA Ops:
  4.8 25.8 %all-to-all-start = ((bf16[8,520,128]{2,1,0:T(8,128)(2,1)}), bf16[8,520,128]{2,1,0:T(8,128)(2,1)S(1)}, u32[]{:S(2)}, u32[]{:S(2)}) async-start(bf16[8,520,128]{2,1,0:T(8,128)(2,1)} %passage_copies.1), calls=%async_computation | async-start | bytes 2129920 | tf_op jit(solution)/shard_map/all_to_all | solution.py:428
  11.7 1.8 %collective-permute-start = (bf16[1,136,128]{2,1,0:T(8,128)(2,1)S(1)}, bf16[1,136,128]{2,1,0:T(8,128)(2,1)S(1)}, u32[]{:S(2)}, u32[]{:S(2)}) collective-permute-start(bf16[1,136,128]{2,1,0:T(8,128)(2,1)S(1)} %bitcast.34), channel_id=1, source_target_pairs={{0,1},{1,0},{2,3},{3,2},{4,5},{5,4},{6,7},{7,6},{8,9},{9,8},{10,11... | collective-permute-start | bytes 104456 | tf_op jit(solution)/shard_map/ppermute | solution.py:542
  13.5 3.5 %collective-permute-start.1 = (bf16[2,136,128]{2,1,0:T(8,128)(2,1)S(1)}, bf16[2,136,128]{2,1,0:T(8,128)(2,1)S(1)}, u32[]{:S(2)}, u32[]{:S(2)}) collective-permute-start(bf16[2,136,128]{2,1,0:T(8,128)(2,1)S(1)} %pad_maximum_fusion.2), channel_id=1, source_target_pairs={{0,4},{4,0},{8,12},{12,8},{1,5},{5,1},{9,13},{13,9},{2,6},{6,2},{1... | collective-permute-start | bytes 208904 | tf_op jit(solution)/shard_map/ppermute | solution.py:542
  17.0 5.8 %collective-permute-start.2 = (bf16[4,136,128]{2,1,0:T(8,128)(2,1)S(1)}, bf16[4,136,128]{2,1,0:T(8,128)(2,1)S(1)}, u32[]{:S(2)}, u32[]{:S(2)}) collective-permute-start(bf16[4,136,128]{2,1,0:T(8,128)(2,1)S(1)} %pad_maximum_fusion.1), channel_id=1, source_target_pairs={{0,8},{4,12},{8,0},{12,4},{1,9},{5,13},{9,1},{13,5},{2,10},{6,14},... | collective-permute-start | bytes 417800 | tf_op jit(solution)/shard_map/ppermute | solution.py:542
  22.9 7.7 %collective-permute-start.3 = (bf16[8,136,128]{2,1,0:T(8,128)(2,1)S(1)}, bf16[8,136,128]{2,1,0:T(8,128)(2,1)S(1)}, u32[]{:S(2)}, u32[]{:S(2)}) collective-permute-start(bf16[8,136,128]{2,1,0:T(8,128)(2,1)S(1)} %pad_maximum_fusion.near_ref), channel_id=1, source_target_pairs={{0,2},{2,0},{1,3},{3,1},{4,6},{6,4},{5,7},{7,5},{8,10},{10,8},{9,1... | collective-permute-start | bytes 835592 | tf_op jit(solution)/shard_map/ppermute | solution.py:543
  67.6 0.7 copy-start.4
  68.3 5.4 %copy-start = (bf16[1024,1024]{1,0:T(8,128)(2,1)S(1)}, bf16[1024,1024]{1,0:T(8,128)(2,1)}, u32[]{:S(2)}) copy-start(bf16[1024,1024]{1,0:T(8,128)(2,1)} %proj_ref.1) | copy-start | bytes 6291460
  68.3 20.0 %all-to-all-start.2 = ((bf16[8,520,128]{2,1,0:T(8,128)(2,1)}), bf16[8,520,128]{2,1,0:T(8,128)(2,1)S(1)}, u32[]{:S(2)}, u32[]{:S(2)}) async-start(bf16[8,520,128]{2,1,0:T(8,128)(2,1)} %get-tuple-element.60), calls=%async_computation.2 | async-start | bytes 2129920 | tf_op jit(solution)/shard_map/all_to_all | solution.py:428
  73.0 7.0 %collective-permute-start.4 = (bf16[2,4,128,128]{3,2,1,0:T(8,128)(2,1)}, bf16[2,4,128,128]{3,2,1,0:T(8,128)(2,1)S(1)}, u32[]{:S(2)}, u32[]{:S(2)}) collective-permute-start(bf16[2,4,128,128]{3,2,1,0:T(8,128)(2,1)} %get-tuple-element.64), channel_id=1, source_target_pairs={{0,1},{1,0},{2,3},{3,2},{4,5},{5,4},{6,7},{7,6},{8,9},{9,8},{10,11... | collective-permute-start | bytes 786440 | tf_op jit(solution)/shard_map/ppermute | solution.py:528
  73.7 1.2 copy-start.1
  74.9 1.2 copy-start.2
  76.2 3.9 %copy-start.5 = (bf16[2,4,128,128]{3,2,1,0:T(8,128)(2,1)S(1)}, bf16[2,4,128,128]{3,2,1,0:T(8,128)(2,1)}, u32[]{:S(2)}) copy-start(bf16[2,4,128,128]{3,2,1,0:T(8,128)(2,1)} %copy-done.4) | copy-start | bytes 786436
  76.2 12.2 %copy-start.3 = (bf16[1024,128]{1,0:T(8,128)(2,1)S(1)}, bf16[1024,128]{1,0:T(8,128)(2,1)}, u32[]{:S(2)}) copy-start(bf16[1024,128]{1,0:T(8,128)(2,1)} %colbert_ref.3) | copy-start | bytes 786436
  76.2 12.2 %copy-start.6 = (f32[1024]{0:T(1024)S(1)}, f32[1024]{0:T(1024)}, u32[]{:S(2)}) copy-start(f32[1024]{0:T(1024)} %param.16) | copy-start | bytes 12292
  88.4 5.8 %copy-start.7 = (bf16[2,4,128,128]{3,2,1,0:T(8,128)(2,1)S(1)}, bf16[2,4,128,128]{3,2,1,0:T(8,128)(2,1)}, u32[]{:S(2)}) copy-start(bf16[2,4,128,128]{3,2,1,0:T(8,128)(2,1)} %add_convert_fusion.1) | copy-start | bytes 786436
  92.5 9.1 %collective-permute-start.5 = (bf16[8,8,72,128]{3,2,1,0:T(8,128)(2,1)S(1)}, bf16[8,8,72,128]{3,2,1,0:T(8,128)(2,1)S(1)}, u32[]{:S(2)}, u32[]{:S(2)}) collective-permute-start(bf16[8,8,72,128]{3,2,1,0:T(8,128)(2,1)S(1)} %get-tuple-element.75), channel_id=1, source_target_pairs={{0,1},{1,0},{2,3},{3,2},{4,5},{5,4},{6,7},{7,6},{8,9},{9,8},{10,11... | collective-permute-start | bytes 3538952 | tf_op jit(solution)/shard_map/ppermute | solution.py:528
  94.1 6.7 %collective-permute-start.6 = (bf16[4,128,128]{2,1,0:T(8,128)(2,1)S(1)}, bf16[4,128,128]{2,1,0:T(8,128)(2,1)S(1)}, u32[]{:S(2)}, u32[]{:S(2)}) collective-permute-start(bf16[4,128,128]{2,1,0:T(8,128)(2,1)S(1)} %dynamic-slice_bitcast_fusion.1), channel_id=1, source_target_pairs={{0,2},{2,0},{1,3},{3,1},{4,6},{6,4},{5,7},{7,5},{8,10},{10,8},{9,1... | collective-permute-start | bytes 393224 | tf_op jit(solution)/shard_map/ppermute | solution.py:528
  102.9 23.9 %all-to-all-start.3 = ((bf16[64,72,128]{2,1,0:T(8,128)(2,1)}), bf16[64,72,128]{2,1,0:T(8,128)(2,1)S(1)}, u32[]{:S(2)}, u32[]{:S(2)}) async-start(bf16[64,72,128]{2,1,0:T(8,128)(2,1)} %bitcast.31), calls=%async_computation.3 | async-start | bytes 2359296 | tf_op jit(solution)/shard_map/all_to_all | solution.py:428
  127.0 25.9 %copy-start.8 = (f32[4,128,128]{2,1,0:T(8,128)S(1)}, f32[4,128,128]{2,1,0:T(8,128)}, u32[]{:S(2)}) copy-start(f32[4,128,128]{2,1,0:T(8,128)} %convert_add_fusion) | copy-start | bytes 786436
  149.6 14.0 %collective-permute-start.9 = (bf16[8,8,72,128]{3,2,1,0:T(8,128)(2,1)S(1)}, bf16[8,8,72,128]{3,2,1,0:T(8,128)(2,1)S(1)}, u32[]{:S(2)}, u32[]{:S(2)}) collective-permute-start(bf16[8,8,72,128]{3,2,1,0:T(8,128)(2,1)S(1)} %bitcast.26), channel_id=1, source_target_pairs={{0,1},{1,0},{2,3},{3,2},{4,5},{5,4},{6,7},{7,6},{8,9},{9,8},{10,11... | collective-permute-start | bytes 3538952 | tf_op jit(solution)/shard_map/ppermute | solution.py:657
  152.9 6.7 %collective-permute-start.7 = (f32[2,128,128]{2,1,0:T(8,128)S(1)}, f32[2,128,128]{2,1,0:T(8,128)S(1)}, u32[]{:S(2)}, u32[]{:S(2)}) collective-permute-start(f32[2,128,128]{2,1,0:T(8,128)S(1)} %dynamic-slice_bitcast_fusion), channel_id=1, source_target_pairs={{0,8},{4,12},{8,0},{12,4},{1,9},{5,13},{9,1},{13,5},{2,10},{6,14},... | collective-permute-start | bytes 393224 | tf_op jit(solution)/shard_map/ppermute | solution.py:528
  159.7 3.2 %collective-permute-start.8 = (f32[128,128]{1,0:T(8,128)S(1)}, f32[128,128]{1,0:T(8,128)S(1)}, u32[]{:S(2)}, u32[]{:S(2)}) collective-permute-start(f32[128,128]{1,0:T(8,128)S(1)} %dynamic-slice_bitcast_fusion.2), channel_id=1, source_target_pairs={{0,4},{4,0},{8,12},{12,8},{1,5},{5,1},{9,13},{13,9},{2,6},{6,2},{1... | collective-permute-start | bytes 196616 | tf_op jit(solution)/shard_map/ppermute | solution.py:528

commit v11 on v9

--- a/solution.py
+++ b/solution.py
@@ -636,7 +636,7 @@
     residual, kept, given = lax.optimization_barrier((residual, kept, given))
     early = early_rows(residual, context, out_proj)
     query_part = pair_summed(kept, given, CORE, SWAP, BF16)
-    query_part = halves_summed(query_part, "neg_1", SWAP, row_side, F32)
+    query_part = halves_summed(query_part, "neg_1", SWAP, row_side, BF16)
     passage_parts = exchange(passage_parts, DP)
     passage_parts, query_part, early = lax.optimization_barrier((passage_parts, query_part, early))
     normed, inv_std, context_t = early

time: 162 us -> 161 us (level)
  blocking collectives: 41.4 us -> 39.5 us
    all_to_all x2, blocking collectives: 41.4 us -> 39.5 us  [exchange(): return lax.all_to_all(pieces, axis, 0, 0, tiled=True)]
where the time goes in v11:
time: 161 us; the launch traced here: 160 us
  blocking collectives  39.5 us (25%)
  starting transfers between devices  37 us (23%)
  waiting for transfers between devices  35.2 us (22%)
  Pallas kernels  33.7 us (21%)
  other arithmetic  5.34 us (3%)
  matrix products  3.52 us (2%)
  between operations  3.19 us (2%)
  local copies, waits for them, and re-layouts  2.7 us (2%)
    all_to_all x2, blocking collectives, exchange(): return lax.all_to_all(pieces, axis, 0, 0, tiled=True)  39.5 us
    ppermute x5, waiting for transfers between devices, pair_summed(): taken = lax.ppermute(given, axis, pairs)  21.4 us
    all_to_all x3, starting transfers between devices, exchange(): return lax.all_to_all(pieces, axis, 0, 0, tiled=True)  20.1 us
    pallas_call x1, Pallas kernels, forward_tile(): pl.pallas_call(functools.partial(forward_kernel, query_len, group), name=...  14.1 us
    pallas_call x1, Pallas kernels, backward_tile(): pl.pallas_call(functools.partial(backward_kernel, query_len, parts), name...  6.12 us
    ppermute x3, waiting for transfers between devices, query_gathered(): held = jnp.concatenate([held, lax.ppermute(held, axis, pairs)])  6.07 us
    ppermute x5, starting transfers between devices, pair_summed(): taken = lax.ppermute(given, axis, pairs)  5.64 us
    ppermute x3, starting transfers between devices, query_gathered(): held = jnp.concatenate([held, lax.ppermute(held, axis, pairs)])  5.07 us
  transfers between devices with their start and end apart: 13, of which 9 were waited for; matrix products, arithmetic and copies ran while one was open for 5% of the time, Pallas kernels for 3%

profile of v11, /device:TPU:1, one launch (start us, length us, event | category | flops | bytes accessed | tf_op | source)
XLA Modules:
  0.0 160.1 jit_solution(1849097460917524395)
XLA Ops:
  1.3 0.7 select_reduce_fusion
  2.1 0.8 pad_maximum_fusion.3
  2.8 1.9 %passage_copies.1 = bf16[8,520,128]{2,1,0:T(8,128)(2,1)} custom-call(s32[1]{0:T(128)S(6)} %copy.18.length_ref, bf16[1,512,128]{2,1,0:T(8,128)(2,1)} %p_ref.1), custom_call_target="tpu_custom_call" | custom-call | tf_op jit(solution)/shard_map/passage_copies/pallas_call | solution.py:568
  4.8 6.9 %all-to-all-start = ((bf16[8,520,128]{2,1,0:T(8,128)(2,1)}), bf16[8,520,128]{2,1,0:T(8,128)(2,1)S(1)}, u32[]{:S(2)}, u32[]{:S(2)}) async-start(bf16[8,520,128]{2,1,0:T(8,128)(2,1)} %passage_copies.1), calls=%async_computation | async-start | bytes 2129920 | tf_op jit(solution)/shard_map/all_to_all | solution.py:428
  11.7 1.0 collective-permute-start
  12.6 0.9 collective-permute-done
  13.5 1.3 collective-permute-start.1
  14.8 2.2 %collective-permute-done.1 = bf16[2,136,128]{2,1,0:T(8,128)(2,1)S(1)} collective-permute-done((bf16[2,136,128]{2,1,0:T(8,128)(2,1)S(1)}, bf16[2,136,128]{2,1,0:T(8,128)(2,1)S(1)}, u32[]{:S(2)}, u32[]{:S(2)}) %collective-permute-start.1) | collective-permute-done | bytes 69664 | tf_op jit(solution)/shard_map/ppermute | solution.py:542
  17.0 2.8 %collective-permute-start.2 = (bf16[4,136,128]{2,1,0:T(8,128)(2,1)S(1)}, bf16[4,136,128]{2,1,0:T(8,128)(2,1)S(1)}, u32[]{:S(2)}, u32[]{:S(2)}) collective-permute-start(bf16[4,136,128]{2,1,0:T(8,128)(2,1)S(1)} %pad_maximum_fusion.1), channel_id=1, source_target_pairs={{0,8},{4,12},{8,0},{12,4},{1,9},{5,13},{9,1},{13,5},{2,10},{6,14},... | collective-permute-start | bytes 417800 | tf_op jit(solution)/shard_map/ppermute | solution.py:542
  19.9 3.0 %collective-permute-done.2 = bf16[4,136,128]{2,1,0:T(8,128)(2,1)S(1)} collective-permute-done((bf16[4,136,128]{2,1,0:T(8,128)(2,1)S(1)}, bf16[4,136,128]{2,1,0:T(8,128)(2,1)S(1)}, u32[]{:S(2)}, u32[]{:S(2)}) %collective-permute-start.2) | collective-permute-done | bytes 139296 | tf_op jit(solution)/shard_map/ppermute | solution.py:542
  22.9 2.7 %collective-permute-start.3 = (bf16[8,136,128]{2,1,0:T(8,128)(2,1)S(1)}, bf16[8,136,128]{2,1,0:T(8,128)(2,1)S(1)}, u32[]{:S(2)}, u32[]{:S(2)}) collective-permute-start(bf16[8,136,128]{2,1,0:T(8,128)(2,1)S(1)} %pad_maximum_fusion.near_ref), channel_id=1, source_target_pairs={{0,2},{2,0},{1,3},{3,1},{4,6},{6,4},{5,7},{7,5},{8,10},{10,8},{9,1... | collective-permute-start | bytes 835592 | tf_op jit(solution)/shard_map/ppermute | solution.py:543
  25.6 5.0 %collective-permute-done.3.far_ref = bf16[8,136,128]{2,1,0:T(8,128)(2,1)S(1)} collective-permute-done((bf16[8,136,128]{2,1,0:T(8,128)(2,1)S(1)}, bf16[8,136,128]{2,1,0:T(8,128)(2,1)S(1)}, u32[]{:S(2)}, u32[]{:S(2)}) %collective-permute-start.3) | collective-permute-done | bytes 278560 | tf_op jit(solution)/shard_map/ppermute | solution.py:543
  30.6 0.0 all-to-all-done.p_ref
  30.6 0.1 broadcast_in_dim.49.ids_ref
  30.7 14.1 %forward_tile.1 = (bf16[8,2048,512]{2,1,0:T(8,128)(2,1)S(1)}, f32[8,2048,128]{2,1,0:T(8,128)S(1)}, bf16[2048,128]{1,0:T(8,128)(2,1)S(1)}, f32[8,2048]{1,0:T(8,12...) custom-call(s32[1]{0:T(128)} %bitcast.1.flip_ref, bf16[8,136,128]{2,1,0:T(8,128)(2,1)S(1)} %pad_maximum_fusion.near_ref, ...), custom_call_target="tpu_custom_call" | custom-call | flops 4294967296 | bytes 33554432 | tf_op jit(solution)/shard_map/forward_tile/pallas_call | solution.py:147
  44.8 16.7 %all_to_all.25.stats_ref = f32[16,8,128]{2,1,0:T(8,128)S(1)} all-to-all(f32[16,8,128]{2,1,0:T(8,128)S(1)} %get-tuple-element.58), channel_id=1, replica_groups=mesh['dp_0'=4,'dp_1'=2,'neg_0'=4,'neg_1'=2,'neg_2'=2] {'neg_0','neg_1','..., dimensions={0} | all-to-all | bytes 131072 | tf_op jit(solution)/shard_map/all_to_all | solution.py:428
  61.5 6.1 %backward_tile.1 = (bf16[8,520,128]{2,1,0:T(8,128)(2,1)}, bf16[2,4,128,128]{3,2,1,0:T(8,128)(2,1)S(1)}, bf16[2,4,128,128]{3,2,1,0:T(8,128)(2,1)}) custom-call(s32[1]{0:T(128)} %bitcast.core_ref, bf16[2048,128]{1,0:T(8,128)(2,1)S(1)} %get-tuple-element.53.own_ref, bf16[8,2048,512]{2,1,0:T(8,128)(2,1)S(1)} %get-tuple-element.54.exp_ref, ...), custom_call_target="tpu_custom_call" | custom-call | flops 2147483648 | bytes 25165824 | tf_op jit(solution)/shard_map/backward_tile/pallas_call | solution.py:248
  67.6 0.4 collective-permute-start.4
  68.0 0.0 copy-start
  68.0 4.7 %all-to-all-start.2 = ((bf16[8,520,128]{2,1,0:T(8,128)(2,1)}), bf16[8,520,128]{2,1,0:T(8,128)(2,1)S(1)}, u32[]{:S(2)}, u32[]{:S(2)}) async-start(bf16[8,520,128]{2,1,0:T(8,128)(2,1)} %get-tuple-element.59), calls=%async_computation.2 | async-start | bytes 2129920 | tf_op jit(solution)/shard_map/all_to_all | solution.py:428
  72.7 0.0 copy-start.1
  72.7 0.0 collective-permute-done.4
  72.7 1.1 add_convert_fusion.1
  73.9 1.3 collective-permute-start.5
  75.2 0.0 copy-done
  75.2 0.0 copy-done.1
  75.2 0.0 copy-start.2
  75.2 1.2 copy-done.2
  76.4 0.0 copy-start.3
  76.4 0.0 copy-start.4
  76.4 3.9 %early_rows.1 = (f32[512,1024]{1,0:T(8,128)}, f32[512,128]{1,0:T(8,128)}, bf16[1024,512]{1,0:T(8,128)(2,1)}) custom-call(bf16[512,1024]{1,0:T(8,128)(2,1)S(1)} %copy-done.1, bf16[512,1024]{1,0:T(8,128)(2,1)S(1)} %copy-done.2, bf16[1024,1024]{1,0:T(8,128)(2,1)S(1)} %copy-done), custom_call_target="tpu_custom_call" | custom-call | flops 1073741824 | bytes 5242880 | tf_op jit(solution)/shard_map/early_rows/pallas_call | solution.py:284
  80.2 8.8 %collective-permute-done.5 = bf16[4,128,128]{2,1,0:T(8,128)(2,1)S(1)} collective-permute-done((bf16[4,128,128]{2,1,0:T(8,128)(2,1)S(1)}, bf16[4,128,128]{2,1,0:T(8,128)(2,1)S(1)}, u32[]{:S(2)}, u32[]{:S(2)}) %collective-permute-start.5) | collective-permute-done | bytes 131104 | tf_op jit(solution)/shard_map/ppermute | solution.py:528
  89.0 0.7 fusion
  89.7 0.0 all-to-all-done.2.parts_ref
  89.7 0.0 copy-done.3
  89.7 0.0 copy-done.4
  89.7 4.1 %late_rows.1 = (bf16[512,1024]{1,0:T(8,128)(2,1)}, bf16[8,8,72,128]{3,2,1,0:T(8,128)(2,1)S(1)}, bf16[8,8,72,128]{3,2,1,0:T(8,128)(2,1)S(1)}, f32[8,128]{1,0:T(8,128)S(1)}) custom-call(s32[1]{0:T(128)} %bitcast.core_ref, bf16[8,520,128]{2,1,0:T(8,128)(2,1)S(1)} %all-to-all-done.2.parts_ref, f32[512,1024]{1,0:T(8,128)} %get-tuple-element.71.normed_far, ...), custom_call_target="tpu_custom_call" | custom-call | flops 1342177280 | bytes 7340032 | tf_op jit(solution)/shard_map/late_rows/pallas_call | solution.py:393
  93.9 0.9 collective-permute-start.6
  94.8 2.5 %collective-permute-done.6 = bf16[8,8,72,128]{3,2,1,0:T(8,128)(2,1)S(1)} collective-permute-done((bf16[8,8,72,128]{3,2,1,0:T(8,128)(2,1)S(1)}, bf16[8,8,72,128]{3,2,1,0:T(8,128)(2,1)S(1)}, u32[]{:S(2)}, u32[]{:S(2)}) %collective-permute-start.6) | collective-permute-done | bytes 1179680 | tf_op jit(solution)/shard_map/ppermute | solution.py:528
  97.3 1.3 add_convert_fusion
  98.6 8.5 %all-to-all-start.3 = ((bf16[64,72,128]{2,1,0:T(8,128)(2,1)}), bf16[64,72,128]{2,1,0:T(8,128)(2,1)S(1)}, u32[]{:S(2)}, u32[]{:S(2)}) async-start(bf16[64,72,128]{2,1,0:T(8,128)(2,1)} %bitcast.32), calls=%async_computation.3 | async-start | bytes 2359296 | tf_op jit(solution)/shard_map/all_to_all | solution.py:428
  107.1 0.9 dynamic-slice_bitcast_fusion.2
  108.0 2.5 %collective-permute-start.7 = (bf16[2,128,128]{2,1,0:T(8,128)(2,1)S(1)}, bf16[2,128,128]{2,1,0:T(8,128)(2,1)S(1)}, u32[]{:S(2)}, u32[]{:S(2)}) collective-permute-start(bf16[2,128,128]{2,1,0:T(8,128)(2,1)S(1)} %dynamic-slice_bitcast_fusion.2), channel_id=1, source_target_pairs={{0,8},{4,12},{8,0},{12,4},{1,9},{5,13},{9,1},{13,5},{2,10},{6,14},... | collective-permute-start | bytes 196616 | tf_op jit(solution)/shard_map/ppermute | solution.py:528
  110.5 0.0 copy-start.5
  110.5 3.5 %convolution_convert_fusion = bf16[512,1024]{1,0:T(8,128)(2,1)} fusion(bf16[512,1024]{1,0:T(8,128)(2,1)} %get-tuple-element.44, bf16[1024,1024]{1,0:T(8,128)(2,1)S(1)} %copy-done), kind=kOutput, calls=%fused_computation.1 | convolution fusion | flops 1074266112 | bytes 4194304 | tf_op jit(solution)/shard_map/dot_general | solution.py:647
  114.0 9.6 %collective-permute-done.7 = bf16[2,128,128]{2,1,0:T(8,128)(2,1)S(1)} collective-permute-done((bf16[2,128,128]{2,1,0:T(8,128)(2,1)S(1)}, bf16[2,128,128]{2,1,0:T(8,128)(2,1)S(1)}, u32[]{:S(2)}, u32[]{:S(2)}) %collective-permute-start.7) | collective-permute-done | bytes 65568 | tf_op jit(solution)/shard_map/ppermute | solution.py:528
  123.7 0.0 copy-done.5
  123.7 2.7 %all-to-all-done.3.parts_ref = bf16[64,72,128]{2,1,0:T(8,128)(2,1)S(1)} async-done(((bf16[64,72,128]{2,1,0:T(8,128)(2,1)}), bf16[64,72,128]{2,1,0:T(8,128)(2,1)S(1)}, u32[]{:S(2)}, u32[]{:S(2)}) %all-to-all-start.3) | async-done | bytes 1179680 | tf_op jit(solution)/shard_map/all_to_all | solution.py:428
  126.4 0.2 summed_copies.1
  126.6 22.8 %all_to_all.26 = bf16[64,72,128]{2,1,0:T(8,128)(2,1)S(1)} all-to-all(bf16[64,72,128]{2,1,0:T(8,128)(2,1)S(1)} %summed_copies.1), channel_id=1, replica_groups=mesh['dp_0'=4,'dp_1'=2,'neg_0'=4,'neg_1'=2,'neg_2'=2] {'dp_0','dp_1','ne..., dimensions={0} | all-to-all | bytes 2359296 | tf_op jit(solution)/shard_map/all_to_all | solution.py:428
  149.4 3.4 %collective-permute-start.9 = (bf16[8,8,72,128]{3,2,1,0:T(8,128)(2,1)S(1)}, bf16[8,8,72,128]{3,2,1,0:T(8,128)(2,1)S(1)}, u32[]{:S(2)}, u32[]{:S(2)}) collective-permute-start(bf16[8,8,72,128]{3,2,1,0:T(8,128)(2,1)S(1)} %bitcast.27), channel_id=1, source_target_pairs={{0,1},{1,0},{2,3},{3,2},{4,5},{5,4},{6,7},{7,6},{8,9},{9,8},{10,11... | collective-permute-start | bytes 3538952 | tf_op jit(solution)/shard_map/ppermute | solution.py:656
  152.8 0.5 collective-permute-start.8
  153.3 0.5 slice.3
  154.5 1.5 own_rows.1._
  156.0 0.5 collective-permute-done.8
  156.5 0.6 bitcast_add_fusion
  157.1 0.0 collective-permute-done.9.other_ref
  157.1 1.9 %finish.1 = (f32[1024,1024]{1,0:T(8,128)}, f32[1024,128]{1,0:T(8,128)}, f32[1,1024]{1,0:T(1,128)}) custom-call(s32[1]{0:T(128)} %bitcast.core_ref, bf16[8,8,72,128]{3,2,1,0:T(8,128)(2,1)S(1)} %bitcast.29, bf16[8,8,72,128]{3,2,1,0:T(8,128)(2,1)S(1)} %collective-permute-done.9.other_ref, ...), custom_call_target="tpu_custom_call", output_to_operand_aliasing={{0}: (5, {})} | custom-call | flops 2097152 | bytes 4194304 | tf_op jit(solution)/shard_map/finish/pallas_call | solution.py:490
  (10 shorter events, 0.1 us)
Async XLA Ops:
  4.8 25.8 %all-to-all-start = ((bf16[8,520,128]{2,1,0:T(8,128)(2,1)}), bf16[8,520,128]{2,1,0:T(8,128)(2,1)S(1)}, u32[]{:S(2)}, u32[]{:S(2)}) async-start(bf16[8,520,128]{2,1,0:T(8,128)(2,1)} %passage_copies.1), calls=%async_computation | async-start | bytes 2129920 | tf_op jit(solution)/shard_map/all_to_all | solution.py:428
  11.7 1.8 %collective-permute-start = (bf16[1,136,128]{2,1,0:T(8,128)(2,1)S(1)}, bf16[1,136,128]{2,1,0:T(8,128)(2,1)S(1)}, u32[]{:S(2)}, u32[]{:S(2)}) collective-permute-start(bf16[1,136,128]{2,1,0:T(8,128)(2,1)S(1)} %bitcast.33), channel_id=1, source_target_pairs={{0,1},{1,0},{2,3},{3,2},{4,5},{5,4},{6,7},{7,6},{8,9},{9,8},{10,11... | collective-permute-start | bytes 104456 | tf_op jit(solution)/shard_map/ppermute | solution.py:542
  13.5 3.5 %collective-permute-start.1 = (bf16[2,136,128]{2,1,0:T(8,128)(2,1)S(1)}, bf16[2,136,128]{2,1,0:T(8,128)(2,1)S(1)}, u32[]{:S(2)}, u32[]{:S(2)}) collective-permute-start(bf16[2,136,128]{2,1,0:T(8,128)(2,1)S(1)} %pad_maximum_fusion.2), channel_id=1, source_target_pairs={{0,4},{4,0},{8,12},{12,8},{1,5},{5,1},{9,13},{13,9},{2,6},{6,2},{1... | collective-permute-start | bytes 208904 | tf_op jit(solution)/shard_map/ppermute | solution.py:542
  17.0 5.8 %collective-permute-start.2 = (bf16[4,136,128]{2,1,0:T(8,128)(2,1)S(1)}, bf16[4,136,128]{2,1,0:T(8,128)(2,1)S(1)}, u32[]{:S(2)}, u32[]{:S(2)}) collective-permute-start(bf16[4,136,128]{2,1,0:T(8,128)(2,1)S(1)} %pad_maximum_fusion.1), channel_id=1, source_target_pairs={{0,8},{4,12},{8,0},{12,4},{1,9},{5,13},{9,1},{13,5},{2,10},{6,14},... | collective-permute-start | bytes 417800 | tf_op jit(solution)/shard_map/ppermute | solution.py:542
  22.9 7.7 %collective-permute-start.3 = (bf16[8,136,128]{2,1,0:T(8,128)(2,1)S(1)}, bf16[8,136,128]{2,1,0:T(8,128)(2,1)S(1)}, u32[]{:S(2)}, u32[]{:S(2)}) collective-permute-start(bf16[8,136,128]{2,1,0:T(8,128)(2,1)S(1)} %pad_maximum_fusion.near_ref), channel_id=1, source_target_pairs={{0,2},{2,0},{1,3},{3,1},{4,6},{6,4},{5,7},{7,5},{8,10},{10,8},{9,1... | collective-permute-start | bytes 835592 | tf_op jit(solution)/shard_map/ppermute | solution.py:543
  67.6 5.1 %collective-permute-start.4 = (bf16[2,4,128,128]{3,2,1,0:T(8,128)(2,1)}, bf16[2,4,128,128]{3,2,1,0:T(8,128)(2,1)}, u32[]{:S(2)}, u32[]{:S(2)}) collective-permute-start(bf16[2,4,128,128]{3,2,1,0:T(8,128)(2,1)} %get-tuple-element.63), channel_id=1, source_target_pairs={{0,1},{1,0},{2,3},{3,2},{4,5},{5,4},{6,7},{7,6},{8,9},{9,8},{10,11... | collective-permute-start | bytes 786440 | tf_op jit(solution)/shard_map/ppermute | solution.py:528
  68.0 7.1 %copy-start = (bf16[1024,1024]{1,0:T(8,128)(2,1)S(1)}, bf16[1024,1024]{1,0:T(8,128)(2,1)}, u32[]{:S(2)}) copy-start(bf16[1024,1024]{1,0:T(8,128)(2,1)} %proj_ref.1) | copy-start | bytes 6291460
  68.0 21.7 %all-to-all-start.2 = ((bf16[8,520,128]{2,1,0:T(8,128)(2,1)}), bf16[8,520,128]{2,1,0:T(8,128)(2,1)S(1)}, u32[]{:S(2)}, u32[]{:S(2)}) async-start(bf16[8,520,128]{2,1,0:T(8,128)(2,1)} %get-tuple-element.59), calls=%async_computation.2 | async-start | bytes 2129920 | tf_op jit(solution)/shard_map/all_to_all | solution.py:428
  72.7 2.4 %copy-start.1 = (bf16[512,1024]{1,0:T(8,128)(2,1)S(1)}, bf16[512,1024]{1,0:T(8,128)(2,1)}, u32[]{:S(2)}) copy-start(bf16[512,1024]{1,0:T(8,128)(2,1)} %resid_ref) | copy-start | bytes 3145732
  73.9 15.1 %collective-permute-start.5 = (bf16[4,128,128]{2,1,0:T(8,128)(2,1)S(1)}, bf16[4,128,128]{2,1,0:T(8,128)(2,1)S(1)}, u32[]{:S(2)}, u32[]{:S(2)}) collective-permute-start(bf16[4,128,128]{2,1,0:T(8,128)(2,1)S(1)} %dynamic-slice_bitcast_fusion), channel_id=1, source_target_pairs={{0,2},{2,0},{1,3},{3,1},{4,6},{6,4},{5,7},{7,5},{8,10},{10,8},{9,1... | collective-permute-start | bytes 393224 | tf_op jit(solution)/shard_map/ppermute | solution.py:528
  75.2 1.2 copy-start.2
  76.4 13.3 %copy-start.3 = (bf16[1024,128]{1,0:T(8,128)(2,1)S(1)}, bf16[1024,128]{1,0:T(8,128)(2,1)}, u32[]{:S(2)}) copy-start(bf16[1024,128]{1,0:T(8,128)(2,1)} %colbert_ref.3) | copy-start | bytes 786436
  76.4 13.3 %copy-start.4 = (f32[1024]{0:T(1024)S(1)}, f32[1024]{0:T(1024)}, u32[]{:S(2)}) copy-start(f32[1024]{0:T(1024)} %param.16) | copy-start | bytes 12292
  93.9 3.4 %collective-permute-start.6 = (bf16[8,8,72,128]{3,2,1,0:T(8,128)(2,1)S(1)}, bf16[8,8,72,128]{3,2,1,0:T(8,128)(2,1)S(1)}, u32[]{:S(2)}, u32[]{:S(2)}) collective-permute-start(bf16[8,8,72,128]{3,2,1,0:T(8,128)(2,1)S(1)} %get-tuple-element.76), channel_id=1, source_target_pairs={{0,1},{1,0},{2,3},{3,2},{4,5},{5,4},{6,7},{7,6},{8,9},{9,8},{10,11... | collective-permute-start | bytes 3538952 | tf_op jit(solution)/shard_map/ppermute | solution.py:528
  98.6 27.8 %all-to-all-start.3 = ((bf16[64,72,128]{2,1,0:T(8,128)(2,1)}), bf16[64,72,128]{2,1,0:T(8,128)(2,1)S(1)}, u32[]{:S(2)}, u32[]{:S(2)}) async-start(bf16[64,72,128]{2,1,0:T(8,128)(2,1)} %bitcast.32), calls=%async_computation.3 | async-start | bytes 2359296 | tf_op jit(solution)/shard_map/all_to_all | solution.py:428
  108.0 15.7 %collective-permute-start.7 = (bf16[2,128,128]{2,1,0:T(8,128)(2,1)S(1)}, bf16[2,128,128]{2,1,0:T(8,128)(2,1)S(1)}, u32[]{:S(2)}, u32[]{:S(2)}) collective-permute-start(bf16[2,128,128]{2,1,0:T(8,128)(2,1)S(1)} %dynamic-slice_bitcast_fusion.2), channel_id=1, source_target_pairs={{0,8},{4,12},{8,0},{12,4},{1,9},{5,13},{9,1},{13,5},{2,10},{6,14},... | collective-permute-start | bytes 196616 | tf_op jit(solution)/shard_map/ppermute | solution.py:528
  110.5 13.2 %copy-start.5 = (bf16[4,128,128]{2,1,0:T(8,128)(2,1)S(1)}, bf16[4,128,128]{2,1,0:T(8,128)(2,1)}, u32[]{:S(2)}) copy-start(bf16[4,128,128]{2,1,0:T(8,128)(2,1)} %fusion) | copy-start | bytes 393220
  149.4 7.7 %collective-permute-start.9 = (bf16[8,8,72,128]{3,2,1,0:T(8,128)(2,1)S(1)}, bf16[8,8,72,128]{3,2,1,0:T(8,128)(2,1)S(1)}, u32[]{:S(2)}, u32[]{:S(2)}) collective-permute-start(bf16[8,8,72,128]{3,2,1,0:T(8,128)(2,1)S(1)} %bitcast.27), channel_id=1, source_target_pairs={{0,1},{1,0},{2,3},{3,2},{4,5},{5,4},{6,7},{7,6},{8,9},{9,8},{10,11... | collective-permute-start | bytes 3538952 | tf_op jit(solution)/shard_map/ppermute | solution.py:656
  152.8 3.7 %collective-permute-start.8 = (f32[128,128]{1,0:T(8,128)S(1)}, f32[128,128]{1,0:T(8,128)S(1)}, u32[]{:S(2)}, u32[]{:S(2)}) collective-permute-start(f32[128,128]{1,0:T(8,128)S(1)} %dynamic-slice_bitcast_fusion.1), channel_id=1, source_target_pairs={{0,4},{4,0},{8,12},{12,8},{1,5},{5,1},{9,13},{13,9},{2,6},{6,2},{1... | collective-permute-start | bytes 196616 | tf_op jit(solution)/shard_map/ppermute | solution.py:528
